TPU v7x, 256 devices: a whole 4x4x8 slice. The times are simulated.
256 devices in a mesh: fsdp: 16 (over z, x_hi), tp: 16 (over x_lo, y, core).
Axes of the slice: x: 4 (x_hi: 2, x_lo: 2; x = x_hi * 2 + x_lo), y: 4, z: 8, core: 2. Of those that a mesh axis runs over, the one named last changes fastest.
Arguments:
- grad_out: bfloat16 [4096, 8192], P('fsdp', 'tp'), may hold values from -6 to 6
- down_q: bfloat16 [14336, 8192], P('fsdp', 'tp'), may hold values from -0.0625 to 0.0625
- scales: bfloat16 [112, 64], P('fsdp', 'tp'), may hold values from 0.25 to 4
- gate_act: bfloat16 [4096, 14336], P('fsdp', 'tp'), may hold values from -6 to 6
- up_act: bfloat16 [4096, 14336], P('fsdp', 'tp'), may hold values from -6 to 6
Outputs:
- grad_gate: bfloat16 [4096, 14336], P('fsdp', 'tp')
- grad_up: bfloat16 [4096, 14336], P('fsdp', 'tp')
All inputs are finite; a program needn't handle non-finite values.
Results may differ from a plain program's by a relative error of at most 0.005.
Values may be sent and summed in bfloat16 or wider, within the bound.
No kernel may reach another device: no remote copies, remote signals or barrier semaphores. Data moves between devices by JAX's collectives and lax.ppermute only.
A program may use at most 128 MiB of HBM per device.

v0:
```python
import jax
import jax.numpy as jnp
from jax import lax
from jax.sharding import PartitionSpec as P

BLOCK = 128


def dequantize(blocks, scales):
    count, height, width = blocks.shape
    grid = blocks.astype(jnp.float32).reshape(count, height, width // BLOCK, BLOCK)
    grid = grid * scales.astype(jnp.float32)[:, None, :, None]
    return grid.reshape(count, height, width).astype(jnp.bfloat16)


def on_device(grad_out, down_q, scales, gate_act, up_act):
    columns = grad_out.shape[1]
    blocks = down_q.reshape(-1, BLOCK, columns)
    flat = dequantize(
        lax.all_gather(blocks, "fsdp", axis=0, tiled=True),
        lax.all_gather(scales, "fsdp", axis=0, tiled=True),
    ).reshape(-1, columns)
    partial_value = lax.dot_general(
        grad_out, flat, (((1,), (1,)), ((), ())), preferred_element_type=jnp.float32
    )
    grad_hidden = lax.psum_scatter(partial_value, "tp", scatter_dimension=1, tiled=True)
    gate_val = gate_act.astype(jnp.float32)
    sigmoid_gate = jax.nn.sigmoid(gate_val)
    grad_up = (grad_hidden * gate_val * sigmoid_gate).astype(jnp.bfloat16)
    slope = sigmoid_gate * (1.0 + gate_val * (1.0 - sigmoid_gate))
    grad_gate = (grad_hidden * up_act.astype(jnp.float32) * slope).astype(jnp.bfloat16)
    return (grad_gate, grad_up)


def solution(mesh):
    return jax.shard_map(
        on_device,
        mesh=mesh,
        in_specs=(
            P("fsdp", "tp"),
            P("fsdp", "tp"),
            P("fsdp", "tp"),
            P("fsdp", "tp"),
            P("fsdp", "tp"),
        ),
        out_specs=(P("fsdp", "tp"), P("fsdp", "tp")),
        check_vma=False,
    )
```

profile of v0, /device:TPU:7, one launch (start us, length us, event | category | flops | bytes accessed | tf_op | source)
XLA Modules:
  0.0 327.1 jit_solution(14206767933081755567)
XLA Ops:
  7.2 0.0 copy-start
  7.2 0.0 all-gather.3.cloned.1.call-start
  7.2 0.7 all-gather.3.cloned.1.call-update
  7.9 0.0 reduce-scatter.2.cloned.1.call-start
  8.0 33.4 %all-gather = bf16[16,7,4]{1,2,0:T(4,128)(2,1)S(1)} all-gather(bf16[1,7,4]{1,2,0:T(4,128)(2,1)} %bitcast.17), channel_id=1, replica_groups=mesh['fsdp'=16,'tp'=16] {'fsdp'}, dimensions={0}, use_global_device_ids=true | all-gather | bytes 952 | tf_op jit(solution)/shard_map/all_gather | solution.py:21
  41.3 0.1 copy.23
  41.5 0.1 copy.24
  41.6 0.1 reshape.18
  41.7 0.1 copy.25
  41.8 0.2 mul.31
  42.0 171.3 %all-gather.3.cloned.1.call-done = bf16[112,128,512]{2,1,0:T(8,128)(2,1)} async-done(((bf16[7,128,512]{2,1,0:T(8,128)(2,1)}), bf16[112,128,512]{2,1,0:T(8,128)(2,1)}) %all-gather.3.cloned.1.call-update) | async-done | bytes 14680080 | tf_op jit(solution)/shard_map/all_gather | solution.py:20
  213.3 8.3 %multiply_convert_fusion = bf16[112,128,512]{2,1,0:T(8,128)(2,1)S(1)} fusion(bf16[112,128,512]{2,1,0:T(8,128)(2,1)} %all-gather.3.cloned.1.call-done, f32[112,512]{1,0:T(8,128)S(1)} %bitcast.16), kind=kLoop, calls=%fused_computation | loop fusion | flops 22020096 | bytes 29589504 | tf_op jit(solution)/shard_map/convert_element_type | solution.py:13
  221.6 0.0 copy-done
  221.7 7.3 %convolution_bitcast_fusion = f32[256,14336]{0,1:T(8,128)} fusion(bf16[14336,512]{1,0:T(8,128)(2,1)S(1)} %bitcast.13, bf16[256,512]{1,0:T(8,128)(2,1)S(1)} %copy-done), kind=kOutput, calls=%fused_computation.1 | convolution fusion | flops 3758096384 | bytes 29622272 | tf_op jit(solution)/shard_map/dot_general | solution.py:23
  229.0 0.0 copy-start.1
  229.0 0.0 copy-start.2
  229.0 0.0 reduce-scatter.2.cloned.1.call-update
  229.0 1.0 copy-done.1
  230.0 0.2 copy.27
  230.2 0.0 copy-done.2
  230.2 0.2 copy.26
  230.4 86.3 %reduce-scatter.2.cloned.1.call-done = f32[256,896]{0,1:T(8,128)} async-done(((f32[256,14336]{0,1:T(8,128)}), f32[256,896]{0,1:T(8,128)}) %reduce-scatter.2.cloned.1.call-update) | async-done | bytes 917520 | tf_op jit(solution)/shard_map/reduce_scatter | solution.py:26
  316.7 1.6 fusion.8
  318.3 1.0 copy.29
  319.3 1.0 copy.28
  (1 shorter events, 0.0 us)
Async XLA Ops:
  7.2 214.5 %copy-start = (bf16[256,512]{1,0:T(8,128)(2,1)S(1)}, bf16[256,512]{1,0:T(8,128)(2,1)}, u32[]{:S(2)}) copy-start(bf16[256,512]{1,0:T(8,128)(2,1)} %param.5) | copy-start | bytes 786436
  7.2 206.1 %all-gather.3.cloned.1.call-start = ((), (), s32[]{:S(2)}) async-start(), calls=%async_computation.1 | async-start | bytes 15597568 | tf_op jit(solution)/shard_map/all_gather | solution.py:20
  7.9 308.8 %reduce-scatter.2.cloned.1.call-start = ((), (), s32[]{:S(2)}) async-start(), calls=%async_computation.2 | async-start | bytes 15597568 | tf_op jit(solution)/shard_map/reduce_scatter | solution.py:26
  229.0 1.0 copy-start.1
  229.0 1.2 copy-start.2
Sparse Core Ops, SparseCore 0:
  10.6 202.6 all-gather.2
  229.1 87.5 reduce-scatter.1
where the time goes:
time: 329 us; the launch traced here: 327 us
  waiting for transfers between devices  258 us (78%)
  blocking collectives  33.4 us (10%)
  between operations  14.1 us (4%)
  other arithmetic  9.95 us (3%)
  matrix products  7.32 us (2%)
  local copies, waits for them, and re-layouts  4.01 us (1%)
    all_gather x1, waiting for transfers between devices, on_device(): lax.all_gather(blocks, 'fsdp', axis=0, tiled=True)  171 us
    reduce_scatter x1, waiting for transfers between devices, on_device(): lax.psum_scatter(partial_value, 'tp', scatter_dimension=1, tiled=True)  86.3 us
    all_gather x1, blocking collectives, on_device(): lax.all_gather(scales, 'fsdp', axis=0, tiled=True)  33.4 us
    convert_element_type x1, other arithmetic, dequantize(): return grid.reshape(count, height, width).astype(jnp.bfloat16)  8.32 us
    dot_general x1, matrix products, on_device(): lax.dot_general(grad_out, flat, (((1,), (1,)), ((), ())), preferred_eleme...  7.32 us
  transfers between devices with their start and end apart: 2, of which 2 were waited for; matrix products, arithmetic and copies ran while one was open for 0% of the time, Pallas kernels for 0%

commit v1 on v0

v1 whole, which is shorter than its diff:
```python
import numpy as np
import jax
import jax.numpy as jnp
from jax import lax
from jax.experimental import pallas as pl
from jax.experimental.pallas import tpu as pltpu
from jax.sharding import Mesh, PartitionSpec as P

BLOCK = 128
Z, XH, XL, Y, C = 8, 2, 2, 4, 2
S = XL * Y
FSDP = ("z", "xh")
TP = ("xl", "y", "c")
ALL = FSDP + TP
BF16, F32 = jnp.bfloat16, jnp.float32

STEP = (0, 2, 4, 6, 1, 3, 5, 7)
PLACE = (0, 1, 3, 5, 6, 7, 4, 2)


def device_index(z, xh, s, c):
    return ((z * XH + xh) * S + s) * C + c


def home_pairs():
    pairs = []
    for z in range(Z):
        sign = 1 if z % 2 == 0 else -1
        for xh in range(XH):
            for s in range(S):
                for c in range(C):
                    to = (z + sign * (STEP[s] + 4 * c)) % Z
                    pairs.append((device_index(z, xh, s, c), device_index(to, xh, z, c)))
    return pairs


def shift(x, axis, size, by):
    return lax.ppermute(x, axis, [(i, (i + by) % size) for i in range(size)])


def dequantize(values, scales):
    rows, cols = values.shape
    grid = values.astype(F32).reshape(rows // BLOCK, BLOCK, cols // BLOCK, BLOCK)
    grid = grid * scales.astype(F32)[:, None, :, None]
    return grid.reshape(rows, cols).astype(BF16)


def product(order, a_own, a_other, w_own, w_other):
    count, rows, depth = a_own.shape
    width = w_own.shape[0]
    dims = (((1,), (1,)), ((), ()))

    def kernel(order_ref, a_own_ref, a_other_ref, w_own_ref, w_other_ref, out_ref):
        total = lax.dot_general(a_own_ref[0], w_own_ref[...], dims, preferred_element_type=F32)
        total += lax.dot_general(a_other_ref[0], w_other_ref[...], dims, preferred_element_type=F32)
        out_ref[0] = total.astype(BF16)

    a_spec = pl.BlockSpec((1, rows, depth), lambda i, order: (order[i], 0, 0))
    w_spec = pl.BlockSpec((width, depth), lambda i, order: (0, 0))
    return pl.pallas_call(
        kernel,
        grid_spec=pltpu.PrefetchScalarGridSpec(
            num_scalar_prefetch=1,
            grid=(count,),
            in_specs=[a_spec, a_spec, w_spec, w_spec],
            out_specs=pl.BlockSpec((1, rows, width), lambda i, order: (i, 0, 0)),
        ),
        out_shape=jax.ShapeDtypeStruct((count, rows, width), BF16),
        compiler_params=pltpu.CompilerParams(vmem_limit_bytes=24 * 2**20),
        cost_estimate=pl.CostEstimate(
            flops=4 * count * rows * depth * width,
            bytes_accessed=2 * (2 * count * rows * depth + 2 * width * depth + count * rows * width),
            transcendentals=0,
        ),
    )(order, a_own, a_other, w_own, w_other)


def on_device(grad_out, down_q, scales, gate_act, up_act):
    z, xh, c = (lax.axis_index(name) for name in ("z", "xh", "c"))

    weight = dequantize(down_q, scales)
    home = xh == c
    at = lambda h, k: h * C + k
    first = lax.ppermute(
        weight, ("xh", "c"), [(at(0, 0), at(1, 0)), (at(1, 1), at(0, 1)), (at(0, 1), at(0, 0)), (at(1, 0), at(1, 1))]
    )
    second = lax.ppermute(weight, ("xh", "c"), [(at(0, 1), at(1, 0)), (at(1, 0), at(0, 1))])
    w_own = jnp.where(home, weight, first)
    w_other = jnp.where(home, first, second)

    half = grad_out.shape[0] // 2
    ahead, behind = [grad_out], [grad_out]
    for _ in range(3):
        behind.append(shift(behind[-1], "z", Z, 1))
        ahead.append(shift(ahead[-1], "z", Z, -1))
    far = jnp.concatenate([shift(behind[3][:half], "z", Z, 1), shift(ahead[3][half:], "z", Z, -1)], 0)
    near_own = jnp.stack([grad_out, ahead[1], behind[1], ahead[2], behind[2]])
    far_own = jnp.stack([ahead[3], far, behind[3]])
    near_other = shift(near_own, "c", C, 1)
    far_other = shift(far_own, "c", C, 1)
    a_own = jnp.concatenate([near_own, far_own], 0)
    a_other = jnp.concatenate([near_other, far_other], 0)

    sign = jnp.where(z % 2 == 0, 1, -1)
    planes = (sign * (jnp.array(STEP, jnp.int32) + 4 * c)) % Z
    order = jnp.array(PLACE, jnp.int32)[planes]

    partial_value = product(order, a_own, a_other, w_own, w_other)
    parts = lax.all_to_all(partial_value, ("xl", "y"), split_axis=0, concat_axis=0, tiled=True)
    summed = parts.astype(F32).sum(0).astype(BF16)
    grad_hidden = lax.ppermute(summed, ALL, home_pairs()).astype(F32)

    gate_val = gate_act.astype(F32)
    sigmoid_gate = jax.nn.sigmoid(gate_val)
    grad_up = (grad_hidden * gate_val * sigmoid_gate).astype(BF16)
    slope = sigmoid_gate * (1.0 + gate_val * (1.0 - sigmoid_gate))
    grad_gate = (grad_hidden * up_act.astype(F32) * slope).astype(BF16)
    return (grad_gate, grad_up)


def solution(mesh):
    fine = Mesh(mesh.devices.reshape(Z, XH, XL, Y, C), ALL)
    spec = P(FSDP, TP)
    return jax.shard_map(
        on_device, mesh=fine, in_specs=(spec,) * 5, out_specs=(spec, spec), check_vma=False
    )
```

time: 329 us -> 129 us (0.39)
  the two profiles are of different devices: /device:TPU:7 before, /device:TPU:2 now
where the time goes in v1:
time: 129 us
  blocking collectives  49.3 us (38%)
  waiting for transfers between devices  33 us (26%)
  starting transfers between devices  21.7 us (17%)
  other arithmetic  9.56 us (7%)
  local copies, waits for them, and re-layouts  7.75 us (6%)
  Pallas kernels  6.49 us (5%)
    all_to_all x1, blocking collectives, on_device(): lax.all_to_all(partial_value, ('xl', 'y'), split_axis=0, concat_axis=0, t...  49.3 us
    ppermute x1, waiting for transfers between devices, on_device(): grad_hidden = lax.ppermute(summed, ALL, home_pairs()).astype(F32)  19.8 us
    ppermute x10, starting transfers between devices, shift(): return lax.ppermute(x, axis, [(i, (i + by) % size) for i in range(size)])  16 us
    ppermute x10, waiting for transfers between devices, shift(): return lax.ppermute(x, axis, [(i, (i + by) % size) for i in range(size)])  13.2 us
    pallas_call x1, Pallas kernels, product(): pl.pallas_call(kernel, grid_spec=pltpu.PrefetchScalarGridSpec(num_scalar_...  6.49 us
    unnamed x17, local copies, waits for them, and re-layouts  3.94 us
    reduce_sum x1, other arithmetic, on_device(): summed = parts.astype(F32).sum(0).astype(BF16)  2.82 us
  transfers between devices with their start and end apart: 13, of which 5 were waited for; matrix products, arithmetic and copies ran while one was open for 9% of the time, Pallas kernels for 0%

profile of v1, /device:TPU:2, one launch (start us, length us, event | category | flops | bytes accessed | tf_op | source)
XLA Modules:
  0.0 128.6 jit_solution(12425498115879176083)
XLA Ops:
  0.6 5.9 %collective-permute-start = (bf16[256,512]{1,0:T(8,128)(2,1)}, bf16[256,512]{1,0:T(8,128)(2,1)S(1)}, u32[]{:S(2)}, u32[]{:S(2)}) collective-permute-start(bf16[256,512]{1,0:T(8,128)(2,1)} %param.7), channel_id=1, source_target_pairs={{0,224},{32,0},{64,32},{96,64},{128,96},{160,128},{192,160},{224,1... | collective-permute-start | bytes 786440 | tf_op jit(solution)/shard_map/ppermute | solution.py:38
  6.6 0.0 collective-permute-start.1
  6.6 0.8 copy.10
  7.3 0.3 mul.37
  7.7 0.0 copy-start.4
  7.7 0.4 fusion
  8.0 2.2 %collective-permute-start.10 = (bf16[896,512]{1,0:T(8,128)(2,1)S(1)}, bf16[896,512]{1,0:T(8,128)(2,1)}, u32[]{:S(2)}, u32[]{:S(2)}) collective-permute-start(bf16[896,512]{1,0:T(8,128)(2,1)S(1)} %fusion), channel_id=1, source_target_pairs={{0,16},{17,1},{1,0},{16,17},{2,18},{19,3},{3,2},{18,19},{4,20},{21... | collective-permute-start | bytes 2752520 | tf_op jit(solution)/shard_map/ppermute | solution.py:84
  10.3 1.6 %collective-permute-start.11 = (bf16[896,512]{1,0:T(8,128)(2,1)S(1)}, bf16[896,512]{1,0:T(8,128)(2,1)}, u32[]{:S(2)}, u32[]{:S(2)}) collective-permute-start(bf16[896,512]{1,0:T(8,128)(2,1)S(1)} %fusion), channel_id=1, source_target_pairs={{1,16},{16,1},{3,18},{18,3},{5,20},{20,5},{7,22},{22,7},{9,24},{24... | collective-permute-start | bytes 2752520 | tf_op jit(solution)/shard_map/ppermute | solution.py:87
  11.9 0.7 bitcast_dynamic-update-slice_fusion.8
  12.6 0.0 collective-permute-done
  12.6 3.4 %collective-permute-start.2 = (bf16[256,512]{1,0:T(8,128)(2,1)S(1)}, bf16[256,512]{1,0:T(8,128)(2,1)S(1)}, u32[]{:S(2)}, u32[]{:S(2)}) collective-permute-start(bf16[256,512]{1,0:T(8,128)(2,1)S(1)} %collective-permute-done), channel_id=1, source_target_pairs={{0,224},{32,0},{64,32},{96,64},{128,96},{160,128},{192,160},{224,1... | collective-permute-start | bytes 786440 | tf_op jit(solution)/shard_map/ppermute | solution.py:38
  16.0 0.0 collective-permute-done.1
  16.0 0.0 collective-permute-start.3
  16.0 0.7 bitcast_dynamic-update-slice_fusion.6
  16.8 1.7 %bitcast_dynamic-update-slice_fusion.4 = (bf16[5,256,512]{2,1,0:T(8,128)(2,1)}, bf16[8,256,512]{2,1,0:T(8,128)(2,1)S(1)}) fusion(bf16[5,256,512]{2,1,0:T(8,128)(2,1)} %get-tuple-element.12, bf16[256,512]{1,0:T(8,128)(2,1)} %collective-permute-done.1, bf16[8,256,512]{2,1,0:T(8,128)(2,1)S(1)} %get-tuple-element.13), kind=kLoop, calls=%fused_computation.25 | loop fusion | bytes 786432
  18.5 7.2 %collective-permute-done.3 = bf16[256,512]{1,0:T(8,128)(2,1)S(1)} collective-permute-done((bf16[256,512]{1,0:T(8,128)(2,1)}, bf16[256,512]{1,0:T(8,128)(2,1)S(1)}, u32[]{:S(2)}, u32[]{:S(2)}) %collective-permute-start.3) | collective-permute-done | bytes 262176 | tf_op jit(solution)/shard_map/ppermute | solution.py:38
  25.7 0.0 collective-permute-start.5
  25.7 0.0 collective-permute-done.2
  25.7 3.2 %collective-permute-start.4 = (bf16[256,512]{1,0:T(8,128)(2,1)S(1)}, bf16[256,512]{1,0:T(8,128)(2,1)S(1)}, u32[]{:S(2)}, u32[]{:S(2)}) collective-permute-start(bf16[256,512]{1,0:T(8,128)(2,1)S(1)} %collective-permute-done.2), channel_id=1, source_target_pairs={{0,224},{32,0},{64,32},{96,64},{128,96},{160,128},{192,160},{224,1... | collective-permute-start | bytes 786440 | tf_op jit(solution)/shard_map/ppermute | solution.py:38
  28.9 0.7 bitcast_dynamic-update-slice_fusion.2
  29.7 0.7 bitcast_dynamic-update-slice_fusion
  30.4 0.0 collective-permute-start.8
  30.4 3.8 %collective-permute-done.5 = bf16[256,512]{1,0:T(8,128)(2,1)S(1)} collective-permute-done((bf16[256,512]{1,0:T(8,128)(2,1)S(1)}, bf16[256,512]{1,0:T(8,128)(2,1)S(1)}, u32[]{:S(2)}, u32[]{:S(2)}) %collective-permute-start.5) | collective-permute-done | bytes 262176 | tf_op jit(solution)/shard_map/ppermute | solution.py:38
  34.2 0.7 slice.10
  34.9 0.0 collective-permute-start.6
  34.9 0.0 collective-permute-done.4
  34.9 0.7 slice.11
  35.6 3.2 %collective-permute-start.7 = (bf16[128,512]{1,0:T(8,128)(2,1)}, bf16[128,512]{1,0:T(8,128)(2,1)}, u32[]{:S(2)}, u32[]{:S(2)}) collective-permute-start(bf16[128,512]{1,0:T(8,128)(2,1)} %slice.11), channel_id=1, source_target_pairs={{0,224},{32,0},{64,32},{96,64},{128,96},{160,128},{192,160},{224,1... | collective-permute-start | bytes 393224 | tf_op jit(solution)/shard_map/ppermute | solution.py:38
  38.9 0.0 copy-done
  38.9 0.6 gather_fusion
  39.5 1.9 %collective-permute-done.6 = bf16[128,512]{1,0:T(8,128)(2,1)} collective-permute-done((bf16[128,512]{1,0:T(8,128)(2,1)}, bf16[128,512]{1,0:T(8,128)(2,1)}, u32[]{:S(2)}, u32[]{:S(2)}) %collective-permute-start.6) | collective-permute-done | bytes 131104 | tf_op jit(solution)/shard_map/ppermute | solution.py:38
  41.4 0.2 collective-permute-done.7
  41.7 1.0 maximum_bitcast_fusion
  42.6 0.1 pad_maximum_fusion.1
  42.7 0.1 collective-permute-start.9
  42.9 1.0 constant_dynamic-update-slice_fusion.1
  43.9 0.0 collective-permute-done.10
  43.9 0.0 collective-permute-done.11
  43.9 1.4 %broadcast_select_fusion = (bf16[896,512]{1,0:T(8,128)(2,1)S(1)}, bf16[896,512]{1,0:T(8,128)(2,1)S(1)}) fusion(bf16[896,512]{1,0:T(8,128)(2,1)} %collective-permute-done.10, bf16[896,512]{1,0:T(8,128)(2,1)} %collective-permute-done.11, pred[]{:T(512)S(6)} %eq.11, bf16[896,512]{1,0:T(8,128)(2,1)S(1)} %fusion), kind=kLoop, calls=%fused_computation.17 | loop fusion | flops 917504 | bytes 4587521 | tf_op jit(solution)/shard_map/jit(_where)/select_n | solution.py:89
  45.3 0.0 collective-permute-done.9
  45.3 0.0 collective-permute-done.8
  45.3 1.5 %pad_maximum_fusion.a_other_ref = bf16[8,256,512]{2,1,0:T(8,128)(2,1)S(1)} fusion(bf16[3,256,512]{2,1,0:T(8,128)(2,1)S(1)} %collective-permute-done.9, bf16[5,256,512]{2,1,0:T(8,128)(2,1)} %collective-permute-done.8), kind=kLoop, calls=%fused_computation.1 | loop fusion | flops 1048576 | bytes 4194304 | tf_op jit(solution)/shard_map/concatenate | solution.py:102
  46.8 6.5 %shard_map.86 = bf16[8,256,896]{2,1,0:T(8,128)(2,1)S(1)} custom-call(s32[8]{0:T(128)S(1)} %gather_fusion, bf16[8,256,512]{2,1,0:T(8,128)(2,1)S(1)} %constant_dynamic-update-slice_fusion.a_own_ref, bf16[8,256,512]{2,1,0:T(8,128)(2,1)S(1)} %pad_maximum_fusion.a_other_ref, bf16[896,512]{1,0:T(8,128)(2,1)S(1)} %get-tuple-element.5.w_own_ref, ...), custom_call_target="tpu_custom_call" | custom-call | flops 3758096384 | bytes 9699328 | tf_op jit(solution)/shard_map/pallas_call | solution.py:60
  53.3 49.3 %all_to_all.5 = bf16[8,256,896]{2,1,0:T(8,128)(2,1)} all-to-all(bf16[8,256,896]{2,1,0:T(8,128)(2,1)S(1)} %shard_map.86), channel_id=1, replica_groups=mesh['z'=8,'xh'=2,'xl'=2,'y'=4,'c'=2] {'xl','y'}, dimensions={0} | all-to-all | bytes 7340032 | tf_op jit(solution)/shard_map/all_to_all | solution.py:109
  102.6 2.8 %reduce_sum.12 = bf16[256,896]{1,0:T(8,128)(2,1)S(1)} reduce(bf16[8,256,896]{2,1,0:T(8,128)(2,1)} %all_to_all.5, bf16[]{:T(256)} %constant.56.clone.1), dimensions={0}, to_apply=%region_0.1 | reduce | flops 1605632 | bytes 4128770 | tf_op jit(solution)/shard_map/reduce_sum | solution.py:110
  105.5 1.9 %collective-permute-start.12 = (bf16[256,896]{1,0:T(8,128)(2,1)S(1)}, bf16[256,896]{1,0:T(8,128)(2,1)S(1)}, u32[]{:S(2)}, u32[]{:S(2)}) collective-permute-start(bf16[256,896]{1,0:T(8,128)(2,1)S(1)} %reduce_sum.12), channel_id=1, source_target_pairs={{0,0},{1,129},{2,64},{3,193},{4,128},{5,1},{6,192},{7,65},{8,32},{... | collective-permute-start | bytes 1376264 | tf_op jit(solution)/shard_map/ppermute | solution.py:111
  107.4 19.8 %collective-permute-done.12 = bf16[256,896]{1,0:T(8,128)(2,1)S(1)} collective-permute-done((bf16[256,896]{1,0:T(8,128)(2,1)S(1)}, bf16[256,896]{1,0:T(8,128)(2,1)S(1)}, u32[]{:S(2)}, u32[]{:S(2)}) %collective-permute-start.12) | collective-permute-done | bytes 458784 | tf_op jit(solution)/shard_map/ppermute | solution.py:111
  127.2 1.4 %fusion.9 = (bf16[256,896]{1,0:T(8,128)(2,1)}, bf16[256,896]{1,0:T(8,128)(2,1)}) fusion(bf16[256,896]{1,0:T(8,128)(2,1)S(1)} %copy-done.2, bf16[256,896]{1,0:T(8,128)(2,1)S(1)} %collective-permute-done.12, bf16[256,896]{1,0:T(8,128)(2,1)S(1)} %copy-done.3), kind=kLoop, calls=%fused_computation.16 | loop fusion | flops 3670016 | bytes 2293760 | tf_op jit(solution)/shard_map/convert_element_type | solution.py:115
  (14 shorter events, 0.1 us)
Async XLA Ops:
  0.6 7.0 %copy-start.1 = (bf16[896,512]{1,0:T(8,128)(2,1)S(1)}, bf16[896,512]{1,0:T(8,128)(2,1)}, u32[]{:S(2)}) copy-start(bf16[896,512]{1,0:T(8,128)(2,1)} %param.8) | copy-start | bytes 2752516
  0.6 12.0 %collective-permute-start = (bf16[256,512]{1,0:T(8,128)(2,1)}, bf16[256,512]{1,0:T(8,128)(2,1)S(1)}, u32[]{:S(2)}, u32[]{:S(2)}) collective-permute-start(bf16[256,512]{1,0:T(8,128)(2,1)} %param.7), channel_id=1, source_target_pairs={{0,224},{32,0},{64,32},{96,64},{128,96},{160,128},{192,160},{224,1... | collective-permute-start | bytes 786440 | tf_op jit(solution)/shard_map/ppermute | solution.py:38
  6.6 9.5 %collective-permute-start.1 = (bf16[256,512]{1,0:T(8,128)(2,1)}, bf16[256,512]{1,0:T(8,128)(2,1)}, u32[]{:S(2)}, u32[]{:S(2)}) collective-permute-start(bf16[256,512]{1,0:T(8,128)(2,1)} %param.7), channel_id=1, source_target_pairs={{0,32},{32,64},{64,96},{96,128},{128,160},{160,192},{192,224},{224... | collective-permute-start | bytes 786440 | tf_op jit(solution)/shard_map/ppermute | solution.py:38
  7.7 4.2 %copy-start.4 = (bf16[256,512]{1,0:T(8,128)(2,1)S(1)}, bf16[256,512]{1,0:T(8,128)(2,1)}, u32[]{:S(2)}) copy-start(bf16[256,512]{1,0:T(8,128)(2,1)} %param.7) | copy-start | bytes 786436
  8.0 35.8 %collective-permute-start.10 = (bf16[896,512]{1,0:T(8,128)(2,1)S(1)}, bf16[896,512]{1,0:T(8,128)(2,1)}, u32[]{:S(2)}, u32[]{:S(2)}) collective-permute-start(bf16[896,512]{1,0:T(8,128)(2,1)S(1)} %fusion), channel_id=1, source_target_pairs={{0,16},{17,1},{1,0},{16,17},{2,18},{19,3},{3,2},{18,19},{4,20},{21... | collective-permute-start | bytes 2752520 | tf_op jit(solution)/shard_map/ppermute | solution.py:84
  10.3 33.6 %collective-permute-start.11 = (bf16[896,512]{1,0:T(8,128)(2,1)S(1)}, bf16[896,512]{1,0:T(8,128)(2,1)}, u32[]{:S(2)}, u32[]{:S(2)}) collective-permute-start(bf16[896,512]{1,0:T(8,128)(2,1)S(1)} %fusion), channel_id=1, source_target_pairs={{1,16},{16,1},{3,18},{18,3},{5,20},{20,5},{7,22},{22,7},{9,24},{24... | collective-permute-start | bytes 2752520 | tf_op jit(solution)/shard_map/ppermute | solution.py:87
  11.9 27.0 %copy-start.5 = (s32[8]{0:T(128)S(1)}, s32[8]{0:T(128)}, u32[]{:S(2)}) copy-start(s32[8]{0:T(128)} %constant.58.clone) | copy-start | bytes 100
  11.9 27.0 %copy-start = (s32[8]{0:T(128)S(1)}, s32[8]{0:T(128)}, u32[]{:S(2)}) copy-start(s32[8]{0:T(128)} %constant.59.clone) | copy-start | bytes 100
  12.6 13.1 %collective-permute-start.2 = (bf16[256,512]{1,0:T(8,128)(2,1)S(1)}, bf16[256,512]{1,0:T(8,128)(2,1)S(1)}, u32[]{:S(2)}, u32[]{:S(2)}) collective-permute-start(bf16[256,512]{1,0:T(8,128)(2,1)S(1)} %collective-permute-done), channel_id=1, source_target_pairs={{0,224},{32,0},{64,32},{96,64},{128,96},{160,128},{192,160},{224,1... | collective-permute-start | bytes 786440 | tf_op jit(solution)/shard_map/ppermute | solution.py:38
  16.0 9.6 %collective-permute-start.3 = (bf16[256,512]{1,0:T(8,128)(2,1)}, bf16[256,512]{1,0:T(8,128)(2,1)S(1)}, u32[]{:S(2)}, u32[]{:S(2)}) collective-permute-start(bf16[256,512]{1,0:T(8,128)(2,1)} %collective-permute-done.1), channel_id=1, source_target_pairs={{0,32},{32,64},{64,96},{96,128},{128,160},{160,192},{192,224},{224... | collective-permute-start | bytes 786440 | tf_op jit(solution)/shard_map/ppermute | solution.py:38
  25.7 8.6 %collective-permute-start.5 = (bf16[256,512]{1,0:T(8,128)(2,1)S(1)}, bf16[256,512]{1,0:T(8,128)(2,1)S(1)}, u32[]{:S(2)}, u32[]{:S(2)}) collective-permute-start(bf16[256,512]{1,0:T(8,128)(2,1)S(1)} %collective-permute-done.3), channel_id=1, source_target_pairs={{0,32},{32,64},{64,96},{96,128},{128,160},{160,192},{192,224},{224... | collective-permute-start | bytes 786440 | tf_op jit(solution)/shard_map/ppermute | solution.py:38
  25.7 9.2 %collective-permute-start.4 = (bf16[256,512]{1,0:T(8,128)(2,1)S(1)}, bf16[256,512]{1,0:T(8,128)(2,1)S(1)}, u32[]{:S(2)}, u32[]{:S(2)}) collective-permute-start(bf16[256,512]{1,0:T(8,128)(2,1)S(1)} %collective-permute-done.2), channel_id=1, source_target_pairs={{0,224},{32,0},{64,32},{96,64},{128,96},{160,128},{192,160},{224,1... | collective-permute-start | bytes 786440 | tf_op jit(solution)/shard_map/ppermute | solution.py:38
  30.4 14.9 %collective-permute-start.8 = (bf16[5,256,512]{2,1,0:T(8,128)(2,1)}, bf16[5,256,512]{2,1,0:T(8,128)(2,1)}, u32[]{:S(2)}, u32[]{:S(2)}) collective-permute-start(bf16[5,256,512]{2,1,0:T(8,128)(2,1)} %get-tuple-element.6), channel_id=1, source_target_pairs={{0,1},{1,0},{2,3},{3,2},{4,5},{5,4},{6,7},{7,6},{8,9},{9,8},{10,11... | collective-permute-start | bytes 3932168 | tf_op jit(solution)/shard_map/ppermute | solution.py:38
  34.9 6.5 %collective-permute-start.6 = (bf16[128,512]{1,0:T(8,128)(2,1)}, bf16[128,512]{1,0:T(8,128)(2,1)}, u32[]{:S(2)}, u32[]{:S(2)}) collective-permute-start(bf16[128,512]{1,0:T(8,128)(2,1)} %slice.10), channel_id=1, source_target_pairs={{0,32},{32,64},{64,96},{96,128},{128,160},{160,192},{192,224},{224... | collective-permute-start | bytes 393224 | tf_op jit(solution)/shard_map/ppermute | solution.py:38
  35.6 6.1 %collective-permute-start.7 = (bf16[128,512]{1,0:T(8,128)(2,1)}, bf16[128,512]{1,0:T(8,128)(2,1)}, u32[]{:S(2)}, u32[]{:S(2)}) collective-permute-start(bf16[128,512]{1,0:T(8,128)(2,1)} %slice.11), channel_id=1, source_target_pairs={{0,224},{32,0},{64,32},{96,64},{128,96},{160,128},{192,160},{224,1... | collective-permute-start | bytes 393224 | tf_op jit(solution)/shard_map/ppermute | solution.py:38
  42.7 2.6 %collective-permute-start.9 = (bf16[3,256,512]{2,1,0:T(8,128)(2,1)S(1)}, bf16[3,256,512]{2,1,0:T(8,128)(2,1)S(1)}, u32[]{:S(2)}, u32[]{:S(2)}) collective-permute-start(bf16[3,256,512]{2,1,0:T(8,128)(2,1)S(1)} %pad_maximum_fusion.1), channel_id=1, source_target_pairs={{0,1},{1,0},{2,3},{3,2},{4,5},{5,4},{6,7},{7,6},{8,9},{9,8},{10,11... | collective-permute-start | bytes 2359304 | tf_op jit(solution)/shard_map/ppermute | solution.py:38
  102.6 24.5 %copy-start.2 = (bf16[256,896]{1,0:T(8,128)(2,1)S(1)}, bf16[256,896]{1,0:T(8,128)(2,1)}, u32[]{:S(2)}) copy-start(bf16[256,896]{1,0:T(8,128)(2,1)} %param.10) | copy-start | bytes 1376260
  102.6 24.5 %copy-start.3 = (bf16[256,896]{1,0:T(8,128)(2,1)S(1)}, bf16[256,896]{1,0:T(8,128)(2,1)}, u32[]{:S(2)}) copy-start(bf16[256,896]{1,0:T(8,128)(2,1)} %param.11) | copy-start | bytes 1376260
  105.5 21.7 %collective-permute-start.12 = (bf16[256,896]{1,0:T(8,128)(2,1)S(1)}, bf16[256,896]{1,0:T(8,128)(2,1)S(1)}, u32[]{:S(2)}, u32[]{:S(2)}) collective-permute-start(bf16[256,896]{1,0:T(8,128)(2,1)S(1)} %reduce_sum.12), channel_id=1, source_target_pairs={{0,0},{1,129},{2,64},{3,193},{4,128},{5,1},{6,192},{7,65},{8,32},{... | collective-permute-start | bytes 1376264 | tf_op jit(solution)/shard_map/ppermute | solution.py:111

commit v2 on v1

v2 whole, which is shorter than its diff:
```python
import numpy as np
import jax
import jax.numpy as jnp
from jax import lax
from jax.experimental import pallas as pl
from jax.experimental.pallas import tpu as pltpu
from jax.sharding import Mesh, PartitionSpec as P

BLOCK = 128
Z, XH, XL, Y, C = 8, 2, 2, 4, 2
FSDP = ("z", "xh")
TP = ("xl", "y", "c")
ALL = FSDP + TP
BF16, F32 = jnp.bfloat16, jnp.float32
NEAR = 5
PLACE = (0, 1, 3, 5, 6, 7, 4, 2)
CHUNKS = ((0, 512), (512, 384))
VMEM = pl.BlockSpec(memory_space=pltpu.VMEM)
SMEM = pl.BlockSpec(memory_space=pltpu.SMEM)


def device_index(z, xh, s, c):
    return ((z * XH + xh) * XL * Y + s) * C + c


def sign_of(z):
    return 1 if z % 2 == 0 else -1


def home_pairs(j):
    pairs = []
    for z in range(Z):
        for xh in range(XH):
            for xl in range(XL):
                for y in range(Y):
                    for c in range(C):
                        to = (z + sign_of(z) * (y + 4 * (j ^ xl))) % Z
                        pairs.append((device_index(z, xh, xl * Y + y, c), device_index(to, xh, z, c)))
    return pairs


def facts():
    rows = []
    for z in range(Z):
        for xh in range(XH):
            for xl in range(XL):
                for y in range(Y):
                    for c in range(C):
                        row = [PLACE[sign_of(z) * ((y + d) % Y + Y * b) % Z] for d in range(Y) for b in range(2)]
                        source = xl * Y + y
                        away = sign_of(source) * (z - source) % Z
                        rows.append(row + [int(xh == c), xl, away // Y])
    return np.array(rows, np.int32)


def weight_pairs(same, cross):
    at = lambda xh, xl, c: (xh * XL + xl) * C + c
    pairs = []
    for xh in range(XH):
        for xl in range(XL):
            for c in range(C):
                a, b = same if xh == c else cross
                pairs.append((at(xh, xl, c), at(xh ^ a, xl ^ b, xh)))
    return pairs


def shift(x, axis, size, by):
    return lax.ppermute(x, axis, [(i, (i + by) % size) for i in range(size)])


def dequantize(values, scales):
    rows, cols = values.shape
    grid = values.astype(F32).reshape(rows // BLOCK, BLOCK, cols // BLOCK, BLOCK)
    grid = grid * scales.astype(F32)[:, None, :, None]
    return grid.reshape(rows, cols).astype(BF16)


def product(own, stacks, weights, start, width):
    rows, depth = stacks[0].shape[1:]
    half = depth // 2
    dims = (((1,), (1,)), ((), ()))

    def kernel(facts_ref, near_own, far_own, near_other, far_other, *refs):
        w_refs, out_refs, (first, second) = refs[:4], refs[4 : 4 + Y], refs[4 + Y :]
        home = facts_ref[2 * Y]
        for d in range(Y):
            for b in range(2):
                slot = facts_ref[2 * d + b]
                here = slice(b * rows, (b + 1) * rows)
                for at_home, one, two in ((1, (near_own, far_own), (near_other, far_other)), (0, (near_other, far_other), (near_own, far_own))):

                    @pl.when((home == at_home) & (slot < NEAR))
                    def _():
                        first[here, :] = one[0][slot]
                        second[here, :] = two[0][slot]

                    @pl.when((home == at_home) & (slot >= NEAR))
                    def _():
                        first[here, :] = one[1][slot - NEAR]
                        second[here, :] = two[1][slot - NEAR]

            total = None
            for lhs, k, w in ((first, 0, 0), (second, 0, 1), (second, 1, 2), (first, 1, 3)):
                term = lax.dot_general(
                    lhs[:, k * half : (k + 1) * half],
                    w_refs[w][start : start + width, :],
                    dims,
                    preferred_element_type=F32,
                )
                total = term if total is None else total + term
            total = total.astype(BF16)
            out_refs[d][0] = total[:rows]
            out_refs[d][1] = total[rows:]

    return pl.pallas_call(
        kernel,
        in_specs=[SMEM] + [VMEM] * 8,
        out_specs=[VMEM] * Y,
        out_shape=[jax.ShapeDtypeStruct((2, rows, width), BF16)] * Y,
        scratch_shapes=[pltpu.VMEM((2 * rows, depth), BF16)] * 2,
        compiler_params=pltpu.CompilerParams(vmem_limit_bytes=32 * 2**20),
        cost_estimate=pl.CostEstimate(
            flops=2 * 2 * Y * rows * 2 * depth * width, bytes_accessed=10 * 2**20, transcendentals=0
        ),
    )(own, *stacks, *weights)


def add_up(own, parts):
    _, rows, width = parts[0].shape

    def kernel(facts_ref, *refs):
        for j in range(2):
            b = jnp.where(facts_ref[2 * Y + 1] == 0, j, 1 - j)
            total = refs[0][b].astype(F32)
            for ref in refs[1:Y]:
                total += ref[b].astype(F32)
            refs[Y + j][...] = total.astype(BF16)

    return pl.pallas_call(
        kernel,
        in_specs=[SMEM] + [VMEM] * Y,
        out_specs=[VMEM] * 2,
        out_shape=[jax.ShapeDtypeStruct((rows, width), BF16)] * 2,
        compiler_params=pltpu.CompilerParams(vmem_limit_bytes=16 * 2**20),
        cost_estimate=pl.CostEstimate(flops=2 * Y * rows * width, bytes_accessed=4 * (Y + 1) * rows * width, transcendentals=0),
    )(own, *parts)


def swiglu_backward(own, hidden, gate_act, up_act):
    rows, width = gate_act.shape
    half = rows // 2

    def kernel(facts_ref, *refs):
        gate_ref, up_ref, grad_gate_ref, grad_up_ref = refs[4:]
        flip = facts_ref[2 * Y + 2] == 1
        for i, (start, count) in enumerate(CHUNKS):
            columns = slice(start, start + count)
            for h in range(2):
                here = slice(h * half, (h + 1) * half)
                value = jnp.where(flip, refs[2 * i + 1 - h][...].astype(F32), refs[2 * i + h][...].astype(F32))
                gate = gate_ref[here, columns].astype(F32)
                sigmoid = jax.nn.sigmoid(gate)
                grad_up_ref[here, columns] = (value * gate * sigmoid).astype(BF16)
                slope = sigmoid * (1.0 + gate * (1.0 - sigmoid))
                grad_gate_ref[here, columns] = (value * up_ref[here, columns].astype(F32) * slope).astype(BF16)

    shape = jax.ShapeDtypeStruct((rows, width), BF16)
    return pl.pallas_call(
        kernel,
        in_specs=[SMEM] + [VMEM] * 6,
        out_specs=[VMEM] * 2,
        out_shape=[shape] * 2,
        compiler_params=pltpu.CompilerParams(vmem_limit_bytes=16 * 2**20),
        cost_estimate=pl.CostEstimate(flops=10 * rows * width, bytes_accessed=10 * rows * width, transcendentals=rows * width),
    )(own, *[x for chunk in hidden for x in chunk], gate_act, up_act)


def on_device(grad_out, down_q, scales, gate_act, up_act):
    xl, c = lax.axis_index("xl"), lax.axis_index("c")

    rows = grad_out.shape[0] // 2
    mine = lax.dynamic_slice_in_dim(grad_out, xl * rows, rows, 0)
    theirs = lax.dynamic_slice_in_dim(grad_out, (1 - xl) * rows, rows, 0)
    tokens = jnp.concatenate([mine, shift(theirs, "xl", XL, 1)], 1)

    weight = dequantize(down_q, scales)
    rounds = (((0, 0), (1, 0)), ((1, 0), (0, 0)), ((1, 1), (0, 1)), ((0, 1), (1, 1)))
    weights = [lax.ppermute(weight, ("xh", "xl", "c"), weight_pairs(*pair)) for pair in rounds]

    ahead, behind = [tokens], [tokens]
    for _ in range(3):
        behind.append(shift(behind[-1], "z", Z, 1))
        ahead.append(shift(ahead[-1], "z", Z, -1))
    around = [(i * C, (i + 1) % Z * C) for i in range(Z)] + [(i * C + 1, (i - 1) % Z * C + 1) for i in range(Z)]
    far = lax.ppermute(jnp.where(c == 0, behind[3], ahead[3]), ("z", "c"), around)
    near_own = jnp.stack([tokens, ahead[1], behind[1], ahead[2], behind[2]])
    far_own = jnp.stack([ahead[3], far, behind[3]])
    stacks = (near_own, far_own, shift(near_own, "c", C, 1), shift(far_own, "c", C, 1))

    own = lax.dynamic_index_in_dim(jnp.asarray(facts()), lax.axis_index(ALL), 0, keepdims=False)
    hidden = []
    for start, width in CHUNKS:
        outs = product(own, stacks, weights, start, width)
        parts = [outs[0]] + [shift(outs[d], "y", Y, d) for d in range(1, Y)]
        sums = add_up(own, parts)
        hidden.append([lax.ppermute(sums[j], ALL, home_pairs(j)) for j in range(2)])

    return tuple(swiglu_backward(own, hidden, gate_act, up_act))


def solution(mesh):
    fine = Mesh(mesh.devices.reshape(Z, XH, XL, Y, C), ALL)
    spec = P(FSDP, TP)
    return jax.shard_map(
        on_device, mesh=fine, in_specs=(spec,) * 5, out_specs=(spec, spec), check_vma=False
    )
```

time: 129 us -> 129 us (level)
  blocking collectives: 49.3 us -> 0 us
  starting transfers between devices: 21.7 us -> 51.2 us
  waiting for transfers between devices: 33 us -> 57.5 us
  other arithmetic: 9.56 us -> 1.45 us
  Pallas kernels: 6.49 us -> 14.6 us
  local copies, waits for them, and re-layouts: 7.75 us -> 2.85 us
    all_to_all x1 -> x0, blocking collectives: 49.3 us -> none  [on_device(): lax.all_to_all(partial_value, ('xl', 'y'), split_axis=0, concat_axis=0, t...]
    ppermute x3 -> x9, starting transfers between devices: 5.73 us -> 26.3 us  [the longest x4 17.8 us: on_device(): hidden.append([lax.ppermute(sums[j], ALL, home_pairs(j)) for j in range(2)])]
    ppermute x3 -> x9, waiting for transfers between devices: 19.8 us -> 39.9 us  [the longest x4 22.5 us: on_device(): lax.ppermute(weight, ('xh', 'xl', 'c'), weight_pairs(*pair))]
    ppermute x10 -> x15, starting transfers between devices: 16 us -> 24.9 us  [shift(): return lax.ppermute(x, axis, [(i, (i + by) % size) for i in range(size)])]
    pallas_call x1 -> x5, Pallas kernels: 6.49 us -> 14.6 us  [the longest x2 11.3 us: product(): pl.pallas_call(kernel, in_specs=[SMEM] + [VMEM] * 8, out_specs=[VMEM] * Y...]
    ppermute x10 -> x15, waiting for transfers between devices: 13.2 us -> 17.5 us  [shift(): return lax.ppermute(x, axis, [(i, (i + by) % size) for i in range(size)])]
    unnamed x17 -> x9, local copies, waits for them, and re-layouts: 3.94 us -> 0.07 us
    reduce_sum x1 -> x0, other arithmetic: 2.82 us -> none  [on_device(): summed = parts.astype(F32).sum(0).astype(BF16)]
  transfers between devices with their start and end apart: 13 -> 24, of which waited for: 5 -> 12; matrix products, arithmetic and copies ran while one was open for 9% -> 3% of each run, Pallas kernels for 0% -> 5%
where the time goes in v2:
time: 129 us
  waiting for transfers between devices  57.5 us (45%)
  starting transfers between devices  51.2 us (40%)
  Pallas kernels  14.6 us (11%)
  local copies, waits for them, and re-layouts  2.85 us (2%)
  other arithmetic  1.45 us (1%)
    ppermute x15, starting transfers between devices, shift(): return lax.ppermute(x, axis, [(i, (i + by) % size) for i in range(size)])  24.9 us
    ppermute x4, waiting for transfers between devices, on_device(): lax.ppermute(weight, ('xh', 'xl', 'c'), weight_pairs(*pair))  22.5 us
    ppermute x4, starting transfers between devices, on_device(): hidden.append([lax.ppermute(sums[j], ALL, home_pairs(j)) for j in range(2)])  17.8 us
    ppermute x15, waiting for transfers between devices, shift(): return lax.ppermute(x, axis, [(i, (i + by) % size) for i in range(size)])  17.5 us
    pallas_call x2, Pallas kernels, product(): pl.pallas_call(kernel, in_specs=[SMEM] + [VMEM] * 8, out_specs=[VMEM] * Y...  11.3 us
    ppermute x4, waiting for transfers between devices, on_device(): hidden.append([lax.ppermute(sums[j], ALL, home_pairs(j)) for j in range(2)])  10 us
    ppermute x4, starting transfers between devices, on_device(): lax.ppermute(weight, ('xh', 'xl', 'c'), weight_pairs(*pair))  8.49 us
    ppermute x1, waiting for transfers between devices, on_device(): lax.ppermute(jnp.where(c == 0, behind[3], ahead[3]), ('z', 'c'), around)  7.37 us
  transfers between devices with their start and end apart: 24, of which 12 were waited for; matrix products, arithmetic and copies ran while one was open for 3% of the time, Pallas kernels for 5%

profile of v2, /device:TPU:2, one launch (start us, length us, event | category | flops | bytes accessed | tf_op | source)
XLA Modules:
  0.0 128.5 jit_solution(4652908145824783734)
XLA Ops:
  0.6 1.0 constant_dynamic-slice_fusion.1
  1.6 0.0 copy-start.2
  1.6 2.4 %collective-permute-start = (bf16[128,512]{1,0:T(8,128)(2,1)S(1)}, bf16[128,512]{1,0:T(8,128)(2,1)S(1)}, u32[]{:S(2)}, u32[]{:S(2)}) collective-permute-start(bf16[128,512]{1,0:T(8,128)(2,1)S(1)} %get-tuple-element.27), channel_id=1, source_target_pairs={{0,8},{8,0},{1,9},{9,1},{2,10},{10,2},{3,11},{11,3},{4,12},{12,4},... | collective-permute-start | bytes 393224 | tf_op jit(solution)/shard_map/ppermute | solution.py:68
  4.0 0.8 copy.8
  4.8 2.2 %collective-permute-done = bf16[128,512]{1,0:T(8,128)(2,1)S(1)} collective-permute-done((bf16[128,512]{1,0:T(8,128)(2,1)S(1)}, bf16[128,512]{1,0:T(8,128)(2,1)S(1)}, u32[]{:S(2)}, u32[]{:S(2)}) %collective-permute-start) | collective-permute-done | bytes 131104 | tf_op jit(solution)/shard_map/ppermute | solution.py:68
  7.0 5.9 %collective-permute-start.1 = (bf16[128,1024]{1,0:T(8,128)(2,1)S(1)}, bf16[128,1024]{1,0:T(8,128)(2,1)S(1)}, u32[]{:S(2)}, u32[]{:S(2)}) collective-permute-start(bf16[128,1024]{1,0:T(8,128)(2,1)S(1)} %pad_maximum_fusion.1), channel_id=1, source_target_pairs={{0,224},{32,0},{64,32},{96,64},{128,96},{160,128},{192,160},{224,1... | collective-permute-start | bytes 786440 | tf_op jit(solution)/shard_map/ppermute | solution.py:68
  12.9 0.0 collective-permute-start.2
  12.9 0.3 mul.35
  13.2 1.3 %fusion = bf16[896,512]{1,0:T(8,128)(2,1)} fusion(f32[112,8,4,128]{3,2,1,0:T(4,128)S(1)} %bitcast.21, bf16[896,512]{1,0:T(8,128)(2,1)S(1)} %copy-done.2), kind=kLoop, calls=%fused_computation.1 | loop fusion | flops 1376256 | bytes 3670016 | tf_op jit(solution)/shard_map/convert_element_type | solution.py:75
  14.5 8.3 %collective-permute-start.10 = (bf16[896,512]{1,0:T(8,128)(2,1)}, bf16[896,512]{1,0:T(8,128)(2,1)}, u32[]{:S(2)}, u32[]{:S(2)}) collective-permute-start(bf16[896,512]{1,0:T(8,128)(2,1)} %fusion), channel_id=1, source_target_pairs={{0,0},{1,16},{8,8},{9,24},{16,1},{17,17},{24,9},{25,25},{2,2},{3,1... | collective-permute-start | bytes 2752520 | tf_op jit(solution)/shard_map/ppermute | solution.py:188
  22.9 0.0 collective-permute-done.1
  22.9 3.3 %collective-permute-start.3 = (bf16[128,1024]{1,0:T(8,128)(2,1)S(1)}, bf16[128,1024]{1,0:T(8,128)(2,1)S(1)}, u32[]{:S(2)}, u32[]{:S(2)}) collective-permute-start(bf16[128,1024]{1,0:T(8,128)(2,1)S(1)} %collective-permute-done.1), channel_id=1, source_target_pairs={{0,224},{32,0},{64,32},{96,64},{128,96},{160,128},{192,160},{224,1... | collective-permute-start | bytes 786440 | tf_op jit(solution)/shard_map/ppermute | solution.py:68
  26.2 5.3 %collective-permute-done.3 = bf16[128,1024]{1,0:T(8,128)(2,1)S(1)} collective-permute-done((bf16[128,1024]{1,0:T(8,128)(2,1)S(1)}, bf16[128,1024]{1,0:T(8,128)(2,1)S(1)}, u32[]{:S(2)}, u32[]{:S(2)}) %collective-permute-start.3) | collective-permute-done | bytes 262176 | tf_op jit(solution)/shard_map/ppermute | solution.py:68
  31.5 3.7 %collective-permute-start.5 = (bf16[128,1024]{1,0:T(8,128)(2,1)S(1)}, bf16[128,1024]{1,0:T(8,128)(2,1)S(1)}, u32[]{:S(2)}, u32[]{:S(2)}) collective-permute-start(bf16[128,1024]{1,0:T(8,128)(2,1)S(1)} %collective-permute-done.3), channel_id=1, source_target_pairs={{0,224},{32,0},{64,32},{96,64},{128,96},{160,128},{192,160},{224,1... | collective-permute-start | bytes 786440 | tf_op jit(solution)/shard_map/ppermute | solution.py:68
  35.2 0.3 collective-permute-done.4
  35.6 0.1 collective-permute-start.8
  35.7 3.4 %collective-permute-done.5 = bf16[128,1024]{1,0:T(8,128)(2,1)S(1)} collective-permute-done((bf16[128,1024]{1,0:T(8,128)(2,1)S(1)}, bf16[128,1024]{1,0:T(8,128)(2,1)S(1)}, u32[]{:S(2)}, u32[]{:S(2)}) %collective-permute-start.5) | collective-permute-done | bytes 262176 | tf_op jit(solution)/shard_map/ppermute | solution.py:68
  39.1 4.0 %collective-permute-done.6 = bf16[128,1024]{1,0:T(8,128)(2,1)S(1)} collective-permute-done((bf16[128,1024]{1,0:T(8,128)(2,1)S(1)}, bf16[128,1024]{1,0:T(8,128)(2,1)S(1)}, u32[]{:S(2)}, u32[]{:S(2)}) %collective-permute-start.6) | collective-permute-done | bytes 262176 | tf_op jit(solution)/shard_map/ppermute | solution.py:68
  43.2 0.1 collective-permute-start.7
  43.2 0.1 collective-permute-start.11
  43.3 0.1 collective-permute-start.12
  43.4 7.4 %collective-permute-done.7 = bf16[128,1024]{1,0:T(8,128)(2,1)S(1)} collective-permute-done((bf16[128,1024]{1,0:T(8,128)(2,1)S(1)}, bf16[128,1024]{1,0:T(8,128)(2,1)S(1)}, u32[]{:S(2)}, u32[]{:S(2)}) %collective-permute-start.7) | collective-permute-done | bytes 262176 | tf_op jit(solution)/shard_map/ppermute | solution.py:195
  50.8 0.1 pad_maximum_fusion.far_own
  50.9 0.1 collective-permute-start.9
  51.0 0.7 fusion.1.facts_ref
  51.7 12.5 %collective-permute-done.11.refs_1_ = bf16[896,512]{1,0:T(8,128)(2,1)} collective-permute-done((bf16[896,512]{1,0:T(8,128)(2,1)}, bf16[896,512]{1,0:T(8,128)(2,1)}, u32[]{:S(2)}, u32[]{:S(2)}) %collective-permute-start.11) | collective-permute-done | bytes 917536 | tf_op jit(solution)/shard_map/ppermute | solution.py:188
  64.2 7.3 %collective-permute-done.12.refs_2_ = bf16[896,512]{1,0:T(8,128)(2,1)} collective-permute-done((bf16[896,512]{1,0:T(8,128)(2,1)}, bf16[896,512]{1,0:T(8,128)(2,1)}, u32[]{:S(2)}, u32[]{:S(2)}) %collective-permute-start.12) | collective-permute-done | bytes 917536 | tf_op jit(solution)/shard_map/ppermute | solution.py:188
  71.5 2.7 %collective-permute-done.13.refs_3_ = bf16[896,512]{1,0:T(8,128)(2,1)} collective-permute-done((bf16[896,512]{1,0:T(8,128)(2,1)}, bf16[896,512]{1,0:T(8,128)(2,1)}, u32[]{:S(2)}, u32[]{:S(2)}) %collective-permute-start.13) | collective-permute-done | bytes 917536 | tf_op jit(solution)/shard_map/ppermute | solution.py:188
  74.3 5.8 %shard_map.77 = (bf16[2,128,512]{2,1,0:T(8,128)(2,1)S(1)}, bf16[2,128,512]{2,1,0:T(8,128)(2,1)S(1)}, bf16[2,128,512]{2,1,0:T(8,128)(2,1)S(1)}, bf16[2,128,512]{2,1,0:T(8,128)(2,1)S(1)}) custom-call(s32[11]{0:T(128)S(1)} %fusion.1.facts_ref, bf16[5,128,1024]{2,1,0:T(8,128)(2,1)S(1)} %bitcast_dynamic-update-slice_fusion.near_own, ...), custom_call_target="tpu_custom_call" | custom-call | flops 2147483648 | bytes 10485760 | tf_op jit(solution)/shard_map/pallas_call | solution.py:115
  80.1 1.7 %collective-permute-start.14 = (bf16[2,128,512]{2,1,0:T(8,128)(2,1)S(1)}, bf16[2,128,512]{2,1,0:T(8,128)(2,1)S(1)}, u32[]{:S(2)}, u32[]{:S(2)}) collective-permute-start(bf16[2,128,512]{2,1,0:T(8,128)(2,1)S(1)} %get-tuple-element.15), channel_id=1, source_target_pairs={{0,2},{2,4},{4,6},{6,0},{1,3},{3,5},{5,7},{7,1},{8,10},{10,12},{12... | collective-permute-start | bytes 786440 | tf_op jit(solution)/shard_map/ppermute | solution.py:68
  81.7 2.9 %collective-permute-start.15 = (bf16[2,128,512]{2,1,0:T(8,128)(2,1)S(1)}, bf16[2,128,512]{2,1,0:T(8,128)(2,1)S(1)}, u32[]{:S(2)}, u32[]{:S(2)}) collective-permute-start(bf16[2,128,512]{2,1,0:T(8,128)(2,1)S(1)} %get-tuple-element.16), channel_id=1, source_target_pairs={{0,4},{2,6},{4,0},{6,2},{1,5},{3,7},{5,1},{7,3},{8,12},{10,14},{12... | collective-permute-start | bytes 786440 | tf_op jit(solution)/shard_map/ppermute | solution.py:68
  84.6 1.4 %collective-permute-start.16 = (bf16[2,128,512]{2,1,0:T(8,128)(2,1)S(1)}, bf16[2,128,512]{2,1,0:T(8,128)(2,1)S(1)}, u32[]{:S(2)}, u32[]{:S(2)}) collective-permute-start(bf16[2,128,512]{2,1,0:T(8,128)(2,1)S(1)} %get-tuple-element.17), channel_id=1, source_target_pairs={{0,6},{2,0},{4,2},{6,4},{1,7},{3,1},{5,3},{7,5},{8,14},{10,8},{12,... | collective-permute-start | bytes 786440 | tf_op jit(solution)/shard_map/ppermute | solution.py:68
  86.0 5.5 %shard_map.79 = (bf16[2,128,384]{2,1,0:T(8,128)(2,1)S(1)}, bf16[2,128,384]{2,1,0:T(8,128)(2,1)S(1)}, bf16[2,128,384]{2,1,0:T(8,128)(2,1)S(1)}, bf16[2,128,384]{2,1,0:T(8,128)(2,1)S(1)}) custom-call(s32[11]{0:T(128)S(1)} %fusion.1.facts_ref, bf16[5,128,1024]{2,1,0:T(8,128)(2,1)S(1)} %bitcast_dynamic-update-slice_fusion.near_own, ...), custom_call_target="tpu_custom_call" | custom-call | flops 1610612736 | bytes 10485760 | tf_op jit(solution)/shard_map/pallas_call | solution.py:115
  91.5 0.0 copy-start
  91.5 0.0 copy-start.1
  91.5 0.7 collective-permute-start.19
  92.3 0.8 collective-permute-start.20
  93.0 2.0 %collective-permute-start.21 = (bf16[2,128,384]{2,1,0:T(8,128)(2,1)S(1)}, bf16[2,128,384]{2,1,0:T(8,128)(2,1)S(1)}, u32[]{:S(2)}, u32[]{:S(2)}) collective-permute-start(bf16[2,128,384]{2,1,0:T(8,128)(2,1)S(1)} %get-tuple-element.23), channel_id=1, source_target_pairs={{0,6},{2,0},{4,2},{6,4},{1,7},{3,1},{5,3},{7,5},{8,14},{10,8},{12,... | collective-permute-start | bytes 589832 | tf_op jit(solution)/shard_map/ppermute | solution.py:68
  95.0 2.3 %collective-permute-done.15.refs_2_ = bf16[2,128,512]{2,1,0:T(8,128)(2,1)S(1)} collective-permute-done((bf16[2,128,512]{2,1,0:T(8,128)(2,1)S(1)}, bf16[2,128,512]{2,1,0:T(8,128)(2,1)S(1)}, u32[]{:S(2)}, u32[]{:S(2)}) %collective-permute-start.15) | collective-permute-done | bytes 262176 | tf_op jit(solution)/shard_map/ppermute | solution.py:68
  97.3 0.7 shard_map.78
  98.0 5.2 %collective-permute-start.17 = (bf16[128,512]{1,0:T(8,128)(2,1)S(1)}, bf16[128,512]{1,0:T(8,128)(2,1)S(1)}, u32[]{:S(2)}, u32[]{:S(2)}) collective-permute-start(bf16[128,512]{1,0:T(8,128)(2,1)S(1)} %get-tuple-element.18), channel_id=1, source_target_pairs={{0,0},{1,1},{2,32},{3,33},{4,64},{5,65},{6,96},{7,97},{8,128},{9,1... | collective-permute-start | bytes 393224 | tf_op jit(solution)/shard_map/ppermute | solution.py:206
  103.2 1.9 %collective-permute-start.18 = (bf16[128,512]{1,0:T(8,128)(2,1)S(1)}, bf16[128,512]{1,0:T(8,128)(2,1)S(1)}, u32[]{:S(2)}, u32[]{:S(2)}) collective-permute-start(bf16[128,512]{1,0:T(8,128)(2,1)S(1)} %get-tuple-element.19), channel_id=1, source_target_pairs={{0,128},{1,129},{2,160},{3,161},{4,192},{5,193},{6,224},{7,225},{8... | collective-permute-start | bytes 393224 | tf_op jit(solution)/shard_map/ppermute | solution.py:206
  105.2 0.7 shard_map.80
  105.8 8.7 %collective-permute-start.22 = (bf16[128,384]{1,0:T(8,128)(2,1)S(1)}, bf16[128,384]{1,0:T(8,128)(2,1)S(1)}, u32[]{:S(2)}, u32[]{:S(2)}) collective-permute-start(bf16[128,384]{1,0:T(8,128)(2,1)S(1)} %get-tuple-element.24), channel_id=1, source_target_pairs={{0,0},{1,1},{2,32},{3,33},{4,64},{5,65},{6,96},{7,97},{8,128},{9,1... | collective-permute-start | bytes 294920 | tf_op jit(solution)/shard_map/ppermute | solution.py:206
  114.6 1.9 %collective-permute-start.23 = (bf16[128,384]{1,0:T(8,128)(2,1)S(1)}, bf16[128,384]{1,0:T(8,128)(2,1)S(1)}, u32[]{:S(2)}, u32[]{:S(2)}) collective-permute-start(bf16[128,384]{1,0:T(8,128)(2,1)S(1)} %get-tuple-element.25), channel_id=1, source_target_pairs={{0,128},{1,129},{2,160},{3,161},{4,192},{5,193},{6,224},{7,225},{8... | collective-permute-start | bytes 294920 | tf_op jit(solution)/shard_map/ppermute | solution.py:206
  116.5 1.2 collective-permute-done.22.refs_2_
  117.7 8.8 %collective-permute-done.23.refs_3_ = bf16[128,384]{1,0:T(8,128)(2,1)S(1)} collective-permute-done((bf16[128,384]{1,0:T(8,128)(2,1)S(1)}, bf16[128,384]{1,0:T(8,128)(2,1)S(1)}, u32[]{:S(2)}, u32[]{:S(2)}) %collective-permute-start.23) | collective-permute-done | bytes 98336 | tf_op jit(solution)/shard_map/ppermute | solution.py:206
  126.6 2.0 %shard_map.81 = (bf16[256,896]{1,0:T(8,128)(2,1)}, bf16[256,896]{1,0:T(8,128)(2,1)}) custom-call(s32[11]{0:T(128)S(1)} %fusion.1.facts_ref, bf16[128,512]{1,0:T(8,128)(2,1)S(1)} %collective-permute-done.17.refs_0_, bf16[128,512]{1,0:T(8,128)(2,1)S(1)} %collective-permute-done.18.refs_1_, bf16[128,384]{1,0:T(8,128)(2,1)S(1)} %collective-permute-done.22.refs_2_, ...), custom_call_target="tpu_custom_call" | custom-call | flops 2293760 | bytes 2293760 | tf_op jit(solution)/shard_map/pallas_call | solution.py:168
  (24 shorter events, 0.2 us)
Async XLA Ops:
  1.6 11.6 %copy-start.2 = (bf16[896,512]{1,0:T(8,128)(2,1)S(1)}, bf16[896,512]{1,0:T(8,128)(2,1)}, u32[]{:S(2)}) copy-start(bf16[896,512]{1,0:T(8,128)(2,1)} %param.7) | copy-start | bytes 2752516
  1.6 5.3 %collective-permute-start = (bf16[128,512]{1,0:T(8,128)(2,1)S(1)}, bf16[128,512]{1,0:T(8,128)(2,1)S(1)}, u32[]{:S(2)}, u32[]{:S(2)}) collective-permute-start(bf16[128,512]{1,0:T(8,128)(2,1)S(1)} %get-tuple-element.27), channel_id=1, source_target_pairs={{0,8},{8,0},{1,9},{9,1},{2,10},{10,2},{3,11},{11,3},{4,12},{12,4},... | collective-permute-start | bytes 393224 | tf_op jit(solution)/shard_map/ppermute | solution.py:68
  7.0 15.9 %collective-permute-start.1 = (bf16[128,1024]{1,0:T(8,128)(2,1)S(1)}, bf16[128,1024]{1,0:T(8,128)(2,1)S(1)}, u32[]{:S(2)}, u32[]{:S(2)}) collective-permute-start(bf16[128,1024]{1,0:T(8,128)(2,1)S(1)} %pad_maximum_fusion.1), channel_id=1, source_target_pairs={{0,224},{32,0},{64,32},{96,64},{128,96},{160,128},{192,160},{224,1... | collective-permute-start | bytes 786440 | tf_op jit(solution)/shard_map/ppermute | solution.py:68
  12.9 13.3 %collective-permute-start.2 = (bf16[128,1024]{1,0:T(8,128)(2,1)S(1)}, bf16[128,1024]{1,0:T(8,128)(2,1)S(1)}, u32[]{:S(2)}, u32[]{:S(2)}) collective-permute-start(bf16[128,1024]{1,0:T(8,128)(2,1)S(1)} %pad_maximum_fusion.1), channel_id=1, source_target_pairs={{0,32},{32,64},{64,96},{96,128},{128,160},{160,192},{192,224},{224... | collective-permute-start | bytes 786440 | tf_op jit(solution)/shard_map/ppermute | solution.py:68
  14.5 36.4 %collective-permute-start.10 = (bf16[896,512]{1,0:T(8,128)(2,1)}, bf16[896,512]{1,0:T(8,128)(2,1)}, u32[]{:S(2)}, u32[]{:S(2)}) collective-permute-start(bf16[896,512]{1,0:T(8,128)(2,1)} %fusion), channel_id=1, source_target_pairs={{0,0},{1,16},{8,8},{9,24},{16,1},{17,17},{24,9},{25,25},{2,2},{3,1... | collective-permute-start | bytes 2752520 | tf_op jit(solution)/shard_map/ppermute | solution.py:188
  22.9 8.6 %collective-permute-start.3 = (bf16[128,1024]{1,0:T(8,128)(2,1)S(1)}, bf16[128,1024]{1,0:T(8,128)(2,1)S(1)}, u32[]{:S(2)}, u32[]{:S(2)}) collective-permute-start(bf16[128,1024]{1,0:T(8,128)(2,1)S(1)} %collective-permute-done.1), channel_id=1, source_target_pairs={{0,224},{32,0},{64,32},{96,64},{128,96},{160,128},{192,160},{224,1... | collective-permute-start | bytes 786440 | tf_op jit(solution)/shard_map/ppermute | solution.py:68
  26.2 9.3 %collective-permute-start.4 = (bf16[128,1024]{1,0:T(8,128)(2,1)S(1)}, bf16[128,1024]{1,0:T(8,128)(2,1)S(1)}, u32[]{:S(2)}, u32[]{:S(2)}) collective-permute-start(bf16[128,1024]{1,0:T(8,128)(2,1)S(1)} %collective-permute-done.2), channel_id=1, source_target_pairs={{0,32},{32,64},{64,96},{96,128},{128,160},{160,192},{192,224},{224... | collective-permute-start | bytes 786440 | tf_op jit(solution)/shard_map/ppermute | solution.py:68
  31.5 7.6 %collective-permute-start.5 = (bf16[128,1024]{1,0:T(8,128)(2,1)S(1)}, bf16[128,1024]{1,0:T(8,128)(2,1)S(1)}, u32[]{:S(2)}, u32[]{:S(2)}) collective-permute-start(bf16[128,1024]{1,0:T(8,128)(2,1)S(1)} %collective-permute-done.3), channel_id=1, source_target_pairs={{0,224},{32,0},{64,32},{96,64},{128,96},{160,128},{192,160},{224,1... | collective-permute-start | bytes 786440 | tf_op jit(solution)/shard_map/ppermute | solution.py:68
  35.5 7.6 %collective-permute-start.6 = (bf16[128,1024]{1,0:T(8,128)(2,1)S(1)}, bf16[128,1024]{1,0:T(8,128)(2,1)S(1)}, u32[]{:S(2)}, u32[]{:S(2)}) collective-permute-start(bf16[128,1024]{1,0:T(8,128)(2,1)S(1)} %collective-permute-done.4), channel_id=1, source_target_pairs={{0,32},{32,64},{64,96},{96,128},{128,160},{160,192},{192,224},{224... | collective-permute-start | bytes 786440 | tf_op jit(solution)/shard_map/ppermute | solution.py:68
  35.6 38.7 %collective-permute-start.8 = (bf16[5,128,1024]{2,1,0:T(8,128)(2,1)S(1)}, bf16[5,128,1024]{2,1,0:T(8,128)(2,1)S(1)}, u32[]{:S(2)}, u32[]{:S(2)}) collective-permute-start(bf16[5,128,1024]{2,1,0:T(8,128)(2,1)S(1)} %bitcast_dynamic-update-slice_fusion.near_own), channel_id=1, source_target_pairs={{0,1},{1,0},{2,3},{3,2},{4,5},{5,4},{6,7},{7,6},{8,9},{9,8},{10,11... | collective-permute-start | bytes 3932168 | tf_op jit(solution)/shard_map/ppermute | solution.py:68
  43.2 7.7 %collective-permute-start.7 = (bf16[128,1024]{1,0:T(8,128)(2,1)S(1)}, bf16[128,1024]{1,0:T(8,128)(2,1)S(1)}, u32[]{:S(2)}, u32[]{:S(2)}) collective-permute-start(bf16[128,1024]{1,0:T(8,128)(2,1)S(1)} %broadcast_select_fusion), channel_id=1, source_target_pairs={{0,32},{32,64},{64,96},{96,128},{128,160},{160,192},{192,224},{224... | collective-permute-start | bytes 786440 | tf_op jit(solution)/shard_map/ppermute | solution.py:195
  43.2 21.0 %collective-permute-start.11 = (bf16[896,512]{1,0:T(8,128)(2,1)}, bf16[896,512]{1,0:T(8,128)(2,1)}, u32[]{:S(2)}, u32[]{:S(2)}) collective-permute-start(bf16[896,512]{1,0:T(8,128)(2,1)} %fusion), channel_id=1, source_target_pairs={{0,16},{1,0},{8,24},{9,8},{16,17},{17,1},{24,25},{25,9},{2,18},{3,... | collective-permute-start | bytes 2752520 | tf_op jit(solution)/shard_map/ppermute | solution.py:188
  43.3 28.2 %collective-permute-start.12 = (bf16[896,512]{1,0:T(8,128)(2,1)}, bf16[896,512]{1,0:T(8,128)(2,1)}, u32[]{:S(2)}, u32[]{:S(2)}) collective-permute-start(bf16[896,512]{1,0:T(8,128)(2,1)} %fusion), channel_id=1, source_target_pairs={{0,24},{1,8},{8,16},{9,0},{16,25},{17,9},{24,17},{25,1},{2,26},{3,... | collective-permute-start | bytes 2752520 | tf_op jit(solution)/shard_map/ppermute | solution.py:188
  50.8 23.5 %collective-permute-start.13 = (bf16[896,512]{1,0:T(8,128)(2,1)}, bf16[896,512]{1,0:T(8,128)(2,1)}, u32[]{:S(2)}, u32[]{:S(2)}) collective-permute-start(bf16[896,512]{1,0:T(8,128)(2,1)} %fusion), channel_id=1, source_target_pairs={{0,8},{1,24},{8,0},{9,16},{16,9},{17,25},{24,1},{25,17},{2,10},{3,... | collective-permute-start | bytes 2752520 | tf_op jit(solution)/shard_map/ppermute | solution.py:188
  50.9 23.4 %collective-permute-start.9 = (bf16[3,128,1024]{2,1,0:T(8,128)(2,1)S(1)}, bf16[3,128,1024]{2,1,0:T(8,128)(2,1)}, u32[]{:S(2)}, u32[]{:S(2)}) collective-permute-start(bf16[3,128,1024]{2,1,0:T(8,128)(2,1)S(1)} %pad_maximum_fusion.far_own), channel_id=1, source_target_pairs={{0,1},{1,0},{2,3},{3,2},{4,5},{5,4},{6,7},{7,6},{8,9},{9,8},{10,11... | collective-permute-start | bytes 2359304 | tf_op jit(solution)/shard_map/ppermute | solution.py:68
  80.1 13.0 %collective-permute-start.14 = (bf16[2,128,512]{2,1,0:T(8,128)(2,1)S(1)}, bf16[2,128,512]{2,1,0:T(8,128)(2,1)S(1)}, u32[]{:S(2)}, u32[]{:S(2)}) collective-permute-start(bf16[2,128,512]{2,1,0:T(8,128)(2,1)S(1)} %get-tuple-element.15), channel_id=1, source_target_pairs={{0,2},{2,4},{4,6},{6,0},{1,3},{3,5},{5,7},{7,1},{8,10},{10,12},{12... | collective-permute-start | bytes 786440 | tf_op jit(solution)/shard_map/ppermute | solution.py:68
  81.7 15.6 %collective-permute-start.15 = (bf16[2,128,512]{2,1,0:T(8,128)(2,1)S(1)}, bf16[2,128,512]{2,1,0:T(8,128)(2,1)S(1)}, u32[]{:S(2)}, u32[]{:S(2)}) collective-permute-start(bf16[2,128,512]{2,1,0:T(8,128)(2,1)S(1)} %get-tuple-element.16), channel_id=1, source_target_pairs={{0,4},{2,6},{4,0},{6,2},{1,5},{3,7},{5,1},{7,3},{8,12},{10,14},{12... | collective-permute-start | bytes 786440 | tf_op jit(solution)/shard_map/ppermute | solution.py:68
  84.6 12.7 %collective-permute-start.16 = (bf16[2,128,512]{2,1,0:T(8,128)(2,1)S(1)}, bf16[2,128,512]{2,1,0:T(8,128)(2,1)S(1)}, u32[]{:S(2)}, u32[]{:S(2)}) collective-permute-start(bf16[2,128,512]{2,1,0:T(8,128)(2,1)S(1)} %get-tuple-element.17), channel_id=1, source_target_pairs={{0,6},{2,0},{4,2},{6,4},{1,7},{3,1},{5,3},{7,5},{8,14},{10,8},{12,... | collective-permute-start | bytes 786440 | tf_op jit(solution)/shard_map/ppermute | solution.py:68
  91.5 35.1 %copy-start = (bf16[256,896]{1,0:T(8,128)(2,1)S(1)}, bf16[256,896]{1,0:T(8,128)(2,1)}, u32[]{:S(2)}) copy-start(bf16[256,896]{1,0:T(8,128)(2,1)} %refs_4_.1) | copy-start | bytes 1376260
  91.5 35.1 %copy-start.1 = (bf16[256,896]{1,0:T(8,128)(2,1)S(1)}, bf16[256,896]{1,0:T(8,128)(2,1)}, u32[]{:S(2)}) copy-start(bf16[256,896]{1,0:T(8,128)(2,1)} %refs_5_.1) | copy-start | bytes 1376260
  91.5 13.6 %collective-permute-start.19 = (bf16[2,128,384]{2,1,0:T(8,128)(2,1)S(1)}, bf16[2,128,384]{2,1,0:T(8,128)(2,1)S(1)}, u32[]{:S(2)}, u32[]{:S(2)}) collective-permute-start(bf16[2,128,384]{2,1,0:T(8,128)(2,1)S(1)} %get-tuple-element.21), channel_id=1, source_target_pairs={{0,2},{2,4},{4,6},{6,0},{1,3},{3,5},{5,7},{7,1},{8,10},{10,12},{12... | collective-permute-start | bytes 589832 | tf_op jit(solution)/shard_map/ppermute | solution.py:68
  92.3 12.9 %collective-permute-start.20 = (bf16[2,128,384]{2,1,0:T(8,128)(2,1)S(1)}, bf16[2,128,384]{2,1,0:T(8,128)(2,1)S(1)}, u32[]{:S(2)}, u32[]{:S(2)}) collective-permute-start(bf16[2,128,384]{2,1,0:T(8,128)(2,1)S(1)} %get-tuple-element.22), channel_id=1, source_target_pairs={{0,4},{2,6},{4,0},{6,2},{1,5},{3,7},{5,1},{7,3},{8,12},{10,14},{12... | collective-permute-start | bytes 589832 | tf_op jit(solution)/shard_map/ppermute | solution.py:68
  93.0 12.1 %collective-permute-start.21 = (bf16[2,128,384]{2,1,0:T(8,128)(2,1)S(1)}, bf16[2,128,384]{2,1,0:T(8,128)(2,1)S(1)}, u32[]{:S(2)}, u32[]{:S(2)}) collective-permute-start(bf16[2,128,384]{2,1,0:T(8,128)(2,1)S(1)} %get-tuple-element.23), channel_id=1, source_target_pairs={{0,6},{2,0},{4,2},{6,4},{1,7},{3,1},{5,3},{7,5},{8,14},{10,8},{12,... | collective-permute-start | bytes 589832 | tf_op jit(solution)/shard_map/ppermute | solution.py:68
  98.0 28.5 %collective-permute-start.17 = (bf16[128,512]{1,0:T(8,128)(2,1)S(1)}, bf16[128,512]{1,0:T(8,128)(2,1)S(1)}, u32[]{:S(2)}, u32[]{:S(2)}) collective-permute-start(bf16[128,512]{1,0:T(8,128)(2,1)S(1)} %get-tuple-element.18), channel_id=1, source_target_pairs={{0,0},{1,1},{2,32},{3,33},{4,64},{5,65},{6,96},{7,97},{8,128},{9,1... | collective-permute-start | bytes 393224 | tf_op jit(solution)/shard_map/ppermute | solution.py:206
  103.2 23.3 %collective-permute-start.18 = (bf16[128,512]{1,0:T(8,128)(2,1)S(1)}, bf16[128,512]{1,0:T(8,128)(2,1)S(1)}, u32[]{:S(2)}, u32[]{:S(2)}) collective-permute-start(bf16[128,512]{1,0:T(8,128)(2,1)S(1)} %get-tuple-element.19), channel_id=1, source_target_pairs={{0,128},{1,129},{2,160},{3,161},{4,192},{5,193},{6,224},{7,225},{8... | collective-permute-start | bytes 393224 | tf_op jit(solution)/shard_map/ppermute | solution.py:206
  105.8 11.9 %collective-permute-start.22 = (bf16[128,384]{1,0:T(8,128)(2,1)S(1)}, bf16[128,384]{1,0:T(8,128)(2,1)S(1)}, u32[]{:S(2)}, u32[]{:S(2)}) collective-permute-start(bf16[128,384]{1,0:T(8,128)(2,1)S(1)} %get-tuple-element.24), channel_id=1, source_target_pairs={{0,0},{1,1},{2,32},{3,33},{4,64},{5,65},{6,96},{7,97},{8,128},{9,1... | collective-permute-start | bytes 294920 | tf_op jit(solution)/shard_map/ppermute | solution.py:206
  114.6 12.0 %collective-permute-start.23 = (bf16[128,384]{1,0:T(8,128)(2,1)S(1)}, bf16[128,384]{1,0:T(8,128)(2,1)S(1)}, u32[]{:S(2)}, u32[]{:S(2)}) collective-permute-start(bf16[128,384]{1,0:T(8,128)(2,1)S(1)} %get-tuple-element.25), channel_id=1, source_target_pairs={{0,128},{1,129},{2,160},{3,161},{4,192},{5,193},{6,224},{7,225},{8... | collective-permute-start | bytes 294920 | tf_op jit(solution)/shard_map/ppermute | solution.py:206

commit v3 on v1

v3 whole, which is shorter than its diff:
```python
import numpy as np
import jax
import jax.numpy as jnp
from jax import lax
from jax.experimental import pallas as pl
from jax.experimental.pallas import tpu as pltpu
from jax.sharding import Mesh, PartitionSpec as P

BLOCK = 128
Z, XH, XL, Y, C = 8, 2, 2, 4, 2
S = XL * Y
FSDP = ("z", "xh")
TP = ("xl", "y", "c")
ALL = FSDP + TP
BF16, F32 = jnp.bfloat16, jnp.float32
VMEM = pl.BlockSpec(memory_space=pltpu.VMEM)
SMEM = pl.BlockSpec(memory_space=pltpu.SMEM)

TURN = (0, 2, 4, 6, 1, 3, 5, 7)


def number_of(z, s):
    return TURN[s] if z % 2 == 0 else 7 - TURN[s]


def half_of(number, c):
    return c if number in (0, 7) else (number - 1) % 2


def device_index(z, xh, s, c):
    return ((z * XH + xh) * S + s) * C + c


def home_pairs(j):
    pairs = []
    for z in range(Z):
        for xh in range(XH):
            for s in range(S):
                for c in range(C):
                    number = number_of(z, s)
                    away = (number + 1) // 2
                    to = (z - away if c == 0 else z + away) % Z
                    pairs.append((device_index(z, xh, s, c), device_index(to, xh, z, j ^ half_of(number, c))))
    return pairs


def facts():
    rows = []
    for z in range(Z):
        for xh in range(XH):
            for xl in range(XL):
                for y in range(Y):
                    for c in range(C):
                        place = [0] * S
                        for s in range(S):
                            place[number_of(z, s)] = 2 * ((s % Y - y) % Y) + ((s // Y) ^ xl)
                        rows.append(place + [c, half_of(number_of(z, xl * Y + y), c) ^ xh])
    return np.array(rows, np.int32)


def shift(x, axis, size, by):
    return lax.ppermute(x, axis, [(i, (i + by) % size) for i in range(size)])


def dequantize(values, scales):
    rows, cols = values.shape
    grid = values.astype(F32).reshape(rows // BLOCK, BLOCK, cols // BLOCK, BLOCK)
    grid = grid * scales.astype(F32)[:, None, :, None]
    return grid.reshape(rows, cols).astype(BF16)


DIMS = (((1,), (1,)), ((), ()))


def times(lhs, w_own, w_other):
    half = lhs.shape[1] // 2
    total = lax.dot_general(lhs[:, :half], w_own, DIMS, preferred_element_type=F32)
    total += lax.dot_general(lhs[:, half:], w_other, DIMS, preferred_element_type=F32)
    return total.astype(BF16)


def params(mib):
    return pltpu.CompilerParams(vmem_limit_bytes=mib * 2**20)


def product_xl(own, tokens, far, w_own, w_other):
    rows, depth = far.shape
    width = w_own.shape[0]

    def kernel(facts_ref, t0, t1, t2, t3, far_ref, w_own_ref, w_other_ref, lhs_ref, keep_ref, send_ref):
        lhs_ref[facts_ref[0]] = t0[pl.ds(pl.multiple_of(facts_ref[S] * rows, rows), rows), :]
        for i, ref in enumerate((t1, t2, t3)):
            for h in range(2):
                lhs_ref[facts_ref[1 + 2 * i + h]] = ref[h * rows : (h + 1) * rows, :]
        lhs_ref[facts_ref[7]] = far_ref[...]
        for d in range(Y):
            pair = lhs_ref[2 * d : 2 * d + 2].reshape(2 * rows, depth)
            total = times(pair, w_own_ref[...], w_other_ref[...])
            keep_ref[d] = total[:rows]
            send_ref[d] = total[rows:]

    part = jax.ShapeDtypeStruct((Y, rows, width), BF16)
    return pl.pallas_call(
        kernel,
        in_specs=[SMEM] + [VMEM] * 7,
        out_specs=[VMEM] * 3,
        out_shape=[jax.ShapeDtypeStruct((S, rows, depth), BF16), part, part],
        compiler_params=params(32),
        cost_estimate=pl.CostEstimate(flops=2 * S * rows * depth * width, bytes_accessed=8 * 2**20, transcendentals=0),
    )(own, *tokens, far, w_own, w_other)


def product_y(lhs, w_own, w_other):
    _, rows, depth = lhs.shape
    width = w_own.shape[0]

    def kernel(lhs_ref, w_own_ref, w_other_ref, *out_refs):
        for d in range(Y):
            pair = lhs_ref[2 * d : 2 * d + 2].reshape(2 * rows, depth)
            total = times(pair, w_own_ref[...], w_other_ref[...])
            out_refs[d][0] = total[:rows]
            out_refs[d][1] = total[rows:]

    return pl.pallas_call(
        kernel,
        in_specs=[VMEM] * 3,
        out_specs=[VMEM] * Y,
        out_shape=[jax.ShapeDtypeStruct((2, rows, width), BF16)] * Y,
        compiler_params=params(32),
        cost_estimate=pl.CostEstimate(flops=2 * S * rows * depth * width, bytes_accessed=6 * 2**20, transcendentals=0),
    )(lhs, w_own, w_other)


def add_y(parts):
    _, rows, width = parts[0].shape

    def kernel(*refs):
        for e in range(2):
            total = refs[0][e].astype(F32)
            for ref in refs[1:Y]:
                total += ref[e].astype(F32)
            refs[Y + e][...] = total.astype(BF16)

    return pl.pallas_call(
        kernel,
        in_specs=[VMEM] * Y,
        out_specs=[VMEM] * 2,
        out_shape=[jax.ShapeDtypeStruct((rows, width), BF16)] * 2,
        compiler_params=params(16),
        cost_estimate=pl.CostEstimate(flops=2 * Y * rows * width, bytes_accessed=4 * (Y + 1) * rows * width, transcendentals=0),
    )(*parts)


def add_xl(kept, received):
    _, rows, width = kept.shape

    def kernel(kept_ref, received_ref, *out_refs):
        for d in range(Y):
            out_refs[d][...] = (kept_ref[d].astype(F32) + received_ref[d].astype(F32)).astype(BF16)

    return pl.pallas_call(
        kernel,
        in_specs=[VMEM] * 2,
        out_specs=[VMEM] * Y,
        out_shape=[jax.ShapeDtypeStruct((rows, width), BF16)] * Y,
        compiler_params=params(16),
        cost_estimate=pl.CostEstimate(flops=Y * rows * width, bytes_accessed=6 * Y * rows * width, transcendentals=0),
    )(kept, received)


def add_last(own, near_parts, cross_parts):
    rows, width = near_parts[0].shape
    count = len(near_parts)

    def kernel(facts_ref, *refs):
        sums = []
        for parts in (refs[:count], refs[count : count + Y]):
            total = parts[0][...].astype(F32)
            for ref in parts[1:]:
                total += ref[...].astype(F32)
            sums.append(total)
        straight = facts_ref[S + 1] == 0
        refs[count + Y][...] = jnp.where(straight, sums[0], sums[1]).astype(BF16)
        refs[count + Y + 1][...] = jnp.where(straight, sums[1], sums[0]).astype(BF16)

    return pl.pallas_call(
        kernel,
        in_specs=[SMEM] + [VMEM] * (count + Y),
        out_specs=[VMEM] * 2,
        out_shape=[jax.ShapeDtypeStruct((rows, width), BF16)] * 2,
        compiler_params=params(16),
        cost_estimate=pl.CostEstimate(flops=8 * rows * width, bytes_accessed=16 * rows * width, transcendentals=0),
    )(own, *near_parts, *cross_parts)


def swiglu_backward(own, hidden, gate_act, up_act):
    rows, width = gate_act.shape
    half = rows // 2

    def kernel(facts_ref, first, second, gate_ref, up_ref, grad_gate_ref, grad_up_ref):
        flip = facts_ref[S] == 1
        for h, (straight, crossed) in enumerate(((first, second), (second, first))):
            here = slice(h * half, (h + 1) * half)
            value = jnp.where(flip, crossed[...].astype(F32), straight[...].astype(F32))
            gate = gate_ref[here, :].astype(F32)
            sigmoid = jax.nn.sigmoid(gate)
            grad_up_ref[here, :] = (value * gate * sigmoid).astype(BF16)
            slope = sigmoid * (1.0 + gate * (1.0 - sigmoid))
            grad_gate_ref[here, :] = (value * up_ref[here, :].astype(F32) * slope).astype(BF16)

    return pl.pallas_call(
        kernel,
        in_specs=[SMEM] + [VMEM] * 4,
        out_specs=[VMEM] * 2,
        out_shape=[jax.ShapeDtypeStruct((rows, width), BF16)] * 2,
        compiler_params=params(16),
        cost_estimate=pl.CostEstimate(flops=10 * rows * width, bytes_accessed=10 * rows * width, transcendentals=rows * width),
    )(own, *hidden, gate_act, up_act)


def on_device(grad_out, down_q, scales, gate_act, up_act):
    c = lax.axis_index("c")
    own = lax.dynamic_index_in_dim(jnp.asarray(facts()), lax.axis_index(ALL), 0, keepdims=False)

    rows = grad_out.shape[0] // 2
    tokens = [jnp.concatenate([grad_out, shift(grad_out, "c", C, 1)], 1)]
    around = [(i * C, (i + 1) % Z * C) for i in range(Z)] + [(i * C + 1, (i - 1) % Z * C + 1) for i in range(Z)]
    for _ in range(3):
        tokens.append(lax.ppermute(tokens[-1], ("z", "c"), around))
    far = lax.ppermute(lax.dynamic_slice_in_dim(tokens[3], c * rows, rows, 0), ("z", "c"), around)

    near_own = dequantize(down_q, scales)
    cross_own = shift(near_own, "xh", XH, 1)
    near_other = shift(near_own, "c", C, 1)
    late, _ = lax.optimization_barrier((cross_own, tokens[3]))
    cross_other = shift(late, "c", C, 1)

    lhs, kept, sent = product_xl(own, tokens, far, cross_own, cross_other)
    cross = add_xl(kept, shift(sent, "xl", XL, 1))
    cross_parts = [cross[0]] + [shift(cross[d], "y", Y, d) for d in range(1, Y)]

    near = product_y(lhs, near_own, near_other)
    kept, sent = add_y([near[0]] + [shift(near[d], "y", Y, d) for d in range(1, Y)])
    near_parts = [kept, shift(sent, "xl", XL, 1)]

    sums = add_last(own, near_parts, cross_parts)
    hidden = [lax.ppermute(sums[j], ALL, home_pairs(j)) for j in range(2)]
    return tuple(swiglu_backward(own, hidden, gate_act, up_act))


def solution(mesh):
    fine = Mesh(mesh.devices.reshape(Z, XH, XL, Y, C), ALL)
    spec = P(FSDP, TP)
    return jax.shard_map(
        on_device, mesh=fine, in_specs=(spec,) * 5, out_specs=(spec, spec), check_vma=False
    )
```

time: 129 us -> 125 us (0.969)
  the two profiles are of different devices: /device:TPU:2 before, /device:TPU:7 now
where the time goes in v3:
time: 125 us
  waiting for transfers between devices  73.3 us (59%)
  starting transfers between devices  34.9 us (28%)
  Pallas kernels  10.3 us (8%)
  local copies, waits for them, and re-layouts  5.32 us (4%)
    ppermute x12, waiting for transfers between devices, shift(): return lax.ppermute(x, axis, [(i, (i + by) % size) for i in range(size)])  37.1 us
    ppermute x2, waiting for transfers between devices, on_device(): hidden = [lax.ppermute(sums[j], ALL, home_pairs(j)) for j in range(2)]  22.6 us
    ppermute x12, starting transfers between devices, shift(): return lax.ppermute(x, axis, [(i, (i + by) % size) for i in range(size)])  12.3 us
    ppermute x3, starting transfers between devices, on_device(): tokens.append(lax.ppermute(tokens[-1], ('z', 'c'), around))  12.2 us
    ppermute x3, waiting for transfers between devices, on_device(): tokens.append(lax.ppermute(tokens[-1], ('z', 'c'), around))  9.58 us
    ppermute x2, starting transfers between devices, on_device(): hidden = [lax.ppermute(sums[j], ALL, home_pairs(j)) for j in range(2)]  9.29 us
    ppermute x1, waiting for transfers between devices, on_device(): lax.ppermute(lax.dynamic_slice_in_dim(tokens[3], c * rows, rows, 0), ('z'...  3.99 us
    pallas_call x1, Pallas kernels, product_xl(): pl.pallas_call(kernel, in_specs=[SMEM] + [VMEM] * 7, out_specs=[VMEM] * 3...  3.72 us
  transfers between devices with their start and end apart: 18, of which 12 were waited for; matrix products, arithmetic and copies ran while one was open for 3% of the time, Pallas kernels for 6%

profile of v3, /device:TPU:7, one launch (start us, length us, event | category | flops | bytes accessed | tf_op | source)
XLA Modules:
  0.0 125.0 jit_solution(6955929211519321034)
XLA Ops:
  0.6 0.8 collective-permute-start
  1.4 1.0 constant_dynamic-update-slice_fusion.1
  2.4 0.4 collective-permute-done
  2.8 5.7 %collective-permute-start.1 = (bf16[256,1024]{1,0:T(8,128)(2,1)S(1)}, bf16[256,1024]{1,0:T(8,128)(2,1)S(1)}, u32[]{:S(2)}, u32[]{:S(2)}) collective-permute-start(bf16[256,1024]{1,0:T(8,128)(2,1)S(1)} %constant_dynamic-update-slice_fusion.t0), channel_id=1, source_target_pairs={{0,32},{32,64},{64,96},{96,128},{128,160},{160,192},{192,224},{224... | collective-permute-start | bytes 1572872 | tf_op jit(solution)/shard_map/ppermute | solution.py:229
  8.5 0.8 copy.8
  9.2 5.4 %collective-permute-done.1.t1 = bf16[256,1024]{1,0:T(8,128)(2,1)S(1)} collective-permute-done((bf16[256,1024]{1,0:T(8,128)(2,1)S(1)}, bf16[256,1024]{1,0:T(8,128)(2,1)S(1)}, u32[]{:S(2)}, u32[]{:S(2)}) %collective-permute-start.1) | collective-permute-done | bytes 524320 | tf_op jit(solution)/shard_map/ppermute | solution.py:229
  14.6 3.1 %collective-permute-start.2 = (bf16[256,1024]{1,0:T(8,128)(2,1)S(1)}, bf16[256,1024]{1,0:T(8,128)(2,1)S(1)}, u32[]{:S(2)}, u32[]{:S(2)}) collective-permute-start(bf16[256,1024]{1,0:T(8,128)(2,1)S(1)} %collective-permute-done.1.t1), channel_id=1, source_target_pairs={{0,32},{32,64},{64,96},{96,128},{128,160},{160,192},{192,224},{224... | collective-permute-start | bytes 1572872 | tf_op jit(solution)/shard_map/ppermute | solution.py:229
  17.7 0.3 mul.31
  18.0 0.4 fusion.w_own_ref
  18.4 1.2 collective-permute-start.5
  19.6 4.2 %collective-permute-done.2.t2 = bf16[256,1024]{1,0:T(8,128)(2,1)S(1)} collective-permute-done((bf16[256,1024]{1,0:T(8,128)(2,1)S(1)}, bf16[256,1024]{1,0:T(8,128)(2,1)S(1)}, u32[]{:S(2)}, u32[]{:S(2)}) %collective-permute-start.2) | collective-permute-done | bytes 524320 | tf_op jit(solution)/shard_map/ppermute | solution.py:229
  23.8 3.4 %collective-permute-start.3 = (bf16[256,1024]{1,0:T(8,128)(2,1)S(1)}, bf16[256,1024]{1,0:T(8,128)(2,1)S(1)}, u32[]{:S(2)}, u32[]{:S(2)}) collective-permute-start(bf16[256,1024]{1,0:T(8,128)(2,1)S(1)} %collective-permute-done.2.t2), channel_id=1, source_target_pairs={{0,32},{32,64},{64,96},{96,128},{128,160},{160,192},{192,224},{224... | collective-permute-start | bytes 1572872 | tf_op jit(solution)/shard_map/ppermute | solution.py:229
  27.2 0.8 copy-done.2
  28.0 13.1 %collective-permute-done.5.w_own_ref = bf16[896,512]{1,0:T(8,128)(2,1)S(1)} collective-permute-done((bf16[896,512]{1,0:T(8,128)(2,1)S(1)}, bf16[896,512]{1,0:T(8,128)(2,1)S(1)}, u32[]{:S(2)}, u32[]{:S(2)}) %collective-permute-start.5) | collective-permute-done | bytes 917536 | tf_op jit(solution)/shard_map/ppermute | solution.py:62
  41.1 0.0 collective-permute-done.3.t3
  41.1 0.5 collective-permute-start.7
  41.6 0.7 constant_dynamic-slice_fusion
  42.3 1.1 collective-permute-start.4
  43.5 0.7 dynamic-slice_bitcast_fusion.facts_ref
  44.2 4.0 %collective-permute-done.4.far_ref = bf16[128,1024]{1,0:T(8,128)(2,1)} collective-permute-done((bf16[128,1024]{1,0:T(8,128)(2,1)}, bf16[128,1024]{1,0:T(8,128)(2,1)}, u32[]{:S(2)}, u32[]{:S(2)}) %collective-permute-start.4) | collective-permute-done | bytes 262176 | tf_op jit(solution)/shard_map/ppermute | solution.py:230
  48.2 0.0 collective-permute-done.6.w_other_ref
  48.2 1.0 copy-done.3
  49.2 3.7 %shard_map.77 = (bf16[8,128,1024]{2,1,0:T(8,128)(2,1)S(1)}, bf16[4,128,896]{2,1,0:T(8,128)(2,1)S(1)}, bf16[4,128,896]{2,1,0:T(8,128)(2,1)S(1)}) custom-call(s32[10]{0:T(128)S(1)} %dynamic-slice_bitcast_fusion.facts_ref, bf16[256,1024]{1,0:T(8,128)(2,1)S(1)} %constant_dynamic-update-slice_fusion.t0, bf16[256,1024]{1,0:T(8,128)(2,1)S(1)} %collective-permute-done.1.t1, ...), custom_call_target="tpu_custom_call" | custom-call | flops 1879048192 | bytes 8388608 | tf_op jit(solution)/shard_map/pallas_call | solution.py:103
  52.9 0.6 collective-permute-start.12
  53.6 3.5 %shard_map.78 = (bf16[2,128,896]{2,1,0:T(8,128)(2,1)S(1)}, bf16[2,128,896]{2,1,0:T(8,128)(2,1)S(1)}, bf16[2,128,896]{2,1,0:T(8,128)(2,1)S(1)}, bf16[2,128,896]{2,1,0:T(8,128)(2,1)S(1)}) custom-call(bf16[8,128,1024]{2,1,0:T(8,128)(2,1)S(1)} %get-tuple-element.19.lhs_ref, bf16[896,512]{1,0:T(8,128)(2,1)S(1)} %fusion.w_own_ref, ...), custom_call_target="tpu_custom_call" | custom-call | flops 1879048192 | bytes 6291456 | tf_op jit(solution)/shard_map/pallas_call | solution.py:124
  57.1 2.8 %collective-permute-start.10 = (bf16[2,128,896]{2,1,0:T(8,128)(2,1)S(1)}, bf16[2,128,896]{2,1,0:T(8,128)(2,1)S(1)}, u32[]{:S(2)}, u32[]{:S(2)}) collective-permute-start(bf16[2,128,896]{2,1,0:T(8,128)(2,1)S(1)} %get-tuple-element.23), channel_id=1, source_target_pairs={{0,6},{2,0},{4,2},{6,4},{1,7},{3,1},{5,3},{7,5},{8,14},{10,8},{12,... | collective-permute-start | bytes 1376264 | tf_op jit(solution)/shard_map/ppermute | solution.py:62
  59.9 1.6 %collective-permute-start.9 = (bf16[2,128,896]{2,1,0:T(8,128)(2,1)S(1)}, bf16[2,128,896]{2,1,0:T(8,128)(2,1)S(1)}, u32[]{:S(2)}, u32[]{:S(2)}) collective-permute-start(bf16[2,128,896]{2,1,0:T(8,128)(2,1)S(1)} %get-tuple-element.22), channel_id=1, source_target_pairs={{0,4},{2,6},{4,0},{6,2},{1,5},{3,7},{5,1},{7,3},{8,12},{10,14},{12... | collective-permute-start | bytes 1376264 | tf_op jit(solution)/shard_map/ppermute | solution.py:62
  61.6 6.8 %collective-permute-done.10.refs_3_ = bf16[2,128,896]{2,1,0:T(8,128)(2,1)S(1)} collective-permute-done((bf16[2,128,896]{2,1,0:T(8,128)(2,1)S(1)}, bf16[2,128,896]{2,1,0:T(8,128)(2,1)S(1)}, u32[]{:S(2)}, u32[]{:S(2)}) %collective-permute-start.10) | collective-permute-done | bytes 458784 | tf_op jit(solution)/shard_map/ppermute | solution.py:62
  68.4 3.1 %collective-permute-done.8.refs_1_ = bf16[2,128,896]{2,1,0:T(8,128)(2,1)S(1)} collective-permute-done((bf16[2,128,896]{2,1,0:T(8,128)(2,1)S(1)}, bf16[2,128,896]{2,1,0:T(8,128)(2,1)S(1)}, u32[]{:S(2)}, u32[]{:S(2)}) %collective-permute-start.8) | collective-permute-done | bytes 458784 | tf_op jit(solution)/shard_map/ppermute | solution.py:62
  71.5 7.8 %collective-permute-done.9.refs_2_ = bf16[2,128,896]{2,1,0:T(8,128)(2,1)S(1)} collective-permute-done((bf16[2,128,896]{2,1,0:T(8,128)(2,1)S(1)}, bf16[2,128,896]{2,1,0:T(8,128)(2,1)S(1)}, u32[]{:S(2)}, u32[]{:S(2)}) %collective-permute-start.9) | collective-permute-done | bytes 458784 | tf_op jit(solution)/shard_map/ppermute | solution.py:62
  79.4 0.2 shard_map.79
  79.6 0.0 copy-start
  79.6 0.0 copy-start.1
  79.6 1.0 collective-permute-start.11
  80.6 0.2 shard_map.80
  80.9 0.1 collective-permute-start.13
  81.0 1.6 %collective-permute-start.14 = (bf16[128,896]{1,0:T(8,128)(2,1)S(1)}, bf16[128,896]{1,0:T(8,128)(2,1)S(1)}, u32[]{:S(2)}, u32[]{:S(2)}) collective-permute-start(bf16[128,896]{1,0:T(8,128)(2,1)S(1)} %get-tuple-element.30), channel_id=1, source_target_pairs={{0,4},{2,6},{4,0},{6,2},{1,5},{3,7},{5,1},{7,3},{8,12},{10,14},{12... | collective-permute-start | bytes 688136 | tf_op jit(solution)/shard_map/ppermute | solution.py:62
  82.6 2.0 %collective-permute-start.15 = (bf16[128,896]{1,0:T(8,128)(2,1)S(1)}, bf16[128,896]{1,0:T(8,128)(2,1)S(1)}, u32[]{:S(2)}, u32[]{:S(2)}) collective-permute-start(bf16[128,896]{1,0:T(8,128)(2,1)S(1)} %get-tuple-element.31), channel_id=1, source_target_pairs={{0,6},{2,0},{4,2},{6,4},{1,7},{3,1},{5,3},{7,5},{8,14},{10,8},{12,... | collective-permute-start | bytes 688136 | tf_op jit(solution)/shard_map/ppermute | solution.py:62
  84.6 0.0 collective-permute-done.11.refs_1_
  84.6 4.9 %collective-permute-done.13.refs_3_ = bf16[128,896]{1,0:T(8,128)(2,1)S(1)} collective-permute-done((bf16[128,896]{1,0:T(8,128)(2,1)S(1)}, bf16[128,896]{1,0:T(8,128)(2,1)S(1)}, u32[]{:S(2)}, u32[]{:S(2)}) %collective-permute-start.13) | collective-permute-done | bytes 229408 | tf_op jit(solution)/shard_map/ppermute | solution.py:62
  89.5 0.0 collective-permute-done.14.refs_4_
  89.5 0.9 collective-permute-done.15.refs_5_
  90.4 0.8 shard_map.81
  91.1 7.6 %collective-permute-start.16 = (bf16[128,896]{1,0:T(8,128)(2,1)S(1)}, bf16[128,896]{1,0:T(8,128)(2,1)S(1)}, u32[]{:S(2)}, u32[]{:S(2)}) collective-permute-start(bf16[128,896]{1,0:T(8,128)(2,1)S(1)} %get-tuple-element.32), channel_id=1, source_target_pairs={{0,0},{1,1},{2,225},{3,33},{4,193},{5,65},{6,161},{7,97},{8,224},{... | collective-permute-start | bytes 688136 | tf_op jit(solution)/shard_map/ppermute | solution.py:247
  98.8 1.7 %collective-permute-start.17 = (bf16[128,896]{1,0:T(8,128)(2,1)S(1)}, bf16[128,896]{1,0:T(8,128)(2,1)S(1)}, u32[]{:S(2)}, u32[]{:S(2)}) collective-permute-start(bf16[128,896]{1,0:T(8,128)(2,1)S(1)} %get-tuple-element.33), channel_id=1, source_target_pairs={{0,1},{1,0},{2,224},{3,32},{4,192},{5,64},{6,160},{7,96},{8,225},{... | collective-permute-start | bytes 688136 | tf_op jit(solution)/shard_map/ppermute | solution.py:247
  100.4 3.7 %collective-permute-done.16.first = bf16[128,896]{1,0:T(8,128)(2,1)S(1)} collective-permute-done((bf16[128,896]{1,0:T(8,128)(2,1)S(1)}, bf16[128,896]{1,0:T(8,128)(2,1)S(1)}, u32[]{:S(2)}, u32[]{:S(2)}) %collective-permute-start.16) | collective-permute-done | bytes 229408 | tf_op jit(solution)/shard_map/ppermute | solution.py:247
  104.2 18.9 %collective-permute-done.17.second = bf16[128,896]{1,0:T(8,128)(2,1)S(1)} collective-permute-done((bf16[128,896]{1,0:T(8,128)(2,1)S(1)}, bf16[128,896]{1,0:T(8,128)(2,1)S(1)}, u32[]{:S(2)}, u32[]{:S(2)}) %collective-permute-start.17) | collective-permute-done | bytes 229408 | tf_op jit(solution)/shard_map/ppermute | solution.py:247
  123.1 1.9 %shard_map.82 = (bf16[256,896]{1,0:T(8,128)(2,1)}, bf16[256,896]{1,0:T(8,128)(2,1)}) custom-call(s32[10]{0:T(128)S(1)} %dynamic-slice_bitcast_fusion.facts_ref, bf16[128,896]{1,0:T(8,128)(2,1)S(1)} %collective-permute-done.16.first, bf16[128,896]{1,0:T(8,128)(2,1)S(1)} %collective-permute-done.17.second, bf16[256,896]{1,0:T(8,128)(2,1)S(1)} %copy-done, ...), custom_call_target="tpu_custom_call" | custom-call | flops 2293760 | bytes 2293760 | tf_op jit(solution)/shard_map/pallas_call | solution.py:211
  (11 shorter events, 0.0 us)
Async XLA Ops:
  0.6 17.4 %copy-start.4 = (bf16[896,512]{1,0:T(8,128)(2,1)S(1)}, bf16[896,512]{1,0:T(8,128)(2,1)}, u32[]{:S(2)}) copy-start(bf16[896,512]{1,0:T(8,128)(2,1)} %param.7) | copy-start | bytes 2752516
  0.6 2.1 %collective-permute-start = (bf16[256,512]{1,0:T(8,128)(2,1)}, bf16[256,512]{1,0:T(8,128)(2,1)S(1)}, u32[]{:S(2)}, u32[]{:S(2)}) collective-permute-start(bf16[256,512]{1,0:T(8,128)(2,1)} %param.6), channel_id=1, source_target_pairs={{0,1},{1,0},{2,3},{3,2},{4,5},{5,4},{6,7},{7,6},{8,9},{9,8},{10,11... | collective-permute-start | bytes 786440 | tf_op jit(solution)/shard_map/ppermute | solution.py:62
  2.8 11.8 %collective-permute-start.1 = (bf16[256,1024]{1,0:T(8,128)(2,1)S(1)}, bf16[256,1024]{1,0:T(8,128)(2,1)S(1)}, u32[]{:S(2)}, u32[]{:S(2)}) collective-permute-start(bf16[256,1024]{1,0:T(8,128)(2,1)S(1)} %constant_dynamic-update-slice_fusion.t0), channel_id=1, source_target_pairs={{0,32},{32,64},{64,96},{96,128},{128,160},{160,192},{192,224},{224... | collective-permute-start | bytes 1572872 | tf_op jit(solution)/shard_map/ppermute | solution.py:229
  14.6 9.2 %collective-permute-start.2 = (bf16[256,1024]{1,0:T(8,128)(2,1)S(1)}, bf16[256,1024]{1,0:T(8,128)(2,1)S(1)}, u32[]{:S(2)}, u32[]{:S(2)}) collective-permute-start(bf16[256,1024]{1,0:T(8,128)(2,1)S(1)} %collective-permute-done.1.t1), channel_id=1, source_target_pairs={{0,32},{32,64},{64,96},{96,128},{128,160},{160,192},{192,224},{224... | collective-permute-start | bytes 1572872 | tf_op jit(solution)/shard_map/ppermute | solution.py:229
  18.4 22.7 %collective-permute-start.5 = (bf16[896,512]{1,0:T(8,128)(2,1)S(1)}, bf16[896,512]{1,0:T(8,128)(2,1)S(1)}, u32[]{:S(2)}, u32[]{:S(2)}) collective-permute-start(bf16[896,512]{1,0:T(8,128)(2,1)S(1)} %fusion.w_own_ref), channel_id=1, source_target_pairs={{0,16},{16,0},{1,17},{17,1},{2,18},{18,2},{3,19},{19,3},{4,20},{20... | collective-permute-start | bytes 2752520 | tf_op jit(solution)/shard_map/ppermute | solution.py:62
  23.8 17.3 %collective-permute-start.3 = (bf16[256,1024]{1,0:T(8,128)(2,1)S(1)}, bf16[256,1024]{1,0:T(8,128)(2,1)S(1)}, u32[]{:S(2)}, u32[]{:S(2)}) collective-permute-start(bf16[256,1024]{1,0:T(8,128)(2,1)S(1)} %collective-permute-done.2.t2), channel_id=1, source_target_pairs={{0,32},{32,64},{64,96},{96,128},{128,160},{160,192},{192,224},{224... | collective-permute-start | bytes 1572872 | tf_op jit(solution)/shard_map/ppermute | solution.py:229
  27.2 0.8 copy-start.2
  41.1 7.1 %collective-permute-start.6 = (bf16[896,512]{1,0:T(8,128)(2,1)S(1)}, bf16[896,512]{1,0:T(8,128)(2,1)}, u32[]{:S(2)}, u32[]{:S(2)}) collective-permute-start(bf16[896,512]{1,0:T(8,128)(2,1)S(1)} %collective-permute-done.5.w_own_ref), channel_id=1, source_target_pairs={{0,1},{1,0},{2,3},{3,2},{4,5},{5,4},{6,7},{7,6},{8,9},{9,8},{10,11... | collective-permute-start | bytes 2752520 | tf_op jit(solution)/shard_map/ppermute | solution.py:62
  41.1 12.5 %collective-permute-start.7 = (bf16[896,512]{1,0:T(8,128)(2,1)S(1)}, bf16[896,512]{1,0:T(8,128)(2,1)}, u32[]{:S(2)}, u32[]{:S(2)}) collective-permute-start(bf16[896,512]{1,0:T(8,128)(2,1)S(1)} %fusion.w_own_ref), channel_id=1, source_target_pairs={{0,1},{1,0},{2,3},{3,2},{4,5},{5,4},{6,7},{7,6},{8,9},{9,8},{10,11... | collective-permute-start | bytes 2752520 | tf_op jit(solution)/shard_map/ppermute | solution.py:62
  42.3 5.8 %collective-permute-start.4 = (bf16[128,1024]{1,0:T(8,128)(2,1)}, bf16[128,1024]{1,0:T(8,128)(2,1)}, u32[]{:S(2)}, u32[]{:S(2)}) collective-permute-start(bf16[128,1024]{1,0:T(8,128)(2,1)} %constant_dynamic-slice_fusion), channel_id=1, source_target_pairs={{0,32},{32,64},{64,96},{96,128},{128,160},{160,192},{192,224},{224... | collective-permute-start | bytes 786440 | tf_op jit(solution)/shard_map/ppermute | solution.py:230
  48.2 1.0 copy-start.3
  52.9 27.7 %collective-permute-start.12 = (bf16[4,128,896]{2,1,0:T(8,128)(2,1)S(1)}, bf16[4,128,896]{2,1,0:T(8,128)(2,1)S(1)}, u32[]{:S(2)}, u32[]{:S(2)}) collective-permute-start(bf16[4,128,896]{2,1,0:T(8,128)(2,1)S(1)} %get-tuple-element.27), channel_id=1, source_target_pairs={{0,8},{8,0},{1,9},{9,1},{2,10},{10,2},{3,11},{11,3},{4,12},{12,4},... | collective-permute-start | bytes 2752520 | tf_op jit(solution)/shard_map/ppermute | solution.py:62
  57.1 11.3 %collective-permute-start.10 = (bf16[2,128,896]{2,1,0:T(8,128)(2,1)S(1)}, bf16[2,128,896]{2,1,0:T(8,128)(2,1)S(1)}, u32[]{:S(2)}, u32[]{:S(2)}) collective-permute-start(bf16[2,128,896]{2,1,0:T(8,128)(2,1)S(1)} %get-tuple-element.23), channel_id=1, source_target_pairs={{0,6},{2,0},{4,2},{6,4},{1,7},{3,1},{5,3},{7,5},{8,14},{10,8},{12,... | collective-permute-start | bytes 1376264 | tf_op jit(solution)/shard_map/ppermute | solution.py:62
  59.9 11.6 %collective-permute-start.8 = (bf16[2,128,896]{2,1,0:T(8,128)(2,1)S(1)}, bf16[2,128,896]{2,1,0:T(8,128)(2,1)S(1)}, u32[]{:S(2)}, u32[]{:S(2)}) collective-permute-start(bf16[2,128,896]{2,1,0:T(8,128)(2,1)S(1)} %get-tuple-element.21), channel_id=1, source_target_pairs={{0,2},{2,4},{4,6},{6,0},{1,3},{3,5},{5,7},{7,1},{8,10},{10,12},{12... | collective-permute-start | bytes 1376264 | tf_op jit(solution)/shard_map/ppermute | solution.py:62
  59.9 19.4 %collective-permute-start.9 = (bf16[2,128,896]{2,1,0:T(8,128)(2,1)S(1)}, bf16[2,128,896]{2,1,0:T(8,128)(2,1)S(1)}, u32[]{:S(2)}, u32[]{:S(2)}) collective-permute-start(bf16[2,128,896]{2,1,0:T(8,128)(2,1)S(1)} %get-tuple-element.22), channel_id=1, source_target_pairs={{0,4},{2,6},{4,0},{6,2},{1,5},{3,7},{5,1},{7,3},{8,12},{10,14},{12... | collective-permute-start | bytes 1376264 | tf_op jit(solution)/shard_map/ppermute | solution.py:62
  79.6 43.5 %copy-start = (bf16[256,896]{1,0:T(8,128)(2,1)S(1)}, bf16[256,896]{1,0:T(8,128)(2,1)}, u32[]{:S(2)}) copy-start(bf16[256,896]{1,0:T(8,128)(2,1)} %gate_ref.1) | copy-start | bytes 1376260
  79.6 43.5 %copy-start.1 = (bf16[256,896]{1,0:T(8,128)(2,1)S(1)}, bf16[256,896]{1,0:T(8,128)(2,1)}, u32[]{:S(2)}) copy-start(bf16[256,896]{1,0:T(8,128)(2,1)} %up_ref.1) | copy-start | bytes 1376260
  79.6 5.0 %collective-permute-start.11 = (bf16[128,896]{1,0:T(8,128)(2,1)S(1)}, bf16[128,896]{1,0:T(8,128)(2,1)S(1)}, u32[]{:S(2)}, u32[]{:S(2)}) collective-permute-start(bf16[128,896]{1,0:T(8,128)(2,1)S(1)} %get-tuple-element.25), channel_id=1, source_target_pairs={{0,8},{8,0},{1,9},{9,1},{2,10},{10,2},{3,11},{11,3},{4,12},{12,4},... | collective-permute-start | bytes 688136 | tf_op jit(solution)/shard_map/ppermute | solution.py:62
  80.9 8.6 %collective-permute-start.13 = (bf16[128,896]{1,0:T(8,128)(2,1)S(1)}, bf16[128,896]{1,0:T(8,128)(2,1)S(1)}, u32[]{:S(2)}, u32[]{:S(2)}) collective-permute-start(bf16[128,896]{1,0:T(8,128)(2,1)S(1)} %get-tuple-element.29), channel_id=1, source_target_pairs={{0,2},{2,4},{4,6},{6,0},{1,3},{3,5},{5,7},{7,1},{8,10},{10,12},{12... | collective-permute-start | bytes 688136 | tf_op jit(solution)/shard_map/ppermute | solution.py:62
  81.0 8.5 %collective-permute-start.14 = (bf16[128,896]{1,0:T(8,128)(2,1)S(1)}, bf16[128,896]{1,0:T(8,128)(2,1)S(1)}, u32[]{:S(2)}, u32[]{:S(2)}) collective-permute-start(bf16[128,896]{1,0:T(8,128)(2,1)S(1)} %get-tuple-element.30), channel_id=1, source_target_pairs={{0,4},{2,6},{4,0},{6,2},{1,5},{3,7},{5,1},{7,3},{8,12},{10,14},{12... | collective-permute-start | bytes 688136 | tf_op jit(solution)/shard_map/ppermute | solution.py:62
  82.6 7.8 %collective-permute-start.15 = (bf16[128,896]{1,0:T(8,128)(2,1)S(1)}, bf16[128,896]{1,0:T(8,128)(2,1)S(1)}, u32[]{:S(2)}, u32[]{:S(2)}) collective-permute-start(bf16[128,896]{1,0:T(8,128)(2,1)S(1)} %get-tuple-element.31), channel_id=1, source_target_pairs={{0,6},{2,0},{4,2},{6,4},{1,7},{3,1},{5,3},{7,5},{8,14},{10,8},{12,... | collective-permute-start | bytes 688136 | tf_op jit(solution)/shard_map/ppermute | solution.py:62
  91.1 13.0 %collective-permute-start.16 = (bf16[128,896]{1,0:T(8,128)(2,1)S(1)}, bf16[128,896]{1,0:T(8,128)(2,1)S(1)}, u32[]{:S(2)}, u32[]{:S(2)}) collective-permute-start(bf16[128,896]{1,0:T(8,128)(2,1)S(1)} %get-tuple-element.32), channel_id=1, source_target_pairs={{0,0},{1,1},{2,225},{3,33},{4,193},{5,65},{6,161},{7,97},{8,224},{... | collective-permute-start | bytes 688136 | tf_op jit(solution)/shard_map/ppermute | solution.py:247
  98.8 24.3 %collective-permute-start.17 = (bf16[128,896]{1,0:T(8,128)(2,1)S(1)}, bf16[128,896]{1,0:T(8,128)(2,1)S(1)}, u32[]{:S(2)}, u32[]{:S(2)}) collective-permute-start(bf16[128,896]{1,0:T(8,128)(2,1)S(1)} %get-tuple-element.33), channel_id=1, source_target_pairs={{0,1},{1,0},{2,224},{3,32},{4,192},{5,64},{6,160},{7,96},{8,225},{... | collective-permute-start | bytes 688136 | tf_op jit(solution)/shard_map/ppermute | solution.py:247

commit v4 on v3

--- a/solution.py
+++ b/solution.py
@@ -16,11 +16,20 @@
 VMEM = pl.BlockSpec(memory_space=pltpu.VMEM)
 SMEM = pl.BlockSpec(memory_space=pltpu.SMEM)
 
-TURN = (0, 2, 4, 6, 1, 3, 5, 7)
-
-
-def number_of(z, s):
-    return TURN[s] if z % 2 == 0 else 7 - TURN[s]
+NUMBER = (
+    ((2, 5, 6, 1, 4, 0, 3, 7), (7, 3, 2, 4, 6, 1, 5, 0)),
+    ((0, 5, 4, 6, 1, 7, 2, 3), (7, 3, 1, 4, 2, 5, 6, 0)),
+    ((4, 2, 7, 0, 6, 1, 5, 3), (7, 5, 1, 4, 3, 2, 0, 6)),
+    ((1, 5, 6, 4, 3, 7, 2, 0), (0, 5, 2, 1, 4, 6, 3, 7)),
+    ((6, 4, 1, 7, 3, 0, 5, 2), (1, 0, 7, 4, 6, 2, 5, 3)),
+    ((1, 3, 2, 7, 4, 6, 0, 5), (4, 6, 7, 0, 1, 3, 2, 5)),
+    ((5, 4, 2, 6, 1, 0, 3, 7), (7, 5, 2, 1, 6, 4, 3, 0)),
+    ((1, 0, 2, 4, 5, 7, 6, 3), (1, 0, 6, 4, 2, 5, 3, 7)),
+)
+
+
+def number_of(z, s, c):
+    return NUMBER[z][c][s]
 
 
 def half_of(number, c):
@@ -37,7 +46,7 @@
         for xh in range(XH):
             for s in range(S):
                 for c in range(C):
-                    number = number_of(z, s)
+                    number = number_of(z, s, c)
                     away = (number + 1) // 2
                     to = (z - away if c == 0 else z + away) % Z
                     pairs.append((device_index(z, xh, s, c), device_index(to, xh, z, j ^ half_of(number, c))))
@@ -53,8 +62,8 @@
                     for c in range(C):
                         place = [0] * S
                         for s in range(S):
-                            place[number_of(z, s)] = 2 * ((s % Y - y) % Y) + ((s // Y) ^ xl)
-                        rows.append(place + [c, half_of(number_of(z, xl * Y + y), c) ^ xh])
+                            place[number_of(z, s, c)] = 2 * ((s % Y - y) % Y) + ((s // Y) ^ xl)
+                        rows.append(place + [c, half_of(number_of(z, xl * Y + y, c), c) ^ xh])
     return np.array(rows, np.int32)
 
 
@@ -83,11 +92,11 @@
     return pltpu.CompilerParams(vmem_limit_bytes=mib * 2**20)
 
 
-def product_xl(own, tokens, far, w_own, w_other):
+def product_y(own, tokens, far, w_own, w_other):
     rows, depth = far.shape
     width = w_own.shape[0]
 
-    def kernel(facts_ref, t0, t1, t2, t3, far_ref, w_own_ref, w_other_ref, lhs_ref, keep_ref, send_ref):
+    def kernel(facts_ref, t0, t1, t2, t3, far_ref, w_own_ref, w_other_ref, lhs_ref, *out_refs):
         lhs_ref[facts_ref[0]] = t0[pl.ds(pl.multiple_of(facts_ref[S] * rows, rows), rows), :]
         for i, ref in enumerate((t1, t2, t3)):
             for h in range(2):
@@ -96,36 +105,36 @@
         for d in range(Y):
             pair = lhs_ref[2 * d : 2 * d + 2].reshape(2 * rows, depth)
             total = times(pair, w_own_ref[...], w_other_ref[...])
-            keep_ref[d] = total[:rows]
-            send_ref[d] = total[rows:]
-
-    part = jax.ShapeDtypeStruct((Y, rows, width), BF16)
+            out_refs[d][0] = total[:rows]
+            out_refs[d][1] = total[rows:]
+
     return pl.pallas_call(
         kernel,
         in_specs=[SMEM] + [VMEM] * 7,
-        out_specs=[VMEM] * 3,
-        out_shape=[jax.ShapeDtypeStruct((S, rows, depth), BF16), part, part],
+        out_specs=[VMEM] * (1 + Y),
+        out_shape=[jax.ShapeDtypeStruct((S, rows, depth), BF16)]
+        + [jax.ShapeDtypeStruct((2, rows, width), BF16)] * Y,
         compiler_params=params(32),
         cost_estimate=pl.CostEstimate(flops=2 * S * rows * depth * width, bytes_accessed=8 * 2**20, transcendentals=0),
     )(own, *tokens, far, w_own, w_other)
 
 
-def product_y(lhs, w_own, w_other):
+def product_xl(lhs, w_own, w_other):
     _, rows, depth = lhs.shape
     width = w_own.shape[0]
 
-    def kernel(lhs_ref, w_own_ref, w_other_ref, *out_refs):
+    def kernel(lhs_ref, w_own_ref, w_other_ref, keep_ref, send_ref):
         for d in range(Y):
             pair = lhs_ref[2 * d : 2 * d + 2].reshape(2 * rows, depth)
             total = times(pair, w_own_ref[...], w_other_ref[...])
-            out_refs[d][0] = total[:rows]
-            out_refs[d][1] = total[rows:]
+            keep_ref[d] = total[:rows]
+            send_ref[d] = total[rows:]
 
     return pl.pallas_call(
         kernel,
         in_specs=[VMEM] * 3,
-        out_specs=[VMEM] * Y,
-        out_shape=[jax.ShapeDtypeStruct((2, rows, width), BF16)] * Y,
+        out_specs=[VMEM] * 2,
+        out_shape=[jax.ShapeDtypeStruct((Y, rows, width), BF16)] * 2,
         compiler_params=params(32),
         cost_estimate=pl.CostEstimate(flops=2 * S * rows * depth * width, bytes_accessed=6 * 2**20, transcendentals=0),
     )(lhs, w_own, w_other)
@@ -222,25 +231,26 @@
     c = lax.axis_index("c")
     own = lax.dynamic_index_in_dim(jnp.asarray(facts()), lax.axis_index(ALL), 0, keepdims=False)
 
+    near_own = dequantize(down_q, scales)
+    cross_own = shift(near_own, "xh", XH, 1)
+
     rows = grad_out.shape[0] // 2
     tokens = [jnp.concatenate([grad_out, shift(grad_out, "c", C, 1)], 1)]
     around = [(i * C, (i + 1) % Z * C) for i in range(Z)] + [(i * C + 1, (i - 1) % Z * C + 1) for i in range(Z)]
-    for _ in range(3):
+    for step in range(3):
+        if step == 2:
+            tokens[-1], cross_own = lax.optimization_barrier((tokens[-1], cross_own))
         tokens.append(lax.ppermute(tokens[-1], ("z", "c"), around))
     far = lax.ppermute(lax.dynamic_slice_in_dim(tokens[3], c * rows, rows, 0), ("z", "c"), around)
-
-    near_own = dequantize(down_q, scales)
-    cross_own = shift(near_own, "xh", XH, 1)
     near_other = shift(near_own, "c", C, 1)
-    late, _ = lax.optimization_barrier((cross_own, tokens[3]))
-    cross_other = shift(late, "c", C, 1)
-
-    lhs, kept, sent = product_xl(own, tokens, far, cross_own, cross_other)
+    cross_other = shift(cross_own, "c", C, 1)
+
+    lhs, *near = product_y(own, tokens, far, near_own, near_other)
+    near_y = [near[0]] + [shift(near[d], "y", Y, d) for d in range(1, Y)]
+    kept, sent = product_xl(lhs, cross_own, cross_other)
     cross = add_xl(kept, shift(sent, "xl", XL, 1))
     cross_parts = [cross[0]] + [shift(cross[d], "y", Y, d) for d in range(1, Y)]
-
-    near = product_y(lhs, near_own, near_other)
-    kept, sent = add_y([near[0]] + [shift(near[d], "y", Y, d) for d in range(1, Y)])
+    kept, sent = add_y(near_y)
     near_parts = [kept, shift(sent, "xl", XL, 1)]
 
     sums = add_last(own, near_parts, cross_parts)

time: 125 us -> 119 us (0.952); the launches traced: 125 us -> 117 us
  waiting for transfers between devices: 73.3 us -> 69.5 us
  starting transfers between devices: 34.9 us -> 32.1 us
  local copies, waits for them, and re-layouts: 5.32 us -> 3.49 us
    ppermute x2, waiting for transfers between devices: 22.6 us -> 16.3 us  [on_device(): hidden = [lax.ppermute(sums[j], ALL, home_pairs(j)) for j in range(2)]]
    ppermute x2, starting transfers between devices: 9.29 us -> 2.97 us  [on_device(): hidden = [lax.ppermute(sums[j], ALL, home_pairs(j)) for j in range(2)]]
    ppermute x12, waiting for transfers between devices: 37.1 us -> 39.6 us  [shift(): return lax.ppermute(x, axis, [(i, (i + by) % size) for i in range(size)])]
    ppermute x1, starting transfers between devices: 1.15 us -> 3.01 us  [on_device(): lax.ppermute(lax.dynamic_slice_in_dim(tokens[3], c * rows, rows, 0), ('z'...]
    unnamed x11 -> x7, local copies, waits for them, and re-layouts: 2.82 us -> 0.99 us
  transfers between devices with their start and end apart: 18 -> 18, of which waited for: 12 -> 11; matrix products, arithmetic and copies ran while one was open for 3% -> 3% of each run, Pallas kernels for 6% -> 4%
where the time goes in v4:
time: 119 us; the launch traced here: 117 us
  waiting for transfers between devices  69.5 us (58%)
  starting transfers between devices  32.1 us (27%)
  Pallas kernels  10.5 us (9%)
  local copies, waits for them, and re-layouts  3.49 us (3%)
    ppermute x12, waiting for transfers between devices, shift(): return lax.ppermute(x, axis, [(i, (i + by) % size) for i in range(size)])  39.6 us
    ppermute x2, waiting for transfers between devices, on_device(): hidden = [lax.ppermute(sums[j], ALL, home_pairs(j)) for j in range(2)]  16.3 us
    ppermute x12, starting transfers between devices, shift(): return lax.ppermute(x, axis, [(i, (i + by) % size) for i in range(size)])  13.3 us
    ppermute x3, starting transfers between devices, on_device(): tokens.append(lax.ppermute(tokens[-1], ('z', 'c'), around))  12.8 us
    ppermute x3, waiting for transfers between devices, on_device(): tokens.append(lax.ppermute(tokens[-1], ('z', 'c'), around))  10.7 us
    pallas_call x1, Pallas kernels, product_y(): pl.pallas_call(kernel, in_specs=[SMEM] + [VMEM] * 7, out_specs=[VMEM] * (...  3.88 us
    pallas_call x1, Pallas kernels, product_xl(): pl.pallas_call(kernel, in_specs=[VMEM] * 3, out_specs=[VMEM] * 2, out_sha...  3.54 us
    ppermute x1, starting transfers between devices, on_device(): lax.ppermute(lax.dynamic_slice_in_dim(tokens[3], c * rows, rows, 0), ('z'...  3.01 us
  transfers between devices with their start and end apart: 18, of which 11 were waited for; matrix products, arithmetic and copies ran while one was open for 3% of the time, Pallas kernels for 4%

profile of v4, /device:TPU:7, one launch (start us, length us, event | category | flops | bytes accessed | tf_op | source)
XLA Modules:
  0.0 116.7 jit_solution(9120989711411898109)
XLA Ops:
  0.6 0.8 collective-permute-start
  1.4 0.8 copy.8
  2.2 1.0 constant_dynamic-update-slice_fusion.1
  3.2 0.0 collective-permute-done
  3.2 5.7 %collective-permute-start.1 = (bf16[256,1024]{1,0:T(8,128)(2,1)S(1)}, bf16[256,1024]{1,0:T(8,128)(2,1)S(1)}, u32[]{:S(2)}, u32[]{:S(2)}) collective-permute-start(bf16[256,1024]{1,0:T(8,128)(2,1)S(1)} %constant_dynamic-update-slice_fusion.t0), channel_id=1, source_target_pairs={{0,32},{32,64},{64,96},{96,128},{128,160},{160,192},{192,224},{224... | collective-permute-start | bytes 1572872 | tf_op jit(solution)/shard_map/ppermute | solution.py:243
  8.8 0.3 mul.30
  9.2 0.4 fusion.w_own_ref
  9.5 1.2 %collective-permute-start.3 = (bf16[896,512]{1,0:T(8,128)(2,1)S(1)}, bf16[896,512]{1,0:T(8,128)(2,1)S(1)}, u32[]{:S(2)}, u32[]{:S(2)}) collective-permute-start(bf16[896,512]{1,0:T(8,128)(2,1)S(1)} %fusion.w_own_ref), channel_id=1, source_target_pairs={{0,16},{16,0},{1,17},{17,1},{2,18},{18,2},{3,19},{19,3},{4,20},{20... | collective-permute-start | bytes 2752520 | tf_op jit(solution)/shard_map/ppermute | solution.py:71
  10.7 4.2 %collective-permute-done.1.t1 = bf16[256,1024]{1,0:T(8,128)(2,1)S(1)} collective-permute-done((bf16[256,1024]{1,0:T(8,128)(2,1)S(1)}, bf16[256,1024]{1,0:T(8,128)(2,1)S(1)}, u32[]{:S(2)}, u32[]{:S(2)}) %collective-permute-start.1) | collective-permute-done | bytes 524320 | tf_op jit(solution)/shard_map/ppermute | solution.py:243
  15.0 3.4 %collective-permute-start.2 = (bf16[256,1024]{1,0:T(8,128)(2,1)S(1)}, bf16[256,1024]{1,0:T(8,128)(2,1)}, u32[]{:S(2)}, u32[]{:S(2)}) collective-permute-start(bf16[256,1024]{1,0:T(8,128)(2,1)S(1)} %collective-permute-done.1.t1), channel_id=1, source_target_pairs={{0,32},{32,64},{64,96},{96,128},{128,160},{160,192},{192,224},{224... | collective-permute-start | bytes 1572872 | tf_op jit(solution)/shard_map/ppermute | solution.py:243
  18.4 0.0 collective-permute-start.6
  18.4 11.7 %collective-permute-done.3.w_own_ref = bf16[896,512]{1,0:T(8,128)(2,1)S(1)} collective-permute-done((bf16[896,512]{1,0:T(8,128)(2,1)S(1)}, bf16[896,512]{1,0:T(8,128)(2,1)S(1)}, u32[]{:S(2)}, u32[]{:S(2)}) %collective-permute-start.3) | collective-permute-done | bytes 917536 | tf_op jit(solution)/shard_map/ppermute | solution.py:71
  30.1 0.0 collective-permute-done.2.t2
  30.1 3.8 %collective-permute-start.4 = (bf16[256,1024]{1,0:T(8,128)(2,1)}, bf16[256,1024]{1,0:T(8,128)(2,1)S(1)}, u32[]{:S(2)}, u32[]{:S(2)}) collective-permute-start(bf16[256,1024]{1,0:T(8,128)(2,1)} %collective-permute-done.2.t2), channel_id=1, source_target_pairs={{0,32},{32,64},{64,96},{96,128},{128,160},{160,192},{192,224},{224... | collective-permute-start | bytes 1572872 | tf_op jit(solution)/shard_map/ppermute | solution.py:243
  33.9 6.4 %collective-permute-done.4.t3 = bf16[256,1024]{1,0:T(8,128)(2,1)S(1)} collective-permute-done((bf16[256,1024]{1,0:T(8,128)(2,1)}, bf16[256,1024]{1,0:T(8,128)(2,1)S(1)}, u32[]{:S(2)}, u32[]{:S(2)}) %collective-permute-start.4) | collective-permute-done | bytes 524320 | tf_op jit(solution)/shard_map/ppermute | solution.py:243
  40.3 0.7 constant_dynamic-slice_fusion
  41.0 3.0 %collective-permute-start.5 = (bf16[128,1024]{1,0:T(8,128)(2,1)}, bf16[128,1024]{1,0:T(8,128)(2,1)}, u32[]{:S(2)}, u32[]{:S(2)}) collective-permute-start(bf16[128,1024]{1,0:T(8,128)(2,1)} %constant_dynamic-slice_fusion), channel_id=1, source_target_pairs={{0,32},{32,64},{64,96},{96,128},{128,160},{160,192},{192,224},{224... | collective-permute-start | bytes 786440 | tf_op jit(solution)/shard_map/ppermute | solution.py:244
  44.0 0.7 dynamic-slice_bitcast_fusion.facts_ref
  44.7 0.0 collective-permute-done.6.w_other_ref
  44.7 2.9 %collective-permute-done.5.far_ref = bf16[128,1024]{1,0:T(8,128)(2,1)} collective-permute-done((bf16[128,1024]{1,0:T(8,128)(2,1)}, bf16[128,1024]{1,0:T(8,128)(2,1)}, u32[]{:S(2)}, u32[]{:S(2)}) %collective-permute-start.5) | collective-permute-done | bytes 262176 | tf_op jit(solution)/shard_map/ppermute | solution.py:244
  47.7 3.9 %shard_map.77 = (bf16[8,128,1024]{2,1,0:T(8,128)(2,1)S(1)}, bf16[2,128,896]{2,1,0:T(8,128)(2,1)S(1)}, bf16[2,128,896]{2,1,0:T(8,128)(2,1)S(1)}, bf16[2,128,896]{2,1,0:T(8,128)(2,1)S(1)}, bf16[2,128,896]{2,1,0:T(8,128)(2,1)S(1)}) custom-call(s32[10]{0:T(128)S(1)} %dynamic-slice_bitcast_fusion.facts_ref, ...), custom_call_target="tpu_custom_call" | custom-call | flops 1879048192 | bytes 8388608 | tf_op jit(solution)/shard_map/pallas_call | solution.py:111
  51.6 0.0 collective-permute-done.11.w_other_ref
  51.6 3.5 %shard_map.79 = (bf16[4,128,896]{2,1,0:T(8,128)(2,1)S(1)}, bf16[4,128,896]{2,1,0:T(8,128)(2,1)S(1)}) custom-call(bf16[8,128,1024]{2,1,0:T(8,128)(2,1)S(1)} %get-tuple-element.26.lhs_ref, bf16[896,512]{1,0:T(8,128)(2,1)S(1)} %collective-permute-done.3.w_own_ref, bf16[896,512]{1,0:T(8,128)(2,1)} %collective-permute-done.11.w_other_ref), custom_call_target="tpu_custom_call" | custom-call | flops 1879048192 | bytes 6291456 | tf_op jit(solution)/shard_map/pallas_call | solution.py:133
  55.1 0.6 collective-permute-start.12
  55.8 1.3 %collective-permute-start.7 = (bf16[2,128,896]{2,1,0:T(8,128)(2,1)S(1)}, bf16[2,128,896]{2,1,0:T(8,128)(2,1)S(1)}, u32[]{:S(2)}, u32[]{:S(2)}) collective-permute-start(bf16[2,128,896]{2,1,0:T(8,128)(2,1)S(1)} %get-tuple-element.21), channel_id=1, source_target_pairs={{0,2},{2,4},{4,6},{6,0},{1,3},{3,5},{5,7},{7,1},{8,10},{10,12},{12... | collective-permute-start | bytes 1376264 | tf_op jit(solution)/shard_map/ppermute | solution.py:71
  57.1 2.6 %collective-permute-start.8 = (bf16[2,128,896]{2,1,0:T(8,128)(2,1)S(1)}, bf16[2,128,896]{2,1,0:T(8,128)(2,1)S(1)}, u32[]{:S(2)}, u32[]{:S(2)}) collective-permute-start(bf16[2,128,896]{2,1,0:T(8,128)(2,1)S(1)} %get-tuple-element.22), channel_id=1, source_target_pairs={{0,4},{2,6},{4,0},{6,2},{1,5},{3,7},{5,1},{7,3},{8,12},{10,14},{12... | collective-permute-start | bytes 1376264 | tf_op jit(solution)/shard_map/ppermute | solution.py:71
  59.7 1.1 collective-permute-start.9
  60.7 5.2 %collective-permute-done.7.refs_1_ = bf16[2,128,896]{2,1,0:T(8,128)(2,1)S(1)} collective-permute-done((bf16[2,128,896]{2,1,0:T(8,128)(2,1)S(1)}, bf16[2,128,896]{2,1,0:T(8,128)(2,1)S(1)}, u32[]{:S(2)}, u32[]{:S(2)}) %collective-permute-start.7) | collective-permute-done | bytes 458784 | tf_op jit(solution)/shard_map/ppermute | solution.py:71
  66.0 10.9 %collective-permute-done.8.refs_2_ = bf16[2,128,896]{2,1,0:T(8,128)(2,1)S(1)} collective-permute-done((bf16[2,128,896]{2,1,0:T(8,128)(2,1)S(1)}, bf16[2,128,896]{2,1,0:T(8,128)(2,1)S(1)}, u32[]{:S(2)}, u32[]{:S(2)}) %collective-permute-start.8) | collective-permute-done | bytes 458784 | tf_op jit(solution)/shard_map/ppermute | solution.py:71
  76.9 1.9 %collective-permute-done.9.refs_3_ = bf16[2,128,896]{2,1,0:T(8,128)(2,1)S(1)} collective-permute-done((bf16[2,128,896]{2,1,0:T(8,128)(2,1)S(1)}, bf16[2,128,896]{2,1,0:T(8,128)(2,1)S(1)}, u32[]{:S(2)}, u32[]{:S(2)}) %collective-permute-start.9) | collective-permute-done | bytes 458784 | tf_op jit(solution)/shard_map/ppermute | solution.py:71
  78.9 0.2 shard_map.78
  79.1 0.0 copy-start
  79.1 0.0 copy-start.1
  79.1 1.0 collective-permute-start.10
  80.1 0.0 collective-permute-done.12.received_ref
  80.1 0.2 shard_map.80
  80.3 1.7 %collective-permute-start.13 = (bf16[128,896]{1,0:T(8,128)(2,1)S(1)}, bf16[128,896]{1,0:T(8,128)(2,1)S(1)}, u32[]{:S(2)}, u32[]{:S(2)}) collective-permute-start(bf16[128,896]{1,0:T(8,128)(2,1)S(1)} %get-tuple-element.31), channel_id=1, source_target_pairs={{0,2},{2,4},{4,6},{6,0},{1,3},{3,5},{5,7},{7,1},{8,10},{10,12},{12... | collective-permute-start | bytes 688136 | tf_op jit(solution)/shard_map/ppermute | solution.py:71
  82.1 3.0 %collective-permute-start.14 = (bf16[128,896]{1,0:T(8,128)(2,1)S(1)}, bf16[128,896]{1,0:T(8,128)(2,1)S(1)}, u32[]{:S(2)}, u32[]{:S(2)}) collective-permute-start(bf16[128,896]{1,0:T(8,128)(2,1)S(1)} %get-tuple-element.32), channel_id=1, source_target_pairs={{0,4},{2,6},{4,0},{6,2},{1,5},{3,7},{5,1},{7,3},{8,12},{10,14},{12... | collective-permute-start | bytes 688136 | tf_op jit(solution)/shard_map/ppermute | solution.py:71
  85.0 0.0 collective-permute-start.15
  85.0 0.0 collective-permute-done.10.refs_1_
  85.0 2.8 %collective-permute-done.13.refs_3_ = bf16[128,896]{1,0:T(8,128)(2,1)S(1)} collective-permute-done((bf16[128,896]{1,0:T(8,128)(2,1)S(1)}, bf16[128,896]{1,0:T(8,128)(2,1)S(1)}, u32[]{:S(2)}, u32[]{:S(2)}) %collective-permute-start.13) | collective-permute-done | bytes 229408 | tf_op jit(solution)/shard_map/ppermute | solution.py:71
  87.8 7.0 %collective-permute-done.14.refs_4_ = bf16[128,896]{1,0:T(8,128)(2,1)S(1)} collective-permute-done((bf16[128,896]{1,0:T(8,128)(2,1)S(1)}, bf16[128,896]{1,0:T(8,128)(2,1)S(1)}, u32[]{:S(2)}, u32[]{:S(2)}) %collective-permute-start.14) | collective-permute-done | bytes 229408 | tf_op jit(solution)/shard_map/ppermute | solution.py:71
  94.8 0.8 shard_map.81
  95.6 0.1 collective-permute-start.16
  95.7 2.9 %collective-permute-start.17 = (bf16[128,896]{1,0:T(8,128)(2,1)S(1)}, bf16[128,896]{1,0:T(8,128)(2,1)S(1)}, u32[]{:S(2)}, u32[]{:S(2)}) collective-permute-start(bf16[128,896]{1,0:T(8,128)(2,1)S(1)} %get-tuple-element.35), channel_id=1, source_target_pairs={{0,224},{1,128},{2,161},{3,65},{4,160},{5,32},{6,225},{7,64},{8,19... | collective-permute-start | bytes 688136 | tf_op jit(solution)/shard_map/ppermute | solution.py:257
  98.5 14.6 %collective-permute-done.16.first = bf16[128,896]{1,0:T(8,128)(2,1)S(1)} collective-permute-done((bf16[128,896]{1,0:T(8,128)(2,1)S(1)}, bf16[128,896]{1,0:T(8,128)(2,1)S(1)}, u32[]{:S(2)}, u32[]{:S(2)}) %collective-permute-start.16) | collective-permute-done | bytes 229408 | tf_op jit(solution)/shard_map/ppermute | solution.py:257
  113.2 1.7 %collective-permute-done.17.second = bf16[128,896]{1,0:T(8,128)(2,1)S(1)} collective-permute-done((bf16[128,896]{1,0:T(8,128)(2,1)S(1)}, bf16[128,896]{1,0:T(8,128)(2,1)S(1)}, u32[]{:S(2)}, u32[]{:S(2)}) %collective-permute-start.17) | collective-permute-done | bytes 229408 | tf_op jit(solution)/shard_map/ppermute | solution.py:257
  114.8 1.9 %shard_map.82 = (bf16[256,896]{1,0:T(8,128)(2,1)}, bf16[256,896]{1,0:T(8,128)(2,1)}) custom-call(s32[10]{0:T(128)S(1)} %dynamic-slice_bitcast_fusion.facts_ref, bf16[128,896]{1,0:T(8,128)(2,1)S(1)} %collective-permute-done.16.first, bf16[128,896]{1,0:T(8,128)(2,1)S(1)} %collective-permute-done.17.second, bf16[256,896]{1,0:T(8,128)(2,1)S(1)} %copy-done, ...), custom_call_target="tpu_custom_call" | custom-call | flops 2293760 | bytes 2293760 | tf_op jit(solution)/shard_map/pallas_call | solution.py:220
  (7 shorter events, 0.0 us)
Async XLA Ops:
  0.6 8.5 %copy-start.2 = (bf16[896,512]{1,0:T(8,128)(2,1)S(1)}, bf16[896,512]{1,0:T(8,128)(2,1)}, u32[]{:S(2)}) copy-start(bf16[896,512]{1,0:T(8,128)(2,1)} %param.7) | copy-start | bytes 2752516
  0.6 2.5 %collective-permute-start = (bf16[256,512]{1,0:T(8,128)(2,1)}, bf16[256,512]{1,0:T(8,128)(2,1)S(1)}, u32[]{:S(2)}, u32[]{:S(2)}) collective-permute-start(bf16[256,512]{1,0:T(8,128)(2,1)} %param.6), channel_id=1, source_target_pairs={{0,1},{1,0},{2,3},{3,2},{4,5},{5,4},{6,7},{7,6},{8,9},{9,8},{10,11... | collective-permute-start | bytes 786440 | tf_op jit(solution)/shard_map/ppermute | solution.py:71
  3.2 11.8 %collective-permute-start.1 = (bf16[256,1024]{1,0:T(8,128)(2,1)S(1)}, bf16[256,1024]{1,0:T(8,128)(2,1)S(1)}, u32[]{:S(2)}, u32[]{:S(2)}) collective-permute-start(bf16[256,1024]{1,0:T(8,128)(2,1)S(1)} %constant_dynamic-update-slice_fusion.t0), channel_id=1, source_target_pairs={{0,32},{32,64},{64,96},{96,128},{128,160},{160,192},{192,224},{224... | collective-permute-start | bytes 1572872 | tf_op jit(solution)/shard_map/ppermute | solution.py:243
  9.5 20.5 %collective-permute-start.3 = (bf16[896,512]{1,0:T(8,128)(2,1)S(1)}, bf16[896,512]{1,0:T(8,128)(2,1)S(1)}, u32[]{:S(2)}, u32[]{:S(2)}) collective-permute-start(bf16[896,512]{1,0:T(8,128)(2,1)S(1)} %fusion.w_own_ref), channel_id=1, source_target_pairs={{0,16},{16,0},{1,17},{17,1},{2,18},{18,2},{3,19},{19,3},{4,20},{20... | collective-permute-start | bytes 2752520 | tf_op jit(solution)/shard_map/ppermute | solution.py:71
  15.0 15.1 %collective-permute-start.2 = (bf16[256,1024]{1,0:T(8,128)(2,1)S(1)}, bf16[256,1024]{1,0:T(8,128)(2,1)}, u32[]{:S(2)}, u32[]{:S(2)}) collective-permute-start(bf16[256,1024]{1,0:T(8,128)(2,1)S(1)} %collective-permute-done.1.t1), channel_id=1, source_target_pairs={{0,32},{32,64},{64,96},{96,128},{128,160},{160,192},{192,224},{224... | collective-permute-start | bytes 1572872 | tf_op jit(solution)/shard_map/ppermute | solution.py:243
  18.4 26.4 %collective-permute-start.6 = (bf16[896,512]{1,0:T(8,128)(2,1)S(1)}, bf16[896,512]{1,0:T(8,128)(2,1)}, u32[]{:S(2)}, u32[]{:S(2)}) collective-permute-start(bf16[896,512]{1,0:T(8,128)(2,1)S(1)} %fusion.w_own_ref), channel_id=1, source_target_pairs={{0,1},{1,0},{2,3},{3,2},{4,5},{5,4},{6,7},{7,6},{8,9},{9,8},{10,11... | collective-permute-start | bytes 2752520 | tf_op jit(solution)/shard_map/ppermute | solution.py:71
  30.1 10.2 %collective-permute-start.4 = (bf16[256,1024]{1,0:T(8,128)(2,1)}, bf16[256,1024]{1,0:T(8,128)(2,1)S(1)}, u32[]{:S(2)}, u32[]{:S(2)}) collective-permute-start(bf16[256,1024]{1,0:T(8,128)(2,1)} %collective-permute-done.2.t2), channel_id=1, source_target_pairs={{0,32},{32,64},{64,96},{96,128},{128,160},{160,192},{192,224},{224... | collective-permute-start | bytes 1572872 | tf_op jit(solution)/shard_map/ppermute | solution.py:243
  33.9 17.7 %collective-permute-start.11 = (bf16[896,512]{1,0:T(8,128)(2,1)S(1)}, bf16[896,512]{1,0:T(8,128)(2,1)}, u32[]{:S(2)}, u32[]{:S(2)}) collective-permute-start(bf16[896,512]{1,0:T(8,128)(2,1)S(1)} %collective-permute-done.3.w_own_ref), channel_id=1, source_target_pairs={{0,1},{1,0},{2,3},{3,2},{4,5},{5,4},{6,7},{7,6},{8,9},{9,8},{10,11... | collective-permute-start | bytes 2752520 | tf_op jit(solution)/shard_map/ppermute | solution.py:71
  41.0 6.6 %collective-permute-start.5 = (bf16[128,1024]{1,0:T(8,128)(2,1)}, bf16[128,1024]{1,0:T(8,128)(2,1)}, u32[]{:S(2)}, u32[]{:S(2)}) collective-permute-start(bf16[128,1024]{1,0:T(8,128)(2,1)} %constant_dynamic-slice_fusion), channel_id=1, source_target_pairs={{0,32},{32,64},{64,96},{96,128},{128,160},{160,192},{192,224},{224... | collective-permute-start | bytes 786440 | tf_op jit(solution)/shard_map/ppermute | solution.py:244
  55.1 25.0 %collective-permute-start.12 = (bf16[4,128,896]{2,1,0:T(8,128)(2,1)S(1)}, bf16[4,128,896]{2,1,0:T(8,128)(2,1)S(1)}, u32[]{:S(2)}, u32[]{:S(2)}) collective-permute-start(bf16[4,128,896]{2,1,0:T(8,128)(2,1)S(1)} %get-tuple-element.29), channel_id=1, source_target_pairs={{0,8},{8,0},{1,9},{9,1},{2,10},{10,2},{3,11},{11,3},{4,12},{12,4},... | collective-permute-start | bytes 2752520 | tf_op jit(solution)/shard_map/ppermute | solution.py:71
  55.8 10.2 %collective-permute-start.7 = (bf16[2,128,896]{2,1,0:T(8,128)(2,1)S(1)}, bf16[2,128,896]{2,1,0:T(8,128)(2,1)S(1)}, u32[]{:S(2)}, u32[]{:S(2)}) collective-permute-start(bf16[2,128,896]{2,1,0:T(8,128)(2,1)S(1)} %get-tuple-element.21), channel_id=1, source_target_pairs={{0,2},{2,4},{4,6},{6,0},{1,3},{3,5},{5,7},{7,1},{8,10},{10,12},{12... | collective-permute-start | bytes 1376264 | tf_op jit(solution)/shard_map/ppermute | solution.py:71
  57.1 19.9 %collective-permute-start.8 = (bf16[2,128,896]{2,1,0:T(8,128)(2,1)S(1)}, bf16[2,128,896]{2,1,0:T(8,128)(2,1)S(1)}, u32[]{:S(2)}, u32[]{:S(2)}) collective-permute-start(bf16[2,128,896]{2,1,0:T(8,128)(2,1)S(1)} %get-tuple-element.22), channel_id=1, source_target_pairs={{0,4},{2,6},{4,0},{6,2},{1,5},{3,7},{5,1},{7,3},{8,12},{10,14},{12... | collective-permute-start | bytes 1376264 | tf_op jit(solution)/shard_map/ppermute | solution.py:71
  59.7 19.2 %collective-permute-start.9 = (bf16[2,128,896]{2,1,0:T(8,128)(2,1)S(1)}, bf16[2,128,896]{2,1,0:T(8,128)(2,1)S(1)}, u32[]{:S(2)}, u32[]{:S(2)}) collective-permute-start(bf16[2,128,896]{2,1,0:T(8,128)(2,1)S(1)} %get-tuple-element.23), channel_id=1, source_target_pairs={{0,6},{2,0},{4,2},{6,4},{1,7},{3,1},{5,3},{7,5},{8,14},{10,8},{12,... | collective-permute-start | bytes 1376264 | tf_op jit(solution)/shard_map/ppermute | solution.py:71
  79.1 35.7 %copy-start = (bf16[256,896]{1,0:T(8,128)(2,1)S(1)}, bf16[256,896]{1,0:T(8,128)(2,1)}, u32[]{:S(2)}) copy-start(bf16[256,896]{1,0:T(8,128)(2,1)} %gate_ref.1) | copy-start | bytes 1376260
  79.1 35.7 %copy-start.1 = (bf16[256,896]{1,0:T(8,128)(2,1)S(1)}, bf16[256,896]{1,0:T(8,128)(2,1)}, u32[]{:S(2)}) copy-start(bf16[256,896]{1,0:T(8,128)(2,1)} %up_ref.1) | copy-start | bytes 1376260
  79.1 5.9 %collective-permute-start.10 = (bf16[128,896]{1,0:T(8,128)(2,1)S(1)}, bf16[128,896]{1,0:T(8,128)(2,1)S(1)}, u32[]{:S(2)}, u32[]{:S(2)}) collective-permute-start(bf16[128,896]{1,0:T(8,128)(2,1)S(1)} %get-tuple-element.25), channel_id=1, source_target_pairs={{0,8},{8,0},{1,9},{9,1},{2,10},{10,2},{3,11},{11,3},{4,12},{12,4},... | collective-permute-start | bytes 688136 | tf_op jit(solution)/shard_map/ppermute | solution.py:71
  80.3 7.5 %collective-permute-start.13 = (bf16[128,896]{1,0:T(8,128)(2,1)S(1)}, bf16[128,896]{1,0:T(8,128)(2,1)S(1)}, u32[]{:S(2)}, u32[]{:S(2)}) collective-permute-start(bf16[128,896]{1,0:T(8,128)(2,1)S(1)} %get-tuple-element.31), channel_id=1, source_target_pairs={{0,2},{2,4},{4,6},{6,0},{1,3},{3,5},{5,7},{7,1},{8,10},{10,12},{12... | collective-permute-start | bytes 688136 | tf_op jit(solution)/shard_map/ppermute | solution.py:71
  82.1 12.8 %collective-permute-start.14 = (bf16[128,896]{1,0:T(8,128)(2,1)S(1)}, bf16[128,896]{1,0:T(8,128)(2,1)S(1)}, u32[]{:S(2)}, u32[]{:S(2)}) collective-permute-start(bf16[128,896]{1,0:T(8,128)(2,1)S(1)} %get-tuple-element.32), channel_id=1, source_target_pairs={{0,4},{2,6},{4,0},{6,2},{1,5},{3,7},{5,1},{7,3},{8,12},{10,14},{12... | collective-permute-start | bytes 688136 | tf_op jit(solution)/shard_map/ppermute | solution.py:71
  85.0 9.8 %collective-permute-start.15 = (bf16[128,896]{1,0:T(8,128)(2,1)S(1)}, bf16[128,896]{1,0:T(8,128)(2,1)S(1)}, u32[]{:S(2)}, u32[]{:S(2)}) collective-permute-start(bf16[128,896]{1,0:T(8,128)(2,1)S(1)} %get-tuple-element.33), channel_id=1, source_target_pairs={{0,6},{2,0},{4,2},{6,4},{1,7},{3,1},{5,3},{7,5},{8,14},{10,8},{12,... | collective-permute-start | bytes 688136 | tf_op jit(solution)/shard_map/ppermute | solution.py:71
  95.6 17.6 %collective-permute-start.16 = (bf16[128,896]{1,0:T(8,128)(2,1)S(1)}, bf16[128,896]{1,0:T(8,128)(2,1)S(1)}, u32[]{:S(2)}, u32[]{:S(2)}) collective-permute-start(bf16[128,896]{1,0:T(8,128)(2,1)S(1)} %get-tuple-element.34), channel_id=1, source_target_pairs={{0,225},{1,129},{2,160},{3,64},{4,161},{5,33},{6,224},{7,65},{8,19... | collective-permute-start | bytes 688136 | tf_op jit(solution)/shard_map/ppermute | solution.py:257
  95.7 19.1 %collective-permute-start.17 = (bf16[128,896]{1,0:T(8,128)(2,1)S(1)}, bf16[128,896]{1,0:T(8,128)(2,1)S(1)}, u32[]{:S(2)}, u32[]{:S(2)}) collective-permute-start(bf16[128,896]{1,0:T(8,128)(2,1)S(1)} %get-tuple-element.35), channel_id=1, source_target_pairs={{0,224},{1,128},{2,161},{3,65},{4,160},{5,32},{6,225},{7,64},{8,19... | collective-permute-start | bytes 688136 | tf_op jit(solution)/shard_map/ppermute | solution.py:257

commit v5 on v4

--- a/solution.py
+++ b/solution.py
@@ -123,18 +123,18 @@
     _, rows, depth = lhs.shape
     width = w_own.shape[0]
 
-    def kernel(lhs_ref, w_own_ref, w_other_ref, keep_ref, send_ref):
+    def kernel(lhs_ref, w_own_ref, w_other_ref, keep_ref, *send_refs):
         for d in range(Y):
             pair = lhs_ref[2 * d : 2 * d + 2].reshape(2 * rows, depth)
             total = times(pair, w_own_ref[...], w_other_ref[...])
             keep_ref[d] = total[:rows]
-            send_ref[d] = total[rows:]
+            send_refs[d // 2][d % 2] = total[rows:]
 
     return pl.pallas_call(
         kernel,
         in_specs=[VMEM] * 3,
-        out_specs=[VMEM] * 2,
-        out_shape=[jax.ShapeDtypeStruct((Y, rows, width), BF16)] * 2,
+        out_specs=[VMEM] * 3,
+        out_shape=[jax.ShapeDtypeStruct((n, rows, width), BF16) for n in (Y, Y // 2, Y // 2)],
         compiler_params=params(32),
         cost_estimate=pl.CostEstimate(flops=2 * S * rows * depth * width, bytes_accessed=6 * 2**20, transcendentals=0),
     )(lhs, w_own, w_other)
@@ -163,18 +163,19 @@
 def add_xl(kept, received):
     _, rows, width = kept.shape
 
-    def kernel(kept_ref, received_ref, *out_refs):
+    def kernel(kept_ref, low_ref, high_ref, *out_refs):
         for d in range(Y):
-            out_refs[d][...] = (kept_ref[d].astype(F32) + received_ref[d].astype(F32)).astype(BF16)
-
-    return pl.pallas_call(
-        kernel,
-        in_specs=[VMEM] * 2,
+            received = (low_ref, high_ref)[d // 2][d % 2]
+            out_refs[d][...] = (kept_ref[d].astype(F32) + received.astype(F32)).astype(BF16)
+
+    return pl.pallas_call(
+        kernel,
+        in_specs=[VMEM] * 3,
         out_specs=[VMEM] * Y,
         out_shape=[jax.ShapeDtypeStruct((rows, width), BF16)] * Y,
         compiler_params=params(16),
         cost_estimate=pl.CostEstimate(flops=Y * rows * width, bytes_accessed=6 * Y * rows * width, transcendentals=0),
-    )(kept, received)
+    )(kept, *received)
 
 
 def add_last(own, near_parts, cross_parts):
@@ -237,18 +238,18 @@
     rows = grad_out.shape[0] // 2
     tokens = [jnp.concatenate([grad_out, shift(grad_out, "c", C, 1)], 1)]
     around = [(i * C, (i + 1) % Z * C) for i in range(Z)] + [(i * C + 1, (i - 1) % Z * C + 1) for i in range(Z)]
+    tokens[0], _ = lax.optimization_barrier((tokens[0], near_own))
     for step in range(3):
-        if step == 2:
-            tokens[-1], cross_own = lax.optimization_barrier((tokens[-1], cross_own))
         tokens.append(lax.ppermute(tokens[-1], ("z", "c"), around))
+    tokens[3], cross_own = lax.optimization_barrier((tokens[3], cross_own))
     far = lax.ppermute(lax.dynamic_slice_in_dim(tokens[3], c * rows, rows, 0), ("z", "c"), around)
     near_other = shift(near_own, "c", C, 1)
     cross_other = shift(cross_own, "c", C, 1)
 
     lhs, *near = product_y(own, tokens, far, near_own, near_other)
     near_y = [near[0]] + [shift(near[d], "y", Y, d) for d in range(1, Y)]
-    kept, sent = product_xl(lhs, cross_own, cross_other)
-    cross = add_xl(kept, shift(sent, "xl", XL, 1))
+    kept, *sent = product_xl(lhs, cross_own, cross_other)
+    cross = add_xl(kept, [shift(part, "xl", XL, 1) for part in sent])
     cross_parts = [cross[0]] + [shift(cross[d], "y", Y, d) for d in range(1, Y)]
     kept, sent = add_y(near_y)
     near_parts = [kept, shift(sent, "xl", XL, 1)]

time: 119 us -> 117 us (0.983); the launches traced: 117 us -> 117 us
  waiting for transfers between devices: 69.5 us -> 62.5 us
  starting transfers between devices: 32.1 us -> 37.8 us
  local copies, waits for them, and re-layouts: 3.49 us -> 4.91 us
    ppermute x2, starting transfers between devices: 2.97 us -> 11.4 us  [on_device(): hidden = [lax.ppermute(sums[j], ALL, home_pairs(j)) for j in range(2)]]
    ppermute x12 -> x13, waiting for transfers between devices: 39.6 us -> 34.3 us  [shift(): return lax.ppermute(x, axis, [(i, (i + by) % size) for i in range(size)])]
    ppermute x2, waiting for transfers between devices: 16.3 us -> 13.9 us  [on_device(): hidden = [lax.ppermute(sums[j], ALL, home_pairs(j)) for j in range(2)]]
    unnamed x7 -> x12, local copies, waits for them, and re-layouts: 0.99 us -> 2.42 us
    ppermute x12 -> x13, starting transfers between devices: 13.3 us -> 12.3 us  [shift(): return lax.ppermute(x, axis, [(i, (i + by) % size) for i in range(size)])]
  transfers between devices with their start and end apart: 18 -> 19, of which waited for: 11 -> 13; matrix products, arithmetic and copies ran while one was open for 3% -> 2% of each run, Pallas kernels for 4% -> 7%
where the time goes in v5:
time: 117 us
  waiting for transfers between devices  62.5 us (53%)
  starting transfers between devices  37.8 us (32%)
  Pallas kernels  10.3 us (9%)
  local copies, waits for them, and re-layouts  4.91 us (4%)
    ppermute x13, waiting for transfers between devices, shift(): return lax.ppermute(x, axis, [(i, (i + by) % size) for i in range(size)])  34.3 us
    ppermute x2, waiting for transfers between devices, on_device(): hidden = [lax.ppermute(sums[j], ALL, home_pairs(j)) for j in range(2)]  13.9 us
    ppermute x13, starting transfers between devices, shift(): return lax.ppermute(x, axis, [(i, (i + by) % size) for i in range(size)])  12.3 us
    ppermute x3, starting transfers between devices, on_device(): tokens.append(lax.ppermute(tokens[-1], ('z', 'c'), around))  12.2 us
    ppermute x2, starting transfers between devices, on_device(): hidden = [lax.ppermute(sums[j], ALL, home_pairs(j)) for j in range(2)]  11.4 us
    ppermute x3, waiting for transfers between devices, on_device(): tokens.append(lax.ppermute(tokens[-1], ('z', 'c'), around))  11.1 us
    pallas_call x1, Pallas kernels, product_y(): pl.pallas_call(kernel, in_specs=[SMEM] + [VMEM] * 7, out_specs=[VMEM] * (...  3.72 us
    pallas_call x1, Pallas kernels, product_xl(): pl.pallas_call(kernel, in_specs=[VMEM] * 3, out_specs=[VMEM] * 3, out_sha...  3.54 us
  transfers between devices with their start and end apart: 19, of which 13 were waited for; matrix products, arithmetic and copies ran while one was open for 2% of the time, Pallas kernels for 7%

profile of v5, /device:TPU:7, one launch (start us, length us, event | category | flops | bytes accessed | tf_op | source)
XLA Modules:
  0.0 116.7 jit_solution(11569356273496570660)
XLA Ops:
  0.6 0.8 collective-permute-start
  1.4 0.8 copy.8
  2.2 0.3 mul.30
  2.5 0.0 copy-start.5
  2.5 0.4 fusion.w_own_ref
  2.9 0.6 copy-done.5
  3.4 0.1 pad_maximum_fusion.t0
  3.5 5.7 %collective-permute-start.1 = (bf16[256,1024]{1,0:T(8,128)(2,1)S(1)}, bf16[256,1024]{1,0:T(8,128)(2,1)S(1)}, u32[]{:S(2)}, u32[]{:S(2)}) collective-permute-start(bf16[256,1024]{1,0:T(8,128)(2,1)S(1)} %pad_maximum_fusion.t0), channel_id=1, source_target_pairs={{0,32},{32,64},{64,96},{96,128},{128,160},{160,192},{192,224},{224... | collective-permute-start | bytes 1572872 | tf_op jit(solution)/shard_map/ppermute | solution.py:243
  9.2 6.1 %collective-permute-done.1.t1 = bf16[256,1024]{1,0:T(8,128)(2,1)S(1)} collective-permute-done((bf16[256,1024]{1,0:T(8,128)(2,1)S(1)}, bf16[256,1024]{1,0:T(8,128)(2,1)S(1)}, u32[]{:S(2)}, u32[]{:S(2)}) %collective-permute-start.1) | collective-permute-done | bytes 524320 | tf_op jit(solution)/shard_map/ppermute | solution.py:243
  15.3 3.1 %collective-permute-start.2 = (bf16[256,1024]{1,0:T(8,128)(2,1)S(1)}, bf16[256,1024]{1,0:T(8,128)(2,1)S(1)}, u32[]{:S(2)}, u32[]{:S(2)}) collective-permute-start(bf16[256,1024]{1,0:T(8,128)(2,1)S(1)} %collective-permute-done.1.t1), channel_id=1, source_target_pairs={{0,32},{32,64},{64,96},{96,128},{128,160},{160,192},{192,224},{224... | collective-permute-start | bytes 1572872 | tf_op jit(solution)/shard_map/ppermute | solution.py:243
  18.4 1.1 collective-permute-start.4
  19.5 5.0 %collective-permute-done.2.t2 = bf16[256,1024]{1,0:T(8,128)(2,1)S(1)} collective-permute-done((bf16[256,1024]{1,0:T(8,128)(2,1)S(1)}, bf16[256,1024]{1,0:T(8,128)(2,1)S(1)}, u32[]{:S(2)}, u32[]{:S(2)}) %collective-permute-start.2) | collective-permute-done | bytes 524320 | tf_op jit(solution)/shard_map/ppermute | solution.py:243
  24.5 3.4 %collective-permute-start.3 = (bf16[256,1024]{1,0:T(8,128)(2,1)S(1)}, bf16[256,1024]{1,0:T(8,128)(2,1)S(1)}, u32[]{:S(2)}, u32[]{:S(2)}) collective-permute-start(bf16[256,1024]{1,0:T(8,128)(2,1)S(1)} %collective-permute-done.2.t2), channel_id=1, source_target_pairs={{0,32},{32,64},{64,96},{96,128},{128,160},{160,192},{192,224},{224... | collective-permute-start | bytes 1572872 | tf_op jit(solution)/shard_map/ppermute | solution.py:243
  27.9 0.8 copy-done.2
  28.7 12.0 %collective-permute-done.4.w_own_ref = bf16[896,512]{1,0:T(8,128)(2,1)S(1)} collective-permute-done((bf16[896,512]{1,0:T(8,128)(2,1)S(1)}, bf16[896,512]{1,0:T(8,128)(2,1)S(1)}, u32[]{:S(2)}, u32[]{:S(2)}) %collective-permute-start.4) | collective-permute-done | bytes 917536 | tf_op jit(solution)/shard_map/ppermute | solution.py:71
  40.7 0.7 constant_dynamic-slice_fusion
  41.5 1.9 %collective-permute-start.5 = (bf16[128,1024]{1,0:T(8,128)(2,1)}, bf16[128,1024]{1,0:T(8,128)(2,1)}, u32[]{:S(2)}, u32[]{:S(2)}) collective-permute-start(bf16[128,1024]{1,0:T(8,128)(2,1)} %constant_dynamic-slice_fusion), channel_id=1, source_target_pairs={{0,32},{32,64},{64,96},{96,128},{128,160},{160,192},{192,224},{224... | collective-permute-start | bytes 786440 | tf_op jit(solution)/shard_map/ppermute | solution.py:245
  43.4 0.7 dynamic-slice_bitcast_fusion.facts_ref
  44.1 3.2 %collective-permute-done.5.far_ref = bf16[128,1024]{1,0:T(8,128)(2,1)} collective-permute-done((bf16[128,1024]{1,0:T(8,128)(2,1)}, bf16[128,1024]{1,0:T(8,128)(2,1)}, u32[]{:S(2)}, u32[]{:S(2)}) %collective-permute-start.5) | collective-permute-done | bytes 262176 | tf_op jit(solution)/shard_map/ppermute | solution.py:245
  47.3 1.0 copy-done.3
  48.3 3.7 %shard_map.77 = (bf16[8,128,1024]{2,1,0:T(8,128)(2,1)S(1)}, bf16[2,128,896]{2,1,0:T(8,128)(2,1)S(1)}, bf16[2,128,896]{2,1,0:T(8,128)(2,1)S(1)}, bf16[2,128,896]{2,1,0:T(8,128)(2,1)S(1)}, bf16[2,128,896]{2,1,0:T(8,128)(2,1)S(1)}) custom-call(s32[10]{0:T(128)S(1)} %dynamic-slice_bitcast_fusion.facts_ref, bf16[256,1024]{1,0:T(8,128)(2,1)S(1)} %pad_maximum_fusion.t0, ...), custom_call_target="tpu_custom_call" | custom-call | flops 1879048192 | bytes 8388608 | tf_op jit(solution)/shard_map/pallas_call | solution.py:111
  52.1 1.4 %collective-permute-start.7 = (bf16[2,128,896]{2,1,0:T(8,128)(2,1)S(1)}, bf16[2,128,896]{2,1,0:T(8,128)(2,1)S(1)}, u32[]{:S(2)}, u32[]{:S(2)}) collective-permute-start(bf16[2,128,896]{2,1,0:T(8,128)(2,1)S(1)} %get-tuple-element.24), channel_id=1, source_target_pairs={{0,2},{2,4},{4,6},{6,0},{1,3},{3,5},{5,7},{7,1},{8,10},{10,12},{12... | collective-permute-start | bytes 1376264 | tf_op jit(solution)/shard_map/ppermute | solution.py:71
  53.4 2.6 %collective-permute-start.8 = (bf16[2,128,896]{2,1,0:T(8,128)(2,1)S(1)}, bf16[2,128,896]{2,1,0:T(8,128)(2,1)S(1)}, u32[]{:S(2)}, u32[]{:S(2)}) collective-permute-start(bf16[2,128,896]{2,1,0:T(8,128)(2,1)S(1)} %get-tuple-element.25), channel_id=1, source_target_pairs={{0,4},{2,6},{4,0},{6,2},{1,5},{3,7},{5,1},{7,3},{8,12},{10,14},{12... | collective-permute-start | bytes 1376264 | tf_op jit(solution)/shard_map/ppermute | solution.py:71
  56.1 1.1 collective-permute-start.9
  57.1 3.5 %shard_map.79 = (bf16[4,128,896]{2,1,0:T(8,128)(2,1)S(1)}, bf16[2,128,896]{2,1,0:T(8,128)(2,1)S(1)}, bf16[2,128,896]{2,1,0:T(8,128)(2,1)S(1)}) custom-call(bf16[8,128,1024]{2,1,0:T(8,128)(2,1)S(1)} %get-tuple-element.29.lhs_ref, bf16[896,512]{1,0:T(8,128)(2,1)S(1)} %collective-permute-done.4.w_own_ref, bf16[896,512]{1,0:T(8,128)(2,1)} %collective-permute-done.11.w_other_ref), custom_call_target="tpu_custom_call" | custom-call | flops 1879048192 | bytes 6291456 | tf_op jit(solution)/shard_map/pallas_call | solution.py:133
  60.7 0.8 collective-permute-start.12
  61.5 0.9 collective-permute-start.13
  62.4 0.5 collective-permute-done.7.refs_1_
  62.9 10.9 %collective-permute-done.8.refs_2_ = bf16[2,128,896]{2,1,0:T(8,128)(2,1)S(1)} collective-permute-done((bf16[2,128,896]{2,1,0:T(8,128)(2,1)S(1)}, bf16[2,128,896]{2,1,0:T(8,128)(2,1)S(1)}, u32[]{:S(2)}, u32[]{:S(2)}) %collective-permute-start.8) | collective-permute-done | bytes 458784 | tf_op jit(solution)/shard_map/ppermute | solution.py:71
  73.9 1.5 %collective-permute-done.9.refs_3_ = bf16[2,128,896]{2,1,0:T(8,128)(2,1)S(1)} collective-permute-done((bf16[2,128,896]{2,1,0:T(8,128)(2,1)S(1)}, bf16[2,128,896]{2,1,0:T(8,128)(2,1)S(1)}, u32[]{:S(2)}, u32[]{:S(2)}) %collective-permute-start.9) | collective-permute-done | bytes 458784 | tf_op jit(solution)/shard_map/ppermute | solution.py:71
  75.3 0.2 shard_map.78
  75.6 0.0 copy-start
  75.6 0.0 copy-start.1
  75.6 0.6 collective-permute-start.10
  76.2 3.1 %collective-permute-done.13.high_ref = bf16[2,128,896]{2,1,0:T(8,128)(2,1)S(1)} collective-permute-done((bf16[2,128,896]{2,1,0:T(8,128)(2,1)S(1)}, bf16[2,128,896]{2,1,0:T(8,128)(2,1)S(1)}, u32[]{:S(2)}, u32[]{:S(2)}) %collective-permute-start.13) | collective-permute-done | bytes 458784 | tf_op jit(solution)/shard_map/ppermute | solution.py:71
  79.4 0.2 shard_map.80
  79.6 0.5 collective-permute-start.14
  80.0 1.1 collective-permute-start.15
  81.1 1.4 %collective-permute-start.16 = (bf16[128,896]{1,0:T(8,128)(2,1)S(1)}, bf16[128,896]{1,0:T(8,128)(2,1)S(1)}, u32[]{:S(2)}, u32[]{:S(2)}) collective-permute-start(bf16[128,896]{1,0:T(8,128)(2,1)S(1)} %get-tuple-element.37), channel_id=1, source_target_pairs={{0,6},{2,0},{4,2},{6,4},{1,7},{3,1},{5,3},{7,5},{8,14},{10,8},{12,... | collective-permute-start | bytes 688136 | tf_op jit(solution)/shard_map/ppermute | solution.py:71
  82.5 1.7 %collective-permute-done.10.refs_1_ = bf16[128,896]{1,0:T(8,128)(2,1)S(1)} collective-permute-done((bf16[128,896]{1,0:T(8,128)(2,1)S(1)}, bf16[128,896]{1,0:T(8,128)(2,1)S(1)}, u32[]{:S(2)}, u32[]{:S(2)}) %collective-permute-start.10) | collective-permute-done | bytes 229408 | tf_op jit(solution)/shard_map/ppermute | solution.py:71
  84.3 3.9 %collective-permute-done.14.refs_3_ = bf16[128,896]{1,0:T(8,128)(2,1)S(1)} collective-permute-done((bf16[128,896]{1,0:T(8,128)(2,1)S(1)}, bf16[128,896]{1,0:T(8,128)(2,1)S(1)}, u32[]{:S(2)}, u32[]{:S(2)}) %collective-permute-start.14) | collective-permute-done | bytes 229408 | tf_op jit(solution)/shard_map/ppermute | solution.py:71
  88.2 0.6 collective-permute-done.16.refs_5_
  88.8 0.8 shard_map.81
  89.6 4.8 %collective-permute-start.17 = (bf16[128,896]{1,0:T(8,128)(2,1)S(1)}, bf16[128,896]{1,0:T(8,128)(2,1)S(1)}, u32[]{:S(2)}, u32[]{:S(2)}) collective-permute-start(bf16[128,896]{1,0:T(8,128)(2,1)S(1)} %get-tuple-element.38), channel_id=1, source_target_pairs={{0,225},{1,129},{2,160},{3,64},{4,161},{5,33},{6,224},{7,65},{8,19... | collective-permute-start | bytes 688136 | tf_op jit(solution)/shard_map/ppermute | solution.py:258
  94.4 6.6 %collective-permute-start.18 = (bf16[128,896]{1,0:T(8,128)(2,1)S(1)}, bf16[128,896]{1,0:T(8,128)(2,1)S(1)}, u32[]{:S(2)}, u32[]{:S(2)}) collective-permute-start(bf16[128,896]{1,0:T(8,128)(2,1)S(1)} %get-tuple-element.39), channel_id=1, source_target_pairs={{0,224},{1,128},{2,161},{3,65},{4,160},{5,32},{6,225},{7,64},{8,19... | collective-permute-start | bytes 688136 | tf_op jit(solution)/shard_map/ppermute | solution.py:258
  101.0 0.9 collective-permute-done.17.first
  101.9 13.0 %collective-permute-done.18.second = bf16[128,896]{1,0:T(8,128)(2,1)S(1)} collective-permute-done((bf16[128,896]{1,0:T(8,128)(2,1)S(1)}, bf16[128,896]{1,0:T(8,128)(2,1)S(1)}, u32[]{:S(2)}, u32[]{:S(2)}) %collective-permute-start.18) | collective-permute-done | bytes 229408 | tf_op jit(solution)/shard_map/ppermute | solution.py:258
  114.9 1.9 %shard_map.82 = (bf16[256,896]{1,0:T(8,128)(2,1)}, bf16[256,896]{1,0:T(8,128)(2,1)}) custom-call(s32[10]{0:T(128)S(1)} %dynamic-slice_bitcast_fusion.facts_ref, bf16[128,896]{1,0:T(8,128)(2,1)S(1)} %collective-permute-done.17.first, bf16[128,896]{1,0:T(8,128)(2,1)S(1)} %collective-permute-done.18.second, bf16[256,896]{1,0:T(8,128)(2,1)S(1)} %copy-done, ...), custom_call_target="tpu_custom_call" | custom-call | flops 2293760 | bytes 2293760 | tf_op jit(solution)/shard_map/pallas_call | solution.py:221
  (14 shorter events, 0.0 us)
Async XLA Ops:
  0.6 1.9 %copy-start.4 = (bf16[896,512]{1,0:T(8,128)(2,1)S(1)}, bf16[896,512]{1,0:T(8,128)(2,1)}, u32[]{:S(2)}) copy-start(bf16[896,512]{1,0:T(8,128)(2,1)} %param.7) | copy-start | bytes 2752516
  0.6 2.2 %collective-permute-start = (bf16[256,512]{1,0:T(8,128)(2,1)}, bf16[256,512]{1,0:T(8,128)(2,1)S(1)}, u32[]{:S(2)}, u32[]{:S(2)}) collective-permute-start(bf16[256,512]{1,0:T(8,128)(2,1)} %param.6), channel_id=1, source_target_pairs={{0,1},{1,0},{2,3},{3,2},{4,5},{5,4},{6,7},{7,6},{8,9},{9,8},{10,11... | collective-permute-start | bytes 786440 | tf_op jit(solution)/shard_map/ppermute | solution.py:71
  2.5 1.0 copy-start.5
  3.5 11.8 %collective-permute-start.1 = (bf16[256,1024]{1,0:T(8,128)(2,1)S(1)}, bf16[256,1024]{1,0:T(8,128)(2,1)S(1)}, u32[]{:S(2)}, u32[]{:S(2)}) collective-permute-start(bf16[256,1024]{1,0:T(8,128)(2,1)S(1)} %pad_maximum_fusion.t0), channel_id=1, source_target_pairs={{0,32},{32,64},{64,96},{96,128},{128,160},{160,192},{192,224},{224... | collective-permute-start | bytes 1572872 | tf_op jit(solution)/shard_map/ppermute | solution.py:243
  15.3 9.2 %collective-permute-start.2 = (bf16[256,1024]{1,0:T(8,128)(2,1)S(1)}, bf16[256,1024]{1,0:T(8,128)(2,1)S(1)}, u32[]{:S(2)}, u32[]{:S(2)}) collective-permute-start(bf16[256,1024]{1,0:T(8,128)(2,1)S(1)} %collective-permute-done.1.t1), channel_id=1, source_target_pairs={{0,32},{32,64},{64,96},{96,128},{128,160},{160,192},{192,224},{224... | collective-permute-start | bytes 1572872 | tf_op jit(solution)/shard_map/ppermute | solution.py:243
  18.4 22.3 %collective-permute-start.4 = (bf16[896,512]{1,0:T(8,128)(2,1)S(1)}, bf16[896,512]{1,0:T(8,128)(2,1)S(1)}, u32[]{:S(2)}, u32[]{:S(2)}) collective-permute-start(bf16[896,512]{1,0:T(8,128)(2,1)S(1)} %fusion.w_own_ref), channel_id=1, source_target_pairs={{0,16},{16,0},{1,17},{17,1},{2,18},{18,2},{3,19},{19,3},{4,20},{20... | collective-permute-start | bytes 2752520 | tf_op jit(solution)/shard_map/ppermute | solution.py:71
  24.5 16.2 %collective-permute-start.3 = (bf16[256,1024]{1,0:T(8,128)(2,1)S(1)}, bf16[256,1024]{1,0:T(8,128)(2,1)S(1)}, u32[]{:S(2)}, u32[]{:S(2)}) collective-permute-start(bf16[256,1024]{1,0:T(8,128)(2,1)S(1)} %collective-permute-done.2.t2), channel_id=1, source_target_pairs={{0,32},{32,64},{64,96},{96,128},{128,160},{160,192},{192,224},{224... | collective-permute-start | bytes 1572872 | tf_op jit(solution)/shard_map/ppermute | solution.py:243
  27.9 0.8 copy-start.2
  28.7 15.4 %collective-permute-start.6 = (bf16[896,512]{1,0:T(8,128)(2,1)S(1)}, bf16[896,512]{1,0:T(8,128)(2,1)}, u32[]{:S(2)}, u32[]{:S(2)}) collective-permute-start(bf16[896,512]{1,0:T(8,128)(2,1)S(1)} %fusion.w_own_ref), channel_id=1, source_target_pairs={{0,1},{1,0},{2,3},{3,2},{4,5},{5,4},{6,7},{7,6},{8,9},{9,8},{10,11... | collective-permute-start | bytes 2752520 | tf_op jit(solution)/shard_map/ppermute | solution.py:71
  40.7 16.4 %collective-permute-start.11 = (bf16[896,512]{1,0:T(8,128)(2,1)S(1)}, bf16[896,512]{1,0:T(8,128)(2,1)}, u32[]{:S(2)}, u32[]{:S(2)}) collective-permute-start(bf16[896,512]{1,0:T(8,128)(2,1)S(1)} %collective-permute-done.4.w_own_ref), channel_id=1, source_target_pairs={{0,1},{1,0},{2,3},{3,2},{4,5},{5,4},{6,7},{7,6},{8,9},{9,8},{10,11... | collective-permute-start | bytes 2752520 | tf_op jit(solution)/shard_map/ppermute | solution.py:71
  41.5 5.8 %collective-permute-start.5 = (bf16[128,1024]{1,0:T(8,128)(2,1)}, bf16[128,1024]{1,0:T(8,128)(2,1)}, u32[]{:S(2)}, u32[]{:S(2)}) collective-permute-start(bf16[128,1024]{1,0:T(8,128)(2,1)} %constant_dynamic-slice_fusion), channel_id=1, source_target_pairs={{0,32},{32,64},{64,96},{96,128},{128,160},{160,192},{192,224},{224... | collective-permute-start | bytes 786440 | tf_op jit(solution)/shard_map/ppermute | solution.py:245
  47.3 1.0 copy-start.3
  52.1 10.9 %collective-permute-start.7 = (bf16[2,128,896]{2,1,0:T(8,128)(2,1)S(1)}, bf16[2,128,896]{2,1,0:T(8,128)(2,1)S(1)}, u32[]{:S(2)}, u32[]{:S(2)}) collective-permute-start(bf16[2,128,896]{2,1,0:T(8,128)(2,1)S(1)} %get-tuple-element.24), channel_id=1, source_target_pairs={{0,2},{2,4},{4,6},{6,0},{1,3},{3,5},{5,7},{7,1},{8,10},{10,12},{12... | collective-permute-start | bytes 1376264 | tf_op jit(solution)/shard_map/ppermute | solution.py:71
  53.4 20.4 %collective-permute-start.8 = (bf16[2,128,896]{2,1,0:T(8,128)(2,1)S(1)}, bf16[2,128,896]{2,1,0:T(8,128)(2,1)S(1)}, u32[]{:S(2)}, u32[]{:S(2)}) collective-permute-start(bf16[2,128,896]{2,1,0:T(8,128)(2,1)S(1)} %get-tuple-element.25), channel_id=1, source_target_pairs={{0,4},{2,6},{4,0},{6,2},{1,5},{3,7},{5,1},{7,3},{8,12},{10,14},{12... | collective-permute-start | bytes 1376264 | tf_op jit(solution)/shard_map/ppermute | solution.py:71
  56.1 19.3 %collective-permute-start.9 = (bf16[2,128,896]{2,1,0:T(8,128)(2,1)S(1)}, bf16[2,128,896]{2,1,0:T(8,128)(2,1)S(1)}, u32[]{:S(2)}, u32[]{:S(2)}) collective-permute-start(bf16[2,128,896]{2,1,0:T(8,128)(2,1)S(1)} %get-tuple-element.26), channel_id=1, source_target_pairs={{0,6},{2,0},{4,2},{6,4},{1,7},{3,1},{5,3},{7,5},{8,14},{10,8},{12,... | collective-permute-start | bytes 1376264 | tf_op jit(solution)/shard_map/ppermute | solution.py:71
  60.7 15.6 %collective-permute-start.12 = (bf16[2,128,896]{2,1,0:T(8,128)(2,1)S(1)}, bf16[2,128,896]{2,1,0:T(8,128)(2,1)S(1)}, u32[]{:S(2)}, u32[]{:S(2)}) collective-permute-start(bf16[2,128,896]{2,1,0:T(8,128)(2,1)S(1)} %get-tuple-element.32), channel_id=1, source_target_pairs={{0,8},{8,0},{1,9},{9,1},{2,10},{10,2},{3,11},{11,3},{4,12},{12,4},... | collective-permute-start | bytes 1376264 | tf_op jit(solution)/shard_map/ppermute | solution.py:71
  61.5 17.9 %collective-permute-start.13 = (bf16[2,128,896]{2,1,0:T(8,128)(2,1)S(1)}, bf16[2,128,896]{2,1,0:T(8,128)(2,1)S(1)}, u32[]{:S(2)}, u32[]{:S(2)}) collective-permute-start(bf16[2,128,896]{2,1,0:T(8,128)(2,1)S(1)} %get-tuple-element.33), channel_id=1, source_target_pairs={{0,8},{8,0},{1,9},{9,1},{2,10},{10,2},{3,11},{11,3},{4,12},{12,4},... | collective-permute-start | bytes 1376264 | tf_op jit(solution)/shard_map/ppermute | solution.py:71
  75.6 39.3 %copy-start = (bf16[256,896]{1,0:T(8,128)(2,1)S(1)}, bf16[256,896]{1,0:T(8,128)(2,1)}, u32[]{:S(2)}) copy-start(bf16[256,896]{1,0:T(8,128)(2,1)} %gate_ref.1) | copy-start | bytes 1376260
  75.6 39.3 %copy-start.1 = (bf16[256,896]{1,0:T(8,128)(2,1)S(1)}, bf16[256,896]{1,0:T(8,128)(2,1)}, u32[]{:S(2)}) copy-start(bf16[256,896]{1,0:T(8,128)(2,1)} %up_ref.1) | copy-start | bytes 1376260
  75.6 8.7 %collective-permute-start.10 = (bf16[128,896]{1,0:T(8,128)(2,1)S(1)}, bf16[128,896]{1,0:T(8,128)(2,1)S(1)}, u32[]{:S(2)}, u32[]{:S(2)}) collective-permute-start(bf16[128,896]{1,0:T(8,128)(2,1)S(1)} %get-tuple-element.28), channel_id=1, source_target_pairs={{0,8},{8,0},{1,9},{9,1},{2,10},{10,2},{3,11},{11,3},{4,12},{12,4},... | collective-permute-start | bytes 688136 | tf_op jit(solution)/shard_map/ppermute | solution.py:71
  79.6 8.6 %collective-permute-start.14 = (bf16[128,896]{1,0:T(8,128)(2,1)S(1)}, bf16[128,896]{1,0:T(8,128)(2,1)S(1)}, u32[]{:S(2)}, u32[]{:S(2)}) collective-permute-start(bf16[128,896]{1,0:T(8,128)(2,1)S(1)} %get-tuple-element.35), channel_id=1, source_target_pairs={{0,2},{2,4},{4,6},{6,0},{1,3},{3,5},{5,7},{7,1},{8,10},{10,12},{12... | collective-permute-start | bytes 688136 | tf_op jit(solution)/shard_map/ppermute | solution.py:71
  80.0 8.1 %collective-permute-start.15 = (bf16[128,896]{1,0:T(8,128)(2,1)S(1)}, bf16[128,896]{1,0:T(8,128)(2,1)S(1)}, u32[]{:S(2)}, u32[]{:S(2)}) collective-permute-start(bf16[128,896]{1,0:T(8,128)(2,1)S(1)} %get-tuple-element.36), channel_id=1, source_target_pairs={{0,4},{2,6},{4,0},{6,2},{1,5},{3,7},{5,1},{7,3},{8,12},{10,14},{12... | collective-permute-start | bytes 688136 | tf_op jit(solution)/shard_map/ppermute | solution.py:71
  81.1 7.7 %collective-permute-start.16 = (bf16[128,896]{1,0:T(8,128)(2,1)S(1)}, bf16[128,896]{1,0:T(8,128)(2,1)S(1)}, u32[]{:S(2)}, u32[]{:S(2)}) collective-permute-start(bf16[128,896]{1,0:T(8,128)(2,1)S(1)} %get-tuple-element.37), channel_id=1, source_target_pairs={{0,6},{2,0},{4,2},{6,4},{1,7},{3,1},{5,3},{7,5},{8,14},{10,8},{12,... | collective-permute-start | bytes 688136 | tf_op jit(solution)/shard_map/ppermute | solution.py:71
  89.6 12.3 %collective-permute-start.17 = (bf16[128,896]{1,0:T(8,128)(2,1)S(1)}, bf16[128,896]{1,0:T(8,128)(2,1)S(1)}, u32[]{:S(2)}, u32[]{:S(2)}) collective-permute-start(bf16[128,896]{1,0:T(8,128)(2,1)S(1)} %get-tuple-element.38), channel_id=1, source_target_pairs={{0,225},{1,129},{2,160},{3,64},{4,161},{5,33},{6,224},{7,65},{8,19... | collective-permute-start | bytes 688136 | tf_op jit(solution)/shard_map/ppermute | solution.py:258
  94.4 20.5 %collective-permute-start.18 = (bf16[128,896]{1,0:T(8,128)(2,1)S(1)}, bf16[128,896]{1,0:T(8,128)(2,1)S(1)}, u32[]{:S(2)}, u32[]{:S(2)}) collective-permute-start(bf16[128,896]{1,0:T(8,128)(2,1)S(1)} %get-tuple-element.39), channel_id=1, source_target_pairs={{0,224},{1,128},{2,161},{3,65},{4,160},{5,32},{6,225},{7,64},{8,19... | collective-permute-start | bytes 688136 | tf_op jit(solution)/shard_map/ppermute | solution.py:258

commit v6 on v5

--- a/solution.py
+++ b/solution.py
@@ -40,7 +40,7 @@
     return ((z * XH + xh) * S + s) * C + c
 
 
-def home_pairs(j):
+def home_pairs(r, h):
     pairs = []
     for z in range(Z):
         for xh in range(XH):
@@ -49,7 +49,8 @@
                     number = number_of(z, s, c)
                     away = (number + 1) // 2
                     to = (z - away if c == 0 else z + away) % Z
-                    pairs.append((device_index(z, xh, s, c), device_index(to, xh, z, j ^ half_of(number, c))))
+                    if half_of(number, c) == h:
+                        pairs.append((device_index(z, xh, s, c), device_index(to, xh, z, xh ^ r)))
     return pairs
 
 
@@ -63,7 +64,7 @@
                         place = [0] * S
                         for s in range(S):
                             place[number_of(z, s, c)] = 2 * ((s % Y - y) % Y) + ((s // Y) ^ xl)
-                        rows.append(place + [c, half_of(number_of(z, xl * Y + y, c), c) ^ xh])
+                        rows.append(place + [c, c ^ xh])
     return np.array(rows, np.int32)
 
 
@@ -178,40 +179,34 @@
     )(kept, *received)
 
 
-def add_last(own, near_parts, cross_parts):
-    rows, width = near_parts[0].shape
-    count = len(near_parts)
-
-    def kernel(facts_ref, *refs):
-        sums = []
-        for parts in (refs[:count], refs[count : count + Y]):
-            total = parts[0][...].astype(F32)
-            for ref in parts[1:]:
-                total += ref[...].astype(F32)
-            sums.append(total)
-        straight = facts_ref[S + 1] == 0
-        refs[count + Y][...] = jnp.where(straight, sums[0], sums[1]).astype(BF16)
-        refs[count + Y + 1][...] = jnp.where(straight, sums[1], sums[0]).astype(BF16)
-
-    return pl.pallas_call(
-        kernel,
-        in_specs=[SMEM] + [VMEM] * (count + Y),
-        out_specs=[VMEM] * 2,
-        out_shape=[jax.ShapeDtypeStruct((rows, width), BF16)] * 2,
-        compiler_params=params(16),
-        cost_estimate=pl.CostEstimate(flops=8 * rows * width, bytes_accessed=16 * rows * width, transcendentals=0),
-    )(own, *near_parts, *cross_parts)
+def add_last(parts):
+    rows, width = parts[0].shape
+
+    def kernel(*refs):
+        total = refs[0][...].astype(F32)
+        for ref in refs[1:-1]:
+            total += ref[...].astype(F32)
+        refs[-1][...] = total.astype(BF16)
+
+    return pl.pallas_call(
+        kernel,
+        in_specs=[VMEM] * len(parts),
+        out_specs=VMEM,
+        out_shape=jax.ShapeDtypeStruct((rows, width), BF16),
+        compiler_params=params(16),
+        cost_estimate=pl.CostEstimate(flops=4 * rows * width, bytes_accessed=8 * rows * width, transcendentals=0),
+    )(*parts)
 
 
 def swiglu_backward(own, hidden, gate_act, up_act):
     rows, width = gate_act.shape
     half = rows // 2
 
-    def kernel(facts_ref, first, second, gate_ref, up_ref, grad_gate_ref, grad_up_ref):
-        flip = facts_ref[S] == 1
-        for h, (straight, crossed) in enumerate(((first, second), (second, first))):
+    def kernel(facts_ref, near0, near1, cross0, cross1, gate_ref, up_ref, grad_gate_ref, grad_up_ref):
+        crossed = facts_ref[S + 1] == 1
+        for h, (near, cross) in enumerate(((near0, cross0), (near1, cross1))):
             here = slice(h * half, (h + 1) * half)
-            value = jnp.where(flip, crossed[...].astype(F32), straight[...].astype(F32))
+            value = jnp.where(crossed, cross[...].astype(F32), near[...].astype(F32))
             gate = gate_ref[here, :].astype(F32)
             sigmoid = jax.nn.sigmoid(gate)
             grad_up_ref[here, :] = (value * gate * sigmoid).astype(BF16)
@@ -220,12 +215,12 @@
 
     return pl.pallas_call(
         kernel,
-        in_specs=[SMEM] + [VMEM] * 4,
+        in_specs=[SMEM] + [VMEM] * 6,
         out_specs=[VMEM] * 2,
         out_shape=[jax.ShapeDtypeStruct((rows, width), BF16)] * 2,
         compiler_params=params(16),
         cost_estimate=pl.CostEstimate(flops=10 * rows * width, bytes_accessed=10 * rows * width, transcendentals=rows * width),
-    )(own, *hidden, gate_act, up_act)
+    )(own, *hidden[0], *hidden[1], gate_act, up_act)
 
 
 def on_device(grad_out, down_q, scales, gate_act, up_act):
@@ -233,17 +228,21 @@
     own = lax.dynamic_index_in_dim(jnp.asarray(facts()), lax.axis_index(ALL), 0, keepdims=False)
 
     near_own = dequantize(down_q, scales)
-    cross_own = shift(near_own, "xh", XH, 1)
+    cut = 5 * BLOCK
+    cross_parts = [shift(near_own[:cut], "xh", XH, 1), shift(near_own[cut:], "xh", XH, 1)]
 
     rows = grad_out.shape[0] // 2
     tokens = [jnp.concatenate([grad_out, shift(grad_out, "c", C, 1)], 1)]
     around = [(i * C, (i + 1) % Z * C) for i in range(Z)] + [(i * C + 1, (i - 1) % Z * C + 1) for i in range(Z)]
     tokens[0], _ = lax.optimization_barrier((tokens[0], near_own))
     for step in range(3):
+        if step == 2:
+            tokens[-1], cross_parts[0] = lax.optimization_barrier((tokens[-1], cross_parts[0]))
         tokens.append(lax.ppermute(tokens[-1], ("z", "c"), around))
-    tokens[3], cross_own = lax.optimization_barrier((tokens[3], cross_own))
+    tokens[3], cross_parts[1] = lax.optimization_barrier((tokens[3], cross_parts[1]))
     far = lax.ppermute(lax.dynamic_slice_in_dim(tokens[3], c * rows, rows, 0), ("z", "c"), around)
     near_other = shift(near_own, "c", C, 1)
+    cross_own = jnp.concatenate(cross_parts, 0)
     cross_other = shift(cross_own, "c", C, 1)
 
     lhs, *near = product_y(own, tokens, far, near_own, near_other)
@@ -254,8 +253,8 @@
     kept, sent = add_y(near_y)
     near_parts = [kept, shift(sent, "xl", XL, 1)]
 
-    sums = add_last(own, near_parts, cross_parts)
-    hidden = [lax.ppermute(sums[j], ALL, home_pairs(j)) for j in range(2)]
+    sums = [add_last(near_parts), add_last(cross_parts)]
+    hidden = [[lax.ppermute(sums[r], ALL, home_pairs(r, h)) for h in range(2)] for r in range(2)]
     return tuple(swiglu_backward(own, hidden, gate_act, up_act))
 
 

time: 117 us -> 116 us (level)
  the two profiles are of different devices: /device:TPU:7 before, /device:TPU:6 now
where the time goes in v6:
time: 116 us
  waiting for transfers between devices  70.8 us (61%)
  starting transfers between devices  30.3 us (26%)
  Pallas kernels  9.74 us (8%)
  local copies, waits for them, and re-layouts  4.11 us (4%)
    ppermute x14, waiting for transfers between devices, shift(): return lax.ppermute(x, axis, [(i, (i + by) % size) for i in range(size)])  39.7 us
    ppermute x14, starting transfers between devices, shift(): return lax.ppermute(x, axis, [(i, (i + by) % size) for i in range(size)])  17.5 us
    ppermute x3, waiting for transfers between devices, on_device(): tokens.append(lax.ppermute(tokens[-1], ('z', 'c'), around))  15 us
    ppermute x4, starting transfers between devices, on_device(): lax.ppermute(sums[r], ALL, home_pairs(r, h))  10.9 us
    ppermute x4, waiting for transfers between devices, on_device(): lax.ppermute(sums[r], ALL, home_pairs(r, h))  8.86 us
    ppermute x1, waiting for transfers between devices, on_device(): lax.ppermute(lax.dynamic_slice_in_dim(tokens[3], c * rows, rows, 0), ('z'...  7.2 us
    pallas_call x1, Pallas kernels, product_y(): pl.pallas_call(kernel, in_specs=[SMEM] + [VMEM] * 7, out_specs=[VMEM] * (...  3.72 us
    pallas_call x1, Pallas kernels, product_xl(): pl.pallas_call(kernel, in_specs=[VMEM] * 3, out_specs=[VMEM] * 3, out_sha...  3.54 us
  transfers between devices with their start and end apart: 22, of which 12 were waited for; matrix products, arithmetic and copies ran while one was open for 3% of the time, Pallas kernels for 7%

profile of v6, /device:TPU:6, one launch (start us, length us, event | category | flops | bytes accessed | tf_op | source)
XLA Modules:
  0.0 116.2 jit_solution(7754057205293609619)
XLA Ops:
  0.6 0.1 collective-permute-start
  0.7 0.8 copy.8
  1.6 0.3 mul.30
  1.9 0.0 copy-start.5
  1.9 0.4 fusion.w_own_ref
  2.3 0.2 collective-permute-done
  2.5 0.4 copy-done.5
  2.8 0.1 pad_maximum_fusion.t0
  2.9 2.0 %collective-permute-start.1 = (bf16[256,1024]{1,0:T(8,128)(2,1)S(1)}, bf16[256,1024]{1,0:T(8,128)(2,1)S(1)}, u32[]{:S(2)}, u32[]{:S(2)}) collective-permute-start(bf16[256,1024]{1,0:T(8,128)(2,1)S(1)} %pad_maximum_fusion.t0), channel_id=1, source_target_pairs={{0,32},{32,64},{64,96},{96,128},{128,160},{160,192},{192,224},{224... | collective-permute-start | bytes 1572872 | tf_op jit(solution)/shard_map/ppermute | solution.py:241
  4.9 1.5 %collective-permute-start.3 = (bf16[640,512]{1,0:T(8,128)(2,1)S(1)}, bf16[640,512]{1,0:T(8,128)(2,1)S(1)}, u32[]{:S(2)}, u32[]{:S(2)}) collective-permute-start(bf16[640,512]{1,0:T(8,128)(2,1)S(1)} %slice.8), channel_id=1, source_target_pairs={{0,16},{16,0},{1,17},{17,1},{2,18},{18,2},{3,19},{19,3},{4,20},{20... | collective-permute-start | bytes 1966088 | tf_op jit(solution)/shard_map/ppermute | solution.py:72
  6.4 9.6 %collective-permute-done.1.t1 = bf16[256,1024]{1,0:T(8,128)(2,1)S(1)} collective-permute-done((bf16[256,1024]{1,0:T(8,128)(2,1)S(1)}, bf16[256,1024]{1,0:T(8,128)(2,1)S(1)}, u32[]{:S(2)}, u32[]{:S(2)}) %collective-permute-start.1) | collective-permute-done | bytes 524320 | tf_op jit(solution)/shard_map/ppermute | solution.py:241
  16.0 0.0 collective-permute-start.2
  16.0 5.0 %collective-permute-done.3 = bf16[640,512]{1,0:T(8,128)(2,1)S(1)} collective-permute-done((bf16[640,512]{1,0:T(8,128)(2,1)S(1)}, bf16[640,512]{1,0:T(8,128)(2,1)S(1)}, u32[]{:S(2)}, u32[]{:S(2)}) %collective-permute-start.3) | collective-permute-done | bytes 655392 | tf_op jit(solution)/shard_map/ppermute | solution.py:72
  21.0 5.4 %collective-permute-done.2.t2 = bf16[256,1024]{1,0:T(8,128)(2,1)S(1)} collective-permute-done((bf16[256,1024]{1,0:T(8,128)(2,1)S(1)}, bf16[256,1024]{1,0:T(8,128)(2,1)S(1)}, u32[]{:S(2)}, u32[]{:S(2)}) %collective-permute-start.2) | collective-permute-done | bytes 524320 | tf_op jit(solution)/shard_map/ppermute | solution.py:241
  26.4 0.0 collective-permute-start.4
  26.4 1.5 %collective-permute-start.5 = (bf16[256,512]{1,0:T(8,128)(2,1)S(1)}, bf16[256,512]{1,0:T(8,128)(2,1)S(1)}, u32[]{:S(2)}, u32[]{:S(2)}) collective-permute-start(bf16[256,512]{1,0:T(8,128)(2,1)S(1)} %slice.9), channel_id=1, source_target_pairs={{0,16},{16,0},{1,17},{17,1},{2,18},{18,2},{3,19},{19,3},{4,20},{20... | collective-permute-start | bytes 786440 | tf_op jit(solution)/shard_map/ppermute | solution.py:72
  27.9 1.1 collective-permute-start.7
  29.1 7.8 %collective-permute-done.5 = bf16[256,512]{1,0:T(8,128)(2,1)S(1)} collective-permute-done((bf16[256,512]{1,0:T(8,128)(2,1)S(1)}, bf16[256,512]{1,0:T(8,128)(2,1)S(1)}, u32[]{:S(2)}, u32[]{:S(2)}) %collective-permute-start.5) | collective-permute-done | bytes 262176 | tf_op jit(solution)/shard_map/ppermute | solution.py:72
  36.9 0.2 collective-permute-start.14
  37.1 0.7 constant_dynamic-slice_fusion
  37.9 0.7 dynamic-slice_bitcast_fusion.facts_ref
  38.6 7.2 %collective-permute-done.6.far_ref = bf16[128,1024]{1,0:T(8,128)(2,1)} collective-permute-done((bf16[128,1024]{1,0:T(8,128)(2,1)}, bf16[128,1024]{1,0:T(8,128)(2,1)}, u32[]{:S(2)}, u32[]{:S(2)}) %collective-permute-start.6) | collective-permute-done | bytes 262176 | tf_op jit(solution)/shard_map/ppermute | solution.py:243
  45.8 1.0 copy-done.3
  46.8 3.7 %shard_map.77 = (bf16[8,128,1024]{2,1,0:T(8,128)(2,1)S(1)}, bf16[2,128,896]{2,1,0:T(8,128)(2,1)S(1)}, bf16[2,128,896]{2,1,0:T(8,128)(2,1)S(1)}, bf16[2,128,896]{2,1,0:T(8,128)(2,1)S(1)}, bf16[2,128,896]{2,1,0:T(8,128)(2,1)S(1)}) custom-call(s32[10]{0:T(128)S(1)} %dynamic-slice_bitcast_fusion.facts_ref, bf16[256,1024]{1,0:T(8,128)(2,1)S(1)} %pad_maximum_fusion.t0, ...), custom_call_target="tpu_custom_call" | custom-call | flops 1879048192 | bytes 8388608 | tf_op jit(solution)/shard_map/pallas_call | solution.py:112
  50.5 3.1 %collective-permute-start.10 = (bf16[2,128,896]{2,1,0:T(8,128)(2,1)S(1)}, bf16[2,128,896]{2,1,0:T(8,128)(2,1)S(1)}, u32[]{:S(2)}, u32[]{:S(2)}) collective-permute-start(bf16[2,128,896]{2,1,0:T(8,128)(2,1)S(1)} %get-tuple-element.27), channel_id=1, source_target_pairs={{0,6},{2,0},{4,2},{6,4},{1,7},{3,1},{5,3},{7,5},{8,14},{10,8},{12,... | collective-permute-start | bytes 1376264 | tf_op jit(solution)/shard_map/ppermute | solution.py:72
  53.6 2.2 %collective-permute-start.9 = (bf16[2,128,896]{2,1,0:T(8,128)(2,1)S(1)}, bf16[2,128,896]{2,1,0:T(8,128)(2,1)S(1)}, u32[]{:S(2)}, u32[]{:S(2)}) collective-permute-start(bf16[2,128,896]{2,1,0:T(8,128)(2,1)S(1)} %get-tuple-element.26), channel_id=1, source_target_pairs={{0,4},{2,6},{4,0},{6,2},{1,5},{3,7},{5,1},{7,3},{8,12},{10,14},{12... | collective-permute-start | bytes 1376264 | tf_op jit(solution)/shard_map/ppermute | solution.py:72
  55.8 3.5 %shard_map.80 = (bf16[4,128,896]{2,1,0:T(8,128)(2,1)S(1)}, bf16[2,128,896]{2,1,0:T(8,128)(2,1)S(1)}, bf16[2,128,896]{2,1,0:T(8,128)(2,1)S(1)}) custom-call(bf16[8,128,1024]{2,1,0:T(8,128)(2,1)S(1)} %get-tuple-element.30.lhs_ref, bf16[896,512]{1,0:T(8,128)(2,1)S(1)} %constant_dynamic-update-slice_fusion.w_own_ref, ...), custom_call_target="tpu_custom_call" | custom-call | flops 1879048192 | bytes 6291456 | tf_op jit(solution)/shard_map/pallas_call | solution.py:134
  59.4 0.9 collective-permute-start.15
  60.3 1.2 %collective-permute-start.16 = (bf16[2,128,896]{2,1,0:T(8,128)(2,1)S(1)}, bf16[2,128,896]{2,1,0:T(8,128)(2,1)S(1)}, u32[]{:S(2)}, u32[]{:S(2)}) collective-permute-start(bf16[2,128,896]{2,1,0:T(8,128)(2,1)S(1)} %get-tuple-element.35), channel_id=1, source_target_pairs={{0,8},{8,0},{1,9},{9,1},{2,10},{10,2},{3,11},{11,3},{4,12},{12,4},... | collective-permute-start | bytes 1376264 | tf_op jit(solution)/shard_map/ppermute | solution.py:72
  61.5 10.2 %collective-permute-done.10.refs_3_ = bf16[2,128,896]{2,1,0:T(8,128)(2,1)S(1)} collective-permute-done((bf16[2,128,896]{2,1,0:T(8,128)(2,1)S(1)}, bf16[2,128,896]{2,1,0:T(8,128)(2,1)S(1)}, u32[]{:S(2)}, u32[]{:S(2)}) %collective-permute-start.10) | collective-permute-done | bytes 458784 | tf_op jit(solution)/shard_map/ppermute | solution.py:72
  71.7 3.4 %collective-permute-done.8.refs_1_ = bf16[2,128,896]{2,1,0:T(8,128)(2,1)S(1)} collective-permute-done((bf16[2,128,896]{2,1,0:T(8,128)(2,1)S(1)}, bf16[2,128,896]{2,1,0:T(8,128)(2,1)S(1)}, u32[]{:S(2)}, u32[]{:S(2)}) %collective-permute-start.8) | collective-permute-done | bytes 458784 | tf_op jit(solution)/shard_map/ppermute | solution.py:72
  75.1 0.2 shard_map.78
  75.4 0.9 collective-permute-start.11
  76.3 5.4 %collective-permute-done.16.high_ref = bf16[2,128,896]{2,1,0:T(8,128)(2,1)S(1)} collective-permute-done((bf16[2,128,896]{2,1,0:T(8,128)(2,1)S(1)}, bf16[2,128,896]{2,1,0:T(8,128)(2,1)S(1)}, u32[]{:S(2)}, u32[]{:S(2)}) %collective-permute-start.16) | collective-permute-done | bytes 458784 | tf_op jit(solution)/shard_map/ppermute | solution.py:72
  81.6 0.2 shard_map.81
  81.9 2.0 %collective-permute-start.17 = (bf16[128,896]{1,0:T(8,128)(2,1)S(1)}, bf16[128,896]{1,0:T(8,128)(2,1)S(1)}, u32[]{:S(2)}, u32[]{:S(2)}) collective-permute-start(bf16[128,896]{1,0:T(8,128)(2,1)S(1)} %get-tuple-element.37), channel_id=1, source_target_pairs={{0,2},{2,4},{4,6},{6,0},{1,3},{3,5},{5,7},{7,1},{8,10},{10,12},{12... | collective-permute-start | bytes 688136 | tf_op jit(solution)/shard_map/ppermute | solution.py:72
  83.8 0.9 collective-permute-start.18
  84.7 1.9 %collective-permute-start.19 = (bf16[128,896]{1,0:T(8,128)(2,1)S(1)}, bf16[128,896]{1,0:T(8,128)(2,1)S(1)}, u32[]{:S(2)}, u32[]{:S(2)}) collective-permute-start(bf16[128,896]{1,0:T(8,128)(2,1)S(1)} %get-tuple-element.39), channel_id=1, source_target_pairs={{0,6},{2,0},{4,2},{6,4},{1,7},{3,1},{5,3},{7,5},{8,14},{10,8},{12,... | collective-permute-start | bytes 688136 | tf_op jit(solution)/shard_map/ppermute | solution.py:72
  86.6 0.1 shard_map.79
  86.7 0.7 collective-permute-start.12
  87.3 1.3 %collective-permute-start.13 = (bf16[128,896]{1,0:T(8,128)(2,1)S(1)}, bf16[128,896]{1,0:T(8,128)(2,1)S(1)}, u32[]{:S(2)}, u32[]{:S(2)}) collective-permute-start(bf16[128,896]{1,0:T(8,128)(2,1)S(1)} %shard_map.79), channel_id=1, source_target_pairs={{0,224},{1,128},{4,160},{5,32},{7,64},{8,192},{9,96},{15,0},{16,24... | collective-permute-start | bytes 688136 | tf_op jit(solution)/shard_map/ppermute | solution.py:257
  88.7 3.0 %collective-permute-done.17.refs_1_ = bf16[128,896]{1,0:T(8,128)(2,1)S(1)} collective-permute-done((bf16[128,896]{1,0:T(8,128)(2,1)S(1)}, bf16[128,896]{1,0:T(8,128)(2,1)S(1)}, u32[]{:S(2)}, u32[]{:S(2)}) %collective-permute-start.17) | collective-permute-done | bytes 229408 | tf_op jit(solution)/shard_map/ppermute | solution.py:72
  91.6 4.8 %collective-permute-done.19.refs_3_ = bf16[128,896]{1,0:T(8,128)(2,1)S(1)} collective-permute-done((bf16[128,896]{1,0:T(8,128)(2,1)S(1)}, bf16[128,896]{1,0:T(8,128)(2,1)S(1)}, u32[]{:S(2)}, u32[]{:S(2)}) %collective-permute-start.19) | collective-permute-done | bytes 229408 | tf_op jit(solution)/shard_map/ppermute | solution.py:72
  96.4 0.1 shard_map.82
  96.5 1.3 %collective-permute-start.20 = (bf16[128,896]{1,0:T(8,128)(2,1)S(1)}, bf16[128,896]{1,0:T(8,128)(2,1)S(1)}, u32[]{:S(2)}, u32[]{:S(2)}) collective-permute-start(bf16[128,896]{1,0:T(8,128)(2,1)S(1)} %shard_map.82), channel_id=1, source_target_pairs={{2,161},{3,65},{6,225},{10,1},{11,33},{12,193},{13,97},{14,129},{1... | collective-permute-start | bytes 688136 | tf_op jit(solution)/shard_map/ppermute | solution.py:257
  97.8 7.6 %collective-permute-start.21 = (bf16[128,896]{1,0:T(8,128)(2,1)S(1)}, bf16[128,896]{1,0:T(8,128)(2,1)S(1)}, u32[]{:S(2)}, u32[]{:S(2)}) collective-permute-start(bf16[128,896]{1,0:T(8,128)(2,1)S(1)} %shard_map.82), channel_id=1, source_target_pairs={{0,225},{1,129},{4,161},{5,33},{7,65},{8,193},{9,97},{15,1},{16,24... | collective-permute-start | bytes 688136 | tf_op jit(solution)/shard_map/ppermute | solution.py:257
  105.4 8.9 %collective-permute-done.20.cross0 = bf16[128,896]{1,0:T(8,128)(2,1)S(1)} collective-permute-done((bf16[128,896]{1,0:T(8,128)(2,1)S(1)}, bf16[128,896]{1,0:T(8,128)(2,1)S(1)}, u32[]{:S(2)}, u32[]{:S(2)}) %collective-permute-start.20) | collective-permute-done | bytes 229408 | tf_op jit(solution)/shard_map/ppermute | solution.py:257
  114.3 1.9 %shard_map.83 = (bf16[256,896]{1,0:T(8,128)(2,1)}, bf16[256,896]{1,0:T(8,128)(2,1)}) custom-call(s32[10]{0:T(128)S(1)} %dynamic-slice_bitcast_fusion.facts_ref, bf16[128,896]{1,0:T(8,128)(2,1)S(1)} %collective-permute-done.12.near0, bf16[128,896]{1,0:T(8,128)(2,1)S(1)} %collective-permute-done.13.near1, bf16[128,896]{1,0:T(8,128)(2,1)S(1)} %collective-permute-done.20.cross0, ...), custom_call_target="tpu_custom_call" | custom-call | flops 2293760 | bytes 2293760 | tf_op jit(solution)/shard_map/pallas_call | solution.py:216
  (25 shorter events, 0.2 us)
Async XLA Ops:
  0.6 1.3 %copy-start.4 = (bf16[896,512]{1,0:T(8,128)(2,1)S(1)}, bf16[896,512]{1,0:T(8,128)(2,1)}, u32[]{:S(2)}) copy-start(bf16[896,512]{1,0:T(8,128)(2,1)} %param.7) | copy-start | bytes 2752516
  0.6 1.8 %collective-permute-start = (bf16[256,512]{1,0:T(8,128)(2,1)}, bf16[256,512]{1,0:T(8,128)(2,1)S(1)}, u32[]{:S(2)}, u32[]{:S(2)}) collective-permute-start(bf16[256,512]{1,0:T(8,128)(2,1)} %param.6), channel_id=1, source_target_pairs={{0,1},{1,0},{2,3},{3,2},{4,5},{5,4},{6,7},{7,6},{8,9},{9,8},{10,11... | collective-permute-start | bytes 786440 | tf_op jit(solution)/shard_map/ppermute | solution.py:72
  1.9 1.0 copy-start.5
  2.9 13.1 %collective-permute-start.1 = (bf16[256,1024]{1,0:T(8,128)(2,1)S(1)}, bf16[256,1024]{1,0:T(8,128)(2,1)S(1)}, u32[]{:S(2)}, u32[]{:S(2)}) collective-permute-start(bf16[256,1024]{1,0:T(8,128)(2,1)S(1)} %pad_maximum_fusion.t0), channel_id=1, source_target_pairs={{0,32},{32,64},{64,96},{96,128},{128,160},{160,192},{192,224},{224... | collective-permute-start | bytes 1572872 | tf_op jit(solution)/shard_map/ppermute | solution.py:241
  4.9 16.0 %collective-permute-start.3 = (bf16[640,512]{1,0:T(8,128)(2,1)S(1)}, bf16[640,512]{1,0:T(8,128)(2,1)S(1)}, u32[]{:S(2)}, u32[]{:S(2)}) collective-permute-start(bf16[640,512]{1,0:T(8,128)(2,1)S(1)} %slice.8), channel_id=1, source_target_pairs={{0,16},{16,0},{1,17},{17,1},{2,18},{18,2},{3,19},{19,3},{4,20},{20... | collective-permute-start | bytes 1966088 | tf_op jit(solution)/shard_map/ppermute | solution.py:72
  16.0 10.4 %collective-permute-start.2 = (bf16[256,1024]{1,0:T(8,128)(2,1)S(1)}, bf16[256,1024]{1,0:T(8,128)(2,1)S(1)}, u32[]{:S(2)}, u32[]{:S(2)}) collective-permute-start(bf16[256,1024]{1,0:T(8,128)(2,1)S(1)} %collective-permute-done.1.t1), channel_id=1, source_target_pairs={{0,32},{32,64},{64,96},{96,128},{128,160},{160,192},{192,224},{224... | collective-permute-start | bytes 1572872 | tf_op jit(solution)/shard_map/ppermute | solution.py:241
  26.4 10.5 %copy-start.2 = (bf16[256,1024]{1,0:T(8,128)(2,1)}, bf16[256,1024]{1,0:T(8,128)(2,1)S(1)}, u32[]{:S(2)}) copy-start(bf16[256,1024]{1,0:T(8,128)(2,1)S(1)} %collective-permute-done.2.t2) | copy-start | bytes 1572868
  26.4 10.5 %collective-permute-start.4 = (bf16[256,1024]{1,0:T(8,128)(2,1)S(1)}, bf16[256,1024]{1,0:T(8,128)(2,1)S(1)}, u32[]{:S(2)}, u32[]{:S(2)}) collective-permute-start(bf16[256,1024]{1,0:T(8,128)(2,1)S(1)} %collective-permute-done.2.t2), channel_id=1, source_target_pairs={{0,32},{32,64},{64,96},{96,128},{128,160},{160,192},{192,224},{224... | collective-permute-start | bytes 1572872 | tf_op jit(solution)/shard_map/ppermute | solution.py:241
  26.4 10.5 %collective-permute-start.5 = (bf16[256,512]{1,0:T(8,128)(2,1)S(1)}, bf16[256,512]{1,0:T(8,128)(2,1)S(1)}, u32[]{:S(2)}, u32[]{:S(2)}) collective-permute-start(bf16[256,512]{1,0:T(8,128)(2,1)S(1)} %slice.9), channel_id=1, source_target_pairs={{0,16},{16,0},{1,17},{17,1},{2,18},{18,2},{3,19},{19,3},{4,20},{20... | collective-permute-start | bytes 786440 | tf_op jit(solution)/shard_map/ppermute | solution.py:72
  27.9 10.6 %collective-permute-start.7 = (bf16[896,512]{1,0:T(8,128)(2,1)S(1)}, bf16[896,512]{1,0:T(8,128)(2,1)}, u32[]{:S(2)}, u32[]{:S(2)}) collective-permute-start(bf16[896,512]{1,0:T(8,128)(2,1)S(1)} %fusion.w_own_ref), channel_id=1, source_target_pairs={{0,1},{1,0},{2,3},{3,2},{4,5},{5,4},{6,7},{7,6},{8,9},{9,8},{10,11... | collective-permute-start | bytes 2752520 | tf_op jit(solution)/shard_map/ppermute | solution.py:72
  36.9 18.9 %collective-permute-start.14 = (bf16[896,512]{1,0:T(8,128)(2,1)S(1)}, bf16[896,512]{1,0:T(8,128)(2,1)}, u32[]{:S(2)}, u32[]{:S(2)}) collective-permute-start(bf16[896,512]{1,0:T(8,128)(2,1)S(1)} %constant_dynamic-update-slice_fusion.w_own_ref), channel_id=1, source_target_pairs={{0,1},{1,0},{2,3},{3,2},{4,5},{5,4},{6,7},{7,6},{8,9},{9,8},{10,11... | collective-permute-start | bytes 2752520 | tf_op jit(solution)/shard_map/ppermute | solution.py:72
  37.9 7.9 %collective-permute-start.6 = (bf16[128,1024]{1,0:T(8,128)(2,1)}, bf16[128,1024]{1,0:T(8,128)(2,1)}, u32[]{:S(2)}, u32[]{:S(2)}) collective-permute-start(bf16[128,1024]{1,0:T(8,128)(2,1)} %constant_dynamic-slice_fusion), channel_id=1, source_target_pairs={{0,32},{32,64},{64,96},{96,128},{128,160},{160,192},{192,224},{224... | collective-permute-start | bytes 786440 | tf_op jit(solution)/shard_map/ppermute | solution.py:243
  45.8 1.0 copy-start.3
  50.5 21.2 %collective-permute-start.10 = (bf16[2,128,896]{2,1,0:T(8,128)(2,1)S(1)}, bf16[2,128,896]{2,1,0:T(8,128)(2,1)S(1)}, u32[]{:S(2)}, u32[]{:S(2)}) collective-permute-start(bf16[2,128,896]{2,1,0:T(8,128)(2,1)S(1)} %get-tuple-element.27), channel_id=1, source_target_pairs={{0,6},{2,0},{4,2},{6,4},{1,7},{3,1},{5,3},{7,5},{8,14},{10,8},{12,... | collective-permute-start | bytes 1376264 | tf_op jit(solution)/shard_map/ppermute | solution.py:72
  53.6 21.5 %collective-permute-start.8 = (bf16[2,128,896]{2,1,0:T(8,128)(2,1)S(1)}, bf16[2,128,896]{2,1,0:T(8,128)(2,1)S(1)}, u32[]{:S(2)}, u32[]{:S(2)}) collective-permute-start(bf16[2,128,896]{2,1,0:T(8,128)(2,1)S(1)} %get-tuple-element.25), channel_id=1, source_target_pairs={{0,2},{2,4},{4,6},{6,0},{1,3},{3,5},{5,7},{7,1},{8,10},{10,12},{12... | collective-permute-start | bytes 1376264 | tf_op jit(solution)/shard_map/ppermute | solution.py:72
  53.6 21.5 %collective-permute-start.9 = (bf16[2,128,896]{2,1,0:T(8,128)(2,1)S(1)}, bf16[2,128,896]{2,1,0:T(8,128)(2,1)S(1)}, u32[]{:S(2)}, u32[]{:S(2)}) collective-permute-start(bf16[2,128,896]{2,1,0:T(8,128)(2,1)S(1)} %get-tuple-element.26), channel_id=1, source_target_pairs={{0,4},{2,6},{4,0},{6,2},{1,5},{3,7},{5,1},{7,3},{8,12},{10,14},{12... | collective-permute-start | bytes 1376264 | tf_op jit(solution)/shard_map/ppermute | solution.py:72
  59.4 16.9 %collective-permute-start.15 = (bf16[2,128,896]{2,1,0:T(8,128)(2,1)S(1)}, bf16[2,128,896]{2,1,0:T(8,128)(2,1)S(1)}, u32[]{:S(2)}, u32[]{:S(2)}) collective-permute-start(bf16[2,128,896]{2,1,0:T(8,128)(2,1)S(1)} %get-tuple-element.34), channel_id=1, source_target_pairs={{0,8},{8,0},{1,9},{9,1},{2,10},{10,2},{3,11},{11,3},{4,12},{12,4},... | collective-permute-start | bytes 1376264 | tf_op jit(solution)/shard_map/ppermute | solution.py:72
  60.3 21.4 %collective-permute-start.16 = (bf16[2,128,896]{2,1,0:T(8,128)(2,1)S(1)}, bf16[2,128,896]{2,1,0:T(8,128)(2,1)S(1)}, u32[]{:S(2)}, u32[]{:S(2)}) collective-permute-start(bf16[2,128,896]{2,1,0:T(8,128)(2,1)S(1)} %get-tuple-element.35), channel_id=1, source_target_pairs={{0,8},{8,0},{1,9},{9,1},{2,10},{10,2},{3,11},{11,3},{4,12},{12,4},... | collective-permute-start | bytes 1376264 | tf_op jit(solution)/shard_map/ppermute | solution.py:72
  75.4 11.3 %collective-permute-start.11 = (bf16[128,896]{1,0:T(8,128)(2,1)S(1)}, bf16[128,896]{1,0:T(8,128)(2,1)S(1)}, u32[]{:S(2)}, u32[]{:S(2)}) collective-permute-start(bf16[128,896]{1,0:T(8,128)(2,1)S(1)} %get-tuple-element.29), channel_id=1, source_target_pairs={{0,8},{8,0},{1,9},{9,1},{2,10},{10,2},{3,11},{11,3},{4,12},{12,4},... | collective-permute-start | bytes 688136 | tf_op jit(solution)/shard_map/ppermute | solution.py:72
  81.6 32.6 %copy-start = (bf16[256,896]{1,0:T(8,128)(2,1)S(1)}, bf16[256,896]{1,0:T(8,128)(2,1)}, u32[]{:S(2)}) copy-start(bf16[256,896]{1,0:T(8,128)(2,1)} %gate_ref.1) | copy-start | bytes 1376260
  81.6 32.6 %copy-start.1 = (bf16[256,896]{1,0:T(8,128)(2,1)S(1)}, bf16[256,896]{1,0:T(8,128)(2,1)}, u32[]{:S(2)}) copy-start(bf16[256,896]{1,0:T(8,128)(2,1)} %up_ref.1) | copy-start | bytes 1376260
  81.9 9.8 %collective-permute-start.17 = (bf16[128,896]{1,0:T(8,128)(2,1)S(1)}, bf16[128,896]{1,0:T(8,128)(2,1)S(1)}, u32[]{:S(2)}, u32[]{:S(2)}) collective-permute-start(bf16[128,896]{1,0:T(8,128)(2,1)S(1)} %get-tuple-element.37), channel_id=1, source_target_pairs={{0,2},{2,4},{4,6},{6,0},{1,3},{3,5},{5,7},{7,1},{8,10},{10,12},{12... | collective-permute-start | bytes 688136 | tf_op jit(solution)/shard_map/ppermute | solution.py:72
  83.8 7.8 %collective-permute-start.18 = (bf16[128,896]{1,0:T(8,128)(2,1)S(1)}, bf16[128,896]{1,0:T(8,128)(2,1)S(1)}, u32[]{:S(2)}, u32[]{:S(2)}) collective-permute-start(bf16[128,896]{1,0:T(8,128)(2,1)S(1)} %get-tuple-element.38), channel_id=1, source_target_pairs={{0,4},{2,6},{4,0},{6,2},{1,5},{3,7},{5,1},{7,3},{8,12},{10,14},{12... | collective-permute-start | bytes 688136 | tf_op jit(solution)/shard_map/ppermute | solution.py:72
  84.7 11.7 %collective-permute-start.19 = (bf16[128,896]{1,0:T(8,128)(2,1)S(1)}, bf16[128,896]{1,0:T(8,128)(2,1)S(1)}, u32[]{:S(2)}, u32[]{:S(2)}) collective-permute-start(bf16[128,896]{1,0:T(8,128)(2,1)S(1)} %get-tuple-element.39), channel_id=1, source_target_pairs={{0,6},{2,0},{4,2},{6,4},{1,7},{3,1},{5,3},{7,5},{8,14},{10,8},{12,... | collective-permute-start | bytes 688136 | tf_op jit(solution)/shard_map/ppermute | solution.py:72
  86.7 18.7 %collective-permute-start.12 = (bf16[128,896]{1,0:T(8,128)(2,1)S(1)}, bf16[128,896]{1,0:T(8,128)(2,1)S(1)}, u32[]{:S(2)}, u32[]{:S(2)}) collective-permute-start(bf16[128,896]{1,0:T(8,128)(2,1)S(1)} %shard_map.79), channel_id=1, source_target_pairs={{2,160},{3,64},{6,224},{10,0},{11,32},{12,192},{13,96},{14,128},{1... | collective-permute-start | bytes 688136 | tf_op jit(solution)/shard_map/ppermute | solution.py:257
  87.3 18.1 %collective-permute-start.13 = (bf16[128,896]{1,0:T(8,128)(2,1)S(1)}, bf16[128,896]{1,0:T(8,128)(2,1)S(1)}, u32[]{:S(2)}, u32[]{:S(2)}) collective-permute-start(bf16[128,896]{1,0:T(8,128)(2,1)S(1)} %shard_map.79), channel_id=1, source_target_pairs={{0,224},{1,128},{4,160},{5,32},{7,64},{8,192},{9,96},{15,0},{16,24... | collective-permute-start | bytes 688136 | tf_op jit(solution)/shard_map/ppermute | solution.py:257
  96.5 17.8 %collective-permute-start.20 = (bf16[128,896]{1,0:T(8,128)(2,1)S(1)}, bf16[128,896]{1,0:T(8,128)(2,1)S(1)}, u32[]{:S(2)}, u32[]{:S(2)}) collective-permute-start(bf16[128,896]{1,0:T(8,128)(2,1)S(1)} %shard_map.82), channel_id=1, source_target_pairs={{2,161},{3,65},{6,225},{10,1},{11,33},{12,193},{13,97},{14,129},{1... | collective-permute-start | bytes 688136 | tf_op jit(solution)/shard_map/ppermute | solution.py:257
  97.8 16.5 %collective-permute-start.21 = (bf16[128,896]{1,0:T(8,128)(2,1)S(1)}, bf16[128,896]{1,0:T(8,128)(2,1)S(1)}, u32[]{:S(2)}, u32[]{:S(2)}) collective-permute-start(bf16[128,896]{1,0:T(8,128)(2,1)S(1)} %shard_map.82), channel_id=1, source_target_pairs={{0,225},{1,129},{4,161},{5,33},{7,65},{8,193},{9,97},{15,1},{16,24... | collective-permute-start | bytes 688136 | tf_op jit(solution)/shard_map/ppermute | solution.py:257

commit v7 on v6

--- a/solution.py
+++ b/solution.py
@@ -63,7 +63,7 @@
                     for c in range(C):
                         place = [0] * S
                         for s in range(S):
-                            place[number_of(z, s, c)] = 2 * ((s % Y - y) % Y) + ((s // Y) ^ xl)
+                            place[number_of(z, s, c)] = ((s // Y) ^ xl) * Y + (s % Y - y) % Y
                         rows.append(place + [c, c ^ xh])
     return np.array(rows, np.int32)
 
@@ -93,51 +93,73 @@
     return pltpu.CompilerParams(vmem_limit_bytes=mib * 2**20)
 
 
-def product_y(own, tokens, far, w_own, w_other):
+def product_send(own, tokens, far, w_own, w_other):
     rows, depth = far.shape
     width = w_own.shape[0]
 
-    def kernel(facts_ref, t0, t1, t2, t3, far_ref, w_own_ref, w_other_ref, lhs_ref, *out_refs):
+    def kernel(facts_ref, t0, t1, t2, t3, far_ref, w_own_ref, w_other_ref, lhs_ref, *send_refs):
         lhs_ref[facts_ref[0]] = t0[pl.ds(pl.multiple_of(facts_ref[S] * rows, rows), rows), :]
         for i, ref in enumerate((t1, t2, t3)):
             for h in range(2):
                 lhs_ref[facts_ref[1 + 2 * i + h]] = ref[h * rows : (h + 1) * rows, :]
         lhs_ref[facts_ref[7]] = far_ref[...]
-        for d in range(Y):
-            pair = lhs_ref[2 * d : 2 * d + 2].reshape(2 * rows, depth)
-            total = times(pair, w_own_ref[...], w_other_ref[...])
-            out_refs[d][0] = total[:rows]
-            out_refs[d][1] = total[rows:]
+        for i in range(2):
+            total = times(lhs_ref[Y + 2 * i : Y + 2 * i + 2].reshape(2 * rows, depth), w_own_ref[...], w_other_ref[...])
+            send_refs[i][0] = total[:rows]
+            send_refs[i][1] = total[rows:]
 
     return pl.pallas_call(
         kernel,
         in_specs=[SMEM] + [VMEM] * 7,
-        out_specs=[VMEM] * (1 + Y),
+        out_specs=[VMEM] * 3,
         out_shape=[jax.ShapeDtypeStruct((S, rows, depth), BF16)]
-        + [jax.ShapeDtypeStruct((2, rows, width), BF16)] * Y,
+        + [jax.ShapeDtypeStruct((2, rows, width), BF16)] * 2,
         compiler_params=params(32),
-        cost_estimate=pl.CostEstimate(flops=2 * S * rows * depth * width, bytes_accessed=8 * 2**20, transcendentals=0),
+        cost_estimate=pl.CostEstimate(flops=S * rows * depth * width, bytes_accessed=7 * 2**20, transcendentals=0),
     )(own, *tokens, far, w_own, w_other)
 
 
-def product_xl(lhs, w_own, w_other):
+def product_y(lhs, w_own, w_other):
     _, rows, depth = lhs.shape
     width = w_own.shape[0]
 
-    def kernel(lhs_ref, w_own_ref, w_other_ref, keep_ref, *send_refs):
-        for d in range(Y):
-            pair = lhs_ref[2 * d : 2 * d + 2].reshape(2 * rows, depth)
-            total = times(pair, w_own_ref[...], w_other_ref[...])
-            keep_ref[d] = total[:rows]
-            send_refs[d // 2][d % 2] = total[rows:]
+    def kernel(lhs_ref, w_own_ref, w_other_ref, *out_refs):
+        for e in range(2):
+            total = times(lhs_ref[Y * e : Y * e + Y].reshape(Y * rows, depth), w_own_ref[...], w_other_ref[...])
+            for d in range(Y):
+                out_refs[d][e] = total[d * rows : (d + 1) * rows]
 
     return pl.pallas_call(
         kernel,
         in_specs=[VMEM] * 3,
-        out_specs=[VMEM] * 3,
-        out_shape=[jax.ShapeDtypeStruct((n, rows, width), BF16) for n in (Y, Y // 2, Y // 2)],
+        out_specs=[VMEM] * Y,
+        out_shape=[jax.ShapeDtypeStruct((2, rows, width), BF16)] * Y,
         compiler_params=params(32),
         cost_estimate=pl.CostEstimate(flops=2 * S * rows * depth * width, bytes_accessed=6 * 2**20, transcendentals=0),
+    )(lhs, w_own, w_other)
+
+
+def product_keep(lhs, w_own, w_other):
+    _, rows, depth = lhs.shape
+    width = w_own.shape[0]
+
+    def kernel(lhs_ref, w_own_ref, w_other_ref, keep_ref):
+        total = times(lhs_ref[...].reshape(Y * rows, depth), w_own_ref[...], w_other_ref[...])
+        for d in range(Y):
+            keep_ref[d] = total[d * rows : (d + 1) * rows]
+
+    return pl.pallas_call(
+        kernel,
+        grid=(1,),
+        in_specs=[
+            pl.BlockSpec((Y, rows, depth), lambda i: (0, 0, 0)),
+            pl.BlockSpec(w_own.shape, lambda i: (0, 0)),
+            pl.BlockSpec(w_own.shape, lambda i: (0, 0)),
+        ],
+        out_specs=pl.BlockSpec((Y, rows, width), lambda i: (0, 0, 0)),
+        out_shape=jax.ShapeDtypeStruct((Y, rows, width), BF16),
+        compiler_params=params(32),
+        cost_estimate=pl.CostEstimate(flops=S * rows * depth * width, bytes_accessed=4 * 2**20, transcendentals=0),
     )(lhs, w_own, w_other)
 
 
@@ -245,9 +267,10 @@
     cross_own = jnp.concatenate(cross_parts, 0)
     cross_other = shift(cross_own, "c", C, 1)
 
-    lhs, *near = product_y(own, tokens, far, near_own, near_other)
+    lhs, *sent = product_send(own, tokens, far, cross_own, cross_other)
+    near = product_y(lhs, near_own, near_other)
     near_y = [near[0]] + [shift(near[d], "y", Y, d) for d in range(1, Y)]
-    kept, *sent = product_xl(lhs, cross_own, cross_other)
+    kept = product_keep(lhs, cross_own, cross_other)
     cross = add_xl(kept, [shift(part, "xl", XL, 1) for part in sent])
     cross_parts = [cross[0]] + [shift(cross[d], "y", Y, d) for d in range(1, Y)]
     kept, sent = add_y(near_y)

time: 116 us -> 120 us (1.034)
  the two profiles are of different devices: /device:TPU:6 before, /device:TPU:7 now
where the time goes in v7:
time: 120 us; the launch traced here: 118 us
  waiting for transfers between devices  57.6 us (48%)
  starting transfers between devices  42 us (35%)
  Pallas kernels  9.26 us (8%)
  local copies, waits for them, and re-layouts  8.05 us (7%)
    ppermute x14, waiting for transfers between devices, shift(): return lax.ppermute(x, axis, [(i, (i + by) % size) for i in range(size)])  34 us
    ppermute x14, starting transfers between devices, shift(): return lax.ppermute(x, axis, [(i, (i + by) % size) for i in range(size)])  16 us
    ppermute x4, waiting for transfers between devices, on_device(): lax.ppermute(sums[r], ALL, home_pairs(r, h))  13.8 us
    ppermute x4, starting transfers between devices, on_device(): lax.ppermute(sums[r], ALL, home_pairs(r, h))  13 us
    ppermute x3, starting transfers between devices, on_device(): tokens.append(lax.ppermute(tokens[-1], ('z', 'c'), around))  12.2 us
    ppermute x3, waiting for transfers between devices, on_device(): tokens.append(lax.ppermute(tokens[-1], ('z', 'c'), around))  5.56 us
    unnamed x21, local copies, waits for them, and re-layouts  4.53 us
    ppermute x1, waiting for transfers between devices, on_device(): lax.ppermute(lax.dynamic_slice_in_dim(tokens[3], c * rows, rows, 0), ('z'...  4.18 us
  transfers between devices with their start and end apart: 22, of which 12 were waited for; matrix products, arithmetic and copies ran while one was open for 3% of the time, Pallas kernels for 6%

profile of v7, /device:TPU:7, one launch (start us, length us, event | category | flops | bytes accessed | tf_op | source)
XLA Modules:
  0.0 118.1 jit_solution(4112936349769140795)
XLA Ops:
  0.6 0.8 collective-permute-start
  1.4 0.8 copy.8
  2.2 0.3 mul.30
  2.5 0.4 fusion.w_own_ref
  2.9 0.6 copy-done.9
  3.5 5.7 %collective-permute-start.1 = (bf16[256,1024]{1,0:T(8,128)(2,1)S(1)}, bf16[256,1024]{1,0:T(8,128)(2,1)S(1)}, u32[]{:S(2)}, u32[]{:S(2)}) collective-permute-start(bf16[256,1024]{1,0:T(8,128)(2,1)S(1)} %pad_maximum_fusion.t0), channel_id=1, source_target_pairs={{0,32},{32,64},{64,96},{96,128},{128,160},{160,192},{192,224},{224... | collective-permute-start | bytes 1572872 | tf_op jit(solution)/shard_map/ppermute | solution.py:263
  9.2 1.2 %collective-permute-start.3 = (bf16[640,512]{1,0:T(8,128)(2,1)S(1)}, bf16[640,512]{1,0:T(8,128)(2,1)S(1)}, u32[]{:S(2)}, u32[]{:S(2)}) collective-permute-start(bf16[640,512]{1,0:T(8,128)(2,1)S(1)} %slice.8), channel_id=1, source_target_pairs={{0,16},{16,0},{1,17},{17,1},{2,18},{18,2},{3,19},{19,3},{4,20},{20... | collective-permute-start | bytes 1966088 | tf_op jit(solution)/shard_map/ppermute | solution.py:72
  10.4 4.9 %collective-permute-done.1.t1 = bf16[256,1024]{1,0:T(8,128)(2,1)S(1)} collective-permute-done((bf16[256,1024]{1,0:T(8,128)(2,1)S(1)}, bf16[256,1024]{1,0:T(8,128)(2,1)S(1)}, u32[]{:S(2)}, u32[]{:S(2)}) %collective-permute-start.1) | collective-permute-done | bytes 524320 | tf_op jit(solution)/shard_map/ppermute | solution.py:263
  15.3 3.4 %collective-permute-start.2 = (bf16[256,1024]{1,0:T(8,128)(2,1)S(1)}, bf16[256,1024]{1,0:T(8,128)(2,1)S(1)}, u32[]{:S(2)}, u32[]{:S(2)}) collective-permute-start(bf16[256,1024]{1,0:T(8,128)(2,1)S(1)} %collective-permute-done.1.t1), channel_id=1, source_target_pairs={{0,32},{32,64},{64,96},{96,128},{128,160},{160,192},{192,224},{224... | collective-permute-start | bytes 1572872 | tf_op jit(solution)/shard_map/ppermute | solution.py:263
  18.7 5.4 %collective-permute-done.3 = bf16[640,512]{1,0:T(8,128)(2,1)S(1)} collective-permute-done((bf16[640,512]{1,0:T(8,128)(2,1)S(1)}, bf16[640,512]{1,0:T(8,128)(2,1)S(1)}, u32[]{:S(2)}, u32[]{:S(2)}) %collective-permute-start.3) | collective-permute-done | bytes 655392 | tf_op jit(solution)/shard_map/ppermute | solution.py:72
  24.1 0.7 collective-permute-done.2.t2
  24.8 3.1 %collective-permute-start.4 = (bf16[256,1024]{1,0:T(8,128)(2,1)S(1)}, bf16[256,1024]{1,0:T(8,128)(2,1)S(1)}, u32[]{:S(2)}, u32[]{:S(2)}) collective-permute-start(bf16[256,1024]{1,0:T(8,128)(2,1)S(1)} %collective-permute-done.2.t2), channel_id=1, source_target_pairs={{0,32},{32,64},{64,96},{96,128},{128,160},{160,192},{192,224},{224... | collective-permute-start | bytes 1572872 | tf_op jit(solution)/shard_map/ppermute | solution.py:263
  28.0 1.2 %collective-permute-start.5 = (bf16[256,512]{1,0:T(8,128)(2,1)S(1)}, bf16[256,512]{1,0:T(8,128)(2,1)S(1)}, u32[]{:S(2)}, u32[]{:S(2)}) collective-permute-start(bf16[256,512]{1,0:T(8,128)(2,1)S(1)} %slice.9), channel_id=1, source_target_pairs={{0,16},{16,0},{1,17},{17,1},{2,18},{18,2},{3,19},{19,3},{4,20},{20... | collective-permute-start | bytes 786440 | tf_op jit(solution)/shard_map/ppermute | solution.py:72
  29.2 8.0 %collective-permute-done.5 = bf16[256,512]{1,0:T(8,128)(2,1)S(1)} collective-permute-done((bf16[256,512]{1,0:T(8,128)(2,1)S(1)}, bf16[256,512]{1,0:T(8,128)(2,1)S(1)}, u32[]{:S(2)}, u32[]{:S(2)}) %collective-permute-start.5) | collective-permute-done | bytes 262176 | tf_op jit(solution)/shard_map/ppermute | solution.py:72
  37.2 0.8 copy-done
  38.0 0.4 collective-permute-start.7
  38.5 1.7 %constant_dynamic-slice_fusion = bf16[128,1024]{1,0:T(8,128)(2,1)} fusion(bf16[256,1024]{1,0:T(8,128)(2,1)} %copy-done, s32[]{:T(128)S(6)} %select_n.8), kind=kLoop, calls=%fused_computation.6 | loop fusion | bytes 524292 | tf_op jit(solution)/shard_map/dynamic_slice | solution.py:265
  40.2 0.9 collective-permute-start.6
  41.0 0.7 dynamic-slice_bitcast_fusion.facts_ref
  41.7 4.2 %collective-permute-done.6.far_ref = bf16[128,1024]{1,0:T(8,128)(2,1)S(1)} collective-permute-done((bf16[128,1024]{1,0:T(8,128)(2,1)}, bf16[128,1024]{1,0:T(8,128)(2,1)S(1)}, u32[]{:S(2)}, u32[]{:S(2)}) %collective-permute-start.6) | collective-permute-done | bytes 262176 | tf_op jit(solution)/shard_map/ppermute | solution.py:265
  45.9 1.0 copy-done.1
  47.0 1.0 copy-done.3
  48.0 1.0 copy-done.5
  49.0 1.9 %shard_map.77 = (bf16[8,128,1024]{2,1,0:T(8,128)(2,1)S(1)}, bf16[2,128,896]{2,1,0:T(8,128)(2,1)S(1)}, bf16[2,128,896]{2,1,0:T(8,128)(2,1)S(1)}) custom-call(s32[10]{0:T(128)S(1)} %dynamic-slice_bitcast_fusion.facts_ref, bf16[256,1024]{1,0:T(8,128)(2,1)S(1)} %pad_maximum_fusion.t0, bf16[256,1024]{1,0:T(8,128)(2,1)S(1)} %copy-done.3, ...), custom_call_target="tpu_custom_call" | custom-call | flops 939524096 | bytes 7340032 | tf_op jit(solution)/shard_map/pallas_call | solution.py:111
  51.0 0.6 collective-permute-start.15
  51.6 0.9 collective-permute-start.16
  52.5 3.6 %shard_map.78 = (bf16[2,128,896]{2,1,0:T(8,128)(2,1)S(1)}, bf16[2,128,896]{2,1,0:T(8,128)(2,1)S(1)}, bf16[2,128,896]{2,1,0:T(8,128)(2,1)S(1)}, bf16[2,128,896]{2,1,0:T(8,128)(2,1)S(1)}) custom-call(bf16[8,128,1024]{2,1,0:T(8,128)(2,1)S(1)} %get-tuple-element.25.lhs_ref, bf16[896,512]{1,0:T(8,128)(2,1)S(1)} %fusion.w_own_ref, ...), custom_call_target="tpu_custom_call" | custom-call | flops 1879048192 | bytes 6291456 | tf_op jit(solution)/shard_map/pallas_call | solution.py:132
  56.1 1.4 %collective-permute-start.9 = (bf16[2,128,896]{2,1,0:T(8,128)(2,1)S(1)}, bf16[2,128,896]{2,1,0:T(8,128)(2,1)S(1)}, u32[]{:S(2)}, u32[]{:S(2)}) collective-permute-start(bf16[2,128,896]{2,1,0:T(8,128)(2,1)S(1)} %get-tuple-element.27), channel_id=1, source_target_pairs={{0,2},{2,4},{4,6},{6,0},{1,3},{3,5},{5,7},{7,1},{8,10},{10,12},{12... | collective-permute-start | bytes 1376264 | tf_op jit(solution)/shard_map/ppermute | solution.py:72
  57.5 2.6 %collective-permute-start.10 = (bf16[2,128,896]{2,1,0:T(8,128)(2,1)S(1)}, bf16[2,128,896]{2,1,0:T(8,128)(2,1)S(1)}, u32[]{:S(2)}, u32[]{:S(2)}) collective-permute-start(bf16[2,128,896]{2,1,0:T(8,128)(2,1)S(1)} %get-tuple-element.28), channel_id=1, source_target_pairs={{0,4},{2,6},{4,0},{6,2},{1,5},{3,7},{5,1},{7,3},{8,12},{10,14},{12... | collective-permute-start | bytes 1376264 | tf_op jit(solution)/shard_map/ppermute | solution.py:72
  60.1 1.1 collective-permute-start.11
  61.1 1.3 %shard_map.81.kept_ref = bf16[4,128,896]{2,1,0:T(8,128)(2,1)S(1)} custom-call(bf16[8,128,1024]{2,1,0:T(8,128)(2,1)S(1)} %get-tuple-element.25.lhs_ref, bf16[896,512]{1,0:T(8,128)(2,1)S(1)} %constant_dynamic-update-slice_fusion.w_own_ref, bf16[896,512]{1,0:T(8,128)(2,1)S(1)} %collective-permute-done.7.w_other_ref), custom_call_target="tpu_custom_call" | custom-call | flops 939524096 | bytes 4194304 | tf_op jit(solution)/shard_map/pallas_call | solution.py:151
  62.4 8.0 %collective-permute-done.16.high_ref = bf16[2,128,896]{2,1,0:T(8,128)(2,1)S(1)} collective-permute-done((bf16[2,128,896]{2,1,0:T(8,128)(2,1)S(1)}, bf16[2,128,896]{2,1,0:T(8,128)(2,1)S(1)}, u32[]{:S(2)}, u32[]{:S(2)}) %collective-permute-start.16) | collective-permute-done | bytes 458784 | tf_op jit(solution)/shard_map/ppermute | solution.py:72
  70.5 0.2 shard_map.82
  70.7 1.4 %collective-permute-start.17 = (bf16[128,896]{1,0:T(8,128)(2,1)S(1)}, bf16[128,896]{1,0:T(8,128)(2,1)S(1)}, u32[]{:S(2)}, u32[]{:S(2)}) collective-permute-start(bf16[128,896]{1,0:T(8,128)(2,1)S(1)} %get-tuple-element.35), channel_id=1, source_target_pairs={{0,2},{2,4},{4,6},{6,0},{1,3},{3,5},{5,7},{7,1},{8,10},{10,12},{12... | collective-permute-start | bytes 688136 | tf_op jit(solution)/shard_map/ppermute | solution.py:72
  72.1 2.6 %collective-permute-start.18 = (bf16[128,896]{1,0:T(8,128)(2,1)S(1)}, bf16[128,896]{1,0:T(8,128)(2,1)S(1)}, u32[]{:S(2)}, u32[]{:S(2)}) collective-permute-start(bf16[128,896]{1,0:T(8,128)(2,1)S(1)} %get-tuple-element.36), channel_id=1, source_target_pairs={{0,4},{2,6},{4,0},{6,2},{1,5},{3,7},{5,1},{7,3},{8,12},{10,14},{12... | collective-permute-start | bytes 688136 | tf_op jit(solution)/shard_map/ppermute | solution.py:72
  74.7 1.1 collective-permute-start.19
  75.7 1.7 %collective-permute-done.10.refs_2_ = bf16[2,128,896]{2,1,0:T(8,128)(2,1)S(1)} collective-permute-done((bf16[2,128,896]{2,1,0:T(8,128)(2,1)S(1)}, bf16[2,128,896]{2,1,0:T(8,128)(2,1)S(1)}, u32[]{:S(2)}, u32[]{:S(2)}) %collective-permute-start.10) | collective-permute-done | bytes 458784 | tf_op jit(solution)/shard_map/ppermute | solution.py:72
  77.5 4.2 %collective-permute-done.11.refs_3_ = bf16[2,128,896]{2,1,0:T(8,128)(2,1)S(1)} collective-permute-done((bf16[2,128,896]{2,1,0:T(8,128)(2,1)S(1)}, bf16[2,128,896]{2,1,0:T(8,128)(2,1)S(1)}, u32[]{:S(2)}, u32[]{:S(2)}) %collective-permute-start.11) | collective-permute-done | bytes 458784 | tf_op jit(solution)/shard_map/ppermute | solution.py:72
  81.7 0.2 shard_map.79
  81.9 0.6 collective-permute-start.12
  82.6 5.2 %collective-permute-done.17.refs_1_ = bf16[128,896]{1,0:T(8,128)(2,1)S(1)} collective-permute-done((bf16[128,896]{1,0:T(8,128)(2,1)S(1)}, bf16[128,896]{1,0:T(8,128)(2,1)S(1)}, u32[]{:S(2)}, u32[]{:S(2)}) %collective-permute-start.17) | collective-permute-done | bytes 229408 | tf_op jit(solution)/shard_map/ppermute | solution.py:72
  87.7 1.5 %collective-permute-done.19.refs_3_ = bf16[128,896]{1,0:T(8,128)(2,1)S(1)} collective-permute-done((bf16[128,896]{1,0:T(8,128)(2,1)S(1)}, bf16[128,896]{1,0:T(8,128)(2,1)S(1)}, u32[]{:S(2)}, u32[]{:S(2)}) %collective-permute-start.19) | collective-permute-done | bytes 229408 | tf_op jit(solution)/shard_map/ppermute | solution.py:72
  89.3 7.3 %collective-permute-start.21 = (bf16[128,896]{1,0:T(8,128)(2,1)S(1)}, bf16[128,896]{1,0:T(8,128)(2,1)S(1)}, u32[]{:S(2)}, u32[]{:S(2)}) collective-permute-start(bf16[128,896]{1,0:T(8,128)(2,1)S(1)} %shard_map.83), channel_id=1, source_target_pairs={{0,225},{1,129},{4,161},{5,33},{7,65},{8,193},{9,97},{15,1},{16,24... | collective-permute-start | bytes 688136 | tf_op jit(solution)/shard_map/ppermute | solution.py:280
  96.6 0.7 collective-permute-start.20
  97.4 3.7 %collective-permute-start.14 = (bf16[128,896]{1,0:T(8,128)(2,1)S(1)}, bf16[128,896]{1,0:T(8,128)(2,1)S(1)}, u32[]{:S(2)}, u32[]{:S(2)}) collective-permute-start(bf16[128,896]{1,0:T(8,128)(2,1)S(1)} %shard_map.80), channel_id=1, source_target_pairs={{0,224},{1,128},{4,160},{5,32},{7,64},{8,192},{9,96},{15,0},{16,24... | collective-permute-start | bytes 688136 | tf_op jit(solution)/shard_map/ppermute | solution.py:280
  101.1 1.3 %collective-permute-start.13 = (bf16[128,896]{1,0:T(8,128)(2,1)S(1)}, bf16[128,896]{1,0:T(8,128)(2,1)S(1)}, u32[]{:S(2)}, u32[]{:S(2)}) collective-permute-start(bf16[128,896]{1,0:T(8,128)(2,1)S(1)} %shard_map.80), channel_id=1, source_target_pairs={{2,160},{3,64},{6,224},{10,0},{11,32},{12,192},{13,96},{14,128},{1... | collective-permute-start | bytes 688136 | tf_op jit(solution)/shard_map/ppermute | solution.py:280
  102.4 13.7 %collective-permute-done.14.near1 = bf16[128,896]{1,0:T(8,128)(2,1)S(1)} collective-permute-done((bf16[128,896]{1,0:T(8,128)(2,1)S(1)}, bf16[128,896]{1,0:T(8,128)(2,1)S(1)}, u32[]{:S(2)}, u32[]{:S(2)}) %collective-permute-start.14) | collective-permute-done | bytes 229408 | tf_op jit(solution)/shard_map/ppermute | solution.py:280
  116.3 1.9 %shard_map.84 = (bf16[256,896]{1,0:T(8,128)(2,1)}, bf16[256,896]{1,0:T(8,128)(2,1)}) custom-call(s32[10]{0:T(128)S(1)} %dynamic-slice_bitcast_fusion.facts_ref, bf16[128,896]{1,0:T(8,128)(2,1)S(1)} %collective-permute-done.13.near0, bf16[128,896]{1,0:T(8,128)(2,1)S(1)} %collective-permute-done.14.near1, bf16[128,896]{1,0:T(8,128)(2,1)S(1)} %collective-permute-done.20.cross0, ...), custom_call_target="tpu_custom_call" | custom-call | flops 2293760 | bytes 2293760 | tf_op jit(solution)/shard_map/pallas_call | solution.py:238
  (34 shorter events, 0.7 us)
Async XLA Ops:
  0.6 1.9 %copy-start.8 = (bf16[896,512]{1,0:T(8,128)(2,1)S(1)}, bf16[896,512]{1,0:T(8,128)(2,1)}, u32[]{:S(2)}) copy-start(bf16[896,512]{1,0:T(8,128)(2,1)} %param.7) | copy-start | bytes 2752516
  0.6 2.2 %collective-permute-start = (bf16[256,512]{1,0:T(8,128)(2,1)}, bf16[256,512]{1,0:T(8,128)(2,1)S(1)}, u32[]{:S(2)}, u32[]{:S(2)}) collective-permute-start(bf16[256,512]{1,0:T(8,128)(2,1)} %param.6), channel_id=1, source_target_pairs={{0,1},{1,0},{2,3},{3,2},{4,5},{5,4},{6,7},{7,6},{8,9},{9,8},{10,11... | collective-permute-start | bytes 786440 | tf_op jit(solution)/shard_map/ppermute | solution.py:72
  2.5 1.0 copy-start.9
  3.5 11.8 %collective-permute-start.1 = (bf16[256,1024]{1,0:T(8,128)(2,1)S(1)}, bf16[256,1024]{1,0:T(8,128)(2,1)S(1)}, u32[]{:S(2)}, u32[]{:S(2)}) collective-permute-start(bf16[256,1024]{1,0:T(8,128)(2,1)S(1)} %pad_maximum_fusion.t0), channel_id=1, source_target_pairs={{0,32},{32,64},{64,96},{96,128},{128,160},{160,192},{192,224},{224... | collective-permute-start | bytes 1572872 | tf_op jit(solution)/shard_map/ppermute | solution.py:263
  9.2 14.9 %collective-permute-start.3 = (bf16[640,512]{1,0:T(8,128)(2,1)S(1)}, bf16[640,512]{1,0:T(8,128)(2,1)S(1)}, u32[]{:S(2)}, u32[]{:S(2)}) collective-permute-start(bf16[640,512]{1,0:T(8,128)(2,1)S(1)} %slice.8), channel_id=1, source_target_pairs={{0,16},{16,0},{1,17},{17,1},{2,18},{18,2},{3,19},{19,3},{4,20},{20... | collective-permute-start | bytes 1966088 | tf_op jit(solution)/shard_map/ppermute | solution.py:72
  15.3 12.7 %copy-start.2 = (bf16[256,1024]{1,0:T(8,128)(2,1)}, bf16[256,1024]{1,0:T(8,128)(2,1)S(1)}, u32[]{:S(2)}) copy-start(bf16[256,1024]{1,0:T(8,128)(2,1)S(1)} %collective-permute-done.1.t1) | copy-start | bytes 1572868
  15.3 9.5 %collective-permute-start.2 = (bf16[256,1024]{1,0:T(8,128)(2,1)S(1)}, bf16[256,1024]{1,0:T(8,128)(2,1)S(1)}, u32[]{:S(2)}, u32[]{:S(2)}) collective-permute-start(bf16[256,1024]{1,0:T(8,128)(2,1)S(1)} %collective-permute-done.1.t1), channel_id=1, source_target_pairs={{0,32},{32,64},{64,96},{96,128},{128,160},{160,192},{192,224},{224... | collective-permute-start | bytes 1572872 | tf_op jit(solution)/shard_map/ppermute | solution.py:263
  24.8 13.5 %copy-start.4 = (bf16[256,1024]{1,0:T(8,128)(2,1)}, bf16[256,1024]{1,0:T(8,128)(2,1)S(1)}, u32[]{:S(2)}) copy-start(bf16[256,1024]{1,0:T(8,128)(2,1)S(1)} %collective-permute-done.2.t2) | copy-start | bytes 1572868
  24.8 12.4 %collective-permute-start.4 = (bf16[256,1024]{1,0:T(8,128)(2,1)S(1)}, bf16[256,1024]{1,0:T(8,128)(2,1)S(1)}, u32[]{:S(2)}, u32[]{:S(2)}) collective-permute-start(bf16[256,1024]{1,0:T(8,128)(2,1)S(1)} %collective-permute-done.2.t2), channel_id=1, source_target_pairs={{0,32},{32,64},{64,96},{96,128},{128,160},{160,192},{192,224},{224... | collective-permute-start | bytes 1572872 | tf_op jit(solution)/shard_map/ppermute | solution.py:263
  28.0 9.2 %collective-permute-start.5 = (bf16[256,512]{1,0:T(8,128)(2,1)S(1)}, bf16[256,512]{1,0:T(8,128)(2,1)S(1)}, u32[]{:S(2)}, u32[]{:S(2)}) collective-permute-start(bf16[256,512]{1,0:T(8,128)(2,1)S(1)} %slice.9), channel_id=1, source_target_pairs={{0,16},{16,0},{1,17},{17,1},{2,18},{18,2},{3,19},{19,3},{4,20},{20... | collective-permute-start | bytes 786440 | tf_op jit(solution)/shard_map/ppermute | solution.py:72
  37.2 0.8 copy-start
  38.0 7.9 %collective-permute-start.7 = (bf16[896,512]{1,0:T(8,128)(2,1)S(1)}, bf16[896,512]{1,0:T(8,128)(2,1)S(1)}, u32[]{:S(2)}, u32[]{:S(2)}) collective-permute-start(bf16[896,512]{1,0:T(8,128)(2,1)S(1)} %constant_dynamic-update-slice_fusion.w_own_ref), channel_id=1, source_target_pairs={{0,1},{1,0},{2,3},{3,2},{4,5},{5,4},{6,7},{7,6},{8,9},{9,8},{10,11... | collective-permute-start | bytes 2752520 | tf_op jit(solution)/shard_map/ppermute | solution.py:72
  38.4 14.2 %collective-permute-start.8 = (bf16[896,512]{1,0:T(8,128)(2,1)S(1)}, bf16[896,512]{1,0:T(8,128)(2,1)}, u32[]{:S(2)}, u32[]{:S(2)}) collective-permute-start(bf16[896,512]{1,0:T(8,128)(2,1)S(1)} %fusion.w_own_ref), channel_id=1, source_target_pairs={{0,1},{1,0},{2,3},{3,2},{4,5},{5,4},{6,7},{7,6},{8,9},{9,8},{10,11... | collective-permute-start | bytes 2752520 | tf_op jit(solution)/shard_map/ppermute | solution.py:72
  40.2 5.7 %collective-permute-start.6 = (bf16[128,1024]{1,0:T(8,128)(2,1)}, bf16[128,1024]{1,0:T(8,128)(2,1)S(1)}, u32[]{:S(2)}, u32[]{:S(2)}) collective-permute-start(bf16[128,1024]{1,0:T(8,128)(2,1)} %constant_dynamic-slice_fusion), channel_id=1, source_target_pairs={{0,32},{32,64},{64,96},{96,128},{128,160},{160,192},{192,224},{224... | collective-permute-start | bytes 786440 | tf_op jit(solution)/shard_map/ppermute | solution.py:265
  45.9 1.0 copy-start.1
  47.0 1.0 copy-start.3
  48.0 1.0 copy-start.5
  51.0 11.5 %collective-permute-start.15 = (bf16[2,128,896]{2,1,0:T(8,128)(2,1)S(1)}, bf16[2,128,896]{2,1,0:T(8,128)(2,1)S(1)}, u32[]{:S(2)}, u32[]{:S(2)}) collective-permute-start(bf16[2,128,896]{2,1,0:T(8,128)(2,1)S(1)} %get-tuple-element.32), channel_id=1, source_target_pairs={{0,8},{8,0},{1,9},{9,1},{2,10},{10,2},{3,11},{11,3},{4,12},{12,4},... | collective-permute-start | bytes 1376264 | tf_op jit(solution)/shard_map/ppermute | solution.py:72
  51.6 18.9 %collective-permute-start.16 = (bf16[2,128,896]{2,1,0:T(8,128)(2,1)S(1)}, bf16[2,128,896]{2,1,0:T(8,128)(2,1)S(1)}, u32[]{:S(2)}, u32[]{:S(2)}) collective-permute-start(bf16[2,128,896]{2,1,0:T(8,128)(2,1)S(1)} %get-tuple-element.33), channel_id=1, source_target_pairs={{0,8},{8,0},{1,9},{9,1},{2,10},{10,2},{3,11},{11,3},{4,12},{12,4},... | collective-permute-start | bytes 1376264 | tf_op jit(solution)/shard_map/ppermute | solution.py:72
  56.1 18.6 %collective-permute-start.9 = (bf16[2,128,896]{2,1,0:T(8,128)(2,1)S(1)}, bf16[2,128,896]{2,1,0:T(8,128)(2,1)S(1)}, u32[]{:S(2)}, u32[]{:S(2)}) collective-permute-start(bf16[2,128,896]{2,1,0:T(8,128)(2,1)S(1)} %get-tuple-element.27), channel_id=1, source_target_pairs={{0,2},{2,4},{4,6},{6,0},{1,3},{3,5},{5,7},{7,1},{8,10},{10,12},{12... | collective-permute-start | bytes 1376264 | tf_op jit(solution)/shard_map/ppermute | solution.py:72
  57.5 20.0 %collective-permute-start.10 = (bf16[2,128,896]{2,1,0:T(8,128)(2,1)S(1)}, bf16[2,128,896]{2,1,0:T(8,128)(2,1)S(1)}, u32[]{:S(2)}, u32[]{:S(2)}) collective-permute-start(bf16[2,128,896]{2,1,0:T(8,128)(2,1)S(1)} %get-tuple-element.28), channel_id=1, source_target_pairs={{0,4},{2,6},{4,0},{6,2},{1,5},{3,7},{5,1},{7,3},{8,12},{10,14},{12... | collective-permute-start | bytes 1376264 | tf_op jit(solution)/shard_map/ppermute | solution.py:72
  60.1 21.6 %collective-permute-start.11 = (bf16[2,128,896]{2,1,0:T(8,128)(2,1)S(1)}, bf16[2,128,896]{2,1,0:T(8,128)(2,1)S(1)}, u32[]{:S(2)}, u32[]{:S(2)}) collective-permute-start(bf16[2,128,896]{2,1,0:T(8,128)(2,1)S(1)} %get-tuple-element.29), channel_id=1, source_target_pairs={{0,6},{2,0},{4,2},{6,4},{1,7},{3,1},{5,3},{7,5},{8,14},{10,8},{12,... | collective-permute-start | bytes 1376264 | tf_op jit(solution)/shard_map/ppermute | solution.py:72
  70.7 17.0 %collective-permute-start.17 = (bf16[128,896]{1,0:T(8,128)(2,1)S(1)}, bf16[128,896]{1,0:T(8,128)(2,1)S(1)}, u32[]{:S(2)}, u32[]{:S(2)}) collective-permute-start(bf16[128,896]{1,0:T(8,128)(2,1)S(1)} %get-tuple-element.35), channel_id=1, source_target_pairs={{0,2},{2,4},{4,6},{6,0},{1,3},{3,5},{5,7},{7,1},{8,10},{10,12},{12... | collective-permute-start | bytes 688136 | tf_op jit(solution)/shard_map/ppermute | solution.py:72
  72.1 15.7 %collective-permute-start.18 = (bf16[128,896]{1,0:T(8,128)(2,1)S(1)}, bf16[128,896]{1,0:T(8,128)(2,1)S(1)}, u32[]{:S(2)}, u32[]{:S(2)}) collective-permute-start(bf16[128,896]{1,0:T(8,128)(2,1)S(1)} %get-tuple-element.36), channel_id=1, source_target_pairs={{0,4},{2,6},{4,0},{6,2},{1,5},{3,7},{5,1},{7,3},{8,12},{10,14},{12... | collective-permute-start | bytes 688136 | tf_op jit(solution)/shard_map/ppermute | solution.py:72
  74.7 14.5 %collective-permute-start.19 = (bf16[128,896]{1,0:T(8,128)(2,1)S(1)}, bf16[128,896]{1,0:T(8,128)(2,1)S(1)}, u32[]{:S(2)}, u32[]{:S(2)}) collective-permute-start(bf16[128,896]{1,0:T(8,128)(2,1)S(1)} %get-tuple-element.37), channel_id=1, source_target_pairs={{0,6},{2,0},{4,2},{6,4},{1,7},{3,1},{5,3},{7,5},{8,14},{10,8},{12,... | collective-permute-start | bytes 688136 | tf_op jit(solution)/shard_map/ppermute | solution.py:72
  81.7 34.6 %copy-start.6 = (bf16[256,896]{1,0:T(8,128)(2,1)S(1)}, bf16[256,896]{1,0:T(8,128)(2,1)}, u32[]{:S(2)}) copy-start(bf16[256,896]{1,0:T(8,128)(2,1)} %gate_ref.1) | copy-start | bytes 1376260
  81.7 34.6 %copy-start.7 = (bf16[256,896]{1,0:T(8,128)(2,1)S(1)}, bf16[256,896]{1,0:T(8,128)(2,1)}, u32[]{:S(2)}) copy-start(bf16[256,896]{1,0:T(8,128)(2,1)} %up_ref.1) | copy-start | bytes 1376260
  81.9 15.3 %collective-permute-start.12 = (bf16[128,896]{1,0:T(8,128)(2,1)S(1)}, bf16[128,896]{1,0:T(8,128)(2,1)S(1)}, u32[]{:S(2)}, u32[]{:S(2)}) collective-permute-start(bf16[128,896]{1,0:T(8,128)(2,1)S(1)} %get-tuple-element.31), channel_id=1, source_target_pairs={{0,8},{8,0},{1,9},{9,1},{2,10},{10,2},{3,11},{11,3},{4,12},{12,4},... | collective-permute-start | bytes 688136 | tf_op jit(solution)/shard_map/ppermute | solution.py:72
  89.3 13.1 %collective-permute-start.21 = (bf16[128,896]{1,0:T(8,128)(2,1)S(1)}, bf16[128,896]{1,0:T(8,128)(2,1)S(1)}, u32[]{:S(2)}, u32[]{:S(2)}) collective-permute-start(bf16[128,896]{1,0:T(8,128)(2,1)S(1)} %shard_map.83), channel_id=1, source_target_pairs={{0,225},{1,129},{4,161},{5,33},{7,65},{8,193},{9,97},{15,1},{16,24... | collective-permute-start | bytes 688136 | tf_op jit(solution)/shard_map/ppermute | solution.py:280
  96.6 5.8 %collective-permute-start.20 = (bf16[128,896]{1,0:T(8,128)(2,1)S(1)}, bf16[128,896]{1,0:T(8,128)(2,1)S(1)}, u32[]{:S(2)}, u32[]{:S(2)}) collective-permute-start(bf16[128,896]{1,0:T(8,128)(2,1)S(1)} %shard_map.83), channel_id=1, source_target_pairs={{2,161},{3,65},{6,225},{10,1},{11,33},{12,193},{13,97},{14,129},{1... | collective-permute-start | bytes 688136 | tf_op jit(solution)/shard_map/ppermute | solution.py:280
  97.4 18.7 %collective-permute-start.14 = (bf16[128,896]{1,0:T(8,128)(2,1)S(1)}, bf16[128,896]{1,0:T(8,128)(2,1)S(1)}, u32[]{:S(2)}, u32[]{:S(2)}) collective-permute-start(bf16[128,896]{1,0:T(8,128)(2,1)S(1)} %shard_map.80), channel_id=1, source_target_pairs={{0,224},{1,128},{4,160},{5,32},{7,64},{8,192},{9,96},{15,0},{16,24... | collective-permute-start | bytes 688136 | tf_op jit(solution)/shard_map/ppermute | solution.py:280
  101.1 15.2 %collective-permute-start.13 = (bf16[128,896]{1,0:T(8,128)(2,1)S(1)}, bf16[128,896]{1,0:T(8,128)(2,1)S(1)}, u32[]{:S(2)}, u32[]{:S(2)}) collective-permute-start(bf16[128,896]{1,0:T(8,128)(2,1)S(1)} %shard_map.80), channel_id=1, source_target_pairs={{2,160},{3,64},{6,224},{10,0},{11,32},{12,192},{13,96},{14,128},{1... | collective-permute-start | bytes 688136 | tf_op jit(solution)/shard_map/ppermute | solution.py:280

commit v8 on v5

--- a/solution.py
+++ b/solution.py
@@ -15,6 +15,7 @@
 BF16, F32 = jnp.bfloat16, jnp.float32
 VMEM = pl.BlockSpec(memory_space=pltpu.VMEM)
 SMEM = pl.BlockSpec(memory_space=pltpu.SMEM)
+HBM = pl.BlockSpec(memory_space=pltpu.MemorySpace.HBM)
 
 NUMBER = (
     ((2, 5, 6, 1, 4, 0, 3, 7), (7, 3, 2, 4, 6, 1, 5, 0)),
@@ -62,7 +63,7 @@
                     for c in range(C):
                         place = [0] * S
                         for s in range(S):
-                            place[number_of(z, s, c)] = 2 * ((s % Y - y) % Y) + ((s // Y) ^ xl)
+                            place[number_of(z, s, c)] = ((s // Y) ^ xl) * Y + (s % Y - y) % Y
                         rows.append(place + [c, half_of(number_of(z, xl * Y + y, c), c) ^ xh])
     return np.array(rows, np.int32)
 
@@ -96,47 +97,50 @@
     rows, depth = far.shape
     width = w_own.shape[0]
 
-    def kernel(facts_ref, t0, t1, t2, t3, far_ref, w_own_ref, w_other_ref, lhs_ref, *out_refs):
-        lhs_ref[facts_ref[0]] = t0[pl.ds(pl.multiple_of(facts_ref[S] * rows, rows), rows), :]
-        for i, ref in enumerate((t1, t2, t3)):
-            for h in range(2):
-                lhs_ref[facts_ref[1 + 2 * i + h]] = ref[h * rows : (h + 1) * rows, :]
-        lhs_ref[facts_ref[7]] = far_ref[...]
-        for d in range(Y):
-            pair = lhs_ref[2 * d : 2 * d + 2].reshape(2 * rows, depth)
-            total = times(pair, w_own_ref[...], w_other_ref[...])
-            out_refs[d][0] = total[:rows]
-            out_refs[d][1] = total[rows:]
-
-    return pl.pallas_call(
-        kernel,
-        in_specs=[SMEM] + [VMEM] * 7,
+    def kernel(facts_ref, t0, t1, t2, t3, far_ref, w_own_ref, w_other_ref, lhs_ref, *refs):
+        out_refs, sems = refs[:Y], refs[Y]
+        blocks = [t0.at[pl.ds(pl.multiple_of(facts_ref[S] * rows, rows), rows), :]]
+        blocks += [ref.at[h * rows : (h + 1) * rows, :] for ref in (t1, t2, t3) for h in range(2)] + [far_ref]
+        copies = [pltpu.make_async_copy(block, lhs_ref.at[facts_ref[i]], sems.at[i]) for i, block in enumerate(blocks)]
+        for copy in copies:
+            copy.start()
+        for copy in copies:
+            copy.wait()
+        for e in range(2):
+            total = times(lhs_ref[Y * e : Y * e + Y].reshape(Y * rows, depth), w_own_ref[...], w_other_ref[...])
+            for d in range(Y):
+                out_refs[d][e] = total[d * rows : (d + 1) * rows]
+
+    return pl.pallas_call(
+        kernel,
+        in_specs=[SMEM] + [HBM] * 5 + [VMEM] * 2,
         out_specs=[VMEM] * (1 + Y),
         out_shape=[jax.ShapeDtypeStruct((S, rows, depth), BF16)]
         + [jax.ShapeDtypeStruct((2, rows, width), BF16)] * Y,
-        compiler_params=params(32),
+        scratch_shapes=[pltpu.SemaphoreType.DMA((S,))],
+        compiler_params=params(56),
         cost_estimate=pl.CostEstimate(flops=2 * S * rows * depth * width, bytes_accessed=8 * 2**20, transcendentals=0),
     )(own, *tokens, far, w_own, w_other)
 
 
-def product_xl(lhs, w_own, w_other):
+def product_xl(lhs, w_own, w_other, e):
     _, rows, depth = lhs.shape
     width = w_own.shape[0]
 
-    def kernel(lhs_ref, w_own_ref, w_other_ref, keep_ref, *send_refs):
+    def kernel(lhs_ref, w_own_ref, w_other_ref, *out_refs):
+        total = times(lhs_ref[...].reshape(Y * rows, depth), w_own_ref[...], w_other_ref[...])
         for d in range(Y):
-            pair = lhs_ref[2 * d : 2 * d + 2].reshape(2 * rows, depth)
-            total = times(pair, w_own_ref[...], w_other_ref[...])
-            keep_ref[d] = total[:rows]
-            send_refs[d // 2][d % 2] = total[rows:]
-
-    return pl.pallas_call(
-        kernel,
-        in_specs=[VMEM] * 3,
-        out_specs=[VMEM] * 3,
-        out_shape=[jax.ShapeDtypeStruct((n, rows, width), BF16) for n in (Y, Y // 2, Y // 2)],
-        compiler_params=params(32),
-        cost_estimate=pl.CostEstimate(flops=2 * S * rows * depth * width, bytes_accessed=6 * 2**20, transcendentals=0),
+            out_refs[d // 2][d % 2] = total[d * rows : (d + 1) * rows]
+
+    whole = lambda *shape: pl.BlockSpec(shape, lambda i: (0,) * len(shape))
+    return pl.pallas_call(
+        kernel,
+        grid=(1,),
+        in_specs=[pl.BlockSpec((Y, rows, depth), lambda i: (e, 0, 0)), whole(width, depth // 2), whole(width, depth // 2)],
+        out_specs=[whole(2, rows, width)] * 2,
+        out_shape=[jax.ShapeDtypeStruct((2, rows, width), BF16)] * 2,
+        compiler_params=params(16),
+        cost_estimate=pl.CostEstimate(flops=S * rows * depth * width, bytes_accessed=4 * 2**20, transcendentals=0),
     )(lhs, w_own, w_other)
 
 
@@ -161,21 +165,22 @@
 
 
 def add_xl(kept, received):
-    _, rows, width = kept.shape
-
-    def kernel(kept_ref, low_ref, high_ref, *out_refs):
+    _, rows, width = kept[0].shape
+
+    def kernel(*refs):
+        kept_refs, received_refs, out_refs = refs[:2], refs[2:4], refs[4:]
         for d in range(Y):
-            received = (low_ref, high_ref)[d // 2][d % 2]
-            out_refs[d][...] = (kept_ref[d].astype(F32) + received.astype(F32)).astype(BF16)
-
-    return pl.pallas_call(
-        kernel,
-        in_specs=[VMEM] * 3,
+            total = kept_refs[d // 2][d % 2].astype(F32) + received_refs[d // 2][d % 2].astype(F32)
+            out_refs[d][...] = total.astype(BF16)
+
+    return pl.pallas_call(
+        kernel,
+        in_specs=[VMEM] * 4,
         out_specs=[VMEM] * Y,
         out_shape=[jax.ShapeDtypeStruct((rows, width), BF16)] * Y,
         compiler_params=params(16),
         cost_estimate=pl.CostEstimate(flops=Y * rows * width, bytes_accessed=6 * Y * rows * width, transcendentals=0),
-    )(kept, *received)
+    )(*kept, *received)
 
 
 def add_last(own, near_parts, cross_parts):
@@ -233,22 +238,27 @@
     own = lax.dynamic_index_in_dim(jnp.asarray(facts()), lax.axis_index(ALL), 0, keepdims=False)
 
     near_own = dequantize(down_q, scales)
-    cross_own = shift(near_own, "xh", XH, 1)
+    near_other = shift(near_own, "c", C, 1)
+    cut = 5 * BLOCK
+    cross_own = [shift(near_own[:cut], "xh", XH, 1), shift(near_own[cut:], "xh", XH, 1)]
 
     rows = grad_out.shape[0] // 2
     tokens = [jnp.concatenate([grad_out, shift(grad_out, "c", C, 1)], 1)]
     around = [(i * C, (i + 1) % Z * C) for i in range(Z)] + [(i * C + 1, (i - 1) % Z * C + 1) for i in range(Z)]
     tokens[0], _ = lax.optimization_barrier((tokens[0], near_own))
     for step in range(3):
+        if step == 2:
+            tokens[2], cross_own[0], near_other = lax.optimization_barrier((tokens[2], cross_own[0], near_other))
         tokens.append(lax.ppermute(tokens[-1], ("z", "c"), around))
-    tokens[3], cross_own = lax.optimization_barrier((tokens[3], cross_own))
+    tokens[3], cross_own[1] = lax.optimization_barrier((tokens[3], cross_own[1]))
     far = lax.ppermute(lax.dynamic_slice_in_dim(tokens[3], c * rows, rows, 0), ("z", "c"), around)
-    near_other = shift(near_own, "c", C, 1)
+    cross_own, far = lax.optimization_barrier((jnp.concatenate(cross_own, 0), far))
     cross_other = shift(cross_own, "c", C, 1)
 
     lhs, *near = product_y(own, tokens, far, near_own, near_other)
     near_y = [near[0]] + [shift(near[d], "y", Y, d) for d in range(1, Y)]
-    kept, *sent = product_xl(lhs, cross_own, cross_other)
+    sent = product_xl(lhs, cross_own, cross_other, 1)
+    kept = product_xl(lhs, cross_own, cross_other, 0)
     cross = add_xl(kept, [shift(part, "xl", XL, 1) for part in sent])
     cross_parts = [cross[0]] + [shift(cross[d], "y", Y, d) for d in range(1, Y)]
     kept, sent = add_y(near_y)

time: 117 us -> 121 us (1.034)
  waiting for transfers between devices: 62.5 us -> 69.3 us
  starting transfers between devices: 37.8 us -> 32.2 us
  Pallas kernels: 10.3 us -> 12.8 us
    ppermute x13 -> x14, waiting for transfers between devices: 34.3 us -> 42.7 us  [shift(): return lax.ppermute(x, axis, [(i, (i + by) % size) for i in range(size)])]
    ppermute x3, waiting for transfers between devices: 11.1 us -> 4.87 us  [on_device(): tokens.append(lax.ppermute(tokens[-1], ('z', 'c'), around))]
    ppermute x2, starting transfers between devices: 11.4 us -> 5.55 us  [on_device(): hidden = [lax.ppermute(sums[j], ALL, home_pairs(j)) for j in range(2)]]
    ppermute x13 -> x14, starting transfers between devices: 12.3 us -> 15.9 us  [shift(): return lax.ppermute(x, axis, [(i, (i + by) % size) for i in range(size)])]
    ppermute x2, waiting for transfers between devices: 13.9 us -> 16.5 us  [on_device(): hidden = [lax.ppermute(sums[j], ALL, home_pairs(j)) for j in range(2)]]
    pallas_call x3 -> x4, Pallas kernels: 7.47 us -> 9.99 us  [the longest x1 7.22 us: product_y(): pl.pallas_call(kernel, in_specs=[SMEM] + [HBM] * 5 + [VMEM] * 2, out_spec...]
    ppermute x1, waiting for transfers between devices: 3.19 us -> 5.34 us  [on_device(): lax.ppermute(lax.dynamic_slice_in_dim(tokens[3], c * rows, rows, 0), ('z'...]
    ppermute x1, starting transfers between devices: 1.95 us -> 0.09 us  [on_device(): lax.ppermute(lax.dynamic_slice_in_dim(tokens[3], c * rows, rows, 0), ('z'...]
  transfers between devices with their start and end apart: 19 -> 20, of which waited for: 13 -> 13; matrix products, arithmetic and copies ran while one was open for 2% -> 2% of each run, Pallas kernels for 7% -> 8%
where the time goes in v8:
time: 121 us
  waiting for transfers between devices  69.3 us (57%)
  starting transfers between devices  32.2 us (27%)
  Pallas kernels  12.8 us (11%)
  local copies, waits for them, and re-layouts  5.4 us (4%)
    ppermute x14, waiting for transfers between devices, shift(): return lax.ppermute(x, axis, [(i, (i + by) % size) for i in range(size)])  42.7 us
    ppermute x2, waiting for transfers between devices, on_device(): hidden = [lax.ppermute(sums[j], ALL, home_pairs(j)) for j in range(2)]  16.5 us
    ppermute x14, starting transfers between devices, shift(): return lax.ppermute(x, axis, [(i, (i + by) % size) for i in range(size)])  15.9 us
    ppermute x3, starting transfers between devices, on_device(): tokens.append(lax.ppermute(tokens[-1], ('z', 'c'), around))  10.7 us
    pallas_call x1, Pallas kernels, product_y(): pl.pallas_call(kernel, in_specs=[SMEM] + [HBM] * 5 + [VMEM] * 2, out_spec...  7.22 us
    ppermute x2, starting transfers between devices, on_device(): hidden = [lax.ppermute(sums[j], ALL, home_pairs(j)) for j in range(2)]  5.55 us
    ppermute x1, waiting for transfers between devices, on_device(): lax.ppermute(lax.dynamic_slice_in_dim(tokens[3], c * rows, rows, 0), ('z'...  5.34 us
    ppermute x3, waiting for transfers between devices, on_device(): tokens.append(lax.ppermute(tokens[-1], ('z', 'c'), around))  4.87 us
  transfers between devices with their start and end apart: 20, of which 13 were waited for; matrix products, arithmetic and copies ran while one was open for 2% of the time, Pallas kernels for 8%

profile of v8, /device:TPU:7, one launch (start us, length us, event | category | flops | bytes accessed | tf_op | source)
XLA Modules:
  0.0 121.1 jit_solution(14289692002903900295)
XLA Ops:
  0.6 0.8 collective-permute-start
  1.4 0.8 copy.8
  2.2 0.3 mul.30
  2.5 0.4 fusion.w_own_ref
  2.9 0.6 copy-done.9
  3.4 0.1 pad_maximum_fusion.1.t0
  3.5 5.7 %collective-permute-start.1 = (bf16[256,1024]{1,0:T(8,128)(2,1)S(1)}, bf16[256,1024]{1,0:T(8,128)(2,1)S(1)}, u32[]{:S(2)}, u32[]{:S(2)}) collective-permute-start(bf16[256,1024]{1,0:T(8,128)(2,1)S(1)} %pad_maximum_fusion.1.t0), channel_id=1, source_target_pairs={{0,32},{32,64},{64,96},{96,128},{128,160},{160,192},{192,224},{224... | collective-permute-start | bytes 1572872 | tf_op jit(solution)/shard_map/ppermute | solution.py:252
  9.2 1.2 %collective-permute-start.3 = (bf16[640,512]{1,0:T(8,128)(2,1)S(1)}, bf16[640,512]{1,0:T(8,128)(2,1)S(1)}, u32[]{:S(2)}, u32[]{:S(2)}) collective-permute-start(bf16[640,512]{1,0:T(8,128)(2,1)S(1)} %slice.8), channel_id=1, source_target_pairs={{0,16},{16,0},{1,17},{17,1},{2,18},{18,2},{3,19},{19,3},{4,20},{20... | collective-permute-start | bytes 1966088 | tf_op jit(solution)/shard_map/ppermute | solution.py:72
  10.4 4.9 %collective-permute-done.1.t1 = bf16[256,1024]{1,0:T(8,128)(2,1)S(1)} collective-permute-done((bf16[256,1024]{1,0:T(8,128)(2,1)S(1)}, bf16[256,1024]{1,0:T(8,128)(2,1)S(1)}, u32[]{:S(2)}, u32[]{:S(2)}) %collective-permute-start.1) | collective-permute-done | bytes 524320 | tf_op jit(solution)/shard_map/ppermute | solution.py:252
  15.3 3.4 %collective-permute-start.2 = (bf16[256,1024]{1,0:T(8,128)(2,1)S(1)}, bf16[256,1024]{1,0:T(8,128)(2,1)}, u32[]{:S(2)}, u32[]{:S(2)}) collective-permute-start(bf16[256,1024]{1,0:T(8,128)(2,1)S(1)} %collective-permute-done.1.t1), channel_id=1, source_target_pairs={{0,32},{32,64},{64,96},{96,128},{128,160},{160,192},{192,224},{224... | collective-permute-start | bytes 1572872 | tf_op jit(solution)/shard_map/ppermute | solution.py:252
  18.7 7.9 %collective-permute-done.3 = bf16[640,512]{1,0:T(8,128)(2,1)S(1)} collective-permute-done((bf16[640,512]{1,0:T(8,128)(2,1)S(1)}, bf16[640,512]{1,0:T(8,128)(2,1)S(1)}, u32[]{:S(2)}, u32[]{:S(2)}) %collective-permute-start.3) | collective-permute-done | bytes 655392 | tf_op jit(solution)/shard_map/ppermute | solution.py:72
  26.6 1.6 %collective-permute-start.5 = (bf16[256,1024]{1,0:T(8,128)(2,1)}, bf16[256,1024]{1,0:T(8,128)(2,1)S(1)}, u32[]{:S(2)}, u32[]{:S(2)}) collective-permute-start(bf16[256,1024]{1,0:T(8,128)(2,1)} %collective-permute-done.2.t2), channel_id=1, source_target_pairs={{0,32},{32,64},{64,96},{96,128},{128,160},{160,192},{192,224},{224... | collective-permute-start | bytes 1572872 | tf_op jit(solution)/shard_map/ppermute | solution.py:252
  28.3 0.9 collective-permute-start.6
  29.2 8.7 %collective-permute-done.6 = bf16[256,512]{1,0:T(8,128)(2,1)S(1)} collective-permute-done((bf16[256,512]{1,0:T(8,128)(2,1)S(1)}, bf16[256,512]{1,0:T(8,128)(2,1)S(1)}, u32[]{:S(2)}, u32[]{:S(2)}) %collective-permute-start.6) | collective-permute-done | bytes 262176 | tf_op jit(solution)/shard_map/ppermute | solution.py:72
  37.9 0.8 copy-done.10
  38.7 0.1 collective-permute-start.7
  38.8 0.1 pad_maximum_fusion.w_own_ref
  38.9 5.3 %collective-permute-done.7.far_ref = bf16[128,1024]{1,0:T(8,128)(2,1)S(1)} collective-permute-done((bf16[128,1024]{1,0:T(8,128)(2,1)S(1)}, bf16[128,1024]{1,0:T(8,128)(2,1)S(1)}, u32[]{:S(2)}, u32[]{:S(2)}) %collective-permute-start.7) | collective-permute-done | bytes 262176 | tf_op jit(solution)/shard_map/ppermute | solution.py:254
  44.2 2.8 %collective-permute-start.12 = (bf16[896,512]{1,0:T(8,128)(2,1)S(1)}, bf16[896,512]{1,0:T(8,128)(2,1)S(1)}, u32[]{:S(2)}, u32[]{:S(2)}) collective-permute-start(bf16[896,512]{1,0:T(8,128)(2,1)S(1)} %pad_maximum_fusion.w_own_ref), channel_id=1, source_target_pairs={{0,1},{1,0},{2,3},{3,2},{4,5},{5,4},{6,7},{7,6},{8,9},{9,8},{10,11... | collective-permute-start | bytes 2752520 | tf_op jit(solution)/shard_map/ppermute | solution.py:72
  47.1 1.3 %dynamic-slice_bitcast_fusion.facts_ref = s32[10]{0:T(128)} fusion(s32[256,10]{1,0:T(8,128)} %constant.40.clone, s32[]{:T(128)S(6)} %select_n.7), kind=kLoop, calls=%fused_computation.4 | loop fusion | bytes 84 | tf_op jit(solution)/shard_map/jit(dynamic_index_in_dim)/squeeze | solution.py:238
  48.3 7.2 %shard_map.77 = (bf16[8,128,1024]{2,1,0:T(8,128)(2,1)}, bf16[2,128,896]{2,1,0:T(8,128)(2,1)}, bf16[2,128,896]{2,1,0:T(8,128)(2,1)}, bf16[2,128,896]{2,1,0:T(8,128)(2,1)}, bf16[2,128,896]{2,1,0:T(8,128)(2,1)}) custom-call(s32[10]{0:T(128)} %dynamic-slice_bitcast_fusion.facts_ref, bf16[256,1024]{1,0:T(8,128)(2,1)} %copy-done.8, bf16[256,1024]{1,0:T(8,128)(2,1)} %copy-done.12, ...), custom_call_target="tpu_custom_call" | custom-call | flops 1879048192 | bytes 8388608 | tf_op jit(solution)/shard_map/pallas_call | solution.py:114
  55.5 1.4 %collective-permute-start.8 = (bf16[2,128,896]{2,1,0:T(8,128)(2,1)}, bf16[2,128,896]{2,1,0:T(8,128)(2,1)S(1)}, u32[]{:S(2)}, u32[]{:S(2)}) collective-permute-start(bf16[2,128,896]{2,1,0:T(8,128)(2,1)} %get-tuple-element.35), channel_id=1, source_target_pairs={{0,2},{2,4},{4,6},{6,0},{1,3},{3,5},{5,7},{7,1},{8,10},{10,12},{12... | collective-permute-start | bytes 1376264 | tf_op jit(solution)/shard_map/ppermute | solution.py:72
  56.9 2.6 %collective-permute-start.9 = (bf16[2,128,896]{2,1,0:T(8,128)(2,1)}, bf16[2,128,896]{2,1,0:T(8,128)(2,1)S(1)}, u32[]{:S(2)}, u32[]{:S(2)}) collective-permute-start(bf16[2,128,896]{2,1,0:T(8,128)(2,1)} %get-tuple-element.36), channel_id=1, source_target_pairs={{0,4},{2,6},{4,0},{6,2},{1,5},{3,7},{5,1},{7,3},{8,12},{10,14},{12... | collective-permute-start | bytes 1376264 | tf_op jit(solution)/shard_map/ppermute | solution.py:72
  59.5 1.1 collective-permute-start.10
  60.6 1.6 %copy-done = bf16[8,128,1024]{2,1,0:T(8,128)(2,1)S(1)} copy-done((bf16[8,128,1024]{2,1,0:T(8,128)(2,1)S(1)}, bf16[8,128,1024]{2,1,0:T(8,128)(2,1)}, u32[]{:S(2)}) %copy-start) | copy-done | bytes 2097176
  62.2 1.3 %shard_map.80 = (bf16[2,128,896]{2,1,0:T(8,128)(2,1)S(1)}, bf16[2,128,896]{2,1,0:T(8,128)(2,1)S(1)}) custom-call(bf16[8,128,1024]{2,1,0:T(8,128)(2,1)S(1)} %copy-done, bf16[896,512]{1,0:T(8,128)(2,1)S(1)} %pad_maximum_fusion.w_own_ref, bf16[896,512]{1,0:T(8,128)(2,1)S(1)} %collective-permute-done.12.w_other_ref), custom_call_target="tpu_custom_call" | custom-call | flops 939524096 | bytes 4194304 | tf_op jit(solution)/shard_map/pallas_call | solution.py:136
  63.5 0.6 collective-permute-start.13
  64.1 0.9 collective-permute-start.14
  65.0 4.3 %collective-permute-done.8.refs_1_ = bf16[2,128,896]{2,1,0:T(8,128)(2,1)S(1)} collective-permute-done((bf16[2,128,896]{2,1,0:T(8,128)(2,1)}, bf16[2,128,896]{2,1,0:T(8,128)(2,1)S(1)}, u32[]{:S(2)}, u32[]{:S(2)}) %collective-permute-start.8) | collective-permute-done | bytes 458784 | tf_op jit(solution)/shard_map/ppermute | solution.py:72
  69.3 10.9 %collective-permute-done.9.refs_2_ = bf16[2,128,896]{2,1,0:T(8,128)(2,1)S(1)} collective-permute-done((bf16[2,128,896]{2,1,0:T(8,128)(2,1)}, bf16[2,128,896]{2,1,0:T(8,128)(2,1)S(1)}, u32[]{:S(2)}, u32[]{:S(2)}) %collective-permute-start.9) | collective-permute-done | bytes 458784 | tf_op jit(solution)/shard_map/ppermute | solution.py:72
  80.2 0.2 shard_map.78
  80.5 0.6 collective-permute-start.11
  81.1 1.3 %shard_map.79 = (bf16[2,128,896]{2,1,0:T(8,128)(2,1)S(1)}, bf16[2,128,896]{2,1,0:T(8,128)(2,1)S(1)}) custom-call(bf16[8,128,1024]{2,1,0:T(8,128)(2,1)S(1)} %copy-done.1, bf16[896,512]{1,0:T(8,128)(2,1)S(1)} %pad_maximum_fusion.w_own_ref, bf16[896,512]{1,0:T(8,128)(2,1)S(1)} %collective-permute-done.12.w_other_ref), custom_call_target="tpu_custom_call" | custom-call | flops 939524096 | bytes 4194304 | tf_op jit(solution)/shard_map/pallas_call | solution.py:136
  82.5 2.1 %collective-permute-done.14.refs_3_ = bf16[2,128,896]{2,1,0:T(8,128)(2,1)S(1)} collective-permute-done((bf16[2,128,896]{2,1,0:T(8,128)(2,1)S(1)}, bf16[2,128,896]{2,1,0:T(8,128)(2,1)S(1)}, u32[]{:S(2)}, u32[]{:S(2)}) %collective-permute-start.14) | collective-permute-done | bytes 458784 | tf_op jit(solution)/shard_map/ppermute | solution.py:72
  84.6 0.2 shard_map.81
  84.8 0.5 collective-permute-start.15
  85.3 1.1 collective-permute-start.16
  86.4 1.4 %collective-permute-start.17 = (bf16[128,896]{1,0:T(8,128)(2,1)S(1)}, bf16[128,896]{1,0:T(8,128)(2,1)S(1)}, u32[]{:S(2)}, u32[]{:S(2)}) collective-permute-start(bf16[128,896]{1,0:T(8,128)(2,1)S(1)} %get-tuple-element.49), channel_id=1, source_target_pairs={{0,6},{2,0},{4,2},{6,4},{1,7},{3,1},{5,3},{7,5},{8,14},{10,8},{12,... | collective-permute-start | bytes 688136 | tf_op jit(solution)/shard_map/ppermute | solution.py:72
  87.8 1.7 %collective-permute-done.11.refs_1_ = bf16[128,896]{1,0:T(8,128)(2,1)S(1)} collective-permute-done((bf16[128,896]{1,0:T(8,128)(2,1)S(1)}, bf16[128,896]{1,0:T(8,128)(2,1)S(1)}, u32[]{:S(2)}, u32[]{:S(2)}) %collective-permute-start.11) | collective-permute-done | bytes 229408 | tf_op jit(solution)/shard_map/ppermute | solution.py:72
  89.5 2.5 %collective-permute-done.15.refs_3_ = bf16[128,896]{1,0:T(8,128)(2,1)S(1)} collective-permute-done((bf16[128,896]{1,0:T(8,128)(2,1)S(1)}, bf16[128,896]{1,0:T(8,128)(2,1)S(1)}, u32[]{:S(2)}, u32[]{:S(2)}) %collective-permute-start.15) | collective-permute-done | bytes 229408 | tf_op jit(solution)/shard_map/ppermute | solution.py:72
  92.0 3.0 %collective-permute-done.16.refs_4_ = bf16[128,896]{1,0:T(8,128)(2,1)S(1)} collective-permute-done((bf16[128,896]{1,0:T(8,128)(2,1)S(1)}, bf16[128,896]{1,0:T(8,128)(2,1)S(1)}, u32[]{:S(2)}, u32[]{:S(2)}) %collective-permute-start.16) | collective-permute-done | bytes 229408 | tf_op jit(solution)/shard_map/ppermute | solution.py:72
  95.1 1.4 %collective-permute-done.17.refs_5_ = bf16[128,896]{1,0:T(8,128)(2,1)S(1)} collective-permute-done((bf16[128,896]{1,0:T(8,128)(2,1)S(1)}, bf16[128,896]{1,0:T(8,128)(2,1)S(1)}, u32[]{:S(2)}, u32[]{:S(2)}) %collective-permute-start.17) | collective-permute-done | bytes 229408 | tf_op jit(solution)/shard_map/ppermute | solution.py:72
  96.5 0.7 shard_map.82
  97.2 0.6 collective-permute-start.18
  97.9 4.9 %collective-permute-start.19 = (bf16[128,896]{1,0:T(8,128)(2,1)S(1)}, bf16[128,896]{1,0:T(8,128)(2,1)S(1)}, u32[]{:S(2)}, u32[]{:S(2)}) collective-permute-start(bf16[128,896]{1,0:T(8,128)(2,1)S(1)} %get-tuple-element.51), channel_id=1, source_target_pairs={{0,224},{1,128},{2,161},{3,65},{4,160},{5,32},{6,225},{7,64},{8,19... | collective-permute-start | bytes 688136 | tf_op jit(solution)/shard_map/ppermute | solution.py:268
  102.8 9.4 %collective-permute-done.18.first = bf16[128,896]{1,0:T(8,128)(2,1)S(1)} collective-permute-done((bf16[128,896]{1,0:T(8,128)(2,1)S(1)}, bf16[128,896]{1,0:T(8,128)(2,1)S(1)}, u32[]{:S(2)}, u32[]{:S(2)}) %collective-permute-start.18) | collective-permute-done | bytes 229408 | tf_op jit(solution)/shard_map/ppermute | solution.py:268
  112.2 7.1 %collective-permute-done.19.second = bf16[128,896]{1,0:T(8,128)(2,1)S(1)} collective-permute-done((bf16[128,896]{1,0:T(8,128)(2,1)S(1)}, bf16[128,896]{1,0:T(8,128)(2,1)S(1)}, u32[]{:S(2)}, u32[]{:S(2)}) %collective-permute-start.19) | collective-permute-done | bytes 229408 | tf_op jit(solution)/shard_map/ppermute | solution.py:268
  119.3 1.9 %shard_map.83 = (bf16[256,896]{1,0:T(8,128)(2,1)}, bf16[256,896]{1,0:T(8,128)(2,1)}) custom-call(s32[10]{0:T(128)S(1)} %copy-done.5, bf16[128,896]{1,0:T(8,128)(2,1)S(1)} %collective-permute-done.18.first, bf16[128,896]{1,0:T(8,128)(2,1)S(1)} %collective-permute-done.19.second, bf16[256,896]{1,0:T(8,128)(2,1)S(1)} %copy-done.3, bf16[256,896]{1,0:T(8,128)(2,1)S(1)} %copy-done.4), custom_call_target="tpu_custom_call" | custom-call | flops 2293760 | bytes 2293760 | tf_op jit(solution)/shard_map/pallas_call | solution.py:226
  (36 shorter events, 0.2 us)
Async XLA Ops:
  0.6 1.9 %copy-start.7 = (bf16[896,512]{1,0:T(8,128)(2,1)S(1)}, bf16[896,512]{1,0:T(8,128)(2,1)}, u32[]{:S(2)}) copy-start(bf16[896,512]{1,0:T(8,128)(2,1)} %param.7) | copy-start | bytes 2752516
  0.6 2.2 %collective-permute-start = (bf16[256,512]{1,0:T(8,128)(2,1)}, bf16[256,512]{1,0:T(8,128)(2,1)S(1)}, u32[]{:S(2)}, u32[]{:S(2)}) collective-permute-start(bf16[256,512]{1,0:T(8,128)(2,1)} %param.6), channel_id=1, source_target_pairs={{0,1},{1,0},{2,3},{3,2},{4,5},{5,4},{6,7},{7,6},{8,9},{9,8},{10,11... | collective-permute-start | bytes 786440 | tf_op jit(solution)/shard_map/ppermute | solution.py:72
  2.5 1.0 copy-start.9
  2.9 36.0 %copy-start.6 = (bf16[896,512]{1,0:T(8,128)(2,1)}, bf16[896,512]{1,0:T(8,128)(2,1)S(1)}, u32[]{:S(2)}) copy-start(bf16[896,512]{1,0:T(8,128)(2,1)S(1)} %fusion.w_own_ref) | copy-start | bytes 2752516
  3.5 35.4 %copy-start.8 = (bf16[256,1024]{1,0:T(8,128)(2,1)}, bf16[256,1024]{1,0:T(8,128)(2,1)S(1)}, u32[]{:S(2)}) copy-start(bf16[256,1024]{1,0:T(8,128)(2,1)S(1)} %pad_maximum_fusion.1.t0) | copy-start | bytes 1572868
  3.5 11.8 %collective-permute-start.1 = (bf16[256,1024]{1,0:T(8,128)(2,1)S(1)}, bf16[256,1024]{1,0:T(8,128)(2,1)S(1)}, u32[]{:S(2)}, u32[]{:S(2)}) collective-permute-start(bf16[256,1024]{1,0:T(8,128)(2,1)S(1)} %pad_maximum_fusion.1.t0), channel_id=1, source_target_pairs={{0,32},{32,64},{64,96},{96,128},{128,160},{160,192},{192,224},{224... | collective-permute-start | bytes 1572872 | tf_op jit(solution)/shard_map/ppermute | solution.py:252
  9.2 17.4 %collective-permute-start.4 = (bf16[896,512]{1,0:T(8,128)(2,1)S(1)}, bf16[896,512]{1,0:T(8,128)(2,1)S(1)}, u32[]{:S(2)}, u32[]{:S(2)}) collective-permute-start(bf16[896,512]{1,0:T(8,128)(2,1)S(1)} %fusion.w_own_ref), channel_id=1, source_target_pairs={{0,1},{1,0},{2,3},{3,2},{4,5},{5,4},{6,7},{7,6},{8,9},{9,8},{10,11... | collective-permute-start | bytes 2752520 | tf_op jit(solution)/shard_map/ppermute | solution.py:72
  9.2 17.4 %collective-permute-start.3 = (bf16[640,512]{1,0:T(8,128)(2,1)S(1)}, bf16[640,512]{1,0:T(8,128)(2,1)S(1)}, u32[]{:S(2)}, u32[]{:S(2)}) collective-permute-start(bf16[640,512]{1,0:T(8,128)(2,1)S(1)} %slice.8), channel_id=1, source_target_pairs={{0,16},{16,0},{1,17},{17,1},{2,18},{18,2},{3,19},{19,3},{4,20},{20... | collective-permute-start | bytes 1966088 | tf_op jit(solution)/shard_map/ppermute | solution.py:72
  15.3 13.9 %copy-start.12 = (bf16[256,1024]{1,0:T(8,128)(2,1)}, bf16[256,1024]{1,0:T(8,128)(2,1)S(1)}, u32[]{:S(2)}) copy-start(bf16[256,1024]{1,0:T(8,128)(2,1)S(1)} %collective-permute-done.1.t1) | copy-start | bytes 1572868
  15.3 11.3 %collective-permute-start.2 = (bf16[256,1024]{1,0:T(8,128)(2,1)S(1)}, bf16[256,1024]{1,0:T(8,128)(2,1)}, u32[]{:S(2)}, u32[]{:S(2)}) collective-permute-start(bf16[256,1024]{1,0:T(8,128)(2,1)S(1)} %collective-permute-done.1.t1), channel_id=1, source_target_pairs={{0,32},{32,64},{64,96},{96,128},{128,160},{160,192},{192,224},{224... | collective-permute-start | bytes 1572872 | tf_op jit(solution)/shard_map/ppermute | solution.py:252
  26.6 2.6 %copy-start.11 = (bf16[896,512]{1,0:T(8,128)(2,1)}, bf16[896,512]{1,0:T(8,128)(2,1)S(1)}, u32[]{:S(2)}) copy-start(bf16[896,512]{1,0:T(8,128)(2,1)S(1)} %collective-permute-done.4.w_other_ref) | copy-start | bytes 2752516
  26.6 11.3 %collective-permute-start.5 = (bf16[256,1024]{1,0:T(8,128)(2,1)}, bf16[256,1024]{1,0:T(8,128)(2,1)S(1)}, u32[]{:S(2)}, u32[]{:S(2)}) collective-permute-start(bf16[256,1024]{1,0:T(8,128)(2,1)} %collective-permute-done.2.t2), channel_id=1, source_target_pairs={{0,32},{32,64},{64,96},{96,128},{128,160},{160,192},{192,224},{224... | collective-permute-start | bytes 1572872 | tf_op jit(solution)/shard_map/ppermute | solution.py:252
  28.3 9.6 %collective-permute-start.6 = (bf16[256,512]{1,0:T(8,128)(2,1)S(1)}, bf16[256,512]{1,0:T(8,128)(2,1)S(1)}, u32[]{:S(2)}, u32[]{:S(2)}) collective-permute-start(bf16[256,512]{1,0:T(8,128)(2,1)S(1)} %slice.9), channel_id=1, source_target_pairs={{0,16},{16,0},{1,17},{17,1},{2,18},{18,2},{3,19},{19,3},{4,20},{20... | collective-permute-start | bytes 786440 | tf_op jit(solution)/shard_map/ppermute | solution.py:72
  37.9 0.8 copy-start.10
  38.7 5.5 %collective-permute-start.7 = (bf16[128,1024]{1,0:T(8,128)(2,1)S(1)}, bf16[128,1024]{1,0:T(8,128)(2,1)S(1)}, u32[]{:S(2)}, u32[]{:S(2)}) collective-permute-start(bf16[128,1024]{1,0:T(8,128)(2,1)S(1)} %constant_dynamic-slice_fusion), channel_id=1, source_target_pairs={{0,32},{32,64},{64,96},{96,128},{128,160},{160,192},{192,224},{224... | collective-permute-start | bytes 786440 | tf_op jit(solution)/shard_map/ppermute | solution.py:254
  44.2 4.1 %copy-start.13 = (bf16[128,1024]{1,0:T(8,128)(2,1)}, bf16[128,1024]{1,0:T(8,128)(2,1)S(1)}, u32[]{:S(2)}) copy-start(bf16[128,1024]{1,0:T(8,128)(2,1)S(1)} %collective-permute-done.7.far_ref) | copy-start | bytes 786436
  44.2 16.4 %collective-permute-start.12 = (bf16[896,512]{1,0:T(8,128)(2,1)S(1)}, bf16[896,512]{1,0:T(8,128)(2,1)S(1)}, u32[]{:S(2)}, u32[]{:S(2)}) collective-permute-start(bf16[896,512]{1,0:T(8,128)(2,1)S(1)} %pad_maximum_fusion.w_own_ref), channel_id=1, source_target_pairs={{0,1},{1,0},{2,3},{3,2},{4,5},{5,4},{6,7},{7,6},{8,9},{9,8},{10,11... | collective-permute-start | bytes 2752520 | tf_op jit(solution)/shard_map/ppermute | solution.py:72
  55.5 13.8 %collective-permute-start.8 = (bf16[2,128,896]{2,1,0:T(8,128)(2,1)}, bf16[2,128,896]{2,1,0:T(8,128)(2,1)S(1)}, u32[]{:S(2)}, u32[]{:S(2)}) collective-permute-start(bf16[2,128,896]{2,1,0:T(8,128)(2,1)} %get-tuple-element.35), channel_id=1, source_target_pairs={{0,2},{2,4},{4,6},{6,0},{1,3},{3,5},{5,7},{7,1},{8,10},{10,12},{12... | collective-permute-start | bytes 1376264 | tf_op jit(solution)/shard_map/ppermute | solution.py:72
  56.9 23.3 %collective-permute-start.9 = (bf16[2,128,896]{2,1,0:T(8,128)(2,1)}, bf16[2,128,896]{2,1,0:T(8,128)(2,1)S(1)}, u32[]{:S(2)}, u32[]{:S(2)}) collective-permute-start(bf16[2,128,896]{2,1,0:T(8,128)(2,1)} %get-tuple-element.36), channel_id=1, source_target_pairs={{0,4},{2,6},{4,0},{6,2},{1,5},{3,7},{5,1},{7,3},{8,12},{10,14},{12... | collective-permute-start | bytes 1376264 | tf_op jit(solution)/shard_map/ppermute | solution.py:72
  59.5 20.7 %collective-permute-start.10 = (bf16[2,128,896]{2,1,0:T(8,128)(2,1)}, bf16[2,128,896]{2,1,0:T(8,128)(2,1)S(1)}, u32[]{:S(2)}, u32[]{:S(2)}) collective-permute-start(bf16[2,128,896]{2,1,0:T(8,128)(2,1)} %get-tuple-element.37), channel_id=1, source_target_pairs={{0,6},{2,0},{4,2},{6,4},{1,7},{3,1},{5,3},{7,5},{8,14},{10,8},{12,... | collective-permute-start | bytes 1376264 | tf_op jit(solution)/shard_map/ppermute | solution.py:72
  60.6 1.6 %copy-start = (bf16[8,128,1024]{2,1,0:T(8,128)(2,1)S(1)}, bf16[8,128,1024]{2,1,0:T(8,128)(2,1)}, u32[]{:S(2)}) copy-start(bf16[8,128,1024]{2,1,0:T(8,128)(2,1)} %get-tuple-element.40.lhs_ref) | copy-start | bytes 6291460
  62.2 18.0 %copy-start.2 = (bf16[2,128,896]{2,1,0:T(8,128)(2,1)S(1)}, bf16[2,128,896]{2,1,0:T(8,128)(2,1)}, u32[]{:S(2)}) copy-start(bf16[2,128,896]{2,1,0:T(8,128)(2,1)} %get-tuple-element.34.refs_0_) | copy-start | bytes 1376260
  62.2 18.9 %copy-start.1 = (bf16[8,128,1024]{2,1,0:T(8,128)(2,1)S(1)}, bf16[8,128,1024]{2,1,0:T(8,128)(2,1)}, u32[]{:S(2)}) copy-start(bf16[8,128,1024]{2,1,0:T(8,128)(2,1)} %get-tuple-element.40.lhs_ref) | copy-start | bytes 6291460
  63.5 19.0 %collective-permute-start.13 = (bf16[2,128,896]{2,1,0:T(8,128)(2,1)S(1)}, bf16[2,128,896]{2,1,0:T(8,128)(2,1)S(1)}, u32[]{:S(2)}, u32[]{:S(2)}) collective-permute-start(bf16[2,128,896]{2,1,0:T(8,128)(2,1)S(1)} %get-tuple-element.44), channel_id=1, source_target_pairs={{0,8},{8,0},{1,9},{9,1},{2,10},{10,2},{3,11},{11,3},{4,12},{12,4},... | collective-permute-start | bytes 1376264 | tf_op jit(solution)/shard_map/ppermute | solution.py:72
  64.1 20.5 %collective-permute-start.14 = (bf16[2,128,896]{2,1,0:T(8,128)(2,1)S(1)}, bf16[2,128,896]{2,1,0:T(8,128)(2,1)S(1)}, u32[]{:S(2)}, u32[]{:S(2)}) collective-permute-start(bf16[2,128,896]{2,1,0:T(8,128)(2,1)S(1)} %get-tuple-element.45), channel_id=1, source_target_pairs={{0,8},{8,0},{1,9},{9,1},{2,10},{10,2},{3,11},{11,3},{4,12},{12,4},... | collective-permute-start | bytes 1376264 | tf_op jit(solution)/shard_map/ppermute | solution.py:72
  80.5 9.0 %collective-permute-start.11 = (bf16[128,896]{1,0:T(8,128)(2,1)S(1)}, bf16[128,896]{1,0:T(8,128)(2,1)S(1)}, u32[]{:S(2)}, u32[]{:S(2)}) collective-permute-start(bf16[128,896]{1,0:T(8,128)(2,1)S(1)} %get-tuple-element.39), channel_id=1, source_target_pairs={{0,8},{8,0},{1,9},{9,1},{2,10},{10,2},{3,11},{11,3},{4,12},{12,4},... | collective-permute-start | bytes 688136 | tf_op jit(solution)/shard_map/ppermute | solution.py:72
  82.4 14.1 %copy-start.5 = (s32[10]{0:T(128)S(1)}, s32[10]{0:T(128)}, u32[]{:S(2)}) copy-start(s32[10]{0:T(128)} %dynamic-slice_bitcast_fusion.facts_ref) | copy-start | bytes 124
  82.4 36.8 %copy-start.3 = (bf16[256,896]{1,0:T(8,128)(2,1)S(1)}, bf16[256,896]{1,0:T(8,128)(2,1)}, u32[]{:S(2)}) copy-start(bf16[256,896]{1,0:T(8,128)(2,1)} %gate_ref.1) | copy-start | bytes 1376260
  82.4 36.8 %copy-start.4 = (bf16[256,896]{1,0:T(8,128)(2,1)S(1)}, bf16[256,896]{1,0:T(8,128)(2,1)}, u32[]{:S(2)}) copy-start(bf16[256,896]{1,0:T(8,128)(2,1)} %up_ref.1) | copy-start | bytes 1376260
  84.8 7.2 %collective-permute-start.15 = (bf16[128,896]{1,0:T(8,128)(2,1)S(1)}, bf16[128,896]{1,0:T(8,128)(2,1)S(1)}, u32[]{:S(2)}, u32[]{:S(2)}) collective-permute-start(bf16[128,896]{1,0:T(8,128)(2,1)S(1)} %get-tuple-element.47), channel_id=1, source_target_pairs={{0,2},{2,4},{4,6},{6,0},{1,3},{3,5},{5,7},{7,1},{8,10},{10,12},{12... | collective-permute-start | bytes 688136 | tf_op jit(solution)/shard_map/ppermute | solution.py:72
  85.3 9.8 %collective-permute-start.16 = (bf16[128,896]{1,0:T(8,128)(2,1)S(1)}, bf16[128,896]{1,0:T(8,128)(2,1)S(1)}, u32[]{:S(2)}, u32[]{:S(2)}) collective-permute-start(bf16[128,896]{1,0:T(8,128)(2,1)S(1)} %get-tuple-element.48), channel_id=1, source_target_pairs={{0,4},{2,6},{4,0},{6,2},{1,5},{3,7},{5,1},{7,3},{8,12},{10,14},{12... | collective-permute-start | bytes 688136 | tf_op jit(solution)/shard_map/ppermute | solution.py:72
  86.4 10.1 %collective-permute-start.17 = (bf16[128,896]{1,0:T(8,128)(2,1)S(1)}, bf16[128,896]{1,0:T(8,128)(2,1)S(1)}, u32[]{:S(2)}, u32[]{:S(2)}) collective-permute-start(bf16[128,896]{1,0:T(8,128)(2,1)S(1)} %get-tuple-element.49), channel_id=1, source_target_pairs={{0,6},{2,0},{4,2},{6,4},{1,7},{3,1},{5,3},{7,5},{8,14},{10,8},{12,... | collective-permute-start | bytes 688136 | tf_op jit(solution)/shard_map/ppermute | solution.py:72
  97.2 14.9 %collective-permute-start.18 = (bf16[128,896]{1,0:T(8,128)(2,1)S(1)}, bf16[128,896]{1,0:T(8,128)(2,1)S(1)}, u32[]{:S(2)}, u32[]{:S(2)}) collective-permute-start(bf16[128,896]{1,0:T(8,128)(2,1)S(1)} %get-tuple-element.50), channel_id=1, source_target_pairs={{0,225},{1,129},{2,160},{3,64},{4,161},{5,33},{6,224},{7,65},{8,19... | collective-permute-start | bytes 688136 | tf_op jit(solution)/shard_map/ppermute | solution.py:268
  97.9 21.4 %collective-permute-start.19 = (bf16[128,896]{1,0:T(8,128)(2,1)S(1)}, bf16[128,896]{1,0:T(8,128)(2,1)S(1)}, u32[]{:S(2)}, u32[]{:S(2)}) collective-permute-start(bf16[128,896]{1,0:T(8,128)(2,1)S(1)} %get-tuple-element.51), channel_id=1, source_target_pairs={{0,224},{1,128},{2,161},{3,65},{4,160},{5,32},{6,225},{7,64},{8,19... | collective-permute-start | bytes 688136 | tf_op jit(solution)/shard_map/ppermute | solution.py:268

commit v9 on v6

--- a/solution.py
+++ b/solution.py
@@ -63,7 +63,7 @@
                     for c in range(C):
                         place = [0] * S
                         for s in range(S):
-                            place[number_of(z, s, c)] = 2 * ((s % Y - y) % Y) + ((s // Y) ^ xl)
+                            place[number_of(z, s, c)] = ((s // Y) ^ xl) * Y + (s % Y - y) % Y
                         rows.append(place + [c, c ^ xh])
     return np.array(rows, np.int32)
 
@@ -103,11 +103,10 @@
             for h in range(2):
                 lhs_ref[facts_ref[1 + 2 * i + h]] = ref[h * rows : (h + 1) * rows, :]
         lhs_ref[facts_ref[7]] = far_ref[...]
-        for d in range(Y):
-            pair = lhs_ref[2 * d : 2 * d + 2].reshape(2 * rows, depth)
-            total = times(pair, w_own_ref[...], w_other_ref[...])
-            out_refs[d][0] = total[:rows]
-            out_refs[d][1] = total[rows:]
+        for e in range(2):
+            total = times(lhs_ref[Y * e : Y * e + Y].reshape(Y * rows, depth), w_own_ref[...], w_other_ref[...])
+            for d in range(Y):
+                out_refs[d][e] = total[d * rows : (d + 1) * rows]
 
     return pl.pallas_call(
         kernel,
@@ -120,24 +119,24 @@
     )(own, *tokens, far, w_own, w_other)
 
 
-def product_xl(lhs, w_own, w_other):
+def product_xl(lhs, w_own, w_other, e):
     _, rows, depth = lhs.shape
     width = w_own.shape[0]
 
-    def kernel(lhs_ref, w_own_ref, w_other_ref, keep_ref, *send_refs):
+    def kernel(lhs_ref, w_own_ref, w_other_ref, *out_refs):
+        total = times(lhs_ref[...].reshape(Y * rows, depth), w_own_ref[...], w_other_ref[...])
         for d in range(Y):
-            pair = lhs_ref[2 * d : 2 * d + 2].reshape(2 * rows, depth)
-            total = times(pair, w_own_ref[...], w_other_ref[...])
-            keep_ref[d] = total[:rows]
-            send_refs[d // 2][d % 2] = total[rows:]
-
-    return pl.pallas_call(
-        kernel,
-        in_specs=[VMEM] * 3,
-        out_specs=[VMEM] * 3,
-        out_shape=[jax.ShapeDtypeStruct((n, rows, width), BF16) for n in (Y, Y // 2, Y // 2)],
-        compiler_params=params(32),
-        cost_estimate=pl.CostEstimate(flops=2 * S * rows * depth * width, bytes_accessed=6 * 2**20, transcendentals=0),
+            out_refs[d // 2][d % 2] = total[d * rows : (d + 1) * rows]
+
+    whole = lambda *shape: pl.BlockSpec(shape, lambda i: (0,) * len(shape))
+    return pl.pallas_call(
+        kernel,
+        grid=(1,),
+        in_specs=[pl.BlockSpec((Y, rows, depth), lambda i: (e, 0, 0)), whole(width, depth // 2), whole(width, depth // 2)],
+        out_specs=[whole(2, rows, width)] * 2,
+        out_shape=[jax.ShapeDtypeStruct((2, rows, width), BF16)] * 2,
+        compiler_params=params(16),
+        cost_estimate=pl.CostEstimate(flops=S * rows * depth * width, bytes_accessed=4 * 2**20, transcendentals=0),
     )(lhs, w_own, w_other)
 
 
@@ -162,21 +161,22 @@
 
 
 def add_xl(kept, received):
-    _, rows, width = kept.shape
-
-    def kernel(kept_ref, low_ref, high_ref, *out_refs):
+    _, rows, width = kept[0].shape
+
+    def kernel(*refs):
+        kept_refs, received_refs, out_refs = refs[:2], refs[2:4], refs[4:]
         for d in range(Y):
-            received = (low_ref, high_ref)[d // 2][d % 2]
-            out_refs[d][...] = (kept_ref[d].astype(F32) + received.astype(F32)).astype(BF16)
-
-    return pl.pallas_call(
-        kernel,
-        in_specs=[VMEM] * 3,
+            total = kept_refs[d // 2][d % 2].astype(F32) + received_refs[d // 2][d % 2].astype(F32)
+            out_refs[d][...] = total.astype(BF16)
+
+    return pl.pallas_call(
+        kernel,
+        in_specs=[VMEM] * 4,
         out_specs=[VMEM] * Y,
         out_shape=[jax.ShapeDtypeStruct((rows, width), BF16)] * Y,
         compiler_params=params(16),
         cost_estimate=pl.CostEstimate(flops=Y * rows * width, bytes_accessed=6 * Y * rows * width, transcendentals=0),
-    )(kept, *received)
+    )(*kept, *received)
 
 
 def add_last(parts):
@@ -228,26 +228,29 @@
     own = lax.dynamic_index_in_dim(jnp.asarray(facts()), lax.axis_index(ALL), 0, keepdims=False)
 
     near_own = dequantize(down_q, scales)
-    cut = 5 * BLOCK
-    cross_parts = [shift(near_own[:cut], "xh", XH, 1), shift(near_own[cut:], "xh", XH, 1)]
+    near_other = shift(near_own, "c", C, 1)
+    cut = 4 * BLOCK
+    cross_own = [shift(near_own[:cut], "xh", XH, 1)]
 
     rows = grad_out.shape[0] // 2
-    tokens = [jnp.concatenate([grad_out, shift(grad_out, "c", C, 1)], 1)]
-    around = [(i * C, (i + 1) % Z * C) for i in range(Z)] + [(i * C + 1, (i - 1) % Z * C + 1) for i in range(Z)]
-    tokens[0], _ = lax.optimization_barrier((tokens[0], near_own))
-    for step in range(3):
-        if step == 2:
-            tokens[-1], cross_parts[0] = lax.optimization_barrier((tokens[-1], cross_parts[0]))
-        tokens.append(lax.ppermute(tokens[-1], ("z", "c"), around))
-    tokens[3], cross_parts[1] = lax.optimization_barrier((tokens[3], cross_parts[1]))
-    far = lax.ppermute(lax.dynamic_slice_in_dim(tokens[3], c * rows, rows, 0), ("z", "c"), around)
-    near_other = shift(near_own, "c", C, 1)
-    cross_own = jnp.concatenate(cross_parts, 0)
+    to = lambda k: [(i * C, (i + k) % Z * C) for i in range(Z)] + [(i * C + 1, (i - k) % Z * C + 1) for i in range(Z)]
+    here = jnp.concatenate([grad_out, shift(grad_out, "c", C, 1)], 1)
+    here, _ = lax.optimization_barrier((here, near_own))
+    two = lax.ppermute(here, ("z", "c"), to(2))
+    one = lax.ppermute(here, ("z", "c"), to(1))
+    last, one = lax.optimization_barrier((near_own[cut:], one))
+    cross_own.append(shift(last, "xh", XH, 1))
+    two, cross_own[0] = lax.optimization_barrier((two, cross_own[0]))
+    three = lax.ppermute(two, ("z", "c"), to(1))
+    far = lax.ppermute(lax.dynamic_slice_in_dim(two, c * rows, rows, 0), ("z", "c"), to(2))
+    cross_own, far, three = lax.optimization_barrier((jnp.concatenate(cross_own, 0), far, three))
+    tokens = [here, one, two, three]
     cross_other = shift(cross_own, "c", C, 1)
 
     lhs, *near = product_y(own, tokens, far, near_own, near_other)
     near_y = [near[0]] + [shift(near[d], "y", Y, d) for d in range(1, Y)]
-    kept, *sent = product_xl(lhs, cross_own, cross_other)
+    sent = product_xl(lhs, cross_own, cross_other, 1)
+    kept = product_xl(lhs, cross_own, cross_other, 0)
     cross = add_xl(kept, [shift(part, "xl", XL, 1) for part in sent])
     cross_parts = [cross[0]] + [shift(cross[d], "y", Y, d) for d in range(1, Y)]
     kept, sent = add_y(near_y)

time: 116 us -> 117 us (level)
  waiting for transfers between devices: 70.8 us -> 64.3 us
  starting transfers between devices: 30.3 us -> 35.9 us
    ppermute x14, waiting for transfers between devices: 39.7 us -> 26.8 us  [shift(): return lax.ppermute(x, axis, [(i, (i + by) % size) for i in range(size)])]
    ppermute x4, starting transfers between devices: 2 us -> 11 us  [the longest x1 5.08 us: on_device(): three = lax.ppermute(two, ('z', 'c'), to(1))]
    ppermute x4, waiting for transfers between devices: 8.86 us -> 13.8 us  [on_device(): lax.ppermute(sums[r], ALL, home_pairs(r, h))]
    ppermute x4, starting transfers between devices: 10.9 us -> 6.78 us  [on_device(): lax.ppermute(sums[r], ALL, home_pairs(r, h))]
    unnamed x13 -> x18, local copies, waits for them, and re-layouts: 1.48 us -> 3.29 us
    ppermute x4, waiting for transfers between devices: 22.2 us -> 23.7 us  [the longest x1 12 us: on_device(): lax.ppermute(lax.dynamic_slice_in_dim(two, c * rows, rows, 0), ('z', 'c')...]
    pallas_call x2 -> x3, Pallas kernels: 3.75 us -> 2.78 us  [the longest x2 2.57 us: product_xl(): pl.pallas_call(kernel, grid=(1,), in_specs=[pl.BlockSpec((Y, rows, depth)...]
  transfers between devices with their start and end apart: 22 -> 22, of which waited for: 12 -> 9; matrix products, arithmetic and copies ran while one was open for 3% -> 3% of each run, Pallas kernels for 7% -> 6%
where the time goes in v9:
time: 117 us
  waiting for transfers between devices  64.3 us (55%)
  starting transfers between devices  35.9 us (31%)
  Pallas kernels  8.87 us (8%)
  local copies, waits for them, and re-layouts  5.2 us (4%)
  other arithmetic  1.51 us (1%)
    ppermute x14, waiting for transfers between devices, shift(): return lax.ppermute(x, axis, [(i, (i + by) % size) for i in range(size)])  26.8 us
    ppermute x14, starting transfers between devices, shift(): return lax.ppermute(x, axis, [(i, (i + by) % size) for i in range(size)])  18.2 us
    ppermute x4, waiting for transfers between devices, on_device(): lax.ppermute(sums[r], ALL, home_pairs(r, h))  13.8 us
    ppermute x1, waiting for transfers between devices, on_device(): lax.ppermute(lax.dynamic_slice_in_dim(two, c * rows, rows, 0), ('z', 'c')...  12 us
    ppermute x4, starting transfers between devices, on_device(): lax.ppermute(sums[r], ALL, home_pairs(r, h))  6.78 us
    ppermute x1, waiting for transfers between devices, on_device(): one = lax.ppermute(here, ('z', 'c'), to(1))  6.27 us
    ppermute x1, waiting for transfers between devices, on_device(): two = lax.ppermute(here, ('z', 'c'), to(2))  5.41 us
    ppermute x1, starting transfers between devices, on_device(): three = lax.ppermute(two, ('z', 'c'), to(1))  5.08 us
  transfers between devices with their start and end apart: 22, of which 9 were waited for; matrix products, arithmetic and copies ran while one was open for 3% of the time, Pallas kernels for 6%

profile of v9, /device:TPU:6, one launch (start us, length us, event | category | flops | bytes accessed | tf_op | source)
XLA Modules:
  0.0 116.7 jit_solution(14059287363637153983)
XLA Ops:
  0.6 0.1 collective-permute-start
  0.7 0.8 copy.8
  1.6 0.3 mul.30
  1.9 0.0 copy-start.8
  1.9 0.4 fusion.w_own_ref
  2.3 0.2 collective-permute-done
  2.5 0.4 copy-done.8
  2.8 0.1 pad_maximum_fusion.1.t0
  2.9 2.0 %collective-permute-start.1 = (bf16[256,1024]{1,0:T(8,128)(2,1)S(1)}, bf16[256,1024]{1,0:T(8,128)(2,1)S(1)}, u32[]{:S(2)}, u32[]{:S(2)}) collective-permute-start(bf16[256,1024]{1,0:T(8,128)(2,1)S(1)} %pad_maximum_fusion.1.t0), channel_id=1, source_target_pairs={{0,32},{32,64},{64,96},{96,128},{128,160},{160,192},{192,224},{224... | collective-permute-start | bytes 1572872 | tf_op jit(solution)/shard_map/ppermute | solution.py:240
  4.9 1.5 %collective-permute-start.3 = (bf16[512,512]{1,0:T(8,128)(2,1)S(1)}, bf16[512,512]{1,0:T(8,128)(2,1)S(1)}, u32[]{:S(2)}, u32[]{:S(2)}) collective-permute-start(bf16[512,512]{1,0:T(8,128)(2,1)S(1)} %slice.9), channel_id=1, source_target_pairs={{0,16},{16,0},{1,17},{17,1},{2,18},{18,2},{3,19},{19,3},{4,20},{20... | collective-permute-start | bytes 1572872 | tf_op jit(solution)/shard_map/ppermute | solution.py:72
  6.4 3.3 %collective-permute-start.2 = (bf16[256,1024]{1,0:T(8,128)(2,1)S(1)}, bf16[256,1024]{1,0:T(8,128)(2,1)S(1)}, u32[]{:S(2)}, u32[]{:S(2)}) collective-permute-start(bf16[256,1024]{1,0:T(8,128)(2,1)S(1)} %pad_maximum_fusion.1.t0), channel_id=1, source_target_pairs={{0,64},{32,96},{64,128},{96,160},{128,192},{160,224},{192,0},{224,... | collective-permute-start | bytes 1572872 | tf_op jit(solution)/shard_map/ppermute | solution.py:239
  9.7 6.3 %collective-permute-done.1.t1 = bf16[256,1024]{1,0:T(8,128)(2,1)S(1)} collective-permute-done((bf16[256,1024]{1,0:T(8,128)(2,1)S(1)}, bf16[256,1024]{1,0:T(8,128)(2,1)S(1)}, u32[]{:S(2)}, u32[]{:S(2)}) %collective-permute-start.1) | collective-permute-done | bytes 524320 | tf_op jit(solution)/shard_map/ppermute | solution.py:240
  16.0 0.8 copy-done.4
  16.8 1.4 %collective-permute-start.4 = (bf16[384,512]{1,0:T(8,128)(2,1)S(1)}, bf16[384,512]{1,0:T(8,128)(2,1)S(1)}, u32[]{:S(2)}, u32[]{:S(2)}) collective-permute-start(bf16[384,512]{1,0:T(8,128)(2,1)S(1)} %slice.8), channel_id=1, source_target_pairs={{0,16},{16,0},{1,17},{17,1},{2,18},{18,2},{3,19},{19,3},{4,20},{20... | collective-permute-start | bytes 1179656 | tf_op jit(solution)/shard_map/ppermute | solution.py:72
  18.2 5.4 %collective-permute-done.2.t2 = bf16[256,1024]{1,0:T(8,128)(2,1)S(1)} collective-permute-done((bf16[256,1024]{1,0:T(8,128)(2,1)S(1)}, bf16[256,1024]{1,0:T(8,128)(2,1)S(1)}, u32[]{:S(2)}, u32[]{:S(2)}) %collective-permute-start.2) | collective-permute-done | bytes 524320 | tf_op jit(solution)/shard_map/ppermute | solution.py:239
  23.6 5.1 %collective-permute-start.6 = (bf16[256,1024]{1,0:T(8,128)(2,1)S(1)}, bf16[256,1024]{1,0:T(8,128)(2,1)}, u32[]{:S(2)}, u32[]{:S(2)}) collective-permute-start(bf16[256,1024]{1,0:T(8,128)(2,1)S(1)} %collective-permute-done.2.t2), channel_id=1, source_target_pairs={{0,32},{32,64},{64,96},{96,128},{128,160},{160,192},{192,224},{224... | collective-permute-start | bytes 1572872 | tf_op jit(solution)/shard_map/ppermute | solution.py:244
  28.7 0.6 collective-permute-start.5
  29.3 1.4 %collective-permute-start.7 = (bf16[896,512]{1,0:T(8,128)(2,1)S(1)}, bf16[896,512]{1,0:T(8,128)(2,1)}, u32[]{:S(2)}, u32[]{:S(2)}) collective-permute-start(bf16[896,512]{1,0:T(8,128)(2,1)S(1)} %fusion.w_own_ref), channel_id=1, source_target_pairs={{0,1},{1,0},{2,3},{3,2},{4,5},{5,4},{6,7},{7,6},{8,9},{9,8},{10,11... | collective-permute-start | bytes 2752520 | tf_op jit(solution)/shard_map/ppermute | solution.py:72
  30.8 1.1 pad_maximum_fusion.w_own_ref
  31.9 12.0 %collective-permute-done.5.far_ref = bf16[128,1024]{1,0:T(8,128)(2,1)S(1)} collective-permute-done((bf16[128,1024]{1,0:T(8,128)(2,1)S(1)}, bf16[128,1024]{1,0:T(8,128)(2,1)S(1)}, u32[]{:S(2)}, u32[]{:S(2)}) %collective-permute-start.5) | collective-permute-done | bytes 262176 | tf_op jit(solution)/shard_map/ppermute | solution.py:245
  44.0 0.7 dynamic-slice_bitcast_fusion.facts_ref
  44.7 1.0 copy-done.3
  45.7 1.0 copy-done.5
  46.8 3.8 %shard_map.77 = (bf16[8,128,1024]{2,1,0:T(8,128)(2,1)S(1)}, bf16[2,128,896]{2,1,0:T(8,128)(2,1)S(1)}, bf16[2,128,896]{2,1,0:T(8,128)(2,1)S(1)}, bf16[2,128,896]{2,1,0:T(8,128)(2,1)S(1)}, bf16[2,128,896]{2,1,0:T(8,128)(2,1)S(1)}) custom-call(s32[10]{0:T(128)S(1)} %dynamic-slice_bitcast_fusion.facts_ref, bf16[256,1024]{1,0:T(8,128)(2,1)S(1)} %pad_maximum_fusion.1.t0, ...), custom_call_target="tpu_custom_call" | custom-call | flops 1879048192 | bytes 8388608 | tf_op jit(solution)/shard_map/pallas_call | solution.py:111
  50.6 3.1 %collective-permute-start.10 = (bf16[2,128,896]{2,1,0:T(8,128)(2,1)S(1)}, bf16[2,128,896]{2,1,0:T(8,128)(2,1)S(1)}, u32[]{:S(2)}, u32[]{:S(2)}) collective-permute-start(bf16[2,128,896]{2,1,0:T(8,128)(2,1)S(1)} %get-tuple-element.35), channel_id=1, source_target_pairs={{0,6},{2,0},{4,2},{6,4},{1,7},{3,1},{5,3},{7,5},{8,14},{10,8},{12,... | collective-permute-start | bytes 1376264 | tf_op jit(solution)/shard_map/ppermute | solution.py:72
  53.7 2.2 %collective-permute-start.9 = (bf16[2,128,896]{2,1,0:T(8,128)(2,1)S(1)}, bf16[2,128,896]{2,1,0:T(8,128)(2,1)S(1)}, u32[]{:S(2)}, u32[]{:S(2)}) collective-permute-start(bf16[2,128,896]{2,1,0:T(8,128)(2,1)S(1)} %get-tuple-element.34), channel_id=1, source_target_pairs={{0,4},{2,6},{4,0},{6,2},{1,5},{3,7},{5,1},{7,3},{8,12},{10,14},{12... | collective-permute-start | bytes 1376264 | tf_op jit(solution)/shard_map/ppermute | solution.py:72
  55.9 1.3 %shard_map.81 = (bf16[2,128,896]{2,1,0:T(8,128)(2,1)S(1)}, bf16[2,128,896]{2,1,0:T(8,128)(2,1)S(1)}) custom-call(bf16[8,128,1024]{2,1,0:T(8,128)(2,1)S(1)} %get-tuple-element.38.lhs_ref, bf16[896,512]{1,0:T(8,128)(2,1)S(1)} %pad_maximum_fusion.w_own_ref, bf16[896,512]{1,0:T(8,128)(2,1)S(1)} %collective-permute-done.14.w_other_ref), custom_call_target="tpu_custom_call" | custom-call | flops 939524096 | bytes 4194304 | tf_op jit(solution)/shard_map/pallas_call | solution.py:132
  57.2 0.9 collective-permute-start.15
  58.1 1.2 %collective-permute-start.16 = (bf16[2,128,896]{2,1,0:T(8,128)(2,1)S(1)}, bf16[2,128,896]{2,1,0:T(8,128)(2,1)S(1)}, u32[]{:S(2)}, u32[]{:S(2)}) collective-permute-start(bf16[2,128,896]{2,1,0:T(8,128)(2,1)S(1)} %get-tuple-element.43), channel_id=1, source_target_pairs={{0,8},{8,0},{1,9},{9,1},{2,10},{10,2},{3,11},{11,3},{4,12},{12,4},... | collective-permute-start | bytes 1376264 | tf_op jit(solution)/shard_map/ppermute | solution.py:72
  59.3 14.6 %collective-permute-done.10.refs_3_ = bf16[2,128,896]{2,1,0:T(8,128)(2,1)S(1)} collective-permute-done((bf16[2,128,896]{2,1,0:T(8,128)(2,1)S(1)}, bf16[2,128,896]{2,1,0:T(8,128)(2,1)S(1)}, u32[]{:S(2)}, u32[]{:S(2)}) %collective-permute-start.10) | collective-permute-done | bytes 458784 | tf_op jit(solution)/shard_map/ppermute | solution.py:72
  73.9 3.4 %collective-permute-done.8.refs_1_ = bf16[2,128,896]{2,1,0:T(8,128)(2,1)S(1)} collective-permute-done((bf16[2,128,896]{2,1,0:T(8,128)(2,1)S(1)}, bf16[2,128,896]{2,1,0:T(8,128)(2,1)S(1)}, u32[]{:S(2)}, u32[]{:S(2)}) %collective-permute-start.8) | collective-permute-done | bytes 458784 | tf_op jit(solution)/shard_map/ppermute | solution.py:72
  77.4 0.2 shard_map.78
  77.6 0.9 collective-permute-start.11
  78.5 1.3 %shard_map.80 = (bf16[2,128,896]{2,1,0:T(8,128)(2,1)S(1)}, bf16[2,128,896]{2,1,0:T(8,128)(2,1)S(1)}) custom-call(bf16[8,128,1024]{2,1,0:T(8,128)(2,1)S(1)} %get-tuple-element.38.lhs_ref, bf16[896,512]{1,0:T(8,128)(2,1)S(1)} %pad_maximum_fusion.w_own_ref, bf16[896,512]{1,0:T(8,128)(2,1)S(1)} %collective-permute-done.14.w_other_ref), custom_call_target="tpu_custom_call" | custom-call | flops 939524096 | bytes 4194304 | tf_op jit(solution)/shard_map/pallas_call | solution.py:132
  79.8 0.0 copy-start
  79.8 0.2 shard_map.82
  80.1 2.7 %collective-permute-start.17 = (bf16[128,896]{1,0:T(8,128)(2,1)S(1)}, bf16[128,896]{1,0:T(8,128)(2,1)S(1)}, u32[]{:S(2)}, u32[]{:S(2)}) collective-permute-start(bf16[128,896]{1,0:T(8,128)(2,1)S(1)} %get-tuple-element.45), channel_id=1, source_target_pairs={{0,2},{2,4},{4,6},{6,0},{1,3},{3,5},{5,7},{7,1},{8,10},{10,12},{12... | collective-permute-start | bytes 688136 | tf_op jit(solution)/shard_map/ppermute | solution.py:72
  82.7 2.8 %collective-permute-start.19 = (bf16[128,896]{1,0:T(8,128)(2,1)S(1)}, bf16[128,896]{1,0:T(8,128)(2,1)S(1)}, u32[]{:S(2)}, u32[]{:S(2)}) collective-permute-start(bf16[128,896]{1,0:T(8,128)(2,1)S(1)} %get-tuple-element.47), channel_id=1, source_target_pairs={{0,6},{2,0},{4,2},{6,4},{1,7},{3,1},{5,3},{7,5},{8,14},{10,8},{12,... | collective-permute-start | bytes 688136 | tf_op jit(solution)/shard_map/ppermute | solution.py:72
  85.5 0.1 shard_map.79
  85.6 0.7 collective-permute-start.12
  86.2 2.6 %collective-permute-start.13 = (bf16[128,896]{1,0:T(8,128)(2,1)S(1)}, bf16[128,896]{1,0:T(8,128)(2,1)S(1)}, u32[]{:S(2)}, u32[]{:S(2)}) collective-permute-start(bf16[128,896]{1,0:T(8,128)(2,1)S(1)} %shard_map.79), channel_id=1, source_target_pairs={{0,224},{1,128},{4,160},{5,32},{7,64},{8,192},{9,96},{15,0},{16,24... | collective-permute-start | bytes 688136 | tf_op jit(solution)/shard_map/ppermute | solution.py:260
  88.8 4.0 %collective-permute-done.17.refs_1_ = bf16[128,896]{1,0:T(8,128)(2,1)S(1)} collective-permute-done((bf16[128,896]{1,0:T(8,128)(2,1)S(1)}, bf16[128,896]{1,0:T(8,128)(2,1)S(1)}, u32[]{:S(2)}, u32[]{:S(2)}) %collective-permute-start.17) | collective-permute-done | bytes 229408 | tf_op jit(solution)/shard_map/ppermute | solution.py:72
  92.9 4.5 %collective-permute-done.19.refs_3_ = bf16[128,896]{1,0:T(8,128)(2,1)S(1)} collective-permute-done((bf16[128,896]{1,0:T(8,128)(2,1)S(1)}, bf16[128,896]{1,0:T(8,128)(2,1)S(1)}, u32[]{:S(2)}, u32[]{:S(2)}) %collective-permute-start.19) | collective-permute-done | bytes 229408 | tf_op jit(solution)/shard_map/ppermute | solution.py:72
  97.4 0.1 shard_map.83
  97.5 1.3 %collective-permute-start.20 = (bf16[128,896]{1,0:T(8,128)(2,1)S(1)}, bf16[128,896]{1,0:T(8,128)(2,1)S(1)}, u32[]{:S(2)}, u32[]{:S(2)}) collective-permute-start(bf16[128,896]{1,0:T(8,128)(2,1)S(1)} %shard_map.83), channel_id=1, source_target_pairs={{2,161},{3,65},{6,225},{10,1},{11,33},{12,193},{13,97},{14,129},{1... | collective-permute-start | bytes 688136 | tf_op jit(solution)/shard_map/ppermute | solution.py:260
  98.8 2.2 %collective-permute-start.21 = (bf16[128,896]{1,0:T(8,128)(2,1)S(1)}, bf16[128,896]{1,0:T(8,128)(2,1)S(1)}, u32[]{:S(2)}, u32[]{:S(2)}) collective-permute-start(bf16[128,896]{1,0:T(8,128)(2,1)S(1)} %shard_map.83), channel_id=1, source_target_pairs={{0,225},{1,129},{4,161},{5,33},{7,65},{8,193},{9,97},{15,1},{16,24... | collective-permute-start | bytes 688136 | tf_op jit(solution)/shard_map/ppermute | solution.py:260
  101.0 13.8 %collective-permute-done.20.cross0 = bf16[128,896]{1,0:T(8,128)(2,1)S(1)} collective-permute-done((bf16[128,896]{1,0:T(8,128)(2,1)S(1)}, bf16[128,896]{1,0:T(8,128)(2,1)S(1)}, u32[]{:S(2)}, u32[]{:S(2)}) %collective-permute-start.20) | collective-permute-done | bytes 229408 | tf_op jit(solution)/shard_map/ppermute | solution.py:260
  114.8 1.9 %shard_map.84 = (bf16[256,896]{1,0:T(8,128)(2,1)}, bf16[256,896]{1,0:T(8,128)(2,1)}) custom-call(s32[10]{0:T(128)S(1)} %dynamic-slice_bitcast_fusion.facts_ref, bf16[128,896]{1,0:T(8,128)(2,1)S(1)} %collective-permute-done.12.near0, bf16[128,896]{1,0:T(8,128)(2,1)S(1)} %collective-permute-done.13.near1, bf16[128,896]{1,0:T(8,128)(2,1)S(1)} %collective-permute-done.20.cross0, ...), custom_call_target="tpu_custom_call" | custom-call | flops 2293760 | bytes 2293760 | tf_op jit(solution)/shard_map/pallas_call | solution.py:216
  (31 shorter events, 0.1 us)
Async XLA Ops:
  0.6 1.3 %copy-start.6 = (bf16[896,512]{1,0:T(8,128)(2,1)S(1)}, bf16[896,512]{1,0:T(8,128)(2,1)}, u32[]{:S(2)}) copy-start(bf16[896,512]{1,0:T(8,128)(2,1)} %param.7) | copy-start | bytes 2752516
  0.6 1.8 %collective-permute-start = (bf16[256,512]{1,0:T(8,128)(2,1)}, bf16[256,512]{1,0:T(8,128)(2,1)S(1)}, u32[]{:S(2)}, u32[]{:S(2)}) collective-permute-start(bf16[256,512]{1,0:T(8,128)(2,1)} %param.6), channel_id=1, source_target_pairs={{0,1},{1,0},{2,3},{3,2},{4,5},{5,4},{6,7},{7,6},{8,9},{9,8},{10,11... | collective-permute-start | bytes 786440 | tf_op jit(solution)/shard_map/ppermute | solution.py:72
  1.9 1.0 copy-start.8
  2.9 13.1 %collective-permute-start.1 = (bf16[256,1024]{1,0:T(8,128)(2,1)S(1)}, bf16[256,1024]{1,0:T(8,128)(2,1)S(1)}, u32[]{:S(2)}, u32[]{:S(2)}) collective-permute-start(bf16[256,1024]{1,0:T(8,128)(2,1)S(1)} %pad_maximum_fusion.1.t0), channel_id=1, source_target_pairs={{0,32},{32,64},{64,96},{96,128},{128,160},{160,192},{192,224},{224... | collective-permute-start | bytes 1572872 | tf_op jit(solution)/shard_map/ppermute | solution.py:240
  4.9 13.3 %collective-permute-start.3 = (bf16[512,512]{1,0:T(8,128)(2,1)S(1)}, bf16[512,512]{1,0:T(8,128)(2,1)S(1)}, u32[]{:S(2)}, u32[]{:S(2)}) collective-permute-start(bf16[512,512]{1,0:T(8,128)(2,1)S(1)} %slice.9), channel_id=1, source_target_pairs={{0,16},{16,0},{1,17},{17,1},{2,18},{18,2},{3,19},{19,3},{4,20},{20... | collective-permute-start | bytes 1572872 | tf_op jit(solution)/shard_map/ppermute | solution.py:72
  6.4 17.2 %collective-permute-start.2 = (bf16[256,1024]{1,0:T(8,128)(2,1)S(1)}, bf16[256,1024]{1,0:T(8,128)(2,1)S(1)}, u32[]{:S(2)}, u32[]{:S(2)}) collective-permute-start(bf16[256,1024]{1,0:T(8,128)(2,1)S(1)} %pad_maximum_fusion.1.t0), channel_id=1, source_target_pairs={{0,64},{32,96},{64,128},{96,160},{128,192},{160,224},{192,0},{224,... | collective-permute-start | bytes 1572872 | tf_op jit(solution)/shard_map/ppermute | solution.py:239
  16.0 0.8 copy-start.4
  16.8 14.0 %collective-permute-start.4 = (bf16[384,512]{1,0:T(8,128)(2,1)S(1)}, bf16[384,512]{1,0:T(8,128)(2,1)S(1)}, u32[]{:S(2)}, u32[]{:S(2)}) collective-permute-start(bf16[384,512]{1,0:T(8,128)(2,1)S(1)} %slice.8), channel_id=1, source_target_pairs={{0,16},{16,0},{1,17},{17,1},{2,18},{18,2},{3,19},{19,3},{4,20},{20... | collective-permute-start | bytes 1179656 | tf_op jit(solution)/shard_map/ppermute | solution.py:72
  18.2 5.4 %copy-start.7 = (bf16[512,512]{1,0:T(8,128)(2,1)}, bf16[512,512]{1,0:T(8,128)(2,1)S(1)}, u32[]{:S(2)}) copy-start(bf16[512,512]{1,0:T(8,128)(2,1)S(1)} %collective-permute-done.3) | copy-start | bytes 1572868
  23.6 20.3 %copy-start.2 = (bf16[256,1024]{1,0:T(8,128)(2,1)}, bf16[256,1024]{1,0:T(8,128)(2,1)S(1)}, u32[]{:S(2)}) copy-start(bf16[256,1024]{1,0:T(8,128)(2,1)S(1)} %collective-permute-done.2.t2) | copy-start | bytes 1572868
  23.6 20.3 %collective-permute-start.6 = (bf16[256,1024]{1,0:T(8,128)(2,1)S(1)}, bf16[256,1024]{1,0:T(8,128)(2,1)}, u32[]{:S(2)}, u32[]{:S(2)}) collective-permute-start(bf16[256,1024]{1,0:T(8,128)(2,1)S(1)} %collective-permute-done.2.t2), channel_id=1, source_target_pairs={{0,32},{32,64},{64,96},{96,128},{128,160},{160,192},{192,224},{224... | collective-permute-start | bytes 1572872 | tf_op jit(solution)/shard_map/ppermute | solution.py:244
  28.7 15.2 %collective-permute-start.5 = (bf16[128,1024]{1,0:T(8,128)(2,1)S(1)}, bf16[128,1024]{1,0:T(8,128)(2,1)S(1)}, u32[]{:S(2)}, u32[]{:S(2)}) collective-permute-start(bf16[128,1024]{1,0:T(8,128)(2,1)S(1)} %constant_dynamic-slice_fusion), channel_id=1, source_target_pairs={{0,64},{32,96},{64,128},{96,160},{128,192},{160,224},{192,0},{224,... | collective-permute-start | bytes 786440 | tf_op jit(solution)/shard_map/ppermute | solution.py:245
  29.3 15.3 %collective-permute-start.7 = (bf16[896,512]{1,0:T(8,128)(2,1)S(1)}, bf16[896,512]{1,0:T(8,128)(2,1)}, u32[]{:S(2)}, u32[]{:S(2)}) collective-permute-start(bf16[896,512]{1,0:T(8,128)(2,1)S(1)} %fusion.w_own_ref), channel_id=1, source_target_pairs={{0,1},{1,0},{2,3},{3,2},{4,5},{5,4},{6,7},{7,6},{8,9},{9,8},{10,11... | collective-permute-start | bytes 2752520 | tf_op jit(solution)/shard_map/ppermute | solution.py:72
  44.0 11.9 %collective-permute-start.14 = (bf16[896,512]{1,0:T(8,128)(2,1)S(1)}, bf16[896,512]{1,0:T(8,128)(2,1)S(1)}, u32[]{:S(2)}, u32[]{:S(2)}) collective-permute-start(bf16[896,512]{1,0:T(8,128)(2,1)S(1)} %pad_maximum_fusion.w_own_ref), channel_id=1, source_target_pairs={{0,1},{1,0},{2,3},{3,2},{4,5},{5,4},{6,7},{7,6},{8,9},{9,8},{10,11... | collective-permute-start | bytes 2752520 | tf_op jit(solution)/shard_map/ppermute | solution.py:72
  44.7 1.0 copy-start.3
  45.7 1.0 copy-start.5
  50.6 23.3 %collective-permute-start.10 = (bf16[2,128,896]{2,1,0:T(8,128)(2,1)S(1)}, bf16[2,128,896]{2,1,0:T(8,128)(2,1)S(1)}, u32[]{:S(2)}, u32[]{:S(2)}) collective-permute-start(bf16[2,128,896]{2,1,0:T(8,128)(2,1)S(1)} %get-tuple-element.35), channel_id=1, source_target_pairs={{0,6},{2,0},{4,2},{6,4},{1,7},{3,1},{5,3},{7,5},{8,14},{10,8},{12,... | collective-permute-start | bytes 1376264 | tf_op jit(solution)/shard_map/ppermute | solution.py:72
  53.7 23.7 %collective-permute-start.8 = (bf16[2,128,896]{2,1,0:T(8,128)(2,1)S(1)}, bf16[2,128,896]{2,1,0:T(8,128)(2,1)S(1)}, u32[]{:S(2)}, u32[]{:S(2)}) collective-permute-start(bf16[2,128,896]{2,1,0:T(8,128)(2,1)S(1)} %get-tuple-element.33), channel_id=1, source_target_pairs={{0,2},{2,4},{4,6},{6,0},{1,3},{3,5},{5,7},{7,1},{8,10},{10,12},{12... | collective-permute-start | bytes 1376264 | tf_op jit(solution)/shard_map/ppermute | solution.py:72
  53.7 23.7 %collective-permute-start.9 = (bf16[2,128,896]{2,1,0:T(8,128)(2,1)S(1)}, bf16[2,128,896]{2,1,0:T(8,128)(2,1)S(1)}, u32[]{:S(2)}, u32[]{:S(2)}) collective-permute-start(bf16[2,128,896]{2,1,0:T(8,128)(2,1)S(1)} %get-tuple-element.34), channel_id=1, source_target_pairs={{0,4},{2,6},{4,0},{6,2},{1,5},{3,7},{5,1},{7,3},{8,12},{10,14},{12... | collective-permute-start | bytes 1376264 | tf_op jit(solution)/shard_map/ppermute | solution.py:72
  57.2 22.6 %collective-permute-start.15 = (bf16[2,128,896]{2,1,0:T(8,128)(2,1)S(1)}, bf16[2,128,896]{2,1,0:T(8,128)(2,1)S(1)}, u32[]{:S(2)}, u32[]{:S(2)}) collective-permute-start(bf16[2,128,896]{2,1,0:T(8,128)(2,1)S(1)} %get-tuple-element.42), channel_id=1, source_target_pairs={{0,8},{8,0},{1,9},{9,1},{2,10},{10,2},{3,11},{11,3},{4,12},{12,4},... | collective-permute-start | bytes 1376264 | tf_op jit(solution)/shard_map/ppermute | solution.py:72
  58.1 21.7 %collective-permute-start.16 = (bf16[2,128,896]{2,1,0:T(8,128)(2,1)S(1)}, bf16[2,128,896]{2,1,0:T(8,128)(2,1)S(1)}, u32[]{:S(2)}, u32[]{:S(2)}) collective-permute-start(bf16[2,128,896]{2,1,0:T(8,128)(2,1)S(1)} %get-tuple-element.43), channel_id=1, source_target_pairs={{0,8},{8,0},{1,9},{9,1},{2,10},{10,2},{3,11},{11,3},{4,12},{12,4},... | collective-permute-start | bytes 1376264 | tf_op jit(solution)/shard_map/ppermute | solution.py:72
  77.6 7.9 %collective-permute-start.11 = (bf16[128,896]{1,0:T(8,128)(2,1)S(1)}, bf16[128,896]{1,0:T(8,128)(2,1)S(1)}, u32[]{:S(2)}, u32[]{:S(2)}) collective-permute-start(bf16[128,896]{1,0:T(8,128)(2,1)S(1)} %get-tuple-element.37), channel_id=1, source_target_pairs={{0,8},{8,0},{1,9},{9,1},{2,10},{10,2},{3,11},{11,3},{4,12},{12,4},... | collective-permute-start | bytes 688136 | tf_op jit(solution)/shard_map/ppermute | solution.py:72
  79.8 35.0 %copy-start = (bf16[256,896]{1,0:T(8,128)(2,1)S(1)}, bf16[256,896]{1,0:T(8,128)(2,1)}, u32[]{:S(2)}) copy-start(bf16[256,896]{1,0:T(8,128)(2,1)} %gate_ref.1) | copy-start | bytes 1376260
  79.8 35.0 %copy-start.1 = (bf16[256,896]{1,0:T(8,128)(2,1)S(1)}, bf16[256,896]{1,0:T(8,128)(2,1)}, u32[]{:S(2)}) copy-start(bf16[256,896]{1,0:T(8,128)(2,1)} %up_ref.1) | copy-start | bytes 1376260
  80.1 12.8 %collective-permute-start.17 = (bf16[128,896]{1,0:T(8,128)(2,1)S(1)}, bf16[128,896]{1,0:T(8,128)(2,1)S(1)}, u32[]{:S(2)}, u32[]{:S(2)}) collective-permute-start(bf16[128,896]{1,0:T(8,128)(2,1)S(1)} %get-tuple-element.45), channel_id=1, source_target_pairs={{0,2},{2,4},{4,6},{6,0},{1,3},{3,5},{5,7},{7,1},{8,10},{10,12},{12... | collective-permute-start | bytes 688136 | tf_op jit(solution)/shard_map/ppermute | solution.py:72
  82.7 10.2 %collective-permute-start.18 = (bf16[128,896]{1,0:T(8,128)(2,1)S(1)}, bf16[128,896]{1,0:T(8,128)(2,1)S(1)}, u32[]{:S(2)}, u32[]{:S(2)}) collective-permute-start(bf16[128,896]{1,0:T(8,128)(2,1)S(1)} %get-tuple-element.46), channel_id=1, source_target_pairs={{0,4},{2,6},{4,0},{6,2},{1,5},{3,7},{5,1},{7,3},{8,12},{10,14},{12... | collective-permute-start | bytes 688136 | tf_op jit(solution)/shard_map/ppermute | solution.py:72
  82.7 14.6 %collective-permute-start.19 = (bf16[128,896]{1,0:T(8,128)(2,1)S(1)}, bf16[128,896]{1,0:T(8,128)(2,1)S(1)}, u32[]{:S(2)}, u32[]{:S(2)}) collective-permute-start(bf16[128,896]{1,0:T(8,128)(2,1)S(1)} %get-tuple-element.47), channel_id=1, source_target_pairs={{0,6},{2,0},{4,2},{6,4},{1,7},{3,1},{5,3},{7,5},{8,14},{10,8},{12,... | collective-permute-start | bytes 688136 | tf_op jit(solution)/shard_map/ppermute | solution.py:72
  85.6 15.4 %collective-permute-start.12 = (bf16[128,896]{1,0:T(8,128)(2,1)S(1)}, bf16[128,896]{1,0:T(8,128)(2,1)S(1)}, u32[]{:S(2)}, u32[]{:S(2)}) collective-permute-start(bf16[128,896]{1,0:T(8,128)(2,1)S(1)} %shard_map.79), channel_id=1, source_target_pairs={{2,160},{3,64},{6,224},{10,0},{11,32},{12,192},{13,96},{14,128},{1... | collective-permute-start | bytes 688136 | tf_op jit(solution)/shard_map/ppermute | solution.py:260
  86.2 14.8 %collective-permute-start.13 = (bf16[128,896]{1,0:T(8,128)(2,1)S(1)}, bf16[128,896]{1,0:T(8,128)(2,1)S(1)}, u32[]{:S(2)}, u32[]{:S(2)}) collective-permute-start(bf16[128,896]{1,0:T(8,128)(2,1)S(1)} %shard_map.79), channel_id=1, source_target_pairs={{0,224},{1,128},{4,160},{5,32},{7,64},{8,192},{9,96},{15,0},{16,24... | collective-permute-start | bytes 688136 | tf_op jit(solution)/shard_map/ppermute | solution.py:260
  97.5 17.4 %collective-permute-start.20 = (bf16[128,896]{1,0:T(8,128)(2,1)S(1)}, bf16[128,896]{1,0:T(8,128)(2,1)S(1)}, u32[]{:S(2)}, u32[]{:S(2)}) collective-permute-start(bf16[128,896]{1,0:T(8,128)(2,1)S(1)} %shard_map.83), channel_id=1, source_target_pairs={{2,161},{3,65},{6,225},{10,1},{11,33},{12,193},{13,97},{14,129},{1... | collective-permute-start | bytes 688136 | tf_op jit(solution)/shard_map/ppermute | solution.py:260
  98.8 16.1 %collective-permute-start.21 = (bf16[128,896]{1,0:T(8,128)(2,1)S(1)}, bf16[128,896]{1,0:T(8,128)(2,1)S(1)}, u32[]{:S(2)}, u32[]{:S(2)}) collective-permute-start(bf16[128,896]{1,0:T(8,128)(2,1)S(1)} %shard_map.83), channel_id=1, source_target_pairs={{0,225},{1,129},{4,161},{5,33},{7,65},{8,193},{9,97},{15,1},{16,24... | collective-permute-start | bytes 688136 | tf_op jit(solution)/shard_map/ppermute | solution.py:260

commit v10 on v8

--- a/solution.py
+++ b/solution.py
@@ -15,7 +15,6 @@
 BF16, F32 = jnp.bfloat16, jnp.float32
 VMEM = pl.BlockSpec(memory_space=pltpu.VMEM)
 SMEM = pl.BlockSpec(memory_space=pltpu.SMEM)
-HBM = pl.BlockSpec(memory_space=pltpu.MemorySpace.HBM)
 
 NUMBER = (
     ((2, 5, 6, 1, 4, 0, 3, 7), (7, 3, 2, 4, 6, 1, 5, 0)),
@@ -93,19 +92,43 @@
     return pltpu.CompilerParams(vmem_limit_bytes=mib * 2**20)
 
 
-def product_y(own, tokens, far, w_own, w_other):
+def times_pieces(lhs, w_refs):
+    count = len(w_refs) // 2
+    return jnp.concatenate([times(lhs, w_refs[i][...], w_refs[count + i][...]) for i in range(count)], 1)
+
+
+def product_send(own, tokens, far, weights):
     rows, depth = far.shape
+    width = sum(w.shape[0] for w in weights) // 2
+    count = len(weights)
+
+    def kernel(facts_ref, t0, t1, t2, t3, far_ref, *refs):
+        w_refs, lhs_ref, send_refs = refs[:count], refs[count], refs[count + 1 :]
+        lhs_ref[facts_ref[0]] = t0[pl.ds(pl.multiple_of(facts_ref[S] * rows, rows), rows), :]
+        for i, ref in enumerate((t1, t2, t3)):
+            for h in range(2):
+                lhs_ref[facts_ref[1 + 2 * i + h]] = ref[h * rows : (h + 1) * rows, :]
+        lhs_ref[facts_ref[7]] = far_ref[...]
+        total = times_pieces(lhs_ref[Y:].reshape(Y * rows, depth), w_refs)
+        for d in range(Y):
+            send_refs[d // 2][d % 2] = total[d * rows : (d + 1) * rows]
+
+    return pl.pallas_call(
+        kernel,
+        in_specs=[SMEM] + [VMEM] * (5 + count),
+        out_specs=[VMEM] * 3,
+        out_shape=[jax.ShapeDtypeStruct((S, rows, depth), BF16)]
+        + [jax.ShapeDtypeStruct((2, rows, width), BF16)] * 2,
+        compiler_params=params(32),
+        cost_estimate=pl.CostEstimate(flops=S * rows * depth * width, bytes_accessed=7 * 2**20, transcendentals=0),
+    )(own, *tokens, far, *weights)
+
+
+def product_y(lhs, w_own, w_other):
+    _, rows, depth = lhs.shape
     width = w_own.shape[0]
 
-    def kernel(facts_ref, t0, t1, t2, t3, far_ref, w_own_ref, w_other_ref, lhs_ref, *refs):
-        out_refs, sems = refs[:Y], refs[Y]
-        blocks = [t0.at[pl.ds(pl.multiple_of(facts_ref[S] * rows, rows), rows), :]]
-        blocks += [ref.at[h * rows : (h + 1) * rows, :] for ref in (t1, t2, t3) for h in range(2)] + [far_ref]
-        copies = [pltpu.make_async_copy(block, lhs_ref.at[facts_ref[i]], sems.at[i]) for i, block in enumerate(blocks)]
-        for copy in copies:
-            copy.start()
-        for copy in copies:
-            copy.wait()
+    def kernel(lhs_ref, w_own_ref, w_other_ref, *out_refs):
         for e in range(2):
             total = times(lhs_ref[Y * e : Y * e + Y].reshape(Y * rows, depth), w_own_ref[...], w_other_ref[...])
             for d in range(Y):
@@ -113,35 +136,34 @@
 
     return pl.pallas_call(
         kernel,
-        in_specs=[SMEM] + [HBM] * 5 + [VMEM] * 2,
-        out_specs=[VMEM] * (1 + Y),
-        out_shape=[jax.ShapeDtypeStruct((S, rows, depth), BF16)]
-        + [jax.ShapeDtypeStruct((2, rows, width), BF16)] * Y,
-        scratch_shapes=[pltpu.SemaphoreType.DMA((S,))],
-        compiler_params=params(56),
-        cost_estimate=pl.CostEstimate(flops=2 * S * rows * depth * width, bytes_accessed=8 * 2**20, transcendentals=0),
-    )(own, *tokens, far, w_own, w_other)
-
-
-def product_xl(lhs, w_own, w_other, e):
+        in_specs=[VMEM] * 3,
+        out_specs=[VMEM] * Y,
+        out_shape=[jax.ShapeDtypeStruct((2, rows, width), BF16)] * Y,
+        compiler_params=params(16),
+        cost_estimate=pl.CostEstimate(flops=2 * S * rows * depth * width, bytes_accessed=6 * 2**20, transcendentals=0),
+    )(lhs, w_own, w_other)
+
+
+def product_keep(lhs, weights):
     _, rows, depth = lhs.shape
-    width = w_own.shape[0]
-
-    def kernel(lhs_ref, w_own_ref, w_other_ref, *out_refs):
-        total = times(lhs_ref[...].reshape(Y * rows, depth), w_own_ref[...], w_other_ref[...])
+    width = sum(w.shape[0] for w in weights) // 2
+    count = len(weights)
+
+    def kernel(lhs_ref, *refs):
+        total = times_pieces(lhs_ref[...].reshape(Y * rows, depth), refs[:count])
         for d in range(Y):
-            out_refs[d // 2][d % 2] = total[d * rows : (d + 1) * rows]
+            refs[count + d // 2][d % 2] = total[d * rows : (d + 1) * rows]
 
     whole = lambda *shape: pl.BlockSpec(shape, lambda i: (0,) * len(shape))
     return pl.pallas_call(
         kernel,
         grid=(1,),
-        in_specs=[pl.BlockSpec((Y, rows, depth), lambda i: (e, 0, 0)), whole(width, depth // 2), whole(width, depth // 2)],
+        in_specs=[whole(Y, rows, depth)] + [whole(*w.shape) for w in weights],
         out_specs=[whole(2, rows, width)] * 2,
         out_shape=[jax.ShapeDtypeStruct((2, rows, width), BF16)] * 2,
         compiler_params=params(16),
         cost_estimate=pl.CostEstimate(flops=S * rows * depth * width, bytes_accessed=4 * 2**20, transcendentals=0),
-    )(lhs, w_own, w_other)
+    )(lhs, *weights)
 
 
 def add_y(parts):
@@ -239,26 +261,27 @@
 
     near_own = dequantize(down_q, scales)
     near_other = shift(near_own, "c", C, 1)
-    cut = 5 * BLOCK
-    cross_own = [shift(near_own[:cut], "xh", XH, 1), shift(near_own[cut:], "xh", XH, 1)]
+    cut = 4 * BLOCK
+    cross_own = [shift(near_own[:cut], "xh", XH, 1)]
 
     rows = grad_out.shape[0] // 2
-    tokens = [jnp.concatenate([grad_out, shift(grad_out, "c", C, 1)], 1)]
-    around = [(i * C, (i + 1) % Z * C) for i in range(Z)] + [(i * C + 1, (i - 1) % Z * C + 1) for i in range(Z)]
-    tokens[0], _ = lax.optimization_barrier((tokens[0], near_own))
-    for step in range(3):
-        if step == 2:
-            tokens[2], cross_own[0], near_other = lax.optimization_barrier((tokens[2], cross_own[0], near_other))
-        tokens.append(lax.ppermute(tokens[-1], ("z", "c"), around))
-    tokens[3], cross_own[1] = lax.optimization_barrier((tokens[3], cross_own[1]))
-    far = lax.ppermute(lax.dynamic_slice_in_dim(tokens[3], c * rows, rows, 0), ("z", "c"), around)
-    cross_own, far = lax.optimization_barrier((jnp.concatenate(cross_own, 0), far))
-    cross_other = shift(cross_own, "c", C, 1)
-
-    lhs, *near = product_y(own, tokens, far, near_own, near_other)
+    to = lambda k: [(i * C, (i + k) % Z * C) for i in range(Z)] + [(i * C + 1, (i - k) % Z * C + 1) for i in range(Z)]
+    here = jnp.concatenate([grad_out, shift(grad_out, "c", C, 1)], 1)
+    here, _ = lax.optimization_barrier((here, near_own))
+    two = lax.ppermute(here, ("z", "c"), to(2))
+    one = lax.ppermute(here, ("z", "c"), to(1))
+    last, one = lax.optimization_barrier((near_own[cut:], one))
+    cross_own.append(shift(last, "xh", XH, 1))
+    two, cross_own[0] = lax.optimization_barrier((two, cross_own[0]))
+    three = lax.ppermute(two, ("z", "c"), to(1))
+    far = lax.ppermute(lax.dynamic_slice_in_dim(two, c * rows, rows, 0), ("z", "c"), to(2))
+    tokens = [here, one, two, three]
+    weights = cross_own + [shift(part, "c", C, 1) for part in cross_own]
+
+    lhs, *sent = product_send(own, tokens, far, weights)
+    near = product_y(lhs, near_own, near_other)
     near_y = [near[0]] + [shift(near[d], "y", Y, d) for d in range(1, Y)]
-    sent = product_xl(lhs, cross_own, cross_other, 1)
-    kept = product_xl(lhs, cross_own, cross_other, 0)
+    kept = product_keep(lhs, weights)
     cross = add_xl(kept, [shift(part, "xl", XL, 1) for part in sent])
     cross_parts = [cross[0]] + [shift(cross[d], "y", Y, d) for d in range(1, Y)]
     kept, sent = add_y(near_y)

time: 121 us -> 109 us (0.901); the launches traced: 121 us -> 108 us
  waiting for transfers between devices: 69.3 us -> 52.9 us
  starting transfers between devices: 32.2 us -> 37.3 us
  Pallas kernels: 12.8 us -> 10.5 us
    ppermute x14 -> x15, waiting for transfers between devices: 42.7 us -> 21.8 us  [shift(): return lax.ppermute(x, axis, [(i, (i + by) % size) for i in range(size)])]
    ppermute x4, waiting for transfers between devices: 10.2 us -> 18.1 us  [the longest x1 7.92 us: on_device(): one = lax.ppermute(here, ('z', 'c'), to(1))]
    ppermute x2, waiting for transfers between devices: 16.5 us -> 13 us  [on_device(): hidden = [lax.ppermute(sums[j], ALL, home_pairs(j)) for j in range(2)]]
    ppermute x14 -> x15, starting transfers between devices: 15.9 us -> 18.4 us  [shift(): return lax.ppermute(x, axis, [(i, (i + by) % size) for i in range(size)])]
    pallas_call x3, Pallas kernels: 9.78 us -> 7.42 us  [the longest x1 3.55 us: product_y(): pl.pallas_call(kernel, in_specs=[VMEM] * 3, out_specs=[VMEM] * Y, out_sha...]
    ppermute x2, starting transfers between devices: 5.55 us -> 7.65 us  [on_device(): hidden = [lax.ppermute(sums[j], ALL, home_pairs(j)) for j in range(2)]]
    dynamic_slice x1, local copies, waits for them, and re-layouts: 0.02 us -> 1.67 us  [on_device(): lax.dynamic_slice_in_dim(two, c * rows, rows, 0)]
    unnamed x28 -> x12, local copies, waits for them, and re-layouts: 2.99 us -> 2.42 us
  transfers between devices with their start and end apart: 20 -> 21, of which waited for: 13 -> 12; matrix products, arithmetic and copies ran while one was open for 2% -> 4% of each run, Pallas kernels for 8% -> 7%
where the time goes in v10:
time: 109 us; the launch traced here: 108 us
  waiting for transfers between devices  52.9 us (49%)
  starting transfers between devices  37.3 us (34%)
  Pallas kernels  10.5 us (10%)
  local copies, waits for them, and re-layouts  5.91 us (5%)
    ppermute x15, waiting for transfers between devices, shift(): return lax.ppermute(x, axis, [(i, (i + by) % size) for i in range(size)])  21.8 us
    ppermute x15, starting transfers between devices, shift(): return lax.ppermute(x, axis, [(i, (i + by) % size) for i in range(size)])  18.4 us
    ppermute x2, waiting for transfers between devices, on_device(): hidden = [lax.ppermute(sums[j], ALL, home_pairs(j)) for j in range(2)]  13 us
    ppermute x1, waiting for transfers between devices, on_device(): one = lax.ppermute(here, ('z', 'c'), to(1))  7.92 us
    ppermute x2, starting transfers between devices, on_device(): hidden = [lax.ppermute(sums[j], ALL, home_pairs(j)) for j in range(2)]  7.65 us
    ppermute x1, starting transfers between devices, on_device(): one = lax.ppermute(here, ('z', 'c'), to(1))  5.65 us
    ppermute x1, waiting for transfers between devices, on_device(): lax.ppermute(lax.dynamic_slice_in_dim(two, c * rows, rows, 0), ('z', 'c')...  5.38 us
    ppermute x1, waiting for transfers between devices, on_device(): two = lax.ppermute(here, ('z', 'c'), to(2))  4.8 us
  transfers between devices with their start and end apart: 21, of which 12 were waited for; matrix products, arithmetic and copies ran while one was open for 4% of the time, Pallas kernels for 7%

profile of v10, /device:TPU:7, one launch (start us, length us, event | category | flops | bytes accessed | tf_op | source)
XLA Modules:
  0.0 107.8 jit_solution(9520478712990238608)
XLA Ops:
  0.6 0.8 collective-permute-start
  1.4 0.8 copy.8
  2.2 0.3 mul.30
  2.5 0.0 copy-start.5
  2.5 0.4 fusion.w_own_ref
  2.9 0.6 copy-done.5
  3.4 0.1 pad_maximum_fusion.t0
  3.5 5.7 %collective-permute-start.1 = (bf16[256,1024]{1,0:T(8,128)(2,1)S(1)}, bf16[256,1024]{1,0:T(8,128)(2,1)S(1)}, u32[]{:S(2)}, u32[]{:S(2)}) collective-permute-start(bf16[256,1024]{1,0:T(8,128)(2,1)S(1)} %pad_maximum_fusion.t0), channel_id=1, source_target_pairs={{0,32},{32,64},{64,96},{96,128},{128,160},{160,192},{192,224},{224... | collective-permute-start | bytes 1572872 | tf_op jit(solution)/shard_map/ppermute | solution.py:272
  9.2 1.2 %collective-permute-start.3 = (bf16[512,512]{1,0:T(8,128)(2,1)S(1)}, bf16[512,512]{1,0:T(8,128)(2,1)S(1)}, u32[]{:S(2)}, u32[]{:S(2)}) collective-permute-start(bf16[512,512]{1,0:T(8,128)(2,1)S(1)} %slice.9), channel_id=1, source_target_pairs={{0,16},{16,0},{1,17},{17,1},{2,18},{18,2},{3,19},{19,3},{4,20},{20... | collective-permute-start | bytes 1572872 | tf_op jit(solution)/shard_map/ppermute | solution.py:71
  10.4 1.2 %collective-permute-start.2 = (bf16[256,1024]{1,0:T(8,128)(2,1)S(1)}, bf16[256,1024]{1,0:T(8,128)(2,1)}, u32[]{:S(2)}, u32[]{:S(2)}) collective-permute-start(bf16[256,1024]{1,0:T(8,128)(2,1)S(1)} %pad_maximum_fusion.t0), channel_id=1, source_target_pairs={{0,64},{32,96},{64,128},{96,160},{128,192},{160,224},{192,0},{224,... | collective-permute-start | bytes 1572872 | tf_op jit(solution)/shard_map/ppermute | solution.py:271
  11.6 7.9 %collective-permute-done.1.t1 = bf16[256,1024]{1,0:T(8,128)(2,1)S(1)} collective-permute-done((bf16[256,1024]{1,0:T(8,128)(2,1)S(1)}, bf16[256,1024]{1,0:T(8,128)(2,1)S(1)}, u32[]{:S(2)}, u32[]{:S(2)}) %collective-permute-start.1) | collective-permute-done | bytes 524320 | tf_op jit(solution)/shard_map/ppermute | solution.py:272
  19.5 0.8 copy-done
  20.3 1.1 %collective-permute-start.6 = (bf16[384,512]{1,0:T(8,128)(2,1)S(1)}, bf16[384,512]{1,0:T(8,128)(2,1)S(1)}, u32[]{:S(2)}, u32[]{:S(2)}) collective-permute-start(bf16[384,512]{1,0:T(8,128)(2,1)S(1)} %slice.8), channel_id=1, source_target_pairs={{0,16},{16,0},{1,17},{17,1},{2,18},{18,2},{3,19},{19,3},{4,20},{20... | collective-permute-start | bytes 1179656 | tf_op jit(solution)/shard_map/ppermute | solution.py:71
  21.5 0.3 collective-permute-done.3.refs_0_
  21.7 4.8 %collective-permute-done.2.t2 = bf16[256,1024]{1,0:T(8,128)(2,1)} collective-permute-done((bf16[256,1024]{1,0:T(8,128)(2,1)S(1)}, bf16[256,1024]{1,0:T(8,128)(2,1)}, u32[]{:S(2)}, u32[]{:S(2)}) %collective-permute-start.2) | collective-permute-done | bytes 524320 | tf_op jit(solution)/shard_map/ppermute | solution.py:271
  26.5 3.0 %collective-permute-start.7 = (bf16[512,512]{1,0:T(8,128)(2,1)S(1)}, bf16[512,512]{1,0:T(8,128)(2,1)S(1)}, u32[]{:S(2)}, u32[]{:S(2)}) collective-permute-start(bf16[512,512]{1,0:T(8,128)(2,1)S(1)} %collective-permute-done.3.refs_0_), channel_id=1, source_target_pairs={{0,1},{1,0},{2,3},{3,2},{4,5},{5,4},{6,7},{7,6},{8,9},{9,8},{10,11... | collective-permute-start | bytes 1572872 | tf_op jit(solution)/shard_map/ppermute | solution.py:71
  29.5 0.8 collective-permute-done.6.refs_1_
  30.3 1.7 %constant_dynamic-slice_fusion = bf16[128,1024]{1,0:T(8,128)(2,1)} fusion(bf16[256,1024]{1,0:T(8,128)(2,1)} %collective-permute-done.2.t2, s32[]{:T(128)S(6)} %select_n.8), kind=kLoop, calls=%fused_computation.4 | loop fusion | bytes 524292 | tf_op jit(solution)/shard_map/dynamic_slice | solution.py:277
  32.0 4.4 %collective-permute-start.5 = (bf16[128,1024]{1,0:T(8,128)(2,1)}, bf16[128,1024]{1,0:T(8,128)(2,1)S(1)}, u32[]{:S(2)}, u32[]{:S(2)}) collective-permute-start(bf16[128,1024]{1,0:T(8,128)(2,1)} %constant_dynamic-slice_fusion), channel_id=1, source_target_pairs={{0,64},{32,96},{64,128},{96,160},{128,192},{160,224},{192,0},{224,... | collective-permute-start | bytes 786440 | tf_op jit(solution)/shard_map/ppermute | solution.py:277
  36.4 0.7 dynamic-slice_bitcast_fusion.facts_ref
  37.1 5.4 %collective-permute-done.5.far_ref = bf16[128,1024]{1,0:T(8,128)(2,1)S(1)} collective-permute-done((bf16[128,1024]{1,0:T(8,128)(2,1)}, bf16[128,1024]{1,0:T(8,128)(2,1)S(1)}, u32[]{:S(2)}, u32[]{:S(2)}) %collective-permute-start.5) | collective-permute-done | bytes 262176 | tf_op jit(solution)/shard_map/ppermute | solution.py:277
  42.5 1.0 copy-done.1
  43.5 2.6 %shard_map.77 = (bf16[8,128,1024]{2,1,0:T(8,128)(2,1)S(1)}, bf16[2,128,896]{2,1,0:T(8,128)(2,1)S(1)}, bf16[2,128,896]{2,1,0:T(8,128)(2,1)S(1)}) custom-call(s32[10]{0:T(128)S(1)} %dynamic-slice_bitcast_fusion.facts_ref, bf16[256,1024]{1,0:T(8,128)(2,1)S(1)} %pad_maximum_fusion.t0, bf16[256,1024]{1,0:T(8,128)(2,1)S(1)} %copy-done.1, ...), custom_call_target="tpu_custom_call" | custom-call | flops 939524096 | bytes 7340032 | tf_op jit(solution)/shard_map/pallas_call | solution.py:116
  46.1 0.6 collective-permute-start.14
  46.8 0.9 collective-permute-start.15
  47.7 3.6 %shard_map.78 = (bf16[2,128,896]{2,1,0:T(8,128)(2,1)S(1)}, bf16[2,128,896]{2,1,0:T(8,128)(2,1)S(1)}, bf16[2,128,896]{2,1,0:T(8,128)(2,1)S(1)}, bf16[2,128,896]{2,1,0:T(8,128)(2,1)S(1)}) custom-call(bf16[8,128,1024]{2,1,0:T(8,128)(2,1)S(1)} %get-tuple-element.29.lhs_ref, bf16[896,512]{1,0:T(8,128)(2,1)S(1)} %fusion.w_own_ref, ...), custom_call_target="tpu_custom_call" | custom-call | flops 1879048192 | bytes 6291456 | tf_op jit(solution)/shard_map/pallas_call | solution.py:137
  51.2 1.4 %collective-permute-start.10 = (bf16[2,128,896]{2,1,0:T(8,128)(2,1)S(1)}, bf16[2,128,896]{2,1,0:T(8,128)(2,1)S(1)}, u32[]{:S(2)}, u32[]{:S(2)}) collective-permute-start(bf16[2,128,896]{2,1,0:T(8,128)(2,1)S(1)} %get-tuple-element.31), channel_id=1, source_target_pairs={{0,2},{2,4},{4,6},{6,0},{1,3},{3,5},{5,7},{7,1},{8,10},{10,12},{12... | collective-permute-start | bytes 1376264 | tf_op jit(solution)/shard_map/ppermute | solution.py:71
  52.6 2.6 %collective-permute-start.11 = (bf16[2,128,896]{2,1,0:T(8,128)(2,1)S(1)}, bf16[2,128,896]{2,1,0:T(8,128)(2,1)S(1)}, u32[]{:S(2)}, u32[]{:S(2)}) collective-permute-start(bf16[2,128,896]{2,1,0:T(8,128)(2,1)S(1)} %get-tuple-element.32), channel_id=1, source_target_pairs={{0,4},{2,6},{4,0},{6,2},{1,5},{3,7},{5,1},{7,3},{8,12},{10,14},{12... | collective-permute-start | bytes 1376264 | tf_op jit(solution)/shard_map/ppermute | solution.py:71
  55.2 1.1 collective-permute-start.12
  56.3 1.3 %shard_map.80 = (bf16[2,128,896]{2,1,0:T(8,128)(2,1)S(1)}, bf16[2,128,896]{2,1,0:T(8,128)(2,1)S(1)}) custom-call(bf16[8,128,1024]{2,1,0:T(8,128)(2,1)S(1)} %get-tuple-element.29.lhs_ref, bf16[512,512]{1,0:T(8,128)(2,1)S(1)} %collective-permute-done.3.refs_0_, bf16[384,512]{1,0:T(8,128)(2,1)S(1)} %collective-permute-done.6.refs_1_, ...), custom_call_target="tpu_custom_call" | custom-call | flops 939524096 | bytes 4194304 | tf_op jit(solution)/shard_map/pallas_call | solution.py:158
  57.6 8.0 %collective-permute-done.15.refs_3_ = bf16[2,128,896]{2,1,0:T(8,128)(2,1)S(1)} collective-permute-done((bf16[2,128,896]{2,1,0:T(8,128)(2,1)S(1)}, bf16[2,128,896]{2,1,0:T(8,128)(2,1)S(1)}, u32[]{:S(2)}, u32[]{:S(2)}) %collective-permute-start.15) | collective-permute-done | bytes 458784 | tf_op jit(solution)/shard_map/ppermute | solution.py:71
  65.6 0.2 shard_map.81
  65.8 0.0 copy-start.2
  65.8 1.4 %collective-permute-start.16 = (bf16[128,896]{1,0:T(8,128)(2,1)S(1)}, bf16[128,896]{1,0:T(8,128)(2,1)S(1)}, u32[]{:S(2)}, u32[]{:S(2)}) collective-permute-start(bf16[128,896]{1,0:T(8,128)(2,1)S(1)} %get-tuple-element.41), channel_id=1, source_target_pairs={{0,2},{2,4},{4,6},{6,0},{1,3},{3,5},{5,7},{7,1},{8,10},{10,12},{12... | collective-permute-start | bytes 688136 | tf_op jit(solution)/shard_map/ppermute | solution.py:71
  67.2 2.6 %collective-permute-start.17 = (bf16[128,896]{1,0:T(8,128)(2,1)S(1)}, bf16[128,896]{1,0:T(8,128)(2,1)S(1)}, u32[]{:S(2)}, u32[]{:S(2)}) collective-permute-start(bf16[128,896]{1,0:T(8,128)(2,1)S(1)} %get-tuple-element.42), channel_id=1, source_target_pairs={{0,4},{2,6},{4,0},{6,2},{1,5},{3,7},{5,1},{7,3},{8,12},{10,14},{12... | collective-permute-start | bytes 688136 | tf_op jit(solution)/shard_map/ppermute | solution.py:71
  69.8 1.1 collective-permute-start.18
  70.9 1.7 %collective-permute-done.11.refs_2_ = bf16[2,128,896]{2,1,0:T(8,128)(2,1)S(1)} collective-permute-done((bf16[2,128,896]{2,1,0:T(8,128)(2,1)S(1)}, bf16[2,128,896]{2,1,0:T(8,128)(2,1)S(1)}, u32[]{:S(2)}, u32[]{:S(2)}) %collective-permute-start.11) | collective-permute-done | bytes 458784 | tf_op jit(solution)/shard_map/ppermute | solution.py:71
  72.6 4.4 %collective-permute-done.12.refs_3_ = bf16[2,128,896]{2,1,0:T(8,128)(2,1)S(1)} collective-permute-done((bf16[2,128,896]{2,1,0:T(8,128)(2,1)S(1)}, bf16[2,128,896]{2,1,0:T(8,128)(2,1)S(1)}, u32[]{:S(2)}, u32[]{:S(2)}) %collective-permute-start.12) | collective-permute-done | bytes 458784 | tf_op jit(solution)/shard_map/ppermute | solution.py:71
  77.0 0.2 shard_map.79
  77.2 0.6 collective-permute-start.13
  77.9 5.0 %collective-permute-done.16.refs_3_ = bf16[128,896]{1,0:T(8,128)(2,1)S(1)} collective-permute-done((bf16[128,896]{1,0:T(8,128)(2,1)S(1)}, bf16[128,896]{1,0:T(8,128)(2,1)S(1)}, u32[]{:S(2)}, u32[]{:S(2)}) %collective-permute-start.16) | collective-permute-done | bytes 229408 | tf_op jit(solution)/shard_map/ppermute | solution.py:71
  82.9 1.6 %collective-permute-done.18.refs_5_ = bf16[128,896]{1,0:T(8,128)(2,1)S(1)} collective-permute-done((bf16[128,896]{1,0:T(8,128)(2,1)S(1)}, bf16[128,896]{1,0:T(8,128)(2,1)S(1)}, u32[]{:S(2)}, u32[]{:S(2)}) %collective-permute-start.18) | collective-permute-done | bytes 229408 | tf_op jit(solution)/shard_map/ppermute | solution.py:71
  84.5 0.7 shard_map.82
  85.3 0.1 collective-permute-start.19
  85.4 7.6 %collective-permute-start.20 = (bf16[128,896]{1,0:T(8,128)(2,1)S(1)}, bf16[128,896]{1,0:T(8,128)(2,1)S(1)}, u32[]{:S(2)}, u32[]{:S(2)}) collective-permute-start(bf16[128,896]{1,0:T(8,128)(2,1)S(1)} %get-tuple-element.45), channel_id=1, source_target_pairs={{0,224},{1,128},{2,161},{3,65},{4,160},{5,32},{6,225},{7,64},{8,19... | collective-permute-start | bytes 688136 | tf_op jit(solution)/shard_map/ppermute | solution.py:291
  92.9 4.9 %collective-permute-done.19.first = bf16[128,896]{1,0:T(8,128)(2,1)S(1)} collective-permute-done((bf16[128,896]{1,0:T(8,128)(2,1)S(1)}, bf16[128,896]{1,0:T(8,128)(2,1)S(1)}, u32[]{:S(2)}, u32[]{:S(2)}) %collective-permute-start.19) | collective-permute-done | bytes 229408 | tf_op jit(solution)/shard_map/ppermute | solution.py:291
  97.8 8.1 %collective-permute-done.20.second = bf16[128,896]{1,0:T(8,128)(2,1)S(1)} collective-permute-done((bf16[128,896]{1,0:T(8,128)(2,1)S(1)}, bf16[128,896]{1,0:T(8,128)(2,1)S(1)}, u32[]{:S(2)}, u32[]{:S(2)}) %collective-permute-start.20) | collective-permute-done | bytes 229408 | tf_op jit(solution)/shard_map/ppermute | solution.py:291
  105.9 1.9 %shard_map.83 = (bf16[256,896]{1,0:T(8,128)(2,1)}, bf16[256,896]{1,0:T(8,128)(2,1)}) custom-call(s32[10]{0:T(128)S(1)} %dynamic-slice_bitcast_fusion.facts_ref, bf16[128,896]{1,0:T(8,128)(2,1)S(1)} %collective-permute-done.19.first, bf16[128,896]{1,0:T(8,128)(2,1)S(1)} %collective-permute-done.20.second, bf16[256,896]{1,0:T(8,128)(2,1)S(1)} %copy-done.2, ...), custom_call_target="tpu_custom_call" | custom-call | flops 2293760 | bytes 2293760 | tf_op jit(solution)/shard_map/pallas_call | solution.py:248
  (21 shorter events, 0.1 us)
Async XLA Ops:
  0.6 1.9 %copy-start.4 = (bf16[896,512]{1,0:T(8,128)(2,1)S(1)}, bf16[896,512]{1,0:T(8,128)(2,1)}, u32[]{:S(2)}) copy-start(bf16[896,512]{1,0:T(8,128)(2,1)} %param.7) | copy-start | bytes 2752516
  0.6 2.2 %collective-permute-start = (bf16[256,512]{1,0:T(8,128)(2,1)}, bf16[256,512]{1,0:T(8,128)(2,1)S(1)}, u32[]{:S(2)}, u32[]{:S(2)}) collective-permute-start(bf16[256,512]{1,0:T(8,128)(2,1)} %param.6), channel_id=1, source_target_pairs={{0,1},{1,0},{2,3},{3,2},{4,5},{5,4},{6,7},{7,6},{8,9},{9,8},{10,11... | collective-permute-start | bytes 786440 | tf_op jit(solution)/shard_map/ppermute | solution.py:71
  2.5 1.0 copy-start.5
  3.5 16.0 %collective-permute-start.1 = (bf16[256,1024]{1,0:T(8,128)(2,1)S(1)}, bf16[256,1024]{1,0:T(8,128)(2,1)S(1)}, u32[]{:S(2)}, u32[]{:S(2)}) collective-permute-start(bf16[256,1024]{1,0:T(8,128)(2,1)S(1)} %pad_maximum_fusion.t0), channel_id=1, source_target_pairs={{0,32},{32,64},{64,96},{96,128},{128,160},{160,192},{192,224},{224... | collective-permute-start | bytes 1572872 | tf_op jit(solution)/shard_map/ppermute | solution.py:272
  9.2 12.5 %collective-permute-start.3 = (bf16[512,512]{1,0:T(8,128)(2,1)S(1)}, bf16[512,512]{1,0:T(8,128)(2,1)S(1)}, u32[]{:S(2)}, u32[]{:S(2)}) collective-permute-start(bf16[512,512]{1,0:T(8,128)(2,1)S(1)} %slice.9), channel_id=1, source_target_pairs={{0,16},{16,0},{1,17},{17,1},{2,18},{18,2},{3,19},{19,3},{4,20},{20... | collective-permute-start | bytes 1572872 | tf_op jit(solution)/shard_map/ppermute | solution.py:71
  10.4 16.1 %collective-permute-start.2 = (bf16[256,1024]{1,0:T(8,128)(2,1)S(1)}, bf16[256,1024]{1,0:T(8,128)(2,1)}, u32[]{:S(2)}, u32[]{:S(2)}) collective-permute-start(bf16[256,1024]{1,0:T(8,128)(2,1)S(1)} %pad_maximum_fusion.t0), channel_id=1, source_target_pairs={{0,64},{32,96},{64,128},{96,160},{128,192},{160,224},{192,0},{224,... | collective-permute-start | bytes 1572872 | tf_op jit(solution)/shard_map/ppermute | solution.py:271
  11.6 36.1 %collective-permute-start.9 = (bf16[896,512]{1,0:T(8,128)(2,1)S(1)}, bf16[896,512]{1,0:T(8,128)(2,1)}, u32[]{:S(2)}, u32[]{:S(2)}) collective-permute-start(bf16[896,512]{1,0:T(8,128)(2,1)S(1)} %fusion.w_own_ref), channel_id=1, source_target_pairs={{0,1},{1,0},{2,3},{3,2},{4,5},{5,4},{6,7},{7,6},{8,9},{9,8},{10,11... | collective-permute-start | bytes 2752520 | tf_op jit(solution)/shard_map/ppermute | solution.py:71
  19.5 0.8 copy-start
  20.3 9.9 %collective-permute-start.6 = (bf16[384,512]{1,0:T(8,128)(2,1)S(1)}, bf16[384,512]{1,0:T(8,128)(2,1)S(1)}, u32[]{:S(2)}, u32[]{:S(2)}) collective-permute-start(bf16[384,512]{1,0:T(8,128)(2,1)S(1)} %slice.8), channel_id=1, source_target_pairs={{0,16},{16,0},{1,17},{17,1},{2,18},{18,2},{3,19},{19,3},{4,20},{20... | collective-permute-start | bytes 1179656 | tf_op jit(solution)/shard_map/ppermute | solution.py:71
  26.5 15.9 %collective-permute-start.4 = (bf16[256,1024]{1,0:T(8,128)(2,1)}, bf16[256,1024]{1,0:T(8,128)(2,1)}, u32[]{:S(2)}, u32[]{:S(2)}) collective-permute-start(bf16[256,1024]{1,0:T(8,128)(2,1)} %collective-permute-done.2.t2), channel_id=1, source_target_pairs={{0,32},{32,64},{64,96},{96,128},{128,160},{160,192},{192,224},{224... | collective-permute-start | bytes 1572872 | tf_op jit(solution)/shard_map/ppermute | solution.py:276
  26.5 15.9 %collective-permute-start.7 = (bf16[512,512]{1,0:T(8,128)(2,1)S(1)}, bf16[512,512]{1,0:T(8,128)(2,1)S(1)}, u32[]{:S(2)}, u32[]{:S(2)}) collective-permute-start(bf16[512,512]{1,0:T(8,128)(2,1)S(1)} %collective-permute-done.3.refs_0_), channel_id=1, source_target_pairs={{0,1},{1,0},{2,3},{3,2},{4,5},{5,4},{6,7},{7,6},{8,9},{9,8},{10,11... | collective-permute-start | bytes 1572872 | tf_op jit(solution)/shard_map/ppermute | solution.py:71
  30.3 12.2 %collective-permute-start.8 = (bf16[384,512]{1,0:T(8,128)(2,1)S(1)}, bf16[384,512]{1,0:T(8,128)(2,1)S(1)}, u32[]{:S(2)}, u32[]{:S(2)}) collective-permute-start(bf16[384,512]{1,0:T(8,128)(2,1)S(1)} %collective-permute-done.6.refs_1_), channel_id=1, source_target_pairs={{0,1},{1,0},{2,3},{3,2},{4,5},{5,4},{6,7},{7,6},{8,9},{9,8},{10,11... | collective-permute-start | bytes 1179656 | tf_op jit(solution)/shard_map/ppermute | solution.py:71
  32.0 10.5 %collective-permute-start.5 = (bf16[128,1024]{1,0:T(8,128)(2,1)}, bf16[128,1024]{1,0:T(8,128)(2,1)S(1)}, u32[]{:S(2)}, u32[]{:S(2)}) collective-permute-start(bf16[128,1024]{1,0:T(8,128)(2,1)} %constant_dynamic-slice_fusion), channel_id=1, source_target_pairs={{0,64},{32,96},{64,128},{96,160},{128,192},{160,224},{192,0},{224,... | collective-permute-start | bytes 786440 | tf_op jit(solution)/shard_map/ppermute | solution.py:277
  42.5 1.0 copy-start.1
  46.1 11.5 %collective-permute-start.14 = (bf16[2,128,896]{2,1,0:T(8,128)(2,1)S(1)}, bf16[2,128,896]{2,1,0:T(8,128)(2,1)S(1)}, u32[]{:S(2)}, u32[]{:S(2)}) collective-permute-start(bf16[2,128,896]{2,1,0:T(8,128)(2,1)S(1)} %get-tuple-element.38), channel_id=1, source_target_pairs={{0,8},{8,0},{1,9},{9,1},{2,10},{10,2},{3,11},{11,3},{4,12},{12,4},... | collective-permute-start | bytes 1376264 | tf_op jit(solution)/shard_map/ppermute | solution.py:71
  46.8 18.8 %collective-permute-start.15 = (bf16[2,128,896]{2,1,0:T(8,128)(2,1)S(1)}, bf16[2,128,896]{2,1,0:T(8,128)(2,1)S(1)}, u32[]{:S(2)}, u32[]{:S(2)}) collective-permute-start(bf16[2,128,896]{2,1,0:T(8,128)(2,1)S(1)} %get-tuple-element.39), channel_id=1, source_target_pairs={{0,8},{8,0},{1,9},{9,1},{2,10},{10,2},{3,11},{11,3},{4,12},{12,4},... | collective-permute-start | bytes 1376264 | tf_op jit(solution)/shard_map/ppermute | solution.py:71
  51.2 18.6 %collective-permute-start.10 = (bf16[2,128,896]{2,1,0:T(8,128)(2,1)S(1)}, bf16[2,128,896]{2,1,0:T(8,128)(2,1)S(1)}, u32[]{:S(2)}, u32[]{:S(2)}) collective-permute-start(bf16[2,128,896]{2,1,0:T(8,128)(2,1)S(1)} %get-tuple-element.31), channel_id=1, source_target_pairs={{0,2},{2,4},{4,6},{6,0},{1,3},{3,5},{5,7},{7,1},{8,10},{10,12},{12... | collective-permute-start | bytes 1376264 | tf_op jit(solution)/shard_map/ppermute | solution.py:71
  52.6 20.0 %collective-permute-start.11 = (bf16[2,128,896]{2,1,0:T(8,128)(2,1)S(1)}, bf16[2,128,896]{2,1,0:T(8,128)(2,1)S(1)}, u32[]{:S(2)}, u32[]{:S(2)}) collective-permute-start(bf16[2,128,896]{2,1,0:T(8,128)(2,1)S(1)} %get-tuple-element.32), channel_id=1, source_target_pairs={{0,4},{2,6},{4,0},{6,2},{1,5},{3,7},{5,1},{7,3},{8,12},{10,14},{12... | collective-permute-start | bytes 1376264 | tf_op jit(solution)/shard_map/ppermute | solution.py:71
  55.2 21.8 %collective-permute-start.12 = (bf16[2,128,896]{2,1,0:T(8,128)(2,1)S(1)}, bf16[2,128,896]{2,1,0:T(8,128)(2,1)S(1)}, u32[]{:S(2)}, u32[]{:S(2)}) collective-permute-start(bf16[2,128,896]{2,1,0:T(8,128)(2,1)S(1)} %get-tuple-element.33), channel_id=1, source_target_pairs={{0,6},{2,0},{4,2},{6,4},{1,7},{3,1},{5,3},{7,5},{8,14},{10,8},{12,... | collective-permute-start | bytes 1376264 | tf_op jit(solution)/shard_map/ppermute | solution.py:71
  65.8 40.1 %copy-start.2 = (bf16[256,896]{1,0:T(8,128)(2,1)S(1)}, bf16[256,896]{1,0:T(8,128)(2,1)}, u32[]{:S(2)}) copy-start(bf16[256,896]{1,0:T(8,128)(2,1)} %gate_ref.1) | copy-start | bytes 1376260
  65.8 40.1 %copy-start.3 = (bf16[256,896]{1,0:T(8,128)(2,1)S(1)}, bf16[256,896]{1,0:T(8,128)(2,1)}, u32[]{:S(2)}) copy-start(bf16[256,896]{1,0:T(8,128)(2,1)} %up_ref.1) | copy-start | bytes 1376260
  65.8 17.1 %collective-permute-start.16 = (bf16[128,896]{1,0:T(8,128)(2,1)S(1)}, bf16[128,896]{1,0:T(8,128)(2,1)S(1)}, u32[]{:S(2)}, u32[]{:S(2)}) collective-permute-start(bf16[128,896]{1,0:T(8,128)(2,1)S(1)} %get-tuple-element.41), channel_id=1, source_target_pairs={{0,2},{2,4},{4,6},{6,0},{1,3},{3,5},{5,7},{7,1},{8,10},{10,12},{12... | collective-permute-start | bytes 688136 | tf_op jit(solution)/shard_map/ppermute | solution.py:71
  67.2 15.7 %collective-permute-start.17 = (bf16[128,896]{1,0:T(8,128)(2,1)S(1)}, bf16[128,896]{1,0:T(8,128)(2,1)S(1)}, u32[]{:S(2)}, u32[]{:S(2)}) collective-permute-start(bf16[128,896]{1,0:T(8,128)(2,1)S(1)} %get-tuple-element.42), channel_id=1, source_target_pairs={{0,4},{2,6},{4,0},{6,2},{1,5},{3,7},{5,1},{7,3},{8,12},{10,14},{12... | collective-permute-start | bytes 688136 | tf_op jit(solution)/shard_map/ppermute | solution.py:71
  69.8 14.7 %collective-permute-start.18 = (bf16[128,896]{1,0:T(8,128)(2,1)S(1)}, bf16[128,896]{1,0:T(8,128)(2,1)S(1)}, u32[]{:S(2)}, u32[]{:S(2)}) collective-permute-start(bf16[128,896]{1,0:T(8,128)(2,1)S(1)} %get-tuple-element.43), channel_id=1, source_target_pairs={{0,6},{2,0},{4,2},{6,4},{1,7},{3,1},{5,3},{7,5},{8,14},{10,8},{12,... | collective-permute-start | bytes 688136 | tf_op jit(solution)/shard_map/ppermute | solution.py:71
  77.2 7.3 %collective-permute-start.13 = (bf16[128,896]{1,0:T(8,128)(2,1)S(1)}, bf16[128,896]{1,0:T(8,128)(2,1)S(1)}, u32[]{:S(2)}, u32[]{:S(2)}) collective-permute-start(bf16[128,896]{1,0:T(8,128)(2,1)S(1)} %get-tuple-element.35), channel_id=1, source_target_pairs={{0,8},{8,0},{1,9},{9,1},{2,10},{10,2},{3,11},{11,3},{4,12},{12,4},... | collective-permute-start | bytes 688136 | tf_op jit(solution)/shard_map/ppermute | solution.py:71
  85.3 12.5 %collective-permute-start.19 = (bf16[128,896]{1,0:T(8,128)(2,1)S(1)}, bf16[128,896]{1,0:T(8,128)(2,1)S(1)}, u32[]{:S(2)}, u32[]{:S(2)}) collective-permute-start(bf16[128,896]{1,0:T(8,128)(2,1)S(1)} %get-tuple-element.44), channel_id=1, source_target_pairs={{0,225},{1,129},{2,160},{3,64},{4,161},{5,33},{6,224},{7,65},{8,19... | collective-permute-start | bytes 688136 | tf_op jit(solution)/shard_map/ppermute | solution.py:291
  85.4 20.5 %collective-permute-start.20 = (bf16[128,896]{1,0:T(8,128)(2,1)S(1)}, bf16[128,896]{1,0:T(8,128)(2,1)S(1)}, u32[]{:S(2)}, u32[]{:S(2)}) collective-permute-start(bf16[128,896]{1,0:T(8,128)(2,1)S(1)} %get-tuple-element.45), channel_id=1, source_target_pairs={{0,224},{1,128},{2,161},{3,65},{4,160},{5,32},{6,225},{7,64},{8,19... | collective-permute-start | bytes 688136 | tf_op jit(solution)/shard_map/ppermute | solution.py:291

commit v11 on v10

--- a/solution.py
+++ b/solution.py
@@ -17,14 +17,14 @@
 SMEM = pl.BlockSpec(memory_space=pltpu.SMEM)
 
 NUMBER = (
-    ((2, 5, 6, 1, 4, 0, 3, 7), (7, 3, 2, 4, 6, 1, 5, 0)),
-    ((0, 5, 4, 6, 1, 7, 2, 3), (7, 3, 1, 4, 2, 5, 6, 0)),
-    ((4, 2, 7, 0, 6, 1, 5, 3), (7, 5, 1, 4, 3, 2, 0, 6)),
-    ((1, 5, 6, 4, 3, 7, 2, 0), (0, 5, 2, 1, 4, 6, 3, 7)),
-    ((6, 4, 1, 7, 3, 0, 5, 2), (1, 0, 7, 4, 6, 2, 5, 3)),
-    ((1, 3, 2, 7, 4, 6, 0, 5), (4, 6, 7, 0, 1, 3, 2, 5)),
-    ((5, 4, 2, 6, 1, 0, 3, 7), (7, 5, 2, 1, 6, 4, 3, 0)),
-    ((1, 0, 2, 4, 5, 7, 6, 3), (1, 0, 6, 4, 2, 5, 3, 7)),
+    ((5, 1, 6, 2, 0, 3, 7, 4), (5, 1, 6, 2, 7, 3, 0, 4)),
+    ((1, 5, 2, 6, 7, 3, 0, 4), (1, 5, 2, 6, 0, 3, 7, 4)),
+    ((5, 1, 6, 2, 0, 3, 7, 4), (5, 1, 6, 2, 7, 3, 0, 4)),
+    ((1, 5, 2, 6, 7, 3, 0, 4), (1, 5, 2, 6, 0, 3, 7, 4)),
+    ((5, 1, 6, 2, 0, 3, 7, 4), (5, 1, 6, 2, 7, 3, 0, 4)),
+    ((1, 5, 2, 6, 7, 3, 0, 4), (1, 5, 2, 6, 0, 3, 7, 4)),
+    ((5, 1, 6, 2, 0, 3, 7, 4), (5, 1, 6, 2, 7, 3, 0, 4)),
+    ((1, 5, 2, 6, 7, 3, 0, 4), (1, 5, 2, 6, 0, 3, 7, 4)),
 )
 
 
@@ -261,7 +261,7 @@
 
     near_own = dequantize(down_q, scales)
     near_other = shift(near_own, "c", C, 1)
-    cut = 4 * BLOCK
+    cut = 6 * BLOCK
     cross_own = [shift(near_own[:cut], "xh", XH, 1)]
 
     rows = grad_out.shape[0] // 2

time: 109 us -> 109 us (level)
  local copies, waits for them, and re-layouts: 5.91 us -> 3.23 us
  starting transfers between devices: 37.3 us -> 38.5 us
  Pallas kernels: 10.5 us -> 11.6 us
    ppermute x1, waiting for transfers between devices: 7.92 us -> 0.01 us  [on_device(): one = lax.ppermute(here, ('z', 'c'), to(1))]
    ppermute x1, waiting for transfers between devices: 4.8 us -> 11 us  [on_device(): two = lax.ppermute(here, ('z', 'c'), to(2))]
    ppermute x1, starting transfers between devices: 0.01 us -> 5.58 us  [on_device(): three = lax.ppermute(two, ('z', 'c'), to(1))]
    ppermute x1, starting transfers between devices: 1.17 us -> 6.1 us  [on_device(): two = lax.ppermute(here, ('z', 'c'), to(2))]
    ppermute x1, starting transfers between devices: 5.65 us -> 0.73 us  [on_device(): one = lax.ppermute(here, ('z', 'c'), to(1))]
    ppermute x15, waiting for transfers between devices: 21.8 us -> 25.1 us  [shift(): return lax.ppermute(x, axis, [(i, (i + by) % size) for i in range(size)])]
    ppermute x1, starting transfers between devices: 4.44 us -> 1.17 us  [on_device(): lax.ppermute(lax.dynamic_slice_in_dim(two, c * rows, rows, 0), ('z', 'c')...]
    unnamed x12 -> x8, local copies, waits for them, and re-layouts: 2.42 us -> 0.02 us
  transfers between devices with their start and end apart: 21 -> 21, of which waited for: 12 -> 12; matrix products, arithmetic and copies ran while one was open for 4% -> 3% of each run, Pallas kernels for 7% -> 8%
where the time goes in v11:
time: 109 us; the launch traced here: 107 us
  waiting for transfers between devices  52.7 us (48%)
  starting transfers between devices  38.5 us (35%)
  Pallas kernels  11.6 us (11%)
  local copies, waits for them, and re-layouts  3.23 us (3%)
    ppermute x15, waiting for transfers between devices, shift(): return lax.ppermute(x, axis, [(i, (i + by) % size) for i in range(size)])  25.1 us
    ppermute x15, starting transfers between devices, shift(): return lax.ppermute(x, axis, [(i, (i + by) % size) for i in range(size)])  16.2 us
    ppermute x2, waiting for transfers between devices, on_device(): hidden = [lax.ppermute(sums[j], ALL, home_pairs(j)) for j in range(2)]  12.8 us
    ppermute x1, waiting for transfers between devices, on_device(): two = lax.ppermute(here, ('z', 'c'), to(2))  11 us
    ppermute x2, starting transfers between devices, on_device(): hidden = [lax.ppermute(sums[j], ALL, home_pairs(j)) for j in range(2)]  8.68 us
    ppermute x1, starting transfers between devices, on_device(): two = lax.ppermute(here, ('z', 'c'), to(2))  6.1 us
    ppermute x1, starting transfers between devices, on_device(): three = lax.ppermute(two, ('z', 'c'), to(1))  5.58 us
    ppermute x1, waiting for transfers between devices, on_device(): lax.ppermute(lax.dynamic_slice_in_dim(two, c * rows, rows, 0), ('z', 'c')...  3.76 us
  transfers between devices with their start and end apart: 21, of which 12 were waited for; matrix products, arithmetic and copies ran while one was open for 3% of the time, Pallas kernels for 8%

profile of v11, /device:TPU:7, one launch (start us, length us, event | category | flops | bytes accessed | tf_op | source)
XLA Modules:
  0.0 107.2 jit_solution(11065669647904483175)
XLA Ops:
  0.6 0.8 collective-permute-start
  1.4 0.8 copy.8
  2.2 0.3 mul.30
  2.5 0.0 copy-start.3
  2.5 0.4 fusion.w_own_ref
  2.9 0.1 slice.9
  2.9 1.2 %collective-permute-start.3 = (bf16[768,512]{1,0:T(8,128)(2,1)S(1)}, bf16[768,512]{1,0:T(8,128)(2,1)S(1)}, u32[]{:S(2)}, u32[]{:S(2)}) collective-permute-start(bf16[768,512]{1,0:T(8,128)(2,1)S(1)} %slice.9), channel_id=1, source_target_pairs={{0,16},{16,0},{1,17},{17,1},{2,18},{18,2},{3,19},{19,3},{4,20},{20... | collective-permute-start | bytes 2359304 | tf_op jit(solution)/shard_map/ppermute | solution.py:71
  4.2 0.1 pad_maximum_fusion.t0
  4.2 6.1 %collective-permute-start.2 = (bf16[256,1024]{1,0:T(8,128)(2,1)S(1)}, bf16[256,1024]{1,0:T(8,128)(2,1)S(1)}, u32[]{:S(2)}, u32[]{:S(2)}) collective-permute-start(bf16[256,1024]{1,0:T(8,128)(2,1)S(1)} %pad_maximum_fusion.t0), channel_id=1, source_target_pairs={{0,64},{32,96},{64,128},{96,160},{128,192},{160,224},{192,0},{224,... | collective-permute-start | bytes 1572872 | tf_op jit(solution)/shard_map/ppermute | solution.py:271
  10.3 0.7 collective-permute-start.1
  11.1 11.0 %collective-permute-done.2.t2 = bf16[256,1024]{1,0:T(8,128)(2,1)S(1)} collective-permute-done((bf16[256,1024]{1,0:T(8,128)(2,1)S(1)}, bf16[256,1024]{1,0:T(8,128)(2,1)S(1)}, u32[]{:S(2)}, u32[]{:S(2)}) %collective-permute-start.2) | collective-permute-done | bytes 524320 | tf_op jit(solution)/shard_map/ppermute | solution.py:271
  22.1 1.6 %collective-permute-done.3.refs_0_ = bf16[768,512]{1,0:T(8,128)(2,1)S(1)} collective-permute-done((bf16[768,512]{1,0:T(8,128)(2,1)S(1)}, bf16[768,512]{1,0:T(8,128)(2,1)S(1)}, u32[]{:S(2)}, u32[]{:S(2)}) %collective-permute-start.3) | collective-permute-done | bytes 786464 | tf_op jit(solution)/shard_map/ppermute | solution.py:71
  23.6 0.8 collective-permute-start.7
  24.5 5.6 %collective-permute-start.4 = (bf16[256,1024]{1,0:T(8,128)(2,1)S(1)}, bf16[256,1024]{1,0:T(8,128)(2,1)}, u32[]{:S(2)}, u32[]{:S(2)}) collective-permute-start(bf16[256,1024]{1,0:T(8,128)(2,1)S(1)} %collective-permute-done.2.t2), channel_id=1, source_target_pairs={{0,32},{32,64},{64,96},{96,128},{128,160},{160,192},{192,224},{224... | collective-permute-start | bytes 1572872 | tf_op jit(solution)/shard_map/ppermute | solution.py:276
  30.1 0.7 slice.8
  30.7 1.1 %collective-permute-start.6 = (bf16[128,512]{1,0:T(8,128)(2,1)}, bf16[128,512]{1,0:T(8,128)(2,1)}, u32[]{:S(2)}, u32[]{:S(2)}) collective-permute-start(bf16[128,512]{1,0:T(8,128)(2,1)} %slice.8), channel_id=1, source_target_pairs={{0,16},{16,0},{1,17},{17,1},{2,18},{18,2},{3,19},{19,3},{4,20},{20... | collective-permute-start | bytes 393224 | tf_op jit(solution)/shard_map/ppermute | solution.py:71
  31.9 0.7 constant_dynamic-slice_fusion
  32.6 1.2 %collective-permute-start.5 = (bf16[128,1024]{1,0:T(8,128)(2,1)}, bf16[128,1024]{1,0:T(8,128)(2,1)}, u32[]{:S(2)}, u32[]{:S(2)}) collective-permute-start(bf16[128,1024]{1,0:T(8,128)(2,1)} %constant_dynamic-slice_fusion), channel_id=1, source_target_pairs={{0,64},{32,96},{64,128},{96,160},{128,192},{160,224},{192,0},{224,... | collective-permute-start | bytes 786440 | tf_op jit(solution)/shard_map/ppermute | solution.py:277
  33.8 2.7 %collective-permute-done.6.refs_1_ = bf16[128,512]{1,0:T(8,128)(2,1)} collective-permute-done((bf16[128,512]{1,0:T(8,128)(2,1)}, bf16[128,512]{1,0:T(8,128)(2,1)}, u32[]{:S(2)}, u32[]{:S(2)}) %collective-permute-start.6) | collective-permute-done | bytes 131104 | tf_op jit(solution)/shard_map/ppermute | solution.py:71
  36.5 0.7 dynamic-slice_bitcast_fusion.facts_ref
  37.2 1.0 collective-permute-done.8.refs_3_
  38.2 3.8 %collective-permute-done.5.far_ref = bf16[128,1024]{1,0:T(8,128)(2,1)} collective-permute-done((bf16[128,1024]{1,0:T(8,128)(2,1)}, bf16[128,1024]{1,0:T(8,128)(2,1)}, u32[]{:S(2)}, u32[]{:S(2)}) %collective-permute-start.5) | collective-permute-done | bytes 262176 | tf_op jit(solution)/shard_map/ppermute | solution.py:277
  42.0 2.7 %shard_map.77 = (bf16[8,128,1024]{2,1,0:T(8,128)(2,1)S(1)}, bf16[2,128,896]{2,1,0:T(8,128)(2,1)S(1)}, bf16[2,128,896]{2,1,0:T(8,128)(2,1)S(1)}) custom-call(s32[10]{0:T(128)S(1)} %dynamic-slice_bitcast_fusion.facts_ref, bf16[256,1024]{1,0:T(8,128)(2,1)S(1)} %pad_maximum_fusion.t0, bf16[256,1024]{1,0:T(8,128)(2,1)} %collective-permute-done.1.t1, ...), custom_call_target="tpu_custom_call" | custom-call | flops 939524096 | bytes 7340032 | tf_op jit(solution)/shard_map/pallas_call | solution.py:116
  44.7 0.6 collective-permute-start.14
  45.3 0.9 collective-permute-start.15
  46.3 3.6 %shard_map.78 = (bf16[2,128,896]{2,1,0:T(8,128)(2,1)S(1)}, bf16[2,128,896]{2,1,0:T(8,128)(2,1)S(1)}, bf16[2,128,896]{2,1,0:T(8,128)(2,1)S(1)}, bf16[2,128,896]{2,1,0:T(8,128)(2,1)S(1)}) custom-call(bf16[8,128,1024]{2,1,0:T(8,128)(2,1)S(1)} %get-tuple-element.29.lhs_ref, bf16[896,512]{1,0:T(8,128)(2,1)S(1)} %fusion.w_own_ref, ...), custom_call_target="tpu_custom_call" | custom-call | flops 1879048192 | bytes 6291456 | tf_op jit(solution)/shard_map/pallas_call | solution.py:137
  49.8 1.4 %collective-permute-start.10 = (bf16[2,128,896]{2,1,0:T(8,128)(2,1)S(1)}, bf16[2,128,896]{2,1,0:T(8,128)(2,1)S(1)}, u32[]{:S(2)}, u32[]{:S(2)}) collective-permute-start(bf16[2,128,896]{2,1,0:T(8,128)(2,1)S(1)} %get-tuple-element.31), channel_id=1, source_target_pairs={{0,2},{2,4},{4,6},{6,0},{1,3},{3,5},{5,7},{7,1},{8,10},{10,12},{12... | collective-permute-start | bytes 1376264 | tf_op jit(solution)/shard_map/ppermute | solution.py:71
  51.2 2.6 %collective-permute-start.11 = (bf16[2,128,896]{2,1,0:T(8,128)(2,1)S(1)}, bf16[2,128,896]{2,1,0:T(8,128)(2,1)S(1)}, u32[]{:S(2)}, u32[]{:S(2)}) collective-permute-start(bf16[2,128,896]{2,1,0:T(8,128)(2,1)S(1)} %get-tuple-element.32), channel_id=1, source_target_pairs={{0,4},{2,6},{4,0},{6,2},{1,5},{3,7},{5,1},{7,3},{8,12},{10,14},{12... | collective-permute-start | bytes 1376264 | tf_op jit(solution)/shard_map/ppermute | solution.py:71
  53.8 1.1 collective-permute-start.12
  54.9 2.3 %shard_map.80 = (bf16[2,128,896]{2,1,0:T(8,128)(2,1)S(1)}, bf16[2,128,896]{2,1,0:T(8,128)(2,1)S(1)}) custom-call(bf16[8,128,1024]{2,1,0:T(8,128)(2,1)S(1)} %get-tuple-element.29.lhs_ref, bf16[768,512]{1,0:T(8,128)(2,1)S(1)} %collective-permute-done.3.refs_0_, bf16[128,512]{1,0:T(8,128)(2,1)} %collective-permute-done.6.refs_1_, ...), custom_call_target="tpu_custom_call" | custom-call | flops 939524096 | bytes 4194304 | tf_op jit(solution)/shard_map/pallas_call | solution.py:158
  57.1 6.7 %collective-permute-done.15.refs_3_ = bf16[2,128,896]{2,1,0:T(8,128)(2,1)S(1)} collective-permute-done((bf16[2,128,896]{2,1,0:T(8,128)(2,1)S(1)}, bf16[2,128,896]{2,1,0:T(8,128)(2,1)S(1)}, u32[]{:S(2)}, u32[]{:S(2)}) %collective-permute-start.15) | collective-permute-done | bytes 458784 | tf_op jit(solution)/shard_map/ppermute | solution.py:71
  63.9 0.2 shard_map.81
  64.1 0.0 copy-start
  64.1 1.4 %collective-permute-start.16 = (bf16[128,896]{1,0:T(8,128)(2,1)S(1)}, bf16[128,896]{1,0:T(8,128)(2,1)S(1)}, u32[]{:S(2)}, u32[]{:S(2)}) collective-permute-start(bf16[128,896]{1,0:T(8,128)(2,1)S(1)} %get-tuple-element.41), channel_id=1, source_target_pairs={{0,2},{2,4},{4,6},{6,0},{1,3},{3,5},{5,7},{7,1},{8,10},{10,12},{12... | collective-permute-start | bytes 688136 | tf_op jit(solution)/shard_map/ppermute | solution.py:71
  65.5 2.6 %collective-permute-start.17 = (bf16[128,896]{1,0:T(8,128)(2,1)S(1)}, bf16[128,896]{1,0:T(8,128)(2,1)S(1)}, u32[]{:S(2)}, u32[]{:S(2)}) collective-permute-start(bf16[128,896]{1,0:T(8,128)(2,1)S(1)} %get-tuple-element.42), channel_id=1, source_target_pairs={{0,4},{2,6},{4,0},{6,2},{1,5},{3,7},{5,1},{7,3},{8,12},{10,14},{12... | collective-permute-start | bytes 688136 | tf_op jit(solution)/shard_map/ppermute | solution.py:71
  68.1 1.1 collective-permute-start.18
  69.2 1.7 %collective-permute-done.11.refs_2_ = bf16[2,128,896]{2,1,0:T(8,128)(2,1)S(1)} collective-permute-done((bf16[2,128,896]{2,1,0:T(8,128)(2,1)S(1)}, bf16[2,128,896]{2,1,0:T(8,128)(2,1)S(1)}, u32[]{:S(2)}, u32[]{:S(2)}) %collective-permute-start.11) | collective-permute-done | bytes 458784 | tf_op jit(solution)/shard_map/ppermute | solution.py:71
  70.9 4.6 %collective-permute-done.12.refs_3_ = bf16[2,128,896]{2,1,0:T(8,128)(2,1)S(1)} collective-permute-done((bf16[2,128,896]{2,1,0:T(8,128)(2,1)S(1)}, bf16[2,128,896]{2,1,0:T(8,128)(2,1)S(1)}, u32[]{:S(2)}, u32[]{:S(2)}) %collective-permute-start.12) | collective-permute-done | bytes 458784 | tf_op jit(solution)/shard_map/ppermute | solution.py:71
  75.6 0.2 shard_map.79
  75.8 0.6 collective-permute-start.13
  76.4 4.4 %collective-permute-done.16.refs_3_ = bf16[128,896]{1,0:T(8,128)(2,1)S(1)} collective-permute-done((bf16[128,896]{1,0:T(8,128)(2,1)S(1)}, bf16[128,896]{1,0:T(8,128)(2,1)S(1)}, u32[]{:S(2)}, u32[]{:S(2)}) %collective-permute-start.16) | collective-permute-done | bytes 229408 | tf_op jit(solution)/shard_map/ppermute | solution.py:71
  80.8 2.3 %collective-permute-done.18.refs_5_ = bf16[128,896]{1,0:T(8,128)(2,1)S(1)} collective-permute-done((bf16[128,896]{1,0:T(8,128)(2,1)S(1)}, bf16[128,896]{1,0:T(8,128)(2,1)S(1)}, u32[]{:S(2)}, u32[]{:S(2)}) %collective-permute-start.18) | collective-permute-done | bytes 229408 | tf_op jit(solution)/shard_map/ppermute | solution.py:71
  83.1 0.7 shard_map.82
  83.9 6.1 %collective-permute-start.19 = (bf16[128,896]{1,0:T(8,128)(2,1)S(1)}, bf16[128,896]{1,0:T(8,128)(2,1)S(1)}, u32[]{:S(2)}, u32[]{:S(2)}) collective-permute-start(bf16[128,896]{1,0:T(8,128)(2,1)S(1)} %get-tuple-element.44), channel_id=1, source_target_pairs={{0,160},{1,96},{2,224},{3,32},{4,161},{5,97},{6,225},{7,33},{8,0},... | collective-permute-start | bytes 688136 | tf_op jit(solution)/shard_map/ppermute | solution.py:291
  90.0 2.5 %collective-permute-start.20 = (bf16[128,896]{1,0:T(8,128)(2,1)S(1)}, bf16[128,896]{1,0:T(8,128)(2,1)S(1)}, u32[]{:S(2)}, u32[]{:S(2)}) collective-permute-start(bf16[128,896]{1,0:T(8,128)(2,1)S(1)} %get-tuple-element.45), channel_id=1, source_target_pairs={{0,161},{1,97},{2,225},{3,33},{4,160},{5,96},{6,224},{7,32},{8,1},... | collective-permute-start | bytes 688136 | tf_op jit(solution)/shard_map/ppermute | solution.py:291
  92.5 2.0 %collective-permute-done.19.first = bf16[128,896]{1,0:T(8,128)(2,1)S(1)} collective-permute-done((bf16[128,896]{1,0:T(8,128)(2,1)S(1)}, bf16[128,896]{1,0:T(8,128)(2,1)S(1)}, u32[]{:S(2)}, u32[]{:S(2)}) %collective-permute-start.19) | collective-permute-done | bytes 229408 | tf_op jit(solution)/shard_map/ppermute | solution.py:291
  94.6 10.8 %collective-permute-done.20.second = bf16[128,896]{1,0:T(8,128)(2,1)S(1)} collective-permute-done((bf16[128,896]{1,0:T(8,128)(2,1)S(1)}, bf16[128,896]{1,0:T(8,128)(2,1)S(1)}, u32[]{:S(2)}, u32[]{:S(2)}) %collective-permute-start.20) | collective-permute-done | bytes 229408 | tf_op jit(solution)/shard_map/ppermute | solution.py:291
  105.3 1.9 %shard_map.83 = (bf16[256,896]{1,0:T(8,128)(2,1)}, bf16[256,896]{1,0:T(8,128)(2,1)}) custom-call(s32[10]{0:T(128)S(1)} %dynamic-slice_bitcast_fusion.facts_ref, bf16[128,896]{1,0:T(8,128)(2,1)S(1)} %collective-permute-done.19.first, bf16[128,896]{1,0:T(8,128)(2,1)S(1)} %collective-permute-done.20.second, bf16[256,896]{1,0:T(8,128)(2,1)S(1)} %copy-done, ...), custom_call_target="tpu_custom_call" | custom-call | flops 2293760 | bytes 2293760 | tf_op jit(solution)/shard_map/pallas_call | solution.py:248
  (17 shorter events, 0.0 us)
Async XLA Ops:
  0.6 1.9 %copy-start.2 = (bf16[896,512]{1,0:T(8,128)(2,1)S(1)}, bf16[896,512]{1,0:T(8,128)(2,1)}, u32[]{:S(2)}) copy-start(bf16[896,512]{1,0:T(8,128)(2,1)} %param.7) | copy-start | bytes 2752516
  0.6 3.5 %collective-permute-start = (bf16[256,512]{1,0:T(8,128)(2,1)}, bf16[256,512]{1,0:T(8,128)(2,1)S(1)}, u32[]{:S(2)}, u32[]{:S(2)}) collective-permute-start(bf16[256,512]{1,0:T(8,128)(2,1)} %param.6), channel_id=1, source_target_pairs={{0,1},{1,0},{2,3},{3,2},{4,5},{5,4},{6,7},{7,6},{8,9},{9,8},{10,11... | collective-permute-start | bytes 786440 | tf_op jit(solution)/shard_map/ppermute | solution.py:71
  2.5 1.7 %copy-start.3 = (bf16[256,512]{1,0:T(8,128)(2,1)S(1)}, bf16[256,512]{1,0:T(8,128)(2,1)}, u32[]{:S(2)}) copy-start(bf16[256,512]{1,0:T(8,128)(2,1)} %param.6) | copy-start | bytes 786436
  2.9 20.7 %collective-permute-start.3 = (bf16[768,512]{1,0:T(8,128)(2,1)S(1)}, bf16[768,512]{1,0:T(8,128)(2,1)S(1)}, u32[]{:S(2)}, u32[]{:S(2)}) collective-permute-start(bf16[768,512]{1,0:T(8,128)(2,1)S(1)} %slice.9), channel_id=1, source_target_pairs={{0,16},{16,0},{1,17},{17,1},{2,18},{18,2},{3,19},{19,3},{4,20},{20... | collective-permute-start | bytes 2359304 | tf_op jit(solution)/shard_map/ppermute | solution.py:71
  4.2 17.8 %collective-permute-start.2 = (bf16[256,1024]{1,0:T(8,128)(2,1)S(1)}, bf16[256,1024]{1,0:T(8,128)(2,1)S(1)}, u32[]{:S(2)}, u32[]{:S(2)}) collective-permute-start(bf16[256,1024]{1,0:T(8,128)(2,1)S(1)} %pad_maximum_fusion.t0), channel_id=1, source_target_pairs={{0,64},{32,96},{64,128},{96,160},{128,192},{160,224},{192,0},{224,... | collective-permute-start | bytes 1572872 | tf_op jit(solution)/shard_map/ppermute | solution.py:271
  10.3 20.4 %collective-permute-start.1 = (bf16[256,1024]{1,0:T(8,128)(2,1)S(1)}, bf16[256,1024]{1,0:T(8,128)(2,1)}, u32[]{:S(2)}, u32[]{:S(2)}) collective-permute-start(bf16[256,1024]{1,0:T(8,128)(2,1)S(1)} %pad_maximum_fusion.t0), channel_id=1, source_target_pairs={{0,32},{32,64},{64,96},{96,128},{128,160},{160,192},{192,224},{224... | collective-permute-start | bytes 1572872 | tf_op jit(solution)/shard_map/ppermute | solution.py:272
  11.1 35.2 %collective-permute-start.9 = (bf16[896,512]{1,0:T(8,128)(2,1)S(1)}, bf16[896,512]{1,0:T(8,128)(2,1)}, u32[]{:S(2)}, u32[]{:S(2)}) collective-permute-start(bf16[896,512]{1,0:T(8,128)(2,1)S(1)} %fusion.w_own_ref), channel_id=1, source_target_pairs={{0,1},{1,0},{2,3},{3,2},{4,5},{5,4},{6,7},{7,6},{8,9},{9,8},{10,11... | collective-permute-start | bytes 2752520 | tf_op jit(solution)/shard_map/ppermute | solution.py:71
  23.6 18.3 %collective-permute-start.7 = (bf16[768,512]{1,0:T(8,128)(2,1)S(1)}, bf16[768,512]{1,0:T(8,128)(2,1)S(1)}, u32[]{:S(2)}, u32[]{:S(2)}) collective-permute-start(bf16[768,512]{1,0:T(8,128)(2,1)S(1)} %collective-permute-done.3.refs_0_), channel_id=1, source_target_pairs={{0,1},{1,0},{2,3},{3,2},{4,5},{5,4},{6,7},{7,6},{8,9},{9,8},{10,11... | collective-permute-start | bytes 2359304 | tf_op jit(solution)/shard_map/ppermute | solution.py:71
  24.5 17.5 %collective-permute-start.4 = (bf16[256,1024]{1,0:T(8,128)(2,1)S(1)}, bf16[256,1024]{1,0:T(8,128)(2,1)}, u32[]{:S(2)}, u32[]{:S(2)}) collective-permute-start(bf16[256,1024]{1,0:T(8,128)(2,1)S(1)} %collective-permute-done.2.t2), channel_id=1, source_target_pairs={{0,32},{32,64},{64,96},{96,128},{128,160},{160,192},{192,224},{224... | collective-permute-start | bytes 1572872 | tf_op jit(solution)/shard_map/ppermute | solution.py:276
  30.7 5.8 %collective-permute-start.6 = (bf16[128,512]{1,0:T(8,128)(2,1)}, bf16[128,512]{1,0:T(8,128)(2,1)}, u32[]{:S(2)}, u32[]{:S(2)}) collective-permute-start(bf16[128,512]{1,0:T(8,128)(2,1)} %slice.8), channel_id=1, source_target_pairs={{0,16},{16,0},{1,17},{17,1},{2,18},{18,2},{3,19},{19,3},{4,20},{20... | collective-permute-start | bytes 393224 | tf_op jit(solution)/shard_map/ppermute | solution.py:71
  32.6 9.4 %collective-permute-start.5 = (bf16[128,1024]{1,0:T(8,128)(2,1)}, bf16[128,1024]{1,0:T(8,128)(2,1)}, u32[]{:S(2)}, u32[]{:S(2)}) collective-permute-start(bf16[128,1024]{1,0:T(8,128)(2,1)} %constant_dynamic-slice_fusion), channel_id=1, source_target_pairs={{0,64},{32,96},{64,128},{96,160},{128,192},{160,224},{192,0},{224,... | collective-permute-start | bytes 786440 | tf_op jit(solution)/shard_map/ppermute | solution.py:277
  36.5 1.7 %collective-permute-start.8 = (bf16[128,512]{1,0:T(8,128)(2,1)}, bf16[128,512]{1,0:T(8,128)(2,1)}, u32[]{:S(2)}, u32[]{:S(2)}) collective-permute-start(bf16[128,512]{1,0:T(8,128)(2,1)} %collective-permute-done.6.refs_1_), channel_id=1, source_target_pairs={{0,1},{1,0},{2,3},{3,2},{4,5},{5,4},{6,7},{7,6},{8,9},{9,8},{10,11... | collective-permute-start | bytes 393224 | tf_op jit(solution)/shard_map/ppermute | solution.py:71
  44.7 12.4 %collective-permute-start.14 = (bf16[2,128,896]{2,1,0:T(8,128)(2,1)S(1)}, bf16[2,128,896]{2,1,0:T(8,128)(2,1)S(1)}, u32[]{:S(2)}, u32[]{:S(2)}) collective-permute-start(bf16[2,128,896]{2,1,0:T(8,128)(2,1)S(1)} %get-tuple-element.38), channel_id=1, source_target_pairs={{0,8},{8,0},{1,9},{9,1},{2,10},{10,2},{3,11},{11,3},{4,12},{12,4},... | collective-permute-start | bytes 1376264 | tf_op jit(solution)/shard_map/ppermute | solution.py:71
  45.3 18.6 %collective-permute-start.15 = (bf16[2,128,896]{2,1,0:T(8,128)(2,1)S(1)}, bf16[2,128,896]{2,1,0:T(8,128)(2,1)S(1)}, u32[]{:S(2)}, u32[]{:S(2)}) collective-permute-start(bf16[2,128,896]{2,1,0:T(8,128)(2,1)S(1)} %get-tuple-element.39), channel_id=1, source_target_pairs={{0,8},{8,0},{1,9},{9,1},{2,10},{10,2},{3,11},{11,3},{4,12},{12,4},... | collective-permute-start | bytes 1376264 | tf_op jit(solution)/shard_map/ppermute | solution.py:71
  49.8 18.3 %collective-permute-start.10 = (bf16[2,128,896]{2,1,0:T(8,128)(2,1)S(1)}, bf16[2,128,896]{2,1,0:T(8,128)(2,1)S(1)}, u32[]{:S(2)}, u32[]{:S(2)}) collective-permute-start(bf16[2,128,896]{2,1,0:T(8,128)(2,1)S(1)} %get-tuple-element.31), channel_id=1, source_target_pairs={{0,2},{2,4},{4,6},{6,0},{1,3},{3,5},{5,7},{7,1},{8,10},{10,12},{12... | collective-permute-start | bytes 1376264 | tf_op jit(solution)/shard_map/ppermute | solution.py:71
  51.2 19.7 %collective-permute-start.11 = (bf16[2,128,896]{2,1,0:T(8,128)(2,1)S(1)}, bf16[2,128,896]{2,1,0:T(8,128)(2,1)S(1)}, u32[]{:S(2)}, u32[]{:S(2)}) collective-permute-start(bf16[2,128,896]{2,1,0:T(8,128)(2,1)S(1)} %get-tuple-element.32), channel_id=1, source_target_pairs={{0,4},{2,6},{4,0},{6,2},{1,5},{3,7},{5,1},{7,3},{8,12},{10,14},{12... | collective-permute-start | bytes 1376264 | tf_op jit(solution)/shard_map/ppermute | solution.py:71
  53.8 21.8 %collective-permute-start.12 = (bf16[2,128,896]{2,1,0:T(8,128)(2,1)S(1)}, bf16[2,128,896]{2,1,0:T(8,128)(2,1)S(1)}, u32[]{:S(2)}, u32[]{:S(2)}) collective-permute-start(bf16[2,128,896]{2,1,0:T(8,128)(2,1)S(1)} %get-tuple-element.33), channel_id=1, source_target_pairs={{0,6},{2,0},{4,2},{6,4},{1,7},{3,1},{5,3},{7,5},{8,14},{10,8},{12,... | collective-permute-start | bytes 1376264 | tf_op jit(solution)/shard_map/ppermute | solution.py:71
  64.1 41.2 %copy-start = (bf16[256,896]{1,0:T(8,128)(2,1)S(1)}, bf16[256,896]{1,0:T(8,128)(2,1)}, u32[]{:S(2)}) copy-start(bf16[256,896]{1,0:T(8,128)(2,1)} %gate_ref.1) | copy-start | bytes 1376260
  64.1 41.2 %copy-start.1 = (bf16[256,896]{1,0:T(8,128)(2,1)S(1)}, bf16[256,896]{1,0:T(8,128)(2,1)}, u32[]{:S(2)}) copy-start(bf16[256,896]{1,0:T(8,128)(2,1)} %up_ref.1) | copy-start | bytes 1376260
  64.1 16.7 %collective-permute-start.16 = (bf16[128,896]{1,0:T(8,128)(2,1)S(1)}, bf16[128,896]{1,0:T(8,128)(2,1)S(1)}, u32[]{:S(2)}, u32[]{:S(2)}) collective-permute-start(bf16[128,896]{1,0:T(8,128)(2,1)S(1)} %get-tuple-element.41), channel_id=1, source_target_pairs={{0,2},{2,4},{4,6},{6,0},{1,3},{3,5},{5,7},{7,1},{8,10},{10,12},{12... | collective-permute-start | bytes 688136 | tf_op jit(solution)/shard_map/ppermute | solution.py:71
  65.5 15.3 %collective-permute-start.17 = (bf16[128,896]{1,0:T(8,128)(2,1)S(1)}, bf16[128,896]{1,0:T(8,128)(2,1)S(1)}, u32[]{:S(2)}, u32[]{:S(2)}) collective-permute-start(bf16[128,896]{1,0:T(8,128)(2,1)S(1)} %get-tuple-element.42), channel_id=1, source_target_pairs={{0,4},{2,6},{4,0},{6,2},{1,5},{3,7},{5,1},{7,3},{8,12},{10,14},{12... | collective-permute-start | bytes 688136 | tf_op jit(solution)/shard_map/ppermute | solution.py:71
  68.1 15.0 %collective-permute-start.18 = (bf16[128,896]{1,0:T(8,128)(2,1)S(1)}, bf16[128,896]{1,0:T(8,128)(2,1)S(1)}, u32[]{:S(2)}, u32[]{:S(2)}) collective-permute-start(bf16[128,896]{1,0:T(8,128)(2,1)S(1)} %get-tuple-element.43), channel_id=1, source_target_pairs={{0,6},{2,0},{4,2},{6,4},{1,7},{3,1},{5,3},{7,5},{8,14},{10,8},{12,... | collective-permute-start | bytes 688136 | tf_op jit(solution)/shard_map/ppermute | solution.py:71
  75.8 7.3 %collective-permute-start.13 = (bf16[128,896]{1,0:T(8,128)(2,1)S(1)}, bf16[128,896]{1,0:T(8,128)(2,1)S(1)}, u32[]{:S(2)}, u32[]{:S(2)}) collective-permute-start(bf16[128,896]{1,0:T(8,128)(2,1)S(1)} %get-tuple-element.35), channel_id=1, source_target_pairs={{0,8},{8,0},{1,9},{9,1},{2,10},{10,2},{3,11},{11,3},{4,12},{12,4},... | collective-permute-start | bytes 688136 | tf_op jit(solution)/shard_map/ppermute | solution.py:71
  83.9 10.7 %collective-permute-start.19 = (bf16[128,896]{1,0:T(8,128)(2,1)S(1)}, bf16[128,896]{1,0:T(8,128)(2,1)S(1)}, u32[]{:S(2)}, u32[]{:S(2)}) collective-permute-start(bf16[128,896]{1,0:T(8,128)(2,1)S(1)} %get-tuple-element.44), channel_id=1, source_target_pairs={{0,160},{1,96},{2,224},{3,32},{4,161},{5,97},{6,225},{7,33},{8,0},... | collective-permute-start | bytes 688136 | tf_op jit(solution)/shard_map/ppermute | solution.py:291
  90.0 15.3 %collective-permute-start.20 = (bf16[128,896]{1,0:T(8,128)(2,1)S(1)}, bf16[128,896]{1,0:T(8,128)(2,1)S(1)}, u32[]{:S(2)}, u32[]{:S(2)}) collective-permute-start(bf16[128,896]{1,0:T(8,128)(2,1)S(1)} %get-tuple-element.45), channel_id=1, source_target_pairs={{0,161},{1,97},{2,225},{3,33},{4,160},{5,96},{6,224},{7,32},{8,1},... | collective-permute-start | bytes 688136 | tf_op jit(solution)/shard_map/ppermute | solution.py:291

commit v12 on v11

--- a/solution.py
+++ b/solution.py
@@ -230,20 +230,36 @@
     )(own, *near_parts, *cross_parts)
 
 
-def swiglu_backward(own, hidden, gate_act, up_act):
+def slopes(gate_act, up_act):
     rows, width = gate_act.shape
+
+    def kernel(gate_ref, up_ref, for_up_ref, for_gate_ref):
+        gate = gate_ref[...].astype(F32)
+        sigmoid = jax.nn.sigmoid(gate)
+        for_up_ref[...] = gate * sigmoid
+        for_gate_ref[...] = up_ref[...].astype(F32) * (sigmoid * (1.0 + gate * (1.0 - sigmoid)))
+
+    return pl.pallas_call(
+        kernel,
+        in_specs=[VMEM] * 2,
+        out_specs=[VMEM] * 2,
+        out_shape=[jax.ShapeDtypeStruct((rows, width), F32)] * 2,
+        compiler_params=params(16),
+        cost_estimate=pl.CostEstimate(flops=8 * rows * width, bytes_accessed=12 * rows * width, transcendentals=rows * width),
+    )(gate_act, up_act)
+
+
+def gradients(own, hidden, for_up, for_gate):
+    rows, width = for_up.shape
     half = rows // 2
 
-    def kernel(facts_ref, first, second, gate_ref, up_ref, grad_gate_ref, grad_up_ref):
+    def kernel(facts_ref, first, second, for_up_ref, for_gate_ref, grad_gate_ref, grad_up_ref):
         flip = facts_ref[S] == 1
         for h, (straight, crossed) in enumerate(((first, second), (second, first))):
             here = slice(h * half, (h + 1) * half)
             value = jnp.where(flip, crossed[...].astype(F32), straight[...].astype(F32))
-            gate = gate_ref[here, :].astype(F32)
-            sigmoid = jax.nn.sigmoid(gate)
-            grad_up_ref[here, :] = (value * gate * sigmoid).astype(BF16)
-            slope = sigmoid * (1.0 + gate * (1.0 - sigmoid))
-            grad_gate_ref[here, :] = (value * up_ref[here, :].astype(F32) * slope).astype(BF16)
+            grad_up_ref[here, :] = (value * for_up_ref[here, :]).astype(BF16)
+            grad_gate_ref[here, :] = (value * for_gate_ref[here, :]).astype(BF16)
 
     return pl.pallas_call(
         kernel,
@@ -251,8 +267,8 @@
         out_specs=[VMEM] * 2,
         out_shape=[jax.ShapeDtypeStruct((rows, width), BF16)] * 2,
         compiler_params=params(16),
-        cost_estimate=pl.CostEstimate(flops=10 * rows * width, bytes_accessed=10 * rows * width, transcendentals=rows * width),
-    )(own, *hidden, gate_act, up_act)
+        cost_estimate=pl.CostEstimate(flops=2 * rows * width, bytes_accessed=12 * rows * width, transcendentals=0),
+    )(own, *hidden, for_up, for_gate)
 
 
 def on_device(grad_out, down_q, scales, gate_act, up_act):
@@ -272,9 +288,9 @@
     one = lax.ppermute(here, ("z", "c"), to(1))
     last, one = lax.optimization_barrier((near_own[cut:], one))
     cross_own.append(shift(last, "xh", XH, 1))
-    two, cross_own[0] = lax.optimization_barrier((two, cross_own[0]))
     three = lax.ppermute(two, ("z", "c"), to(1))
-    far = lax.ppermute(lax.dynamic_slice_in_dim(two, c * rows, rows, 0), ("z", "c"), to(2))
+    gated, cross_own[0] = lax.optimization_barrier((two, cross_own[0]))
+    far = lax.ppermute(lax.dynamic_slice_in_dim(gated, c * rows, rows, 0), ("z", "c"), to(2))
     tokens = [here, one, two, three]
     weights = cross_own + [shift(part, "c", C, 1) for part in cross_own]
 
@@ -289,7 +305,7 @@
 
     sums = add_last(own, near_parts, cross_parts)
     hidden = [lax.ppermute(sums[j], ALL, home_pairs(j)) for j in range(2)]
-    return tuple(swiglu_backward(own, hidden, gate_act, up_act))
+    return tuple(gradients(own, hidden, *slopes(gate_act, up_act)))
 
 
 def solution(mesh):

time: 109 us -> 108 us (level)
  transfers between devices with their start and end apart: 21 -> 21, of which waited for: 12 -> 12; matrix products, arithmetic and copies ran while one was open for 3% -> 3% of each run, Pallas kernels for 8% -> 9%
where the time goes in v12:
time: 108 us; the launch traced here: 107 us
  waiting for transfers between devices  52.3 us (48%)
  starting transfers between devices  38.5 us (36%)
  Pallas kernels  11.8 us (11%)
  local copies, waits for them, and re-layouts  3.23 us (3%)
    ppermute x15, waiting for transfers between devices, shift(): return lax.ppermute(x, axis, [(i, (i + by) % size) for i in range(size)])  25.1 us
    ppermute x15, starting transfers between devices, shift(): return lax.ppermute(x, axis, [(i, (i + by) % size) for i in range(size)])  16.2 us
    ppermute x2, waiting for transfers between devices, on_device(): hidden = [lax.ppermute(sums[j], ALL, home_pairs(j)) for j in range(2)]  12.4 us
    ppermute x1, waiting for transfers between devices, on_device(): two = lax.ppermute(here, ('z', 'c'), to(2))  11 us
    ppermute x2, starting transfers between devices, on_device(): hidden = [lax.ppermute(sums[j], ALL, home_pairs(j)) for j in range(2)]  8.68 us
    ppermute x1, starting transfers between devices, on_device(): two = lax.ppermute(here, ('z', 'c'), to(2))  6.1 us
    ppermute x1, starting transfers between devices, on_device(): three = lax.ppermute(two, ('z', 'c'), to(1))  5.58 us
    ppermute x1, waiting for transfers between devices, on_device(): lax.ppermute(lax.dynamic_slice_in_dim(gated, c * rows, rows, 0), ('z', 'c...  3.76 us
  transfers between devices with their start and end apart: 21, of which 12 were waited for; matrix products, arithmetic and copies ran while one was open for 3% of the time, Pallas kernels for 9%

profile of v12, /device:TPU:7, one launch (start us, length us, event | category | flops | bytes accessed | tf_op | source)
XLA Modules:
  0.0 107.0 jit_solution(7520312973431113457)
XLA Ops:
  0.6 0.8 collective-permute-start
  1.4 0.8 copy.8
  2.2 0.3 mul.30
  2.5 0.0 copy-start.3
  2.5 0.4 fusion.w_own_ref
  2.9 0.1 slice.9
  2.9 1.2 %collective-permute-start.4 = (bf16[768,512]{1,0:T(8,128)(2,1)S(1)}, bf16[768,512]{1,0:T(8,128)(2,1)S(1)}, u32[]{:S(2)}, u32[]{:S(2)}) collective-permute-start(bf16[768,512]{1,0:T(8,128)(2,1)S(1)} %slice.9), channel_id=1, source_target_pairs={{0,16},{16,0},{1,17},{17,1},{2,18},{18,2},{3,19},{19,3},{4,20},{20... | collective-permute-start | bytes 2359304 | tf_op jit(solution)/shard_map/ppermute | solution.py:71
  4.2 0.1 pad_maximum_fusion.t0
  4.2 6.1 %collective-permute-start.2 = (bf16[256,1024]{1,0:T(8,128)(2,1)S(1)}, bf16[256,1024]{1,0:T(8,128)(2,1)S(1)}, u32[]{:S(2)}, u32[]{:S(2)}) collective-permute-start(bf16[256,1024]{1,0:T(8,128)(2,1)S(1)} %pad_maximum_fusion.t0), channel_id=1, source_target_pairs={{0,64},{32,96},{64,128},{96,160},{128,192},{160,224},{192,0},{224,... | collective-permute-start | bytes 1572872 | tf_op jit(solution)/shard_map/ppermute | solution.py:287
  10.3 0.7 collective-permute-start.1
  11.1 11.0 %collective-permute-done.2.t2 = bf16[256,1024]{1,0:T(8,128)(2,1)S(1)} collective-permute-done((bf16[256,1024]{1,0:T(8,128)(2,1)S(1)}, bf16[256,1024]{1,0:T(8,128)(2,1)S(1)}, u32[]{:S(2)}, u32[]{:S(2)}) %collective-permute-start.2) | collective-permute-done | bytes 524320 | tf_op jit(solution)/shard_map/ppermute | solution.py:287
  22.1 1.6 %collective-permute-done.4.refs_0_ = bf16[768,512]{1,0:T(8,128)(2,1)S(1)} collective-permute-done((bf16[768,512]{1,0:T(8,128)(2,1)S(1)}, bf16[768,512]{1,0:T(8,128)(2,1)S(1)}, u32[]{:S(2)}, u32[]{:S(2)}) %collective-permute-start.4) | collective-permute-done | bytes 786464 | tf_op jit(solution)/shard_map/ppermute | solution.py:71
  23.6 0.8 collective-permute-start.7
  24.5 5.6 %collective-permute-start.3 = (bf16[256,1024]{1,0:T(8,128)(2,1)S(1)}, bf16[256,1024]{1,0:T(8,128)(2,1)}, u32[]{:S(2)}, u32[]{:S(2)}) collective-permute-start(bf16[256,1024]{1,0:T(8,128)(2,1)S(1)} %collective-permute-done.2.t2), channel_id=1, source_target_pairs={{0,32},{32,64},{64,96},{96,128},{128,160},{160,192},{192,224},{224... | collective-permute-start | bytes 1572872 | tf_op jit(solution)/shard_map/ppermute | solution.py:291
  30.1 0.7 slice.8
  30.7 1.1 %collective-permute-start.6 = (bf16[128,512]{1,0:T(8,128)(2,1)}, bf16[128,512]{1,0:T(8,128)(2,1)}, u32[]{:S(2)}, u32[]{:S(2)}) collective-permute-start(bf16[128,512]{1,0:T(8,128)(2,1)} %slice.8), channel_id=1, source_target_pairs={{0,16},{16,0},{1,17},{17,1},{2,18},{18,2},{3,19},{19,3},{4,20},{20... | collective-permute-start | bytes 393224 | tf_op jit(solution)/shard_map/ppermute | solution.py:71
  31.9 0.7 constant_dynamic-slice_fusion
  32.6 1.2 %collective-permute-start.5 = (bf16[128,1024]{1,0:T(8,128)(2,1)}, bf16[128,1024]{1,0:T(8,128)(2,1)}, u32[]{:S(2)}, u32[]{:S(2)}) collective-permute-start(bf16[128,1024]{1,0:T(8,128)(2,1)} %constant_dynamic-slice_fusion), channel_id=1, source_target_pairs={{0,64},{32,96},{64,128},{96,160},{128,192},{160,224},{192,0},{224,... | collective-permute-start | bytes 786440 | tf_op jit(solution)/shard_map/ppermute | solution.py:293
  33.8 2.7 %collective-permute-done.6.refs_1_ = bf16[128,512]{1,0:T(8,128)(2,1)} collective-permute-done((bf16[128,512]{1,0:T(8,128)(2,1)}, bf16[128,512]{1,0:T(8,128)(2,1)}, u32[]{:S(2)}, u32[]{:S(2)}) %collective-permute-start.6) | collective-permute-done | bytes 131104 | tf_op jit(solution)/shard_map/ppermute | solution.py:71
  36.5 0.7 dynamic-slice_bitcast_fusion.facts_ref
  37.2 1.0 collective-permute-done.8.refs_3_
  38.2 3.8 %collective-permute-done.5.far_ref = bf16[128,1024]{1,0:T(8,128)(2,1)} collective-permute-done((bf16[128,1024]{1,0:T(8,128)(2,1)}, bf16[128,1024]{1,0:T(8,128)(2,1)}, u32[]{:S(2)}, u32[]{:S(2)}) %collective-permute-start.5) | collective-permute-done | bytes 262176 | tf_op jit(solution)/shard_map/ppermute | solution.py:293
  42.0 2.7 %shard_map.77 = (bf16[8,128,1024]{2,1,0:T(8,128)(2,1)S(1)}, bf16[2,128,896]{2,1,0:T(8,128)(2,1)S(1)}, bf16[2,128,896]{2,1,0:T(8,128)(2,1)S(1)}) custom-call(s32[10]{0:T(128)S(1)} %dynamic-slice_bitcast_fusion.facts_ref, bf16[256,1024]{1,0:T(8,128)(2,1)S(1)} %pad_maximum_fusion.t0, bf16[256,1024]{1,0:T(8,128)(2,1)} %collective-permute-done.1.t1, ...), custom_call_target="tpu_custom_call" | custom-call | flops 939524096 | bytes 7340032 | tf_op jit(solution)/shard_map/pallas_call | solution.py:116
  44.7 0.6 collective-permute-start.14
  45.3 0.9 collective-permute-start.15
  46.3 3.6 %shard_map.78 = (bf16[2,128,896]{2,1,0:T(8,128)(2,1)S(1)}, bf16[2,128,896]{2,1,0:T(8,128)(2,1)S(1)}, bf16[2,128,896]{2,1,0:T(8,128)(2,1)S(1)}, bf16[2,128,896]{2,1,0:T(8,128)(2,1)S(1)}) custom-call(bf16[8,128,1024]{2,1,0:T(8,128)(2,1)S(1)} %get-tuple-element.31.lhs_ref, bf16[896,512]{1,0:T(8,128)(2,1)S(1)} %fusion.w_own_ref, ...), custom_call_target="tpu_custom_call" | custom-call | flops 1879048192 | bytes 6291456 | tf_op jit(solution)/shard_map/pallas_call | solution.py:137
  49.8 1.4 %collective-permute-start.10 = (bf16[2,128,896]{2,1,0:T(8,128)(2,1)S(1)}, bf16[2,128,896]{2,1,0:T(8,128)(2,1)S(1)}, u32[]{:S(2)}, u32[]{:S(2)}) collective-permute-start(bf16[2,128,896]{2,1,0:T(8,128)(2,1)S(1)} %get-tuple-element.33), channel_id=1, source_target_pairs={{0,2},{2,4},{4,6},{6,0},{1,3},{3,5},{5,7},{7,1},{8,10},{10,12},{12... | collective-permute-start | bytes 1376264 | tf_op jit(solution)/shard_map/ppermute | solution.py:71
  51.2 2.6 %collective-permute-start.11 = (bf16[2,128,896]{2,1,0:T(8,128)(2,1)S(1)}, bf16[2,128,896]{2,1,0:T(8,128)(2,1)S(1)}, u32[]{:S(2)}, u32[]{:S(2)}) collective-permute-start(bf16[2,128,896]{2,1,0:T(8,128)(2,1)S(1)} %get-tuple-element.34), channel_id=1, source_target_pairs={{0,4},{2,6},{4,0},{6,2},{1,5},{3,7},{5,1},{7,3},{8,12},{10,14},{12... | collective-permute-start | bytes 1376264 | tf_op jit(solution)/shard_map/ppermute | solution.py:71
  53.8 1.1 collective-permute-start.12
  54.9 2.3 %shard_map.80 = (bf16[2,128,896]{2,1,0:T(8,128)(2,1)S(1)}, bf16[2,128,896]{2,1,0:T(8,128)(2,1)S(1)}) custom-call(bf16[8,128,1024]{2,1,0:T(8,128)(2,1)S(1)} %get-tuple-element.31.lhs_ref, bf16[768,512]{1,0:T(8,128)(2,1)S(1)} %collective-permute-done.4.refs_0_, bf16[128,512]{1,0:T(8,128)(2,1)} %collective-permute-done.6.refs_1_, ...), custom_call_target="tpu_custom_call" | custom-call | flops 939524096 | bytes 4194304 | tf_op jit(solution)/shard_map/pallas_call | solution.py:158
  57.1 6.7 %collective-permute-done.15.refs_3_ = bf16[2,128,896]{2,1,0:T(8,128)(2,1)S(1)} collective-permute-done((bf16[2,128,896]{2,1,0:T(8,128)(2,1)S(1)}, bf16[2,128,896]{2,1,0:T(8,128)(2,1)S(1)}, u32[]{:S(2)}, u32[]{:S(2)}) %collective-permute-start.15) | collective-permute-done | bytes 458784 | tf_op jit(solution)/shard_map/ppermute | solution.py:71
  63.9 0.2 shard_map.81
  64.1 1.4 %collective-permute-start.16 = (bf16[128,896]{1,0:T(8,128)(2,1)S(1)}, bf16[128,896]{1,0:T(8,128)(2,1)S(1)}, u32[]{:S(2)}, u32[]{:S(2)}) collective-permute-start(bf16[128,896]{1,0:T(8,128)(2,1)S(1)} %get-tuple-element.43), channel_id=1, source_target_pairs={{0,2},{2,4},{4,6},{6,0},{1,3},{3,5},{5,7},{7,1},{8,10},{10,12},{12... | collective-permute-start | bytes 688136 | tf_op jit(solution)/shard_map/ppermute | solution.py:71
  65.5 2.6 %collective-permute-start.17 = (bf16[128,896]{1,0:T(8,128)(2,1)S(1)}, bf16[128,896]{1,0:T(8,128)(2,1)S(1)}, u32[]{:S(2)}, u32[]{:S(2)}) collective-permute-start(bf16[128,896]{1,0:T(8,128)(2,1)S(1)} %get-tuple-element.44), channel_id=1, source_target_pairs={{0,4},{2,6},{4,0},{6,2},{1,5},{3,7},{5,1},{7,3},{8,12},{10,14},{12... | collective-permute-start | bytes 688136 | tf_op jit(solution)/shard_map/ppermute | solution.py:71
  68.1 1.1 collective-permute-start.18
  69.2 1.7 %collective-permute-done.11.refs_2_ = bf16[2,128,896]{2,1,0:T(8,128)(2,1)S(1)} collective-permute-done((bf16[2,128,896]{2,1,0:T(8,128)(2,1)S(1)}, bf16[2,128,896]{2,1,0:T(8,128)(2,1)S(1)}, u32[]{:S(2)}, u32[]{:S(2)}) %collective-permute-start.11) | collective-permute-done | bytes 458784 | tf_op jit(solution)/shard_map/ppermute | solution.py:71
  70.9 4.6 %collective-permute-done.12.refs_3_ = bf16[2,128,896]{2,1,0:T(8,128)(2,1)S(1)} collective-permute-done((bf16[2,128,896]{2,1,0:T(8,128)(2,1)S(1)}, bf16[2,128,896]{2,1,0:T(8,128)(2,1)S(1)}, u32[]{:S(2)}, u32[]{:S(2)}) %collective-permute-start.12) | collective-permute-done | bytes 458784 | tf_op jit(solution)/shard_map/ppermute | solution.py:71
  75.6 0.2 shard_map.79
  75.8 0.6 collective-permute-start.13
  76.4 4.4 %collective-permute-done.16.refs_3_ = bf16[128,896]{1,0:T(8,128)(2,1)S(1)} collective-permute-done((bf16[128,896]{1,0:T(8,128)(2,1)S(1)}, bf16[128,896]{1,0:T(8,128)(2,1)S(1)}, u32[]{:S(2)}, u32[]{:S(2)}) %collective-permute-start.16) | collective-permute-done | bytes 229408 | tf_op jit(solution)/shard_map/ppermute | solution.py:71
  80.8 2.3 %collective-permute-done.18.refs_5_ = bf16[128,896]{1,0:T(8,128)(2,1)S(1)} collective-permute-done((bf16[128,896]{1,0:T(8,128)(2,1)S(1)}, bf16[128,896]{1,0:T(8,128)(2,1)S(1)}, u32[]{:S(2)}, u32[]{:S(2)}) %collective-permute-start.18) | collective-permute-done | bytes 229408 | tf_op jit(solution)/shard_map/ppermute | solution.py:71
  83.1 0.7 shard_map.82
  83.9 6.1 %collective-permute-start.19 = (bf16[128,896]{1,0:T(8,128)(2,1)S(1)}, bf16[128,896]{1,0:T(8,128)(2,1)S(1)}, u32[]{:S(2)}, u32[]{:S(2)}) collective-permute-start(bf16[128,896]{1,0:T(8,128)(2,1)S(1)} %get-tuple-element.46), channel_id=1, source_target_pairs={{0,160},{1,96},{2,224},{3,32},{4,161},{5,97},{6,225},{7,33},{8,0},... | collective-permute-start | bytes 688136 | tf_op jit(solution)/shard_map/ppermute | solution.py:307
  90.0 2.5 %collective-permute-start.20 = (bf16[128,896]{1,0:T(8,128)(2,1)S(1)}, bf16[128,896]{1,0:T(8,128)(2,1)S(1)}, u32[]{:S(2)}, u32[]{:S(2)}) collective-permute-start(bf16[128,896]{1,0:T(8,128)(2,1)S(1)} %get-tuple-element.47), channel_id=1, source_target_pairs={{0,161},{1,97},{2,225},{3,33},{4,160},{5,96},{6,224},{7,32},{8,1},... | collective-permute-start | bytes 688136 | tf_op jit(solution)/shard_map/ppermute | solution.py:307
  92.6 0.4 shard_map.83
  93.0 1.6 %collective-permute-done.19.first = bf16[128,896]{1,0:T(8,128)(2,1)S(1)} collective-permute-done((bf16[128,896]{1,0:T(8,128)(2,1)S(1)}, bf16[128,896]{1,0:T(8,128)(2,1)S(1)}, u32[]{:S(2)}, u32[]{:S(2)}) %collective-permute-start.19) | collective-permute-done | bytes 229408 | tf_op jit(solution)/shard_map/ppermute | solution.py:307
  94.6 10.8 %collective-permute-done.20.second = bf16[128,896]{1,0:T(8,128)(2,1)S(1)} collective-permute-done((bf16[128,896]{1,0:T(8,128)(2,1)S(1)}, bf16[128,896]{1,0:T(8,128)(2,1)S(1)}, u32[]{:S(2)}, u32[]{:S(2)}) %collective-permute-start.20) | collective-permute-done | bytes 229408 | tf_op jit(solution)/shard_map/ppermute | solution.py:307
  105.3 1.6 %shard_map.84 = (bf16[256,896]{1,0:T(8,128)(2,1)}, bf16[256,896]{1,0:T(8,128)(2,1)}) custom-call(s32[10]{0:T(128)S(1)} %dynamic-slice_bitcast_fusion.facts_ref, bf16[128,896]{1,0:T(8,128)(2,1)S(1)} %collective-permute-done.19.first, bf16[128,896]{1,0:T(8,128)(2,1)S(1)} %collective-permute-done.20.second, f32[256,896]{1,0:T(8,128)S(1)} %get-tuple-element.48.for_up_ref, ...), custom_call_target="tpu_custom_call" | custom-call | flops 458752 | bytes 2752512 | tf_op jit(solution)/shard_map/pallas_call | solution.py:264
  (18 shorter events, 0.0 us)
Async XLA Ops:
  0.6 1.9 %copy-start.2 = (bf16[896,512]{1,0:T(8,128)(2,1)S(1)}, bf16[896,512]{1,0:T(8,128)(2,1)}, u32[]{:S(2)}) copy-start(bf16[896,512]{1,0:T(8,128)(2,1)} %param.7) | copy-start | bytes 2752516
  0.6 3.5 %collective-permute-start = (bf16[256,512]{1,0:T(8,128)(2,1)}, bf16[256,512]{1,0:T(8,128)(2,1)S(1)}, u32[]{:S(2)}, u32[]{:S(2)}) collective-permute-start(bf16[256,512]{1,0:T(8,128)(2,1)} %param.6), channel_id=1, source_target_pairs={{0,1},{1,0},{2,3},{3,2},{4,5},{5,4},{6,7},{7,6},{8,9},{9,8},{10,11... | collective-permute-start | bytes 786440 | tf_op jit(solution)/shard_map/ppermute | solution.py:71
  2.5 1.7 %copy-start.3 = (bf16[256,512]{1,0:T(8,128)(2,1)S(1)}, bf16[256,512]{1,0:T(8,128)(2,1)}, u32[]{:S(2)}) copy-start(bf16[256,512]{1,0:T(8,128)(2,1)} %param.6) | copy-start | bytes 786436
  2.9 20.7 %collective-permute-start.4 = (bf16[768,512]{1,0:T(8,128)(2,1)S(1)}, bf16[768,512]{1,0:T(8,128)(2,1)S(1)}, u32[]{:S(2)}, u32[]{:S(2)}) collective-permute-start(bf16[768,512]{1,0:T(8,128)(2,1)S(1)} %slice.9), channel_id=1, source_target_pairs={{0,16},{16,0},{1,17},{17,1},{2,18},{18,2},{3,19},{19,3},{4,20},{20... | collective-permute-start | bytes 2359304 | tf_op jit(solution)/shard_map/ppermute | solution.py:71
  4.2 17.8 %collective-permute-start.2 = (bf16[256,1024]{1,0:T(8,128)(2,1)S(1)}, bf16[256,1024]{1,0:T(8,128)(2,1)S(1)}, u32[]{:S(2)}, u32[]{:S(2)}) collective-permute-start(bf16[256,1024]{1,0:T(8,128)(2,1)S(1)} %pad_maximum_fusion.t0), channel_id=1, source_target_pairs={{0,64},{32,96},{64,128},{96,160},{128,192},{160,224},{192,0},{224,... | collective-permute-start | bytes 1572872 | tf_op jit(solution)/shard_map/ppermute | solution.py:287
  10.3 20.4 %collective-permute-start.1 = (bf16[256,1024]{1,0:T(8,128)(2,1)S(1)}, bf16[256,1024]{1,0:T(8,128)(2,1)}, u32[]{:S(2)}, u32[]{:S(2)}) collective-permute-start(bf16[256,1024]{1,0:T(8,128)(2,1)S(1)} %pad_maximum_fusion.t0), channel_id=1, source_target_pairs={{0,32},{32,64},{64,96},{96,128},{128,160},{160,192},{192,224},{224... | collective-permute-start | bytes 1572872 | tf_op jit(solution)/shard_map/ppermute | solution.py:288
  11.1 35.2 %collective-permute-start.9 = (bf16[896,512]{1,0:T(8,128)(2,1)S(1)}, bf16[896,512]{1,0:T(8,128)(2,1)}, u32[]{:S(2)}, u32[]{:S(2)}) collective-permute-start(bf16[896,512]{1,0:T(8,128)(2,1)S(1)} %fusion.w_own_ref), channel_id=1, source_target_pairs={{0,1},{1,0},{2,3},{3,2},{4,5},{5,4},{6,7},{7,6},{8,9},{9,8},{10,11... | collective-permute-start | bytes 2752520 | tf_op jit(solution)/shard_map/ppermute | solution.py:71
  23.6 18.3 %collective-permute-start.7 = (bf16[768,512]{1,0:T(8,128)(2,1)S(1)}, bf16[768,512]{1,0:T(8,128)(2,1)S(1)}, u32[]{:S(2)}, u32[]{:S(2)}) collective-permute-start(bf16[768,512]{1,0:T(8,128)(2,1)S(1)} %collective-permute-done.4.refs_0_), channel_id=1, source_target_pairs={{0,1},{1,0},{2,3},{3,2},{4,5},{5,4},{6,7},{7,6},{8,9},{9,8},{10,11... | collective-permute-start | bytes 2359304 | tf_op jit(solution)/shard_map/ppermute | solution.py:71
  24.5 17.5 %collective-permute-start.3 = (bf16[256,1024]{1,0:T(8,128)(2,1)S(1)}, bf16[256,1024]{1,0:T(8,128)(2,1)}, u32[]{:S(2)}, u32[]{:S(2)}) collective-permute-start(bf16[256,1024]{1,0:T(8,128)(2,1)S(1)} %collective-permute-done.2.t2), channel_id=1, source_target_pairs={{0,32},{32,64},{64,96},{96,128},{128,160},{160,192},{192,224},{224... | collective-permute-start | bytes 1572872 | tf_op jit(solution)/shard_map/ppermute | solution.py:291
  30.7 5.8 %collective-permute-start.6 = (bf16[128,512]{1,0:T(8,128)(2,1)}, bf16[128,512]{1,0:T(8,128)(2,1)}, u32[]{:S(2)}, u32[]{:S(2)}) collective-permute-start(bf16[128,512]{1,0:T(8,128)(2,1)} %slice.8), channel_id=1, source_target_pairs={{0,16},{16,0},{1,17},{17,1},{2,18},{18,2},{3,19},{19,3},{4,20},{20... | collective-permute-start | bytes 393224 | tf_op jit(solution)/shard_map/ppermute | solution.py:71
  32.6 9.4 %collective-permute-start.5 = (bf16[128,1024]{1,0:T(8,128)(2,1)}, bf16[128,1024]{1,0:T(8,128)(2,1)}, u32[]{:S(2)}, u32[]{:S(2)}) collective-permute-start(bf16[128,1024]{1,0:T(8,128)(2,1)} %constant_dynamic-slice_fusion), channel_id=1, source_target_pairs={{0,64},{32,96},{64,128},{96,160},{128,192},{160,224},{192,0},{224,... | collective-permute-start | bytes 786440 | tf_op jit(solution)/shard_map/ppermute | solution.py:293
  36.5 1.7 %collective-permute-start.8 = (bf16[128,512]{1,0:T(8,128)(2,1)}, bf16[128,512]{1,0:T(8,128)(2,1)}, u32[]{:S(2)}, u32[]{:S(2)}) collective-permute-start(bf16[128,512]{1,0:T(8,128)(2,1)} %collective-permute-done.6.refs_1_), channel_id=1, source_target_pairs={{0,1},{1,0},{2,3},{3,2},{4,5},{5,4},{6,7},{7,6},{8,9},{9,8},{10,11... | collective-permute-start | bytes 393224 | tf_op jit(solution)/shard_map/ppermute | solution.py:71
  44.7 12.4 %collective-permute-start.14 = (bf16[2,128,896]{2,1,0:T(8,128)(2,1)S(1)}, bf16[2,128,896]{2,1,0:T(8,128)(2,1)S(1)}, u32[]{:S(2)}, u32[]{:S(2)}) collective-permute-start(bf16[2,128,896]{2,1,0:T(8,128)(2,1)S(1)} %get-tuple-element.40), channel_id=1, source_target_pairs={{0,8},{8,0},{1,9},{9,1},{2,10},{10,2},{3,11},{11,3},{4,12},{12,4},... | collective-permute-start | bytes 1376264 | tf_op jit(solution)/shard_map/ppermute | solution.py:71
  45.3 18.6 %collective-permute-start.15 = (bf16[2,128,896]{2,1,0:T(8,128)(2,1)S(1)}, bf16[2,128,896]{2,1,0:T(8,128)(2,1)S(1)}, u32[]{:S(2)}, u32[]{:S(2)}) collective-permute-start(bf16[2,128,896]{2,1,0:T(8,128)(2,1)S(1)} %get-tuple-element.41), channel_id=1, source_target_pairs={{0,8},{8,0},{1,9},{9,1},{2,10},{10,2},{3,11},{11,3},{4,12},{12,4},... | collective-permute-start | bytes 1376264 | tf_op jit(solution)/shard_map/ppermute | solution.py:71
  49.8 18.3 %collective-permute-start.10 = (bf16[2,128,896]{2,1,0:T(8,128)(2,1)S(1)}, bf16[2,128,896]{2,1,0:T(8,128)(2,1)S(1)}, u32[]{:S(2)}, u32[]{:S(2)}) collective-permute-start(bf16[2,128,896]{2,1,0:T(8,128)(2,1)S(1)} %get-tuple-element.33), channel_id=1, source_target_pairs={{0,2},{2,4},{4,6},{6,0},{1,3},{3,5},{5,7},{7,1},{8,10},{10,12},{12... | collective-permute-start | bytes 1376264 | tf_op jit(solution)/shard_map/ppermute | solution.py:71
  51.2 19.7 %collective-permute-start.11 = (bf16[2,128,896]{2,1,0:T(8,128)(2,1)S(1)}, bf16[2,128,896]{2,1,0:T(8,128)(2,1)S(1)}, u32[]{:S(2)}, u32[]{:S(2)}) collective-permute-start(bf16[2,128,896]{2,1,0:T(8,128)(2,1)S(1)} %get-tuple-element.34), channel_id=1, source_target_pairs={{0,4},{2,6},{4,0},{6,2},{1,5},{3,7},{5,1},{7,3},{8,12},{10,14},{12... | collective-permute-start | bytes 1376264 | tf_op jit(solution)/shard_map/ppermute | solution.py:71
  53.8 21.8 %collective-permute-start.12 = (bf16[2,128,896]{2,1,0:T(8,128)(2,1)S(1)}, bf16[2,128,896]{2,1,0:T(8,128)(2,1)S(1)}, u32[]{:S(2)}, u32[]{:S(2)}) collective-permute-start(bf16[2,128,896]{2,1,0:T(8,128)(2,1)S(1)} %get-tuple-element.35), channel_id=1, source_target_pairs={{0,6},{2,0},{4,2},{6,4},{1,7},{3,1},{5,3},{7,5},{8,14},{10,8},{12,... | collective-permute-start | bytes 1376264 | tf_op jit(solution)/shard_map/ppermute | solution.py:71
  64.1 28.4 %copy-start = (bf16[256,896]{1,0:T(8,128)(2,1)S(1)}, bf16[256,896]{1,0:T(8,128)(2,1)}, u32[]{:S(2)}) copy-start(bf16[256,896]{1,0:T(8,128)(2,1)} %gate_ref.1) | copy-start | bytes 1376260
  64.1 28.4 %copy-start.1 = (bf16[256,896]{1,0:T(8,128)(2,1)S(1)}, bf16[256,896]{1,0:T(8,128)(2,1)}, u32[]{:S(2)}) copy-start(bf16[256,896]{1,0:T(8,128)(2,1)} %up_ref.1) | copy-start | bytes 1376260
  64.1 16.7 %collective-permute-start.16 = (bf16[128,896]{1,0:T(8,128)(2,1)S(1)}, bf16[128,896]{1,0:T(8,128)(2,1)S(1)}, u32[]{:S(2)}, u32[]{:S(2)}) collective-permute-start(bf16[128,896]{1,0:T(8,128)(2,1)S(1)} %get-tuple-element.43), channel_id=1, source_target_pairs={{0,2},{2,4},{4,6},{6,0},{1,3},{3,5},{5,7},{7,1},{8,10},{10,12},{12... | collective-permute-start | bytes 688136 | tf_op jit(solution)/shard_map/ppermute | solution.py:71
  65.5 15.3 %collective-permute-start.17 = (bf16[128,896]{1,0:T(8,128)(2,1)S(1)}, bf16[128,896]{1,0:T(8,128)(2,1)S(1)}, u32[]{:S(2)}, u32[]{:S(2)}) collective-permute-start(bf16[128,896]{1,0:T(8,128)(2,1)S(1)} %get-tuple-element.44), channel_id=1, source_target_pairs={{0,4},{2,6},{4,0},{6,2},{1,5},{3,7},{5,1},{7,3},{8,12},{10,14},{12... | collective-permute-start | bytes 688136 | tf_op jit(solution)/shard_map/ppermute | solution.py:71
  68.1 15.0 %collective-permute-start.18 = (bf16[128,896]{1,0:T(8,128)(2,1)S(1)}, bf16[128,896]{1,0:T(8,128)(2,1)S(1)}, u32[]{:S(2)}, u32[]{:S(2)}) collective-permute-start(bf16[128,896]{1,0:T(8,128)(2,1)S(1)} %get-tuple-element.45), channel_id=1, source_target_pairs={{0,6},{2,0},{4,2},{6,4},{1,7},{3,1},{5,3},{7,5},{8,14},{10,8},{12,... | collective-permute-start | bytes 688136 | tf_op jit(solution)/shard_map/ppermute | solution.py:71
  75.8 7.3 %collective-permute-start.13 = (bf16[128,896]{1,0:T(8,128)(2,1)S(1)}, bf16[128,896]{1,0:T(8,128)(2,1)S(1)}, u32[]{:S(2)}, u32[]{:S(2)}) collective-permute-start(bf16[128,896]{1,0:T(8,128)(2,1)S(1)} %get-tuple-element.37), channel_id=1, source_target_pairs={{0,8},{8,0},{1,9},{9,1},{2,10},{10,2},{3,11},{11,3},{4,12},{12,4},... | collective-permute-start | bytes 688136 | tf_op jit(solution)/shard_map/ppermute | solution.py:71
  83.9 10.7 %collective-permute-start.19 = (bf16[128,896]{1,0:T(8,128)(2,1)S(1)}, bf16[128,896]{1,0:T(8,128)(2,1)S(1)}, u32[]{:S(2)}, u32[]{:S(2)}) collective-permute-start(bf16[128,896]{1,0:T(8,128)(2,1)S(1)} %get-tuple-element.46), channel_id=1, source_target_pairs={{0,160},{1,96},{2,224},{3,32},{4,161},{5,97},{6,225},{7,33},{8,0},... | collective-permute-start | bytes 688136 | tf_op jit(solution)/shard_map/ppermute | solution.py:307
  90.0 15.3 %collective-permute-start.20 = (bf16[128,896]{1,0:T(8,128)(2,1)S(1)}, bf16[128,896]{1,0:T(8,128)(2,1)S(1)}, u32[]{:S(2)}, u32[]{:S(2)}) collective-permute-start(bf16[128,896]{1,0:T(8,128)(2,1)S(1)} %get-tuple-element.47), channel_id=1, source_target_pairs={{0,161},{1,97},{2,225},{3,33},{4,160},{5,96},{6,224},{7,32},{8,1},... | collective-permute-start | bytes 688136 | tf_op jit(solution)/shard_map/ppermute | solution.py:307

commit v13 on v12

--- a/solution.py
+++ b/solution.py
@@ -277,7 +277,7 @@
 
     near_own = dequantize(down_q, scales)
     near_other = shift(near_own, "c", C, 1)
-    cut = 6 * BLOCK
+    cut = 5 * BLOCK
     cross_own = [shift(near_own[:cut], "xh", XH, 1)]
 
     rows = grad_out.shape[0] // 2
@@ -286,11 +286,10 @@
     here, _ = lax.optimization_barrier((here, near_own))
     two = lax.ppermute(here, ("z", "c"), to(2))
     one = lax.ppermute(here, ("z", "c"), to(1))
-    last, one = lax.optimization_barrier((near_own[cut:], one))
+    last, one, cross_own[0] = lax.optimization_barrier((near_own[cut:], one, cross_own[0]))
     cross_own.append(shift(last, "xh", XH, 1))
     three = lax.ppermute(two, ("z", "c"), to(1))
-    gated, cross_own[0] = lax.optimization_barrier((two, cross_own[0]))
-    far = lax.ppermute(lax.dynamic_slice_in_dim(gated, c * rows, rows, 0), ("z", "c"), to(2))
+    far = lax.ppermute(lax.dynamic_slice_in_dim(two, c * rows, rows, 0), ("z", "c"), to(2))
     tokens = [here, one, two, three]
     weights = cross_own + [shift(part, "c", C, 1) for part in cross_own]
 

time: 108 us -> 111 us (1.028)
  the two profiles are of different devices: /device:TPU:7 before, /device:TPU:10 now
where the time goes in v13:
time: 111 us; the launch traced here: 110 us
  waiting for transfers between devices  50.6 us (46%)
  starting transfers between devices  41.7 us (38%)
  Pallas kernels  11.6 us (10%)
  local copies, waits for them, and re-layouts  5.17 us (5%)
    ppermute x15, waiting for transfers between devices, shift(): return lax.ppermute(x, axis, [(i, (i + by) % size) for i in range(size)])  25.5 us
    ppermute x15, starting transfers between devices, shift(): return lax.ppermute(x, axis, [(i, (i + by) % size) for i in range(size)])  20.2 us
    ppermute x1, waiting for transfers between devices, on_device(): lax.ppermute(lax.dynamic_slice_in_dim(two, c * rows, rows, 0), ('z', 'c')...  12.1 us
    ppermute x2, waiting for transfers between devices, on_device(): hidden = [lax.ppermute(sums[j], ALL, home_pairs(j)) for j in range(2)]  12 us
    ppermute x2, starting transfers between devices, on_device(): hidden = [lax.ppermute(sums[j], ALL, home_pairs(j)) for j in range(2)]  10.6 us
    ppermute x1, starting transfers between devices, on_device(): three = lax.ppermute(two, ('z', 'c'), to(1))  5.08 us
    pallas_call x1, Pallas kernels, product_y(): pl.pallas_call(kernel, in_specs=[VMEM] * 3, out_specs=[VMEM] * Y, out_sha...  3.56 us
    ppermute x1, starting transfers between devices, on_device(): two = lax.ppermute(here, ('z', 'c'), to(2))  3.27 us
  transfers between devices with their start and end apart: 21, of which 11 were waited for; matrix products, arithmetic and copies ran while one was open for 3% of the time, Pallas kernels for 8%

profile of v13, /device:TPU:10, one launch (start us, length us, event | category | flops | bytes accessed | tf_op | source)
XLA Modules:
  0.0 110.3 jit_solution(13295354947619655965)
XLA Ops:
  0.6 0.1 collective-permute-start
  0.7 0.8 copy.8
  1.6 0.3 mul.30
  1.9 0.4 fusion.w_own_ref
  2.3 2.2 %collective-permute-start.2 = (bf16[640,512]{1,0:T(8,128)(2,1)S(1)}, bf16[640,512]{1,0:T(8,128)(2,1)S(1)}, u32[]{:S(2)}, u32[]{:S(2)}) collective-permute-start(bf16[640,512]{1,0:T(8,128)(2,1)S(1)} %slice.9), channel_id=1, source_target_pairs={{0,16},{16,0},{1,17},{17,1},{2,18},{18,2},{3,19},{19,3},{4,20},{20... | collective-permute-start | bytes 1966088 | tf_op jit(solution)/shard_map/ppermute | solution.py:71
  4.5 0.1 pad_maximum_fusion.t0
  4.6 2.0 %collective-permute-start.1 = (bf16[256,1024]{1,0:T(8,128)(2,1)S(1)}, bf16[256,1024]{1,0:T(8,128)(2,1)S(1)}, u32[]{:S(2)}, u32[]{:S(2)}) collective-permute-start(bf16[256,1024]{1,0:T(8,128)(2,1)S(1)} %pad_maximum_fusion.t0), channel_id=1, source_target_pairs={{0,32},{32,64},{64,96},{96,128},{128,160},{160,192},{192,224},{224... | collective-permute-start | bytes 1572872 | tf_op jit(solution)/shard_map/ppermute | solution.py:288
  6.6 3.3 %collective-permute-start.3 = (bf16[256,1024]{1,0:T(8,128)(2,1)S(1)}, bf16[256,1024]{1,0:T(8,128)(2,1)S(1)}, u32[]{:S(2)}, u32[]{:S(2)}) collective-permute-start(bf16[256,1024]{1,0:T(8,128)(2,1)S(1)} %pad_maximum_fusion.t0), channel_id=1, source_target_pairs={{0,64},{32,96},{64,128},{96,160},{128,192},{160,224},{192,0},{224,... | collective-permute-start | bytes 1572872 | tf_op jit(solution)/shard_map/ppermute | solution.py:287
  9.9 1.7 %collective-permute-start.9 = (bf16[896,512]{1,0:T(8,128)(2,1)S(1)}, bf16[896,512]{1,0:T(8,128)(2,1)}, u32[]{:S(2)}, u32[]{:S(2)}) collective-permute-start(bf16[896,512]{1,0:T(8,128)(2,1)S(1)} %fusion.w_own_ref), channel_id=1, source_target_pairs={{0,1},{1,0},{2,3},{3,2},{4,5},{5,4},{6,7},{7,6},{8,9},{9,8},{10,11... | collective-permute-start | bytes 2752520 | tf_op jit(solution)/shard_map/ppermute | solution.py:71
  11.6 0.7 slice.8
  12.3 8.7 %collective-permute-done.2.refs_0_ = bf16[640,512]{1,0:T(8,128)(2,1)S(1)} collective-permute-done((bf16[640,512]{1,0:T(8,128)(2,1)S(1)}, bf16[640,512]{1,0:T(8,128)(2,1)S(1)}, u32[]{:S(2)}, u32[]{:S(2)}) %collective-permute-start.2) | collective-permute-done | bytes 655392 | tf_op jit(solution)/shard_map/ppermute | solution.py:71
  21.0 0.8 copy-done
  21.8 1.2 %collective-permute-start.7 = (bf16[640,512]{1,0:T(8,128)(2,1)S(1)}, bf16[640,512]{1,0:T(8,128)(2,1)S(1)}, u32[]{:S(2)}, u32[]{:S(2)}) collective-permute-start(bf16[640,512]{1,0:T(8,128)(2,1)S(1)} %collective-permute-done.2.refs_0_), channel_id=1, source_target_pairs={{0,1},{1,0},{2,3},{3,2},{4,5},{5,4},{6,7},{7,6},{8,9},{9,8},{10,11... | collective-permute-start | bytes 1966088 | tf_op jit(solution)/shard_map/ppermute | solution.py:71
  23.0 1.4 %collective-permute-start.6 = (bf16[256,512]{1,0:T(8,128)(2,1)}, bf16[256,512]{1,0:T(8,128)(2,1)S(1)}, u32[]{:S(2)}, u32[]{:S(2)}) collective-permute-start(bf16[256,512]{1,0:T(8,128)(2,1)} %slice.8), channel_id=1, source_target_pairs={{0,16},{16,0},{1,17},{17,1},{2,18},{18,2},{3,19},{19,3},{4,20},{20... | collective-permute-start | bytes 786440 | tf_op jit(solution)/shard_map/ppermute | solution.py:71
  24.4 0.9 collective-permute-done.3.t2
  25.3 5.1 %collective-permute-start.4 = (bf16[256,1024]{1,0:T(8,128)(2,1)S(1)}, bf16[256,1024]{1,0:T(8,128)(2,1)}, u32[]{:S(2)}, u32[]{:S(2)}) collective-permute-start(bf16[256,1024]{1,0:T(8,128)(2,1)S(1)} %collective-permute-done.3.t2), channel_id=1, source_target_pairs={{0,32},{32,64},{64,96},{96,128},{128,160},{160,192},{192,224},{224... | collective-permute-start | bytes 1572872 | tf_op jit(solution)/shard_map/ppermute | solution.py:291
  30.4 0.7 constant_dynamic-slice_fusion
  31.1 0.5 collective-permute-start.5
  31.7 1.2 %collective-permute-done.6.refs_1_ = bf16[256,512]{1,0:T(8,128)(2,1)S(1)} collective-permute-done((bf16[256,512]{1,0:T(8,128)(2,1)}, bf16[256,512]{1,0:T(8,128)(2,1)S(1)}, u32[]{:S(2)}, u32[]{:S(2)}) %collective-permute-start.6) | collective-permute-done | bytes 262176 | tf_op jit(solution)/shard_map/ppermute | solution.py:71
  32.9 0.7 dynamic-slice_bitcast_fusion.facts_ref
  33.6 12.1 %collective-permute-done.5.far_ref = bf16[128,1024]{1,0:T(8,128)(2,1)} collective-permute-done((bf16[128,1024]{1,0:T(8,128)(2,1)}, bf16[128,1024]{1,0:T(8,128)(2,1)}, u32[]{:S(2)}, u32[]{:S(2)}) %collective-permute-start.5) | collective-permute-done | bytes 262176 | tf_op jit(solution)/shard_map/ppermute | solution.py:292
  45.8 1.0 copy-done.1
  46.8 2.6 %shard_map.77 = (bf16[8,128,1024]{2,1,0:T(8,128)(2,1)S(1)}, bf16[2,128,896]{2,1,0:T(8,128)(2,1)S(1)}, bf16[2,128,896]{2,1,0:T(8,128)(2,1)S(1)}) custom-call(s32[10]{0:T(128)S(1)} %dynamic-slice_bitcast_fusion.facts_ref, bf16[256,1024]{1,0:T(8,128)(2,1)S(1)} %pad_maximum_fusion.t0, bf16[256,1024]{1,0:T(8,128)(2,1)S(1)} %copy-done.1, ...), custom_call_target="tpu_custom_call" | custom-call | flops 939524096 | bytes 7340032 | tf_op jit(solution)/shard_map/pallas_call | solution.py:116
  49.4 1.5 %collective-permute-start.14 = (bf16[2,128,896]{2,1,0:T(8,128)(2,1)S(1)}, bf16[2,128,896]{2,1,0:T(8,128)(2,1)S(1)}, u32[]{:S(2)}, u32[]{:S(2)}) collective-permute-start(bf16[2,128,896]{2,1,0:T(8,128)(2,1)S(1)} %get-tuple-element.38), channel_id=1, source_target_pairs={{0,8},{8,0},{1,9},{9,1},{2,10},{10,2},{3,11},{11,3},{4,12},{12,4},... | collective-permute-start | bytes 1376264 | tf_op jit(solution)/shard_map/ppermute | solution.py:71
  50.9 0.6 collective-permute-start.15
  51.5 3.6 %shard_map.78 = (bf16[2,128,896]{2,1,0:T(8,128)(2,1)S(1)}, bf16[2,128,896]{2,1,0:T(8,128)(2,1)S(1)}, bf16[2,128,896]{2,1,0:T(8,128)(2,1)S(1)}, bf16[2,128,896]{2,1,0:T(8,128)(2,1)S(1)}) custom-call(bf16[8,128,1024]{2,1,0:T(8,128)(2,1)S(1)} %get-tuple-element.29.lhs_ref, bf16[896,512]{1,0:T(8,128)(2,1)S(1)} %fusion.w_own_ref, ...), custom_call_target="tpu_custom_call" | custom-call | flops 1879048192 | bytes 6291456 | tf_op jit(solution)/shard_map/pallas_call | solution.py:137
  55.1 1.7 %collective-permute-start.10 = (bf16[2,128,896]{2,1,0:T(8,128)(2,1)S(1)}, bf16[2,128,896]{2,1,0:T(8,128)(2,1)S(1)}, u32[]{:S(2)}, u32[]{:S(2)}) collective-permute-start(bf16[2,128,896]{2,1,0:T(8,128)(2,1)S(1)} %get-tuple-element.31), channel_id=1, source_target_pairs={{0,2},{2,4},{4,6},{6,0},{1,3},{3,5},{5,7},{7,1},{8,10},{10,12},{12... | collective-permute-start | bytes 1376264 | tf_op jit(solution)/shard_map/ppermute | solution.py:71
  56.7 1.0 collective-permute-start.11
  57.7 2.4 %collective-permute-start.12 = (bf16[2,128,896]{2,1,0:T(8,128)(2,1)S(1)}, bf16[2,128,896]{2,1,0:T(8,128)(2,1)S(1)}, u32[]{:S(2)}, u32[]{:S(2)}) collective-permute-start(bf16[2,128,896]{2,1,0:T(8,128)(2,1)S(1)} %get-tuple-element.33), channel_id=1, source_target_pairs={{0,6},{2,0},{4,2},{6,4},{1,7},{3,1},{5,3},{7,5},{8,14},{10,8},{12,... | collective-permute-start | bytes 1376264 | tf_op jit(solution)/shard_map/ppermute | solution.py:71
  60.1 2.2 %shard_map.80 = (bf16[2,128,896]{2,1,0:T(8,128)(2,1)S(1)}, bf16[2,128,896]{2,1,0:T(8,128)(2,1)S(1)}) custom-call(bf16[8,128,1024]{2,1,0:T(8,128)(2,1)S(1)} %get-tuple-element.29.lhs_ref, bf16[640,512]{1,0:T(8,128)(2,1)S(1)} %collective-permute-done.2.refs_0_, bf16[256,512]{1,0:T(8,128)(2,1)S(1)} %collective-permute-done.6.refs_1_, ...), custom_call_target="tpu_custom_call" | custom-call | flops 939524096 | bytes 4194304 | tf_op jit(solution)/shard_map/pallas_call | solution.py:158
  62.3 0.4 collective-permute-done.14.refs_2_
  62.7 4.9 %collective-permute-done.15.refs_3_ = bf16[2,128,896]{2,1,0:T(8,128)(2,1)S(1)} collective-permute-done((bf16[2,128,896]{2,1,0:T(8,128)(2,1)S(1)}, bf16[2,128,896]{2,1,0:T(8,128)(2,1)S(1)}, u32[]{:S(2)}, u32[]{:S(2)}) %collective-permute-start.15) | collective-permute-done | bytes 458784 | tf_op jit(solution)/shard_map/ppermute | solution.py:71
  67.6 0.2 shard_map.81
  67.9 1.7 %collective-permute-start.16 = (bf16[128,896]{1,0:T(8,128)(2,1)S(1)}, bf16[128,896]{1,0:T(8,128)(2,1)S(1)}, u32[]{:S(2)}, u32[]{:S(2)}) collective-permute-start(bf16[128,896]{1,0:T(8,128)(2,1)S(1)} %get-tuple-element.41), channel_id=1, source_target_pairs={{0,2},{2,4},{4,6},{6,0},{1,3},{3,5},{5,7},{7,1},{8,10},{10,12},{12... | collective-permute-start | bytes 688136 | tf_op jit(solution)/shard_map/ppermute | solution.py:71
  69.5 0.9 collective-permute-start.17
  70.5 2.4 %collective-permute-start.18 = (bf16[128,896]{1,0:T(8,128)(2,1)S(1)}, bf16[128,896]{1,0:T(8,128)(2,1)S(1)}, u32[]{:S(2)}, u32[]{:S(2)}) collective-permute-start(bf16[128,896]{1,0:T(8,128)(2,1)S(1)} %get-tuple-element.43), channel_id=1, source_target_pairs={{0,6},{2,0},{4,2},{6,4},{1,7},{3,1},{5,3},{7,5},{8,14},{10,8},{12,... | collective-permute-start | bytes 688136 | tf_op jit(solution)/shard_map/ppermute | solution.py:71
  72.9 5.7 %collective-permute-done.12.refs_3_ = bf16[2,128,896]{2,1,0:T(8,128)(2,1)S(1)} collective-permute-done((bf16[2,128,896]{2,1,0:T(8,128)(2,1)S(1)}, bf16[2,128,896]{2,1,0:T(8,128)(2,1)S(1)}, u32[]{:S(2)}, u32[]{:S(2)}) %collective-permute-start.12) | collective-permute-done | bytes 458784 | tf_op jit(solution)/shard_map/ppermute | solution.py:71
  78.6 0.2 shard_map.79
  78.8 1.5 %collective-permute-start.13 = (bf16[128,896]{1,0:T(8,128)(2,1)S(1)}, bf16[128,896]{1,0:T(8,128)(2,1)S(1)}, u32[]{:S(2)}, u32[]{:S(2)}) collective-permute-start(bf16[128,896]{1,0:T(8,128)(2,1)S(1)} %get-tuple-element.35), channel_id=1, source_target_pairs={{0,8},{8,0},{1,9},{9,1},{2,10},{10,2},{3,11},{11,3},{4,12},{12,4},... | collective-permute-start | bytes 688136 | tf_op jit(solution)/shard_map/ppermute | solution.py:71
  80.3 2.8 %collective-permute-done.17.refs_4_ = bf16[128,896]{1,0:T(8,128)(2,1)S(1)} collective-permute-done((bf16[128,896]{1,0:T(8,128)(2,1)S(1)}, bf16[128,896]{1,0:T(8,128)(2,1)S(1)}, u32[]{:S(2)}, u32[]{:S(2)}) %collective-permute-start.17) | collective-permute-done | bytes 229408 | tf_op jit(solution)/shard_map/ppermute | solution.py:71
  83.1 1.8 %collective-permute-done.18.refs_5_ = bf16[128,896]{1,0:T(8,128)(2,1)S(1)} collective-permute-done((bf16[128,896]{1,0:T(8,128)(2,1)S(1)}, bf16[128,896]{1,0:T(8,128)(2,1)S(1)}, u32[]{:S(2)}, u32[]{:S(2)}) %collective-permute-start.18) | collective-permute-done | bytes 229408 | tf_op jit(solution)/shard_map/ppermute | solution.py:71
  84.9 0.7 shard_map.82
  85.6 7.8 %collective-permute-start.19 = (bf16[128,896]{1,0:T(8,128)(2,1)S(1)}, bf16[128,896]{1,0:T(8,128)(2,1)S(1)}, u32[]{:S(2)}, u32[]{:S(2)}) collective-permute-start(bf16[128,896]{1,0:T(8,128)(2,1)S(1)} %get-tuple-element.44), channel_id=1, source_target_pairs={{0,160},{1,96},{2,224},{3,32},{4,161},{5,97},{6,225},{7,33},{8,0},... | collective-permute-start | bytes 688136 | tf_op jit(solution)/shard_map/ppermute | solution.py:306
  93.4 2.8 %collective-permute-start.20 = (bf16[128,896]{1,0:T(8,128)(2,1)S(1)}, bf16[128,896]{1,0:T(8,128)(2,1)S(1)}, u32[]{:S(2)}, u32[]{:S(2)}) collective-permute-start(bf16[128,896]{1,0:T(8,128)(2,1)S(1)} %get-tuple-element.45), channel_id=1, source_target_pairs={{0,161},{1,97},{2,225},{3,33},{4,160},{5,96},{6,224},{7,32},{8,1},... | collective-permute-start | bytes 688136 | tf_op jit(solution)/shard_map/ppermute | solution.py:306
  96.3 0.4 shard_map.83
  96.7 0.4 collective-permute-done.19.first
  97.1 11.5 %collective-permute-done.20.second = bf16[128,896]{1,0:T(8,128)(2,1)S(1)} collective-permute-done((bf16[128,896]{1,0:T(8,128)(2,1)S(1)}, bf16[128,896]{1,0:T(8,128)(2,1)S(1)}, u32[]{:S(2)}, u32[]{:S(2)}) %collective-permute-start.20) | collective-permute-done | bytes 229408 | tf_op jit(solution)/shard_map/ppermute | solution.py:306
  108.6 1.6 %shard_map.84 = (bf16[256,896]{1,0:T(8,128)(2,1)}, bf16[256,896]{1,0:T(8,128)(2,1)}) custom-call(s32[10]{0:T(128)S(1)} %dynamic-slice_bitcast_fusion.facts_ref, bf16[128,896]{1,0:T(8,128)(2,1)S(1)} %collective-permute-done.19.first, bf16[128,896]{1,0:T(8,128)(2,1)S(1)} %collective-permute-done.20.second, f32[256,896]{1,0:T(8,128)S(1)} %get-tuple-element.46.for_up_ref, ...), custom_call_target="tpu_custom_call" | custom-call | flops 458752 | bytes 2752512 | tf_op jit(solution)/shard_map/pallas_call | solution.py:264
  (22 shorter events, 0.1 us)
Async XLA Ops:
  0.6 1.3 %copy-start.4 = (bf16[896,512]{1,0:T(8,128)(2,1)S(1)}, bf16[896,512]{1,0:T(8,128)(2,1)}, u32[]{:S(2)}) copy-start(bf16[896,512]{1,0:T(8,128)(2,1)} %param.7) | copy-start | bytes 2752516
  0.6 3.9 %collective-permute-start = (bf16[256,512]{1,0:T(8,128)(2,1)}, bf16[256,512]{1,0:T(8,128)(2,1)S(1)}, u32[]{:S(2)}, u32[]{:S(2)}) collective-permute-start(bf16[256,512]{1,0:T(8,128)(2,1)} %param.6), channel_id=1, source_target_pairs={{0,1},{1,0},{2,3},{3,2},{4,5},{5,4},{6,7},{7,6},{8,9},{9,8},{10,11... | collective-permute-start | bytes 786440 | tf_op jit(solution)/shard_map/ppermute | solution.py:71
  1.9 2.6 %copy-start.5 = (bf16[256,512]{1,0:T(8,128)(2,1)S(1)}, bf16[256,512]{1,0:T(8,128)(2,1)}, u32[]{:S(2)}) copy-start(bf16[256,512]{1,0:T(8,128)(2,1)} %param.6) | copy-start | bytes 786436
  2.3 18.7 %collective-permute-start.2 = (bf16[640,512]{1,0:T(8,128)(2,1)S(1)}, bf16[640,512]{1,0:T(8,128)(2,1)S(1)}, u32[]{:S(2)}, u32[]{:S(2)}) collective-permute-start(bf16[640,512]{1,0:T(8,128)(2,1)S(1)} %slice.9), channel_id=1, source_target_pairs={{0,16},{16,0},{1,17},{17,1},{2,18},{18,2},{3,19},{19,3},{4,20},{20... | collective-permute-start | bytes 1966088 | tf_op jit(solution)/shard_map/ppermute | solution.py:71
  4.6 16.4 %collective-permute-start.1 = (bf16[256,1024]{1,0:T(8,128)(2,1)S(1)}, bf16[256,1024]{1,0:T(8,128)(2,1)S(1)}, u32[]{:S(2)}, u32[]{:S(2)}) collective-permute-start(bf16[256,1024]{1,0:T(8,128)(2,1)S(1)} %pad_maximum_fusion.t0), channel_id=1, source_target_pairs={{0,32},{32,64},{64,96},{96,128},{128,160},{160,192},{192,224},{224... | collective-permute-start | bytes 1572872 | tf_op jit(solution)/shard_map/ppermute | solution.py:288
  6.6 18.7 %collective-permute-start.3 = (bf16[256,1024]{1,0:T(8,128)(2,1)S(1)}, bf16[256,1024]{1,0:T(8,128)(2,1)S(1)}, u32[]{:S(2)}, u32[]{:S(2)}) collective-permute-start(bf16[256,1024]{1,0:T(8,128)(2,1)S(1)} %pad_maximum_fusion.t0), channel_id=1, source_target_pairs={{0,64},{32,96},{64,128},{96,160},{128,192},{160,224},{192,0},{224,... | collective-permute-start | bytes 1572872 | tf_op jit(solution)/shard_map/ppermute | solution.py:287
  9.9 41.6 %collective-permute-start.9 = (bf16[896,512]{1,0:T(8,128)(2,1)S(1)}, bf16[896,512]{1,0:T(8,128)(2,1)}, u32[]{:S(2)}, u32[]{:S(2)}) collective-permute-start(bf16[896,512]{1,0:T(8,128)(2,1)S(1)} %fusion.w_own_ref), channel_id=1, source_target_pairs={{0,1},{1,0},{2,3},{3,2},{4,5},{5,4},{6,7},{7,6},{8,9},{9,8},{10,11... | collective-permute-start | bytes 2752520 | tf_op jit(solution)/shard_map/ppermute | solution.py:71
  21.0 0.8 copy-start
  21.8 23.9 %collective-permute-start.7 = (bf16[640,512]{1,0:T(8,128)(2,1)S(1)}, bf16[640,512]{1,0:T(8,128)(2,1)S(1)}, u32[]{:S(2)}, u32[]{:S(2)}) collective-permute-start(bf16[640,512]{1,0:T(8,128)(2,1)S(1)} %collective-permute-done.2.refs_0_), channel_id=1, source_target_pairs={{0,1},{1,0},{2,3},{3,2},{4,5},{5,4},{6,7},{7,6},{8,9},{9,8},{10,11... | collective-permute-start | bytes 1966088 | tf_op jit(solution)/shard_map/ppermute | solution.py:71
  23.0 9.9 %collective-permute-start.6 = (bf16[256,512]{1,0:T(8,128)(2,1)}, bf16[256,512]{1,0:T(8,128)(2,1)S(1)}, u32[]{:S(2)}, u32[]{:S(2)}) collective-permute-start(bf16[256,512]{1,0:T(8,128)(2,1)} %slice.8), channel_id=1, source_target_pairs={{0,16},{16,0},{1,17},{17,1},{2,18},{18,2},{3,19},{19,3},{4,20},{20... | collective-permute-start | bytes 786440 | tf_op jit(solution)/shard_map/ppermute | solution.py:71
  25.3 20.4 %collective-permute-start.4 = (bf16[256,1024]{1,0:T(8,128)(2,1)S(1)}, bf16[256,1024]{1,0:T(8,128)(2,1)}, u32[]{:S(2)}, u32[]{:S(2)}) collective-permute-start(bf16[256,1024]{1,0:T(8,128)(2,1)S(1)} %collective-permute-done.3.t2), channel_id=1, source_target_pairs={{0,32},{32,64},{64,96},{96,128},{128,160},{160,192},{192,224},{224... | collective-permute-start | bytes 1572872 | tf_op jit(solution)/shard_map/ppermute | solution.py:291
  31.1 14.6 %collective-permute-start.5 = (bf16[128,1024]{1,0:T(8,128)(2,1)}, bf16[128,1024]{1,0:T(8,128)(2,1)}, u32[]{:S(2)}, u32[]{:S(2)}) collective-permute-start(bf16[128,1024]{1,0:T(8,128)(2,1)} %constant_dynamic-slice_fusion), channel_id=1, source_target_pairs={{0,64},{32,96},{64,128},{96,160},{128,192},{160,224},{192,0},{224,... | collective-permute-start | bytes 786440 | tf_op jit(solution)/shard_map/ppermute | solution.py:292
  32.9 12.8 %collective-permute-start.8 = (bf16[256,512]{1,0:T(8,128)(2,1)S(1)}, bf16[256,512]{1,0:T(8,128)(2,1)}, u32[]{:S(2)}, u32[]{:S(2)}) collective-permute-start(bf16[256,512]{1,0:T(8,128)(2,1)S(1)} %collective-permute-done.6.refs_1_), channel_id=1, source_target_pairs={{0,1},{1,0},{2,3},{3,2},{4,5},{5,4},{6,7},{7,6},{8,9},{9,8},{10,11... | collective-permute-start | bytes 786440 | tf_op jit(solution)/shard_map/ppermute | solution.py:71
  45.8 1.0 copy-start.1
  49.4 13.3 %collective-permute-start.14 = (bf16[2,128,896]{2,1,0:T(8,128)(2,1)S(1)}, bf16[2,128,896]{2,1,0:T(8,128)(2,1)S(1)}, u32[]{:S(2)}, u32[]{:S(2)}) collective-permute-start(bf16[2,128,896]{2,1,0:T(8,128)(2,1)S(1)} %get-tuple-element.38), channel_id=1, source_target_pairs={{0,8},{8,0},{1,9},{9,1},{2,10},{10,2},{3,11},{11,3},{4,12},{12,4},... | collective-permute-start | bytes 1376264 | tf_op jit(solution)/shard_map/ppermute | solution.py:71
  50.9 16.7 %collective-permute-start.15 = (bf16[2,128,896]{2,1,0:T(8,128)(2,1)S(1)}, bf16[2,128,896]{2,1,0:T(8,128)(2,1)S(1)}, u32[]{:S(2)}, u32[]{:S(2)}) collective-permute-start(bf16[2,128,896]{2,1,0:T(8,128)(2,1)S(1)} %get-tuple-element.39), channel_id=1, source_target_pairs={{0,8},{8,0},{1,9},{9,1},{2,10},{10,2},{3,11},{11,3},{4,12},{12,4},... | collective-permute-start | bytes 1376264 | tf_op jit(solution)/shard_map/ppermute | solution.py:71
  55.1 15.4 %collective-permute-start.10 = (bf16[2,128,896]{2,1,0:T(8,128)(2,1)S(1)}, bf16[2,128,896]{2,1,0:T(8,128)(2,1)S(1)}, u32[]{:S(2)}, u32[]{:S(2)}) collective-permute-start(bf16[2,128,896]{2,1,0:T(8,128)(2,1)S(1)} %get-tuple-element.31), channel_id=1, source_target_pairs={{0,2},{2,4},{4,6},{6,0},{1,3},{3,5},{5,7},{7,1},{8,10},{10,12},{12... | collective-permute-start | bytes 1376264 | tf_op jit(solution)/shard_map/ppermute | solution.py:71
  56.7 16.1 %collective-permute-start.11 = (bf16[2,128,896]{2,1,0:T(8,128)(2,1)S(1)}, bf16[2,128,896]{2,1,0:T(8,128)(2,1)S(1)}, u32[]{:S(2)}, u32[]{:S(2)}) collective-permute-start(bf16[2,128,896]{2,1,0:T(8,128)(2,1)S(1)} %get-tuple-element.32), channel_id=1, source_target_pairs={{0,4},{2,6},{4,0},{6,2},{1,5},{3,7},{5,1},{7,3},{8,12},{10,14},{12... | collective-permute-start | bytes 1376264 | tf_op jit(solution)/shard_map/ppermute | solution.py:71
  57.7 20.8 %collective-permute-start.12 = (bf16[2,128,896]{2,1,0:T(8,128)(2,1)S(1)}, bf16[2,128,896]{2,1,0:T(8,128)(2,1)S(1)}, u32[]{:S(2)}, u32[]{:S(2)}) collective-permute-start(bf16[2,128,896]{2,1,0:T(8,128)(2,1)S(1)} %get-tuple-element.33), channel_id=1, source_target_pairs={{0,6},{2,0},{4,2},{6,4},{1,7},{3,1},{5,3},{7,5},{8,14},{10,8},{12,... | collective-permute-start | bytes 1376264 | tf_op jit(solution)/shard_map/ppermute | solution.py:71
  67.8 28.4 %copy-start.2 = (bf16[256,896]{1,0:T(8,128)(2,1)S(1)}, bf16[256,896]{1,0:T(8,128)(2,1)}, u32[]{:S(2)}) copy-start(bf16[256,896]{1,0:T(8,128)(2,1)} %gate_ref.1) | copy-start | bytes 1376260
  67.8 28.4 %copy-start.3 = (bf16[256,896]{1,0:T(8,128)(2,1)S(1)}, bf16[256,896]{1,0:T(8,128)(2,1)}, u32[]{:S(2)}) copy-start(bf16[256,896]{1,0:T(8,128)(2,1)} %up_ref.1) | copy-start | bytes 1376260
  67.9 12.4 %collective-permute-start.16 = (bf16[128,896]{1,0:T(8,128)(2,1)S(1)}, bf16[128,896]{1,0:T(8,128)(2,1)S(1)}, u32[]{:S(2)}, u32[]{:S(2)}) collective-permute-start(bf16[128,896]{1,0:T(8,128)(2,1)S(1)} %get-tuple-element.41), channel_id=1, source_target_pairs={{0,2},{2,4},{4,6},{6,0},{1,3},{3,5},{5,7},{7,1},{8,10},{10,12},{12... | collective-permute-start | bytes 688136 | tf_op jit(solution)/shard_map/ppermute | solution.py:71
  69.5 13.6 %collective-permute-start.17 = (bf16[128,896]{1,0:T(8,128)(2,1)S(1)}, bf16[128,896]{1,0:T(8,128)(2,1)S(1)}, u32[]{:S(2)}, u32[]{:S(2)}) collective-permute-start(bf16[128,896]{1,0:T(8,128)(2,1)S(1)} %get-tuple-element.42), channel_id=1, source_target_pairs={{0,4},{2,6},{4,0},{6,2},{1,5},{3,7},{5,1},{7,3},{8,12},{10,14},{12... | collective-permute-start | bytes 688136 | tf_op jit(solution)/shard_map/ppermute | solution.py:71
  70.5 14.4 %collective-permute-start.18 = (bf16[128,896]{1,0:T(8,128)(2,1)S(1)}, bf16[128,896]{1,0:T(8,128)(2,1)S(1)}, u32[]{:S(2)}, u32[]{:S(2)}) collective-permute-start(bf16[128,896]{1,0:T(8,128)(2,1)S(1)} %get-tuple-element.43), channel_id=1, source_target_pairs={{0,6},{2,0},{4,2},{6,4},{1,7},{3,1},{5,3},{7,5},{8,14},{10,8},{12,... | collective-permute-start | bytes 688136 | tf_op jit(solution)/shard_map/ppermute | solution.py:71
  78.8 6.1 %collective-permute-start.13 = (bf16[128,896]{1,0:T(8,128)(2,1)S(1)}, bf16[128,896]{1,0:T(8,128)(2,1)S(1)}, u32[]{:S(2)}, u32[]{:S(2)}) collective-permute-start(bf16[128,896]{1,0:T(8,128)(2,1)S(1)} %get-tuple-element.35), channel_id=1, source_target_pairs={{0,8},{8,0},{1,9},{9,1},{2,10},{10,2},{3,11},{11,3},{4,12},{12,4},... | collective-permute-start | bytes 688136 | tf_op jit(solution)/shard_map/ppermute | solution.py:71
  85.6 11.4 %collective-permute-start.19 = (bf16[128,896]{1,0:T(8,128)(2,1)S(1)}, bf16[128,896]{1,0:T(8,128)(2,1)S(1)}, u32[]{:S(2)}, u32[]{:S(2)}) collective-permute-start(bf16[128,896]{1,0:T(8,128)(2,1)S(1)} %get-tuple-element.44), channel_id=1, source_target_pairs={{0,160},{1,96},{2,224},{3,32},{4,161},{5,97},{6,225},{7,33},{8,0},... | collective-permute-start | bytes 688136 | tf_op jit(solution)/shard_map/ppermute | solution.py:306
  93.4 15.2 %collective-permute-start.20 = (bf16[128,896]{1,0:T(8,128)(2,1)S(1)}, bf16[128,896]{1,0:T(8,128)(2,1)S(1)}, u32[]{:S(2)}, u32[]{:S(2)}) collective-permute-start(bf16[128,896]{1,0:T(8,128)(2,1)S(1)} %get-tuple-element.45), channel_id=1, source_target_pairs={{0,161},{1,97},{2,225},{3,33},{4,160},{5,96},{6,224},{7,32},{8,1},... | collective-permute-start | bytes 688136 | tf_op jit(solution)/shard_map/ppermute | solution.py:306

commit v14 on v12

--- a/solution.py
+++ b/solution.py
@@ -103,7 +103,7 @@
     count = len(weights)
 
     def kernel(facts_ref, t0, t1, t2, t3, far_ref, *refs):
-        w_refs, lhs_ref, send_refs = refs[:count], refs[count], refs[count + 1 :]
+        w_refs, lhs_ref, send_ref = refs[:count], refs[count], refs[count + 1]
         lhs_ref[facts_ref[0]] = t0[pl.ds(pl.multiple_of(facts_ref[S] * rows, rows), rows), :]
         for i, ref in enumerate((t1, t2, t3)):
             for h in range(2):
@@ -111,14 +111,13 @@
         lhs_ref[facts_ref[7]] = far_ref[...]
         total = times_pieces(lhs_ref[Y:].reshape(Y * rows, depth), w_refs)
         for d in range(Y):
-            send_refs[d // 2][d % 2] = total[d * rows : (d + 1) * rows]
+            send_ref[d] = total[d * rows : (d + 1) * rows]
 
     return pl.pallas_call(
         kernel,
         in_specs=[SMEM] + [VMEM] * (5 + count),
-        out_specs=[VMEM] * 3,
-        out_shape=[jax.ShapeDtypeStruct((S, rows, depth), BF16)]
-        + [jax.ShapeDtypeStruct((2, rows, width), BF16)] * 2,
+        out_specs=[VMEM] * 2,
+        out_shape=[jax.ShapeDtypeStruct((n, rows, w), BF16) for n, w in ((S, depth), (Y, width))],
         compiler_params=params(32),
         cost_estimate=pl.CostEstimate(flops=S * rows * depth * width, bytes_accessed=7 * 2**20, transcendentals=0),
     )(own, *tokens, far, *weights)
@@ -190,19 +189,19 @@
     _, rows, width = kept[0].shape
 
     def kernel(*refs):
-        kept_refs, received_refs, out_refs = refs[:2], refs[2:4], refs[4:]
+        kept_refs, received_ref, out_refs = refs[:2], refs[2], refs[3:]
         for d in range(Y):
-            total = kept_refs[d // 2][d % 2].astype(F32) + received_refs[d // 2][d % 2].astype(F32)
+            total = kept_refs[d // 2][d % 2].astype(F32) + received_ref[d].astype(F32)
             out_refs[d][...] = total.astype(BF16)
 
     return pl.pallas_call(
         kernel,
-        in_specs=[VMEM] * 4,
+        in_specs=[VMEM] * 3,
         out_specs=[VMEM] * Y,
         out_shape=[jax.ShapeDtypeStruct((rows, width), BF16)] * Y,
         compiler_params=params(16),
         cost_estimate=pl.CostEstimate(flops=Y * rows * width, bytes_accessed=6 * Y * rows * width, transcendentals=0),
-    )(*kept, *received)
+    )(*kept, received)
 
 
 def add_last(own, near_parts, cross_parts):
@@ -294,11 +293,11 @@
     tokens = [here, one, two, three]
     weights = cross_own + [shift(part, "c", C, 1) for part in cross_own]
 
-    lhs, *sent = product_send(own, tokens, far, weights)
+    lhs, sent = product_send(own, tokens, far, weights)
     near = product_y(lhs, near_own, near_other)
     near_y = [near[0]] + [shift(near[d], "y", Y, d) for d in range(1, Y)]
     kept = product_keep(lhs, weights)
-    cross = add_xl(kept, [shift(part, "xl", XL, 1) for part in sent])
+    cross = add_xl(kept, shift(sent, "xl", XL, 1))
     cross_parts = [cross[0]] + [shift(cross[d], "y", Y, d) for d in range(1, Y)]
     kept, sent = add_y(near_y)
     near_parts = [kept, shift(sent, "xl", XL, 1)]

time: 108 us -> 114 us (1.056)
  waiting for transfers between devices: 52.3 us -> 59.3 us
  starting transfers between devices: 38.5 us -> 36.7 us
    ppermute x15 -> x14, waiting for transfers between devices: 25.1 us -> 31.1 us  [shift(): return lax.ppermute(x, axis, [(i, (i + by) % size) for i in range(size)])]
    ppermute x15 -> x14, starting transfers between devices: 16.2 us -> 15.3 us  [shift(): return lax.ppermute(x, axis, [(i, (i + by) % size) for i in range(size)])]
  transfers between devices with their start and end apart: 21 -> 20, of which waited for: 12 -> 12; matrix products, arithmetic and copies ran while one was open for 3% -> 3% of each run, Pallas kernels for 9% -> 8%
where the time goes in v14:
time: 114 us; the launch traced here: 112 us
  waiting for transfers between devices  59.3 us (52%)
  starting transfers between devices  36.7 us (32%)
  Pallas kernels  11.8 us (10%)
  local copies, waits for them, and re-layouts  3.23 us (3%)
    ppermute x14, waiting for transfers between devices, shift(): return lax.ppermute(x, axis, [(i, (i + by) % size) for i in range(size)])  31.1 us
    ppermute x14, starting transfers between devices, shift(): return lax.ppermute(x, axis, [(i, (i + by) % size) for i in range(size)])  15.3 us
    ppermute x2, waiting for transfers between devices, on_device(): hidden = [lax.ppermute(sums[j], ALL, home_pairs(j)) for j in range(2)]  13.4 us
    ppermute x1, waiting for transfers between devices, on_device(): two = lax.ppermute(here, ('z', 'c'), to(2))  11 us
    ppermute x2, starting transfers between devices, on_device(): hidden = [lax.ppermute(sums[j], ALL, home_pairs(j)) for j in range(2)]  7.78 us
    ppermute x1, starting transfers between devices, on_device(): two = lax.ppermute(here, ('z', 'c'), to(2))  6.1 us
    ppermute x1, starting transfers between devices, on_device(): three = lax.ppermute(two, ('z', 'c'), to(1))  5.58 us
    ppermute x1, waiting for transfers between devices, on_device(): lax.ppermute(lax.dynamic_slice_in_dim(gated, c * rows, rows, 0), ('z', 'c...  3.76 us
  transfers between devices with their start and end apart: 20, of which 12 were waited for; matrix products, arithmetic and copies ran while one was open for 3% of the time, Pallas kernels for 8%

profile of v14, /device:TPU:7, one launch (start us, length us, event | category | flops | bytes accessed | tf_op | source)
XLA Modules:
  0.0 112.2 jit_solution(12474569259850541324)
XLA Ops:
  0.6 0.8 collective-permute-start
  1.4 0.8 copy.8
  2.2 0.3 mul.30
  2.5 0.0 copy-start.3
  2.5 0.4 fusion.w_own_ref
  2.9 0.1 slice.9
  2.9 1.2 %collective-permute-start.4 = (bf16[768,512]{1,0:T(8,128)(2,1)S(1)}, bf16[768,512]{1,0:T(8,128)(2,1)S(1)}, u32[]{:S(2)}, u32[]{:S(2)}) collective-permute-start(bf16[768,512]{1,0:T(8,128)(2,1)S(1)} %slice.9), channel_id=1, source_target_pairs={{0,16},{16,0},{1,17},{17,1},{2,18},{18,2},{3,19},{19,3},{4,20},{20... | collective-permute-start | bytes 2359304 | tf_op jit(solution)/shard_map/ppermute | solution.py:71
  4.2 0.1 pad_maximum_fusion.t0
  4.2 6.1 %collective-permute-start.2 = (bf16[256,1024]{1,0:T(8,128)(2,1)S(1)}, bf16[256,1024]{1,0:T(8,128)(2,1)S(1)}, u32[]{:S(2)}, u32[]{:S(2)}) collective-permute-start(bf16[256,1024]{1,0:T(8,128)(2,1)S(1)} %pad_maximum_fusion.t0), channel_id=1, source_target_pairs={{0,64},{32,96},{64,128},{96,160},{128,192},{160,224},{192,0},{224,... | collective-permute-start | bytes 1572872 | tf_op jit(solution)/shard_map/ppermute | solution.py:286
  10.3 0.7 collective-permute-start.1
  11.1 11.0 %collective-permute-done.2.t2 = bf16[256,1024]{1,0:T(8,128)(2,1)S(1)} collective-permute-done((bf16[256,1024]{1,0:T(8,128)(2,1)S(1)}, bf16[256,1024]{1,0:T(8,128)(2,1)S(1)}, u32[]{:S(2)}, u32[]{:S(2)}) %collective-permute-start.2) | collective-permute-done | bytes 524320 | tf_op jit(solution)/shard_map/ppermute | solution.py:286
  22.1 1.6 %collective-permute-done.4.refs_0_ = bf16[768,512]{1,0:T(8,128)(2,1)S(1)} collective-permute-done((bf16[768,512]{1,0:T(8,128)(2,1)S(1)}, bf16[768,512]{1,0:T(8,128)(2,1)S(1)}, u32[]{:S(2)}, u32[]{:S(2)}) %collective-permute-start.4) | collective-permute-done | bytes 786464 | tf_op jit(solution)/shard_map/ppermute | solution.py:71
  23.6 0.8 collective-permute-start.7
  24.5 5.6 %collective-permute-start.3 = (bf16[256,1024]{1,0:T(8,128)(2,1)S(1)}, bf16[256,1024]{1,0:T(8,128)(2,1)}, u32[]{:S(2)}, u32[]{:S(2)}) collective-permute-start(bf16[256,1024]{1,0:T(8,128)(2,1)S(1)} %collective-permute-done.2.t2), channel_id=1, source_target_pairs={{0,32},{32,64},{64,96},{96,128},{128,160},{160,192},{192,224},{224... | collective-permute-start | bytes 1572872 | tf_op jit(solution)/shard_map/ppermute | solution.py:290
  30.1 0.7 slice.8
  30.7 1.1 %collective-permute-start.6 = (bf16[128,512]{1,0:T(8,128)(2,1)}, bf16[128,512]{1,0:T(8,128)(2,1)}, u32[]{:S(2)}, u32[]{:S(2)}) collective-permute-start(bf16[128,512]{1,0:T(8,128)(2,1)} %slice.8), channel_id=1, source_target_pairs={{0,16},{16,0},{1,17},{17,1},{2,18},{18,2},{3,19},{19,3},{4,20},{20... | collective-permute-start | bytes 393224 | tf_op jit(solution)/shard_map/ppermute | solution.py:71
  31.9 0.7 constant_dynamic-slice_fusion
  32.6 1.2 %collective-permute-start.5 = (bf16[128,1024]{1,0:T(8,128)(2,1)}, bf16[128,1024]{1,0:T(8,128)(2,1)}, u32[]{:S(2)}, u32[]{:S(2)}) collective-permute-start(bf16[128,1024]{1,0:T(8,128)(2,1)} %constant_dynamic-slice_fusion), channel_id=1, source_target_pairs={{0,64},{32,96},{64,128},{96,160},{128,192},{160,224},{192,0},{224,... | collective-permute-start | bytes 786440 | tf_op jit(solution)/shard_map/ppermute | solution.py:292
  33.8 2.7 %collective-permute-done.6.refs_1_ = bf16[128,512]{1,0:T(8,128)(2,1)} collective-permute-done((bf16[128,512]{1,0:T(8,128)(2,1)}, bf16[128,512]{1,0:T(8,128)(2,1)}, u32[]{:S(2)}, u32[]{:S(2)}) %collective-permute-start.6) | collective-permute-done | bytes 131104 | tf_op jit(solution)/shard_map/ppermute | solution.py:71
  36.5 0.7 dynamic-slice_bitcast_fusion.facts_ref
  37.2 1.0 collective-permute-done.8.refs_3_
  38.2 3.8 %collective-permute-done.5.far_ref = bf16[128,1024]{1,0:T(8,128)(2,1)} collective-permute-done((bf16[128,1024]{1,0:T(8,128)(2,1)}, bf16[128,1024]{1,0:T(8,128)(2,1)}, u32[]{:S(2)}, u32[]{:S(2)}) %collective-permute-start.5) | collective-permute-done | bytes 262176 | tf_op jit(solution)/shard_map/ppermute | solution.py:292
  42.0 2.7 %shard_map.77 = (bf16[8,128,1024]{2,1,0:T(8,128)(2,1)S(1)}, bf16[4,128,896]{2,1,0:T(8,128)(2,1)S(1)}) custom-call(s32[10]{0:T(128)S(1)} %dynamic-slice_bitcast_fusion.facts_ref, bf16[256,1024]{1,0:T(8,128)(2,1)S(1)} %pad_maximum_fusion.t0, bf16[256,1024]{1,0:T(8,128)(2,1)} %collective-permute-done.1.t1, bf16[256,1024]{1,0:T(8,128)(2,1)S(1)} %collective-permute-done.2.t2, ...), custom_call_target="tpu_custom_call" | custom-call | flops 939524096 | bytes 7340032 | tf_op jit(solution)/shard_map/pallas_call | solution.py:116
  44.7 0.6 collective-permute-start.14
  45.3 3.6 %shard_map.78 = (bf16[2,128,896]{2,1,0:T(8,128)(2,1)S(1)}, bf16[2,128,896]{2,1,0:T(8,128)(2,1)S(1)}, bf16[2,128,896]{2,1,0:T(8,128)(2,1)S(1)}, bf16[2,128,896]{2,1,0:T(8,128)(2,1)S(1)}) custom-call(bf16[8,128,1024]{2,1,0:T(8,128)(2,1)S(1)} %get-tuple-element.30.lhs_ref, bf16[896,512]{1,0:T(8,128)(2,1)S(1)} %fusion.w_own_ref, ...), custom_call_target="tpu_custom_call" | custom-call | flops 1879048192 | bytes 6291456 | tf_op jit(solution)/shard_map/pallas_call | solution.py:136
  48.9 1.4 %collective-permute-start.10 = (bf16[2,128,896]{2,1,0:T(8,128)(2,1)S(1)}, bf16[2,128,896]{2,1,0:T(8,128)(2,1)S(1)}, u32[]{:S(2)}, u32[]{:S(2)}) collective-permute-start(bf16[2,128,896]{2,1,0:T(8,128)(2,1)S(1)} %get-tuple-element.32), channel_id=1, source_target_pairs={{0,2},{2,4},{4,6},{6,0},{1,3},{3,5},{5,7},{7,1},{8,10},{10,12},{12... | collective-permute-start | bytes 1376264 | tf_op jit(solution)/shard_map/ppermute | solution.py:71
  50.2 2.6 %collective-permute-start.11 = (bf16[2,128,896]{2,1,0:T(8,128)(2,1)S(1)}, bf16[2,128,896]{2,1,0:T(8,128)(2,1)S(1)}, u32[]{:S(2)}, u32[]{:S(2)}) collective-permute-start(bf16[2,128,896]{2,1,0:T(8,128)(2,1)S(1)} %get-tuple-element.33), channel_id=1, source_target_pairs={{0,4},{2,6},{4,0},{6,2},{1,5},{3,7},{5,1},{7,3},{8,12},{10,14},{12... | collective-permute-start | bytes 1376264 | tf_op jit(solution)/shard_map/ppermute | solution.py:71
  52.9 1.1 collective-permute-start.12
  53.9 2.3 %shard_map.80 = (bf16[2,128,896]{2,1,0:T(8,128)(2,1)S(1)}, bf16[2,128,896]{2,1,0:T(8,128)(2,1)S(1)}) custom-call(bf16[8,128,1024]{2,1,0:T(8,128)(2,1)S(1)} %get-tuple-element.30.lhs_ref, bf16[768,512]{1,0:T(8,128)(2,1)S(1)} %collective-permute-done.4.refs_0_, bf16[128,512]{1,0:T(8,128)(2,1)} %collective-permute-done.6.refs_1_, ...), custom_call_target="tpu_custom_call" | custom-call | flops 939524096 | bytes 4194304 | tf_op jit(solution)/shard_map/pallas_call | solution.py:157
  56.2 4.6 %collective-permute-done.10.refs_1_ = bf16[2,128,896]{2,1,0:T(8,128)(2,1)S(1)} collective-permute-done((bf16[2,128,896]{2,1,0:T(8,128)(2,1)S(1)}, bf16[2,128,896]{2,1,0:T(8,128)(2,1)S(1)}, u32[]{:S(2)}, u32[]{:S(2)}) %collective-permute-start.10) | collective-permute-done | bytes 458784 | tf_op jit(solution)/shard_map/ppermute | solution.py:71
  60.8 11.0 %collective-permute-done.11.refs_2_ = bf16[2,128,896]{2,1,0:T(8,128)(2,1)S(1)} collective-permute-done((bf16[2,128,896]{2,1,0:T(8,128)(2,1)S(1)}, bf16[2,128,896]{2,1,0:T(8,128)(2,1)S(1)}, u32[]{:S(2)}, u32[]{:S(2)}) %collective-permute-start.11) | collective-permute-done | bytes 458784 | tf_op jit(solution)/shard_map/ppermute | solution.py:71
  71.7 0.4 collective-permute-done.12.refs_3_
  72.1 0.2 shard_map.79
  72.4 0.0 copy-start
  72.4 0.0 copy-start.1
  72.4 1.0 collective-permute-start.13
  73.4 0.2 shard_map.81
  73.7 1.8 %collective-permute-start.15 = (bf16[128,896]{1,0:T(8,128)(2,1)S(1)}, bf16[128,896]{1,0:T(8,128)(2,1)S(1)}, u32[]{:S(2)}, u32[]{:S(2)}) collective-permute-start(bf16[128,896]{1,0:T(8,128)(2,1)S(1)} %get-tuple-element.41), channel_id=1, source_target_pairs={{0,2},{2,4},{4,6},{6,0},{1,3},{3,5},{5,7},{7,1},{8,10},{10,12},{12... | collective-permute-start | bytes 688136 | tf_op jit(solution)/shard_map/ppermute | solution.py:71
  75.5 2.9 %collective-permute-start.16 = (bf16[128,896]{1,0:T(8,128)(2,1)S(1)}, bf16[128,896]{1,0:T(8,128)(2,1)S(1)}, u32[]{:S(2)}, u32[]{:S(2)}) collective-permute-start(bf16[128,896]{1,0:T(8,128)(2,1)S(1)} %get-tuple-element.42), channel_id=1, source_target_pairs={{0,4},{2,6},{4,0},{6,2},{1,5},{3,7},{5,1},{7,3},{8,12},{10,14},{12... | collective-permute-start | bytes 688136 | tf_op jit(solution)/shard_map/ppermute | solution.py:71
  78.3 2.9 %collective-permute-done.15.refs_3_ = bf16[128,896]{1,0:T(8,128)(2,1)S(1)} collective-permute-done((bf16[128,896]{1,0:T(8,128)(2,1)S(1)}, bf16[128,896]{1,0:T(8,128)(2,1)S(1)}, u32[]{:S(2)}, u32[]{:S(2)}) %collective-permute-start.15) | collective-permute-done | bytes 229408 | tf_op jit(solution)/shard_map/ppermute | solution.py:71
  81.2 6.9 %collective-permute-done.16.refs_4_ = bf16[128,896]{1,0:T(8,128)(2,1)S(1)} collective-permute-done((bf16[128,896]{1,0:T(8,128)(2,1)S(1)}, bf16[128,896]{1,0:T(8,128)(2,1)S(1)}, u32[]{:S(2)}, u32[]{:S(2)}) %collective-permute-start.16) | collective-permute-done | bytes 229408 | tf_op jit(solution)/shard_map/ppermute | solution.py:71
  88.1 0.7 shard_map.82
  88.9 6.1 %collective-permute-start.18 = (bf16[128,896]{1,0:T(8,128)(2,1)S(1)}, bf16[128,896]{1,0:T(8,128)(2,1)S(1)}, u32[]{:S(2)}, u32[]{:S(2)}) collective-permute-start(bf16[128,896]{1,0:T(8,128)(2,1)S(1)} %get-tuple-element.44), channel_id=1, source_target_pairs={{0,160},{1,96},{2,224},{3,32},{4,161},{5,97},{6,225},{7,33},{8,0},... | collective-permute-start | bytes 688136 | tf_op jit(solution)/shard_map/ppermute | solution.py:306
  95.0 1.6 %collective-permute-start.19 = (bf16[128,896]{1,0:T(8,128)(2,1)S(1)}, bf16[128,896]{1,0:T(8,128)(2,1)S(1)}, u32[]{:S(2)}, u32[]{:S(2)}) collective-permute-start(bf16[128,896]{1,0:T(8,128)(2,1)S(1)} %get-tuple-element.45), channel_id=1, source_target_pairs={{0,161},{1,97},{2,225},{3,33},{4,160},{5,96},{6,224},{7,32},{8,1},... | collective-permute-start | bytes 688136 | tf_op jit(solution)/shard_map/ppermute | solution.py:306
  96.7 0.4 shard_map.83
  97.1 2.6 %collective-permute-done.18.first = bf16[128,896]{1,0:T(8,128)(2,1)S(1)} collective-permute-done((bf16[128,896]{1,0:T(8,128)(2,1)S(1)}, bf16[128,896]{1,0:T(8,128)(2,1)S(1)}, u32[]{:S(2)}, u32[]{:S(2)}) %collective-permute-start.18) | collective-permute-done | bytes 229408 | tf_op jit(solution)/shard_map/ppermute | solution.py:306
  99.7 10.9 %collective-permute-done.19.second = bf16[128,896]{1,0:T(8,128)(2,1)S(1)} collective-permute-done((bf16[128,896]{1,0:T(8,128)(2,1)S(1)}, bf16[128,896]{1,0:T(8,128)(2,1)S(1)}, u32[]{:S(2)}, u32[]{:S(2)}) %collective-permute-start.19) | collective-permute-done | bytes 229408 | tf_op jit(solution)/shard_map/ppermute | solution.py:306
  110.5 1.6 %shard_map.84 = (bf16[256,896]{1,0:T(8,128)(2,1)}, bf16[256,896]{1,0:T(8,128)(2,1)}) custom-call(s32[10]{0:T(128)S(1)} %dynamic-slice_bitcast_fusion.facts_ref, bf16[128,896]{1,0:T(8,128)(2,1)S(1)} %collective-permute-done.18.first, bf16[128,896]{1,0:T(8,128)(2,1)S(1)} %collective-permute-done.19.second, f32[256,896]{1,0:T(8,128)S(1)} %get-tuple-element.46.for_up_ref, ...), custom_call_target="tpu_custom_call" | custom-call | flops 458752 | bytes 2752512 | tf_op jit(solution)/shard_map/pallas_call | solution.py:263
  (16 shorter events, 0.0 us)
Async XLA Ops:
  0.6 1.9 %copy-start.2 = (bf16[896,512]{1,0:T(8,128)(2,1)S(1)}, bf16[896,512]{1,0:T(8,128)(2,1)}, u32[]{:S(2)}) copy-start(bf16[896,512]{1,0:T(8,128)(2,1)} %param.7) | copy-start | bytes 2752516
  0.6 3.5 %collective-permute-start = (bf16[256,512]{1,0:T(8,128)(2,1)}, bf16[256,512]{1,0:T(8,128)(2,1)S(1)}, u32[]{:S(2)}, u32[]{:S(2)}) collective-permute-start(bf16[256,512]{1,0:T(8,128)(2,1)} %param.6), channel_id=1, source_target_pairs={{0,1},{1,0},{2,3},{3,2},{4,5},{5,4},{6,7},{7,6},{8,9},{9,8},{10,11... | collective-permute-start | bytes 786440 | tf_op jit(solution)/shard_map/ppermute | solution.py:71
  2.5 1.7 %copy-start.3 = (bf16[256,512]{1,0:T(8,128)(2,1)S(1)}, bf16[256,512]{1,0:T(8,128)(2,1)}, u32[]{:S(2)}) copy-start(bf16[256,512]{1,0:T(8,128)(2,1)} %param.6) | copy-start | bytes 786436
  2.9 20.7 %collective-permute-start.4 = (bf16[768,512]{1,0:T(8,128)(2,1)S(1)}, bf16[768,512]{1,0:T(8,128)(2,1)S(1)}, u32[]{:S(2)}, u32[]{:S(2)}) collective-permute-start(bf16[768,512]{1,0:T(8,128)(2,1)S(1)} %slice.9), channel_id=1, source_target_pairs={{0,16},{16,0},{1,17},{17,1},{2,18},{18,2},{3,19},{19,3},{4,20},{20... | collective-permute-start | bytes 2359304 | tf_op jit(solution)/shard_map/ppermute | solution.py:71
  4.2 17.8 %collective-permute-start.2 = (bf16[256,1024]{1,0:T(8,128)(2,1)S(1)}, bf16[256,1024]{1,0:T(8,128)(2,1)S(1)}, u32[]{:S(2)}, u32[]{:S(2)}) collective-permute-start(bf16[256,1024]{1,0:T(8,128)(2,1)S(1)} %pad_maximum_fusion.t0), channel_id=1, source_target_pairs={{0,64},{32,96},{64,128},{96,160},{128,192},{160,224},{192,0},{224,... | collective-permute-start | bytes 1572872 | tf_op jit(solution)/shard_map/ppermute | solution.py:286
  10.3 20.4 %collective-permute-start.1 = (bf16[256,1024]{1,0:T(8,128)(2,1)S(1)}, bf16[256,1024]{1,0:T(8,128)(2,1)}, u32[]{:S(2)}, u32[]{:S(2)}) collective-permute-start(bf16[256,1024]{1,0:T(8,128)(2,1)S(1)} %pad_maximum_fusion.t0), channel_id=1, source_target_pairs={{0,32},{32,64},{64,96},{96,128},{128,160},{160,192},{192,224},{224... | collective-permute-start | bytes 1572872 | tf_op jit(solution)/shard_map/ppermute | solution.py:287
  23.6 18.3 %collective-permute-start.7 = (bf16[768,512]{1,0:T(8,128)(2,1)S(1)}, bf16[768,512]{1,0:T(8,128)(2,1)S(1)}, u32[]{:S(2)}, u32[]{:S(2)}) collective-permute-start(bf16[768,512]{1,0:T(8,128)(2,1)S(1)} %collective-permute-done.4.refs_0_), channel_id=1, source_target_pairs={{0,1},{1,0},{2,3},{3,2},{4,5},{5,4},{6,7},{7,6},{8,9},{9,8},{10,11... | collective-permute-start | bytes 2359304 | tf_op jit(solution)/shard_map/ppermute | solution.py:71
  24.5 20.8 %collective-permute-start.9 = (bf16[896,512]{1,0:T(8,128)(2,1)S(1)}, bf16[896,512]{1,0:T(8,128)(2,1)}, u32[]{:S(2)}, u32[]{:S(2)}) collective-permute-start(bf16[896,512]{1,0:T(8,128)(2,1)S(1)} %fusion.w_own_ref), channel_id=1, source_target_pairs={{0,1},{1,0},{2,3},{3,2},{4,5},{5,4},{6,7},{7,6},{8,9},{9,8},{10,11... | collective-permute-start | bytes 2752520 | tf_op jit(solution)/shard_map/ppermute | solution.py:71
  24.5 17.5 %collective-permute-start.3 = (bf16[256,1024]{1,0:T(8,128)(2,1)S(1)}, bf16[256,1024]{1,0:T(8,128)(2,1)}, u32[]{:S(2)}, u32[]{:S(2)}) collective-permute-start(bf16[256,1024]{1,0:T(8,128)(2,1)S(1)} %collective-permute-done.2.t2), channel_id=1, source_target_pairs={{0,32},{32,64},{64,96},{96,128},{128,160},{160,192},{192,224},{224... | collective-permute-start | bytes 1572872 | tf_op jit(solution)/shard_map/ppermute | solution.py:290
  30.7 5.8 %collective-permute-start.6 = (bf16[128,512]{1,0:T(8,128)(2,1)}, bf16[128,512]{1,0:T(8,128)(2,1)}, u32[]{:S(2)}, u32[]{:S(2)}) collective-permute-start(bf16[128,512]{1,0:T(8,128)(2,1)} %slice.8), channel_id=1, source_target_pairs={{0,16},{16,0},{1,17},{17,1},{2,18},{18,2},{3,19},{19,3},{4,20},{20... | collective-permute-start | bytes 393224 | tf_op jit(solution)/shard_map/ppermute | solution.py:71
  32.6 9.4 %collective-permute-start.5 = (bf16[128,1024]{1,0:T(8,128)(2,1)}, bf16[128,1024]{1,0:T(8,128)(2,1)}, u32[]{:S(2)}, u32[]{:S(2)}) collective-permute-start(bf16[128,1024]{1,0:T(8,128)(2,1)} %constant_dynamic-slice_fusion), channel_id=1, source_target_pairs={{0,64},{32,96},{64,128},{96,160},{128,192},{160,224},{192,0},{224,... | collective-permute-start | bytes 786440 | tf_op jit(solution)/shard_map/ppermute | solution.py:292
  36.5 1.7 %collective-permute-start.8 = (bf16[128,512]{1,0:T(8,128)(2,1)}, bf16[128,512]{1,0:T(8,128)(2,1)}, u32[]{:S(2)}, u32[]{:S(2)}) collective-permute-start(bf16[128,512]{1,0:T(8,128)(2,1)} %collective-permute-done.6.refs_1_), channel_id=1, source_target_pairs={{0,1},{1,0},{2,3},{3,2},{4,5},{5,4},{6,7},{7,6},{8,9},{9,8},{10,11... | collective-permute-start | bytes 393224 | tf_op jit(solution)/shard_map/ppermute | solution.py:71
  44.7 28.7 %collective-permute-start.14 = (bf16[4,128,896]{2,1,0:T(8,128)(2,1)S(1)}, bf16[4,128,896]{2,1,0:T(8,128)(2,1)S(1)}, u32[]{:S(2)}, u32[]{:S(2)}) collective-permute-start(bf16[4,128,896]{2,1,0:T(8,128)(2,1)S(1)} %get-tuple-element.39), channel_id=1, source_target_pairs={{0,8},{8,0},{1,9},{9,1},{2,10},{10,2},{3,11},{11,3},{4,12},{12,4},... | collective-permute-start | bytes 2752520 | tf_op jit(solution)/shard_map/ppermute | solution.py:71
  48.9 11.9 %collective-permute-start.10 = (bf16[2,128,896]{2,1,0:T(8,128)(2,1)S(1)}, bf16[2,128,896]{2,1,0:T(8,128)(2,1)S(1)}, u32[]{:S(2)}, u32[]{:S(2)}) collective-permute-start(bf16[2,128,896]{2,1,0:T(8,128)(2,1)S(1)} %get-tuple-element.32), channel_id=1, source_target_pairs={{0,2},{2,4},{4,6},{6,0},{1,3},{3,5},{5,7},{7,1},{8,10},{10,12},{12... | collective-permute-start | bytes 1376264 | tf_op jit(solution)/shard_map/ppermute | solution.py:71
  50.2 21.5 %collective-permute-start.11 = (bf16[2,128,896]{2,1,0:T(8,128)(2,1)S(1)}, bf16[2,128,896]{2,1,0:T(8,128)(2,1)S(1)}, u32[]{:S(2)}, u32[]{:S(2)}) collective-permute-start(bf16[2,128,896]{2,1,0:T(8,128)(2,1)S(1)} %get-tuple-element.33), channel_id=1, source_target_pairs={{0,4},{2,6},{4,0},{6,2},{1,5},{3,7},{5,1},{7,3},{8,12},{10,14},{12... | collective-permute-start | bytes 1376264 | tf_op jit(solution)/shard_map/ppermute | solution.py:71
  52.9 19.3 %collective-permute-start.12 = (bf16[2,128,896]{2,1,0:T(8,128)(2,1)S(1)}, bf16[2,128,896]{2,1,0:T(8,128)(2,1)S(1)}, u32[]{:S(2)}, u32[]{:S(2)}) collective-permute-start(bf16[2,128,896]{2,1,0:T(8,128)(2,1)S(1)} %get-tuple-element.34), channel_id=1, source_target_pairs={{0,6},{2,0},{4,2},{6,4},{1,7},{3,1},{5,3},{7,5},{8,14},{10,8},{12,... | collective-permute-start | bytes 1376264 | tf_op jit(solution)/shard_map/ppermute | solution.py:71
  72.4 24.3 %copy-start = (bf16[256,896]{1,0:T(8,128)(2,1)S(1)}, bf16[256,896]{1,0:T(8,128)(2,1)}, u32[]{:S(2)}) copy-start(bf16[256,896]{1,0:T(8,128)(2,1)} %gate_ref.1) | copy-start | bytes 1376260
  72.4 24.3 %copy-start.1 = (bf16[256,896]{1,0:T(8,128)(2,1)S(1)}, bf16[256,896]{1,0:T(8,128)(2,1)}, u32[]{:S(2)}) copy-start(bf16[256,896]{1,0:T(8,128)(2,1)} %up_ref.1) | copy-start | bytes 1376260
  72.4 5.9 %collective-permute-start.13 = (bf16[128,896]{1,0:T(8,128)(2,1)S(1)}, bf16[128,896]{1,0:T(8,128)(2,1)S(1)}, u32[]{:S(2)}, u32[]{:S(2)}) collective-permute-start(bf16[128,896]{1,0:T(8,128)(2,1)S(1)} %get-tuple-element.36), channel_id=1, source_target_pairs={{0,8},{8,0},{1,9},{9,1},{2,10},{10,2},{3,11},{11,3},{4,12},{12,4},... | collective-permute-start | bytes 688136 | tf_op jit(solution)/shard_map/ppermute | solution.py:71
  73.7 7.6 %collective-permute-start.15 = (bf16[128,896]{1,0:T(8,128)(2,1)S(1)}, bf16[128,896]{1,0:T(8,128)(2,1)S(1)}, u32[]{:S(2)}, u32[]{:S(2)}) collective-permute-start(bf16[128,896]{1,0:T(8,128)(2,1)S(1)} %get-tuple-element.41), channel_id=1, source_target_pairs={{0,2},{2,4},{4,6},{6,0},{1,3},{3,5},{5,7},{7,1},{8,10},{10,12},{12... | collective-permute-start | bytes 688136 | tf_op jit(solution)/shard_map/ppermute | solution.py:71
  75.5 12.7 %collective-permute-start.16 = (bf16[128,896]{1,0:T(8,128)(2,1)S(1)}, bf16[128,896]{1,0:T(8,128)(2,1)S(1)}, u32[]{:S(2)}, u32[]{:S(2)}) collective-permute-start(bf16[128,896]{1,0:T(8,128)(2,1)S(1)} %get-tuple-element.42), channel_id=1, source_target_pairs={{0,4},{2,6},{4,0},{6,2},{1,5},{3,7},{5,1},{7,3},{8,12},{10,14},{12... | collective-permute-start | bytes 688136 | tf_op jit(solution)/shard_map/ppermute | solution.py:71
  78.3 9.8 %collective-permute-start.17 = (bf16[128,896]{1,0:T(8,128)(2,1)S(1)}, bf16[128,896]{1,0:T(8,128)(2,1)S(1)}, u32[]{:S(2)}, u32[]{:S(2)}) collective-permute-start(bf16[128,896]{1,0:T(8,128)(2,1)S(1)} %get-tuple-element.43), channel_id=1, source_target_pairs={{0,6},{2,0},{4,2},{6,4},{1,7},{3,1},{5,3},{7,5},{8,14},{10,8},{12,... | collective-permute-start | bytes 688136 | tf_op jit(solution)/shard_map/ppermute | solution.py:71
  88.9 10.8 %collective-permute-start.18 = (bf16[128,896]{1,0:T(8,128)(2,1)S(1)}, bf16[128,896]{1,0:T(8,128)(2,1)S(1)}, u32[]{:S(2)}, u32[]{:S(2)}) collective-permute-start(bf16[128,896]{1,0:T(8,128)(2,1)S(1)} %get-tuple-element.44), channel_id=1, source_target_pairs={{0,160},{1,96},{2,224},{3,32},{4,161},{5,97},{6,225},{7,33},{8,0},... | collective-permute-start | bytes 688136 | tf_op jit(solution)/shard_map/ppermute | solution.py:306
  95.0 15.5 %collective-permute-start.19 = (bf16[128,896]{1,0:T(8,128)(2,1)S(1)}, bf16[128,896]{1,0:T(8,128)(2,1)S(1)}, u32[]{:S(2)}, u32[]{:S(2)}) collective-permute-start(bf16[128,896]{1,0:T(8,128)(2,1)S(1)} %get-tuple-element.45), channel_id=1, source_target_pairs={{0,161},{1,97},{2,225},{3,33},{4,160},{5,96},{6,224},{7,32},{8,1},... | collective-permute-start | bytes 688136 | tf_op jit(solution)/shard_map/ppermute | solution.py:306

commit v15 on v12

--- a/solution.py
+++ b/solution.py
@@ -289,8 +289,7 @@
     last, one = lax.optimization_barrier((near_own[cut:], one))
     cross_own.append(shift(last, "xh", XH, 1))
     three = lax.ppermute(two, ("z", "c"), to(1))
-    gated, cross_own[0] = lax.optimization_barrier((two, cross_own[0]))
-    far = lax.ppermute(lax.dynamic_slice_in_dim(gated, c * rows, rows, 0), ("z", "c"), to(2))
+    far = lax.ppermute(lax.dynamic_slice_in_dim(two, c * rows, rows, 0), ("z", "c"), to(2))
     tokens = [here, one, two, three]
     weights = cross_own + [shift(part, "c", C, 1) for part in cross_own]
 

time: 108 us -> 109 us (level)
  starting transfers between devices: 38.5 us -> 45.2 us
  waiting for transfers between devices: 52.3 us -> 46.9 us
    ppermute x1, waiting for transfers between devices: 11 us -> 0.01 us  [on_device(): two = lax.ppermute(here, ('z', 'c'), to(2))]
    ppermute x15, waiting for transfers between devices: 25.1 us -> 32.4 us  [shift(): return lax.ppermute(x, axis, [(i, (i + by) % size) for i in range(size)])]
    ppermute x2, starting transfers between devices: 8.68 us -> 11.8 us  [on_device(): hidden = [lax.ppermute(sums[j], ALL, home_pairs(j)) for j in range(2)]]
    ppermute x15, starting transfers between devices: 16.2 us -> 18.4 us  [shift(): return lax.ppermute(x, axis, [(i, (i + by) % size) for i in range(size)])]
    ppermute x1, waiting for transfers between devices: 3.76 us -> 1.67 us  [on_device(): lax.ppermute(lax.dynamic_slice_in_dim(two, c * rows, rows, 0), ('z', 'c')...]
    ppermute x1, starting transfers between devices: 1.17 us -> 2.61 us  [on_device(): lax.ppermute(lax.dynamic_slice_in_dim(two, c * rows, rows, 0), ('z', 'c')...]
  transfers between devices with their start and end apart: 21 -> 21, of which waited for: 12 -> 11; matrix products, arithmetic and copies ran while one was open for 3% -> 2% of each run, Pallas kernels for 9% -> 9%
where the time goes in v15:
time: 109 us; the launch traced here: 108 us
  waiting for transfers between devices  46.9 us (43%)
  starting transfers between devices  45.2 us (41%)
  Pallas kernels  11.8 us (11%)
  local copies, waits for them, and re-layouts  3.32 us (3%)
    ppermute x15, waiting for transfers between devices, shift(): return lax.ppermute(x, axis, [(i, (i + by) % size) for i in range(size)])  32.4 us
    ppermute x15, starting transfers between devices, shift(): return lax.ppermute(x, axis, [(i, (i + by) % size) for i in range(size)])  18.4 us
    ppermute x2, waiting for transfers between devices, on_device(): hidden = [lax.ppermute(sums[j], ALL, home_pairs(j)) for j in range(2)]  12.9 us
    ppermute x2, starting transfers between devices, on_device(): hidden = [lax.ppermute(sums[j], ALL, home_pairs(j)) for j in range(2)]  11.8 us
    ppermute x1, starting transfers between devices, on_device(): two = lax.ppermute(here, ('z', 'c'), to(2))  6.1 us
    ppermute x1, starting transfers between devices, on_device(): three = lax.ppermute(two, ('z', 'c'), to(1))  5.58 us
    pallas_call x1, Pallas kernels, product_y(): pl.pallas_call(kernel, in_specs=[VMEM] * 3, out_specs=[VMEM] * Y, out_sha...  3.55 us
    pallas_call x1, Pallas kernels, product_send(): pl.pallas_call(kernel, in_specs=[SMEM] + [VMEM] * (5 + count), out_specs=...  2.73 us
  transfers between devices with their start and end apart: 21, of which 11 were waited for; matrix products, arithmetic and copies ran while one was open for 2% of the time, Pallas kernels for 9%

profile of v15, /device:TPU:7, one launch (start us, length us, event | category | flops | bytes accessed | tf_op | source)
XLA Modules:
  0.0 108.4 jit_solution(4459210693277216479)
XLA Ops:
  0.6 0.9 copy.8
  1.5 0.3 mul.30
  1.8 0.0 copy-done.2
  1.8 0.4 fusion.w_own_ref
  2.2 0.1 slice.9
  2.3 1.2 %collective-permute-start.5 = (bf16[768,512]{1,0:T(8,128)(2,1)S(1)}, bf16[768,512]{1,0:T(8,128)(2,1)S(1)}, u32[]{:S(2)}, u32[]{:S(2)}) collective-permute-start(bf16[768,512]{1,0:T(8,128)(2,1)S(1)} %slice.9), channel_id=1, source_target_pairs={{0,16},{16,0},{1,17},{17,1},{2,18},{18,2},{3,19},{19,3},{4,20},{20... | collective-permute-start | bytes 2359304 | tf_op jit(solution)/shard_map/ppermute | solution.py:71
  3.5 1.0 collective-permute-start
  4.4 1.2 %collective-permute-done = bf16[256,512]{1,0:T(8,128)(2,1)S(1)} collective-permute-done((bf16[256,512]{1,0:T(8,128)(2,1)S(1)}, bf16[256,512]{1,0:T(8,128)(2,1)S(1)}, u32[]{:S(2)}, u32[]{:S(2)}) %collective-permute-start) | collective-permute-done | bytes 262176 | tf_op jit(solution)/shard_map/ppermute | solution.py:71
  5.6 0.1 pad_maximum_fusion.t0
  5.6 6.1 %collective-permute-start.2 = (bf16[256,1024]{1,0:T(8,128)(2,1)S(1)}, bf16[256,1024]{1,0:T(8,128)(2,1)S(1)}, u32[]{:S(2)}, u32[]{:S(2)}) collective-permute-start(bf16[256,1024]{1,0:T(8,128)(2,1)S(1)} %pad_maximum_fusion.t0), channel_id=1, source_target_pairs={{0,64},{32,96},{64,128},{96,160},{128,192},{160,224},{192,0},{224,... | collective-permute-start | bytes 1572872 | tf_op jit(solution)/shard_map/ppermute | solution.py:287
  11.7 0.7 collective-permute-start.1
  12.5 9.8 %collective-permute-done.5.refs_0_ = bf16[768,512]{1,0:T(8,128)(2,1)S(1)} collective-permute-done((bf16[768,512]{1,0:T(8,128)(2,1)S(1)}, bf16[768,512]{1,0:T(8,128)(2,1)S(1)}, u32[]{:S(2)}, u32[]{:S(2)}) %collective-permute-start.5) | collective-permute-done | bytes 786464 | tf_op jit(solution)/shard_map/ppermute | solution.py:71
  22.3 1.5 %collective-permute-start.7 = (bf16[768,512]{1,0:T(8,128)(2,1)S(1)}, bf16[768,512]{1,0:T(8,128)(2,1)S(1)}, u32[]{:S(2)}, u32[]{:S(2)}) collective-permute-start(bf16[768,512]{1,0:T(8,128)(2,1)S(1)} %collective-permute-done.5.refs_0_), channel_id=1, source_target_pairs={{0,1},{1,0},{2,3},{3,2},{4,5},{5,4},{6,7},{7,6},{8,9},{9,8},{10,11... | collective-permute-start | bytes 2359304 | tf_op jit(solution)/shard_map/ppermute | solution.py:71
  23.8 5.6 %collective-permute-start.3 = (bf16[256,1024]{1,0:T(8,128)(2,1)S(1)}, bf16[256,1024]{1,0:T(8,128)(2,1)}, u32[]{:S(2)}, u32[]{:S(2)}) collective-permute-start(bf16[256,1024]{1,0:T(8,128)(2,1)S(1)} %collective-permute-done.2.t2), channel_id=1, source_target_pairs={{0,32},{32,64},{64,96},{96,128},{128,160},{160,192},{192,224},{224... | collective-permute-start | bytes 1572872 | tf_op jit(solution)/shard_map/ppermute | solution.py:291
  29.4 0.7 slice.8
  30.0 1.1 %collective-permute-start.6 = (bf16[128,512]{1,0:T(8,128)(2,1)}, bf16[128,512]{1,0:T(8,128)(2,1)}, u32[]{:S(2)}, u32[]{:S(2)}) collective-permute-start(bf16[128,512]{1,0:T(8,128)(2,1)} %slice.8), channel_id=1, source_target_pairs={{0,16},{16,0},{1,17},{17,1},{2,18},{18,2},{3,19},{19,3},{4,20},{20... | collective-permute-start | bytes 393224 | tf_op jit(solution)/shard_map/ppermute | solution.py:71
  31.2 0.7 constant_dynamic-slice_fusion
  31.9 2.6 %collective-permute-start.4 = (bf16[128,1024]{1,0:T(8,128)(2,1)}, bf16[128,1024]{1,0:T(8,128)(2,1)}, u32[]{:S(2)}, u32[]{:S(2)}) collective-permute-start(bf16[128,1024]{1,0:T(8,128)(2,1)} %constant_dynamic-slice_fusion), channel_id=1, source_target_pairs={{0,64},{32,96},{64,128},{96,160},{128,192},{160,224},{192,0},{224,... | collective-permute-start | bytes 786440 | tf_op jit(solution)/shard_map/ppermute | solution.py:292
  34.5 2.0 %collective-permute-done.6.refs_1_ = bf16[128,512]{1,0:T(8,128)(2,1)} collective-permute-done((bf16[128,512]{1,0:T(8,128)(2,1)}, bf16[128,512]{1,0:T(8,128)(2,1)}, u32[]{:S(2)}, u32[]{:S(2)}) %collective-permute-start.6) | collective-permute-done | bytes 131104 | tf_op jit(solution)/shard_map/ppermute | solution.py:71
  36.5 1.2 %collective-permute-start.8 = (bf16[128,512]{1,0:T(8,128)(2,1)}, bf16[128,512]{1,0:T(8,128)(2,1)}, u32[]{:S(2)}, u32[]{:S(2)}) collective-permute-start(bf16[128,512]{1,0:T(8,128)(2,1)} %collective-permute-done.6.refs_1_), channel_id=1, source_target_pairs={{0,1},{1,0},{2,3},{3,2},{4,5},{5,4},{6,7},{7,6},{8,9},{9,8},{10,11... | collective-permute-start | bytes 393224 | tf_op jit(solution)/shard_map/ppermute | solution.py:71
  37.8 0.7 dynamic-slice_bitcast_fusion.facts_ref
  38.5 0.6 collective-permute-done.8.refs_3_
  39.1 1.7 %collective-permute-done.4.far_ref = bf16[128,1024]{1,0:T(8,128)(2,1)} collective-permute-done((bf16[128,1024]{1,0:T(8,128)(2,1)}, bf16[128,1024]{1,0:T(8,128)(2,1)}, u32[]{:S(2)}, u32[]{:S(2)}) %collective-permute-start.4) | collective-permute-done | bytes 262176 | tf_op jit(solution)/shard_map/ppermute | solution.py:292
  40.8 2.7 %shard_map.77 = (bf16[8,128,1024]{2,1,0:T(8,128)(2,1)S(1)}, bf16[2,128,896]{2,1,0:T(8,128)(2,1)S(1)}, bf16[2,128,896]{2,1,0:T(8,128)(2,1)S(1)}) custom-call(s32[10]{0:T(128)S(1)} %dynamic-slice_bitcast_fusion.facts_ref, bf16[256,1024]{1,0:T(8,128)(2,1)S(1)} %pad_maximum_fusion.t0, bf16[256,1024]{1,0:T(8,128)(2,1)} %collective-permute-done.1.t1, ...), custom_call_target="tpu_custom_call" | custom-call | flops 939524096 | bytes 7340032 | tf_op jit(solution)/shard_map/pallas_call | solution.py:116
  43.5 0.6 collective-permute-start.14
  44.2 0.9 collective-permute-start.15
  45.1 3.6 %shard_map.78 = (bf16[2,128,896]{2,1,0:T(8,128)(2,1)S(1)}, bf16[2,128,896]{2,1,0:T(8,128)(2,1)S(1)}, bf16[2,128,896]{2,1,0:T(8,128)(2,1)S(1)}, bf16[2,128,896]{2,1,0:T(8,128)(2,1)S(1)}) custom-call(bf16[8,128,1024]{2,1,0:T(8,128)(2,1)S(1)} %get-tuple-element.27.lhs_ref, bf16[896,512]{1,0:T(8,128)(2,1)S(1)} %fusion.w_own_ref, ...), custom_call_target="tpu_custom_call" | custom-call | flops 1879048192 | bytes 6291456 | tf_op jit(solution)/shard_map/pallas_call | solution.py:137
  48.6 1.4 %collective-permute-start.10 = (bf16[2,128,896]{2,1,0:T(8,128)(2,1)S(1)}, bf16[2,128,896]{2,1,0:T(8,128)(2,1)S(1)}, u32[]{:S(2)}, u32[]{:S(2)}) collective-permute-start(bf16[2,128,896]{2,1,0:T(8,128)(2,1)S(1)} %get-tuple-element.29), channel_id=1, source_target_pairs={{0,2},{2,4},{4,6},{6,0},{1,3},{3,5},{5,7},{7,1},{8,10},{10,12},{12... | collective-permute-start | bytes 1376264 | tf_op jit(solution)/shard_map/ppermute | solution.py:71
  50.0 2.6 %collective-permute-start.11 = (bf16[2,128,896]{2,1,0:T(8,128)(2,1)S(1)}, bf16[2,128,896]{2,1,0:T(8,128)(2,1)S(1)}, u32[]{:S(2)}, u32[]{:S(2)}) collective-permute-start(bf16[2,128,896]{2,1,0:T(8,128)(2,1)S(1)} %get-tuple-element.30), channel_id=1, source_target_pairs={{0,4},{2,6},{4,0},{6,2},{1,5},{3,7},{5,1},{7,3},{8,12},{10,14},{12... | collective-permute-start | bytes 1376264 | tf_op jit(solution)/shard_map/ppermute | solution.py:71
  52.6 1.1 collective-permute-start.12
  53.7 2.3 %shard_map.80 = (bf16[2,128,896]{2,1,0:T(8,128)(2,1)S(1)}, bf16[2,128,896]{2,1,0:T(8,128)(2,1)S(1)}) custom-call(bf16[8,128,1024]{2,1,0:T(8,128)(2,1)S(1)} %get-tuple-element.27.lhs_ref, bf16[768,512]{1,0:T(8,128)(2,1)S(1)} %collective-permute-done.5.refs_0_, bf16[128,512]{1,0:T(8,128)(2,1)} %collective-permute-done.6.refs_1_, ...), custom_call_target="tpu_custom_call" | custom-call | flops 939524096 | bytes 4194304 | tf_op jit(solution)/shard_map/pallas_call | solution.py:158
  56.0 5.8 %collective-permute-done.15.refs_3_ = bf16[2,128,896]{2,1,0:T(8,128)(2,1)S(1)} collective-permute-done((bf16[2,128,896]{2,1,0:T(8,128)(2,1)S(1)}, bf16[2,128,896]{2,1,0:T(8,128)(2,1)S(1)}, u32[]{:S(2)}, u32[]{:S(2)}) %collective-permute-start.15) | collective-permute-done | bytes 458784 | tf_op jit(solution)/shard_map/ppermute | solution.py:71
  61.8 0.2 shard_map.81
  62.0 1.4 %collective-permute-start.16 = (bf16[128,896]{1,0:T(8,128)(2,1)S(1)}, bf16[128,896]{1,0:T(8,128)(2,1)S(1)}, u32[]{:S(2)}, u32[]{:S(2)}) collective-permute-start(bf16[128,896]{1,0:T(8,128)(2,1)S(1)} %get-tuple-element.39), channel_id=1, source_target_pairs={{0,2},{2,4},{4,6},{6,0},{1,3},{3,5},{5,7},{7,1},{8,10},{10,12},{12... | collective-permute-start | bytes 688136 | tf_op jit(solution)/shard_map/ppermute | solution.py:71
  63.4 2.6 %collective-permute-start.17 = (bf16[128,896]{1,0:T(8,128)(2,1)S(1)}, bf16[128,896]{1,0:T(8,128)(2,1)S(1)}, u32[]{:S(2)}, u32[]{:S(2)}) collective-permute-start(bf16[128,896]{1,0:T(8,128)(2,1)S(1)} %get-tuple-element.40), channel_id=1, source_target_pairs={{0,4},{2,6},{4,0},{6,2},{1,5},{3,7},{5,1},{7,3},{8,12},{10,14},{12... | collective-permute-start | bytes 688136 | tf_op jit(solution)/shard_map/ppermute | solution.py:71
  66.0 1.1 collective-permute-start.18
  67.1 1.7 %collective-permute-done.11.refs_2_ = bf16[2,128,896]{2,1,0:T(8,128)(2,1)S(1)} collective-permute-done((bf16[2,128,896]{2,1,0:T(8,128)(2,1)S(1)}, bf16[2,128,896]{2,1,0:T(8,128)(2,1)S(1)}, u32[]{:S(2)}, u32[]{:S(2)}) %collective-permute-start.11) | collective-permute-done | bytes 458784 | tf_op jit(solution)/shard_map/ppermute | solution.py:71
  68.8 4.7 %collective-permute-done.12.refs_3_ = bf16[2,128,896]{2,1,0:T(8,128)(2,1)S(1)} collective-permute-done((bf16[2,128,896]{2,1,0:T(8,128)(2,1)S(1)}, bf16[2,128,896]{2,1,0:T(8,128)(2,1)S(1)}, u32[]{:S(2)}, u32[]{:S(2)}) %collective-permute-start.12) | collective-permute-done | bytes 458784 | tf_op jit(solution)/shard_map/ppermute | solution.py:71
  73.5 0.2 shard_map.79
  73.7 0.6 collective-permute-start.13
  74.4 3.9 %collective-permute-done.17.refs_4_ = bf16[128,896]{1,0:T(8,128)(2,1)S(1)} collective-permute-done((bf16[128,896]{1,0:T(8,128)(2,1)S(1)}, bf16[128,896]{1,0:T(8,128)(2,1)S(1)}, u32[]{:S(2)}, u32[]{:S(2)}) %collective-permute-start.17) | collective-permute-done | bytes 229408 | tf_op jit(solution)/shard_map/ppermute | solution.py:71
  78.3 2.6 %collective-permute-done.18.refs_5_ = bf16[128,896]{1,0:T(8,128)(2,1)S(1)} collective-permute-done((bf16[128,896]{1,0:T(8,128)(2,1)S(1)}, bf16[128,896]{1,0:T(8,128)(2,1)S(1)}, u32[]{:S(2)}, u32[]{:S(2)}) %collective-permute-start.18) | collective-permute-done | bytes 229408 | tf_op jit(solution)/shard_map/ppermute | solution.py:71
  80.9 0.7 shard_map.82
  81.6 5.0 %collective-permute-start.19 = (bf16[128,896]{1,0:T(8,128)(2,1)S(1)}, bf16[128,896]{1,0:T(8,128)(2,1)S(1)}, u32[]{:S(2)}, u32[]{:S(2)}) collective-permute-start(bf16[128,896]{1,0:T(8,128)(2,1)S(1)} %get-tuple-element.42), channel_id=1, source_target_pairs={{0,160},{1,96},{2,224},{3,32},{4,161},{5,97},{6,225},{7,33},{8,0},... | collective-permute-start | bytes 688136 | tf_op jit(solution)/shard_map/ppermute | solution.py:306
  86.7 6.8 %collective-permute-start.20 = (bf16[128,896]{1,0:T(8,128)(2,1)S(1)}, bf16[128,896]{1,0:T(8,128)(2,1)S(1)}, u32[]{:S(2)}, u32[]{:S(2)}) collective-permute-start(bf16[128,896]{1,0:T(8,128)(2,1)S(1)} %get-tuple-element.43), channel_id=1, source_target_pairs={{0,161},{1,97},{2,225},{3,33},{4,160},{5,96},{6,224},{7,32},{8,1},... | collective-permute-start | bytes 688136 | tf_op jit(solution)/shard_map/ppermute | solution.py:306
  93.5 0.4 shard_map.83
  93.9 12.9 %collective-permute-done.20.second = bf16[128,896]{1,0:T(8,128)(2,1)S(1)} collective-permute-done((bf16[128,896]{1,0:T(8,128)(2,1)S(1)}, bf16[128,896]{1,0:T(8,128)(2,1)S(1)}, u32[]{:S(2)}, u32[]{:S(2)}) %collective-permute-start.20) | collective-permute-done | bytes 229408 | tf_op jit(solution)/shard_map/ppermute | solution.py:306
  106.8 1.6 %shard_map.84 = (bf16[256,896]{1,0:T(8,128)(2,1)}, bf16[256,896]{1,0:T(8,128)(2,1)}) custom-call(s32[10]{0:T(128)S(1)} %dynamic-slice_bitcast_fusion.facts_ref, bf16[128,896]{1,0:T(8,128)(2,1)S(1)} %collective-permute-done.19.first, bf16[128,896]{1,0:T(8,128)(2,1)S(1)} %collective-permute-done.20.second, f32[256,896]{1,0:T(8,128)S(1)} %get-tuple-element.44.for_up_ref, ...), custom_call_target="tpu_custom_call" | custom-call | flops 458752 | bytes 2752512 | tf_op jit(solution)/shard_map/pallas_call | solution.py:264
  (18 shorter events, 0.0 us)
Async XLA Ops:
  0.6 1.2 %copy-start.2 = (bf16[896,512]{1,0:T(8,128)(2,1)S(1)}, bf16[896,512]{1,0:T(8,128)(2,1)}, u32[]{:S(2)}) copy-start(bf16[896,512]{1,0:T(8,128)(2,1)} %param.7) | copy-start | bytes 2752516
  1.8 1.6 %copy-start.3 = (bf16[256,512]{1,0:T(8,128)(2,1)S(1)}, bf16[256,512]{1,0:T(8,128)(2,1)}, u32[]{:S(2)}) copy-start(bf16[256,512]{1,0:T(8,128)(2,1)} %param.6) | copy-start | bytes 786436
  2.3 20.0 %collective-permute-start.5 = (bf16[768,512]{1,0:T(8,128)(2,1)S(1)}, bf16[768,512]{1,0:T(8,128)(2,1)S(1)}, u32[]{:S(2)}, u32[]{:S(2)}) collective-permute-start(bf16[768,512]{1,0:T(8,128)(2,1)S(1)} %slice.9), channel_id=1, source_target_pairs={{0,16},{16,0},{1,17},{17,1},{2,18},{18,2},{3,19},{19,3},{4,20},{20... | collective-permute-start | bytes 2359304 | tf_op jit(solution)/shard_map/ppermute | solution.py:71
  3.5 2.1 %collective-permute-start = (bf16[256,512]{1,0:T(8,128)(2,1)S(1)}, bf16[256,512]{1,0:T(8,128)(2,1)S(1)}, u32[]{:S(2)}, u32[]{:S(2)}) collective-permute-start(bf16[256,512]{1,0:T(8,128)(2,1)S(1)} %copy-done.3), channel_id=1, source_target_pairs={{0,1},{1,0},{2,3},{3,2},{4,5},{5,4},{6,7},{7,6},{8,9},{9,8},{10,11... | collective-permute-start | bytes 786440 | tf_op jit(solution)/shard_map/ppermute | solution.py:71
  5.6 18.2 %collective-permute-start.2 = (bf16[256,1024]{1,0:T(8,128)(2,1)S(1)}, bf16[256,1024]{1,0:T(8,128)(2,1)S(1)}, u32[]{:S(2)}, u32[]{:S(2)}) collective-permute-start(bf16[256,1024]{1,0:T(8,128)(2,1)S(1)} %pad_maximum_fusion.t0), channel_id=1, source_target_pairs={{0,64},{32,96},{64,128},{96,160},{128,192},{160,224},{192,0},{224,... | collective-permute-start | bytes 1572872 | tf_op jit(solution)/shard_map/ppermute | solution.py:287
  11.7 18.3 %collective-permute-start.1 = (bf16[256,1024]{1,0:T(8,128)(2,1)S(1)}, bf16[256,1024]{1,0:T(8,128)(2,1)}, u32[]{:S(2)}, u32[]{:S(2)}) collective-permute-start(bf16[256,1024]{1,0:T(8,128)(2,1)S(1)} %pad_maximum_fusion.t0), channel_id=1, source_target_pairs={{0,32},{32,64},{64,96},{96,128},{128,160},{160,192},{192,224},{224... | collective-permute-start | bytes 1572872 | tf_op jit(solution)/shard_map/ppermute | solution.py:288
  12.5 32.6 %collective-permute-start.9 = (bf16[896,512]{1,0:T(8,128)(2,1)S(1)}, bf16[896,512]{1,0:T(8,128)(2,1)}, u32[]{:S(2)}, u32[]{:S(2)}) collective-permute-start(bf16[896,512]{1,0:T(8,128)(2,1)S(1)} %fusion.w_own_ref), channel_id=1, source_target_pairs={{0,1},{1,0},{2,3},{3,2},{4,5},{5,4},{6,7},{7,6},{8,9},{9,8},{10,11... | collective-permute-start | bytes 2752520 | tf_op jit(solution)/shard_map/ppermute | solution.py:71
  22.3 18.5 %collective-permute-start.7 = (bf16[768,512]{1,0:T(8,128)(2,1)S(1)}, bf16[768,512]{1,0:T(8,128)(2,1)S(1)}, u32[]{:S(2)}, u32[]{:S(2)}) collective-permute-start(bf16[768,512]{1,0:T(8,128)(2,1)S(1)} %collective-permute-done.5.refs_0_), channel_id=1, source_target_pairs={{0,1},{1,0},{2,3},{3,2},{4,5},{5,4},{6,7},{7,6},{8,9},{9,8},{10,11... | collective-permute-start | bytes 2359304 | tf_op jit(solution)/shard_map/ppermute | solution.py:71
  23.8 17.0 %collective-permute-start.3 = (bf16[256,1024]{1,0:T(8,128)(2,1)S(1)}, bf16[256,1024]{1,0:T(8,128)(2,1)}, u32[]{:S(2)}, u32[]{:S(2)}) collective-permute-start(bf16[256,1024]{1,0:T(8,128)(2,1)S(1)} %collective-permute-done.2.t2), channel_id=1, source_target_pairs={{0,32},{32,64},{64,96},{96,128},{128,160},{160,192},{192,224},{224... | collective-permute-start | bytes 1572872 | tf_op jit(solution)/shard_map/ppermute | solution.py:291
  30.0 6.5 %collective-permute-start.6 = (bf16[128,512]{1,0:T(8,128)(2,1)}, bf16[128,512]{1,0:T(8,128)(2,1)}, u32[]{:S(2)}, u32[]{:S(2)}) collective-permute-start(bf16[128,512]{1,0:T(8,128)(2,1)} %slice.8), channel_id=1, source_target_pairs={{0,16},{16,0},{1,17},{17,1},{2,18},{18,2},{3,19},{19,3},{4,20},{20... | collective-permute-start | bytes 393224 | tf_op jit(solution)/shard_map/ppermute | solution.py:71
  31.9 8.9 %collective-permute-start.4 = (bf16[128,1024]{1,0:T(8,128)(2,1)}, bf16[128,1024]{1,0:T(8,128)(2,1)}, u32[]{:S(2)}, u32[]{:S(2)}) collective-permute-start(bf16[128,1024]{1,0:T(8,128)(2,1)} %constant_dynamic-slice_fusion), channel_id=1, source_target_pairs={{0,64},{32,96},{64,128},{96,160},{128,192},{160,224},{192,0},{224,... | collective-permute-start | bytes 786440 | tf_op jit(solution)/shard_map/ppermute | solution.py:292
  36.5 2.6 %collective-permute-start.8 = (bf16[128,512]{1,0:T(8,128)(2,1)}, bf16[128,512]{1,0:T(8,128)(2,1)}, u32[]{:S(2)}, u32[]{:S(2)}) collective-permute-start(bf16[128,512]{1,0:T(8,128)(2,1)} %collective-permute-done.6.refs_1_), channel_id=1, source_target_pairs={{0,1},{1,0},{2,3},{3,2},{4,5},{5,4},{6,7},{7,6},{8,9},{9,8},{10,11... | collective-permute-start | bytes 393224 | tf_op jit(solution)/shard_map/ppermute | solution.py:71
  43.5 12.4 %collective-permute-start.14 = (bf16[2,128,896]{2,1,0:T(8,128)(2,1)S(1)}, bf16[2,128,896]{2,1,0:T(8,128)(2,1)S(1)}, u32[]{:S(2)}, u32[]{:S(2)}) collective-permute-start(bf16[2,128,896]{2,1,0:T(8,128)(2,1)S(1)} %get-tuple-element.36), channel_id=1, source_target_pairs={{0,8},{8,0},{1,9},{9,1},{2,10},{10,2},{3,11},{11,3},{4,12},{12,4},... | collective-permute-start | bytes 1376264 | tf_op jit(solution)/shard_map/ppermute | solution.py:71
  44.2 17.6 %collective-permute-start.15 = (bf16[2,128,896]{2,1,0:T(8,128)(2,1)S(1)}, bf16[2,128,896]{2,1,0:T(8,128)(2,1)S(1)}, u32[]{:S(2)}, u32[]{:S(2)}) collective-permute-start(bf16[2,128,896]{2,1,0:T(8,128)(2,1)S(1)} %get-tuple-element.37), channel_id=1, source_target_pairs={{0,8},{8,0},{1,9},{9,1},{2,10},{10,2},{3,11},{11,3},{4,12},{12,4},... | collective-permute-start | bytes 1376264 | tf_op jit(solution)/shard_map/ppermute | solution.py:71
  48.6 17.4 %collective-permute-start.10 = (bf16[2,128,896]{2,1,0:T(8,128)(2,1)S(1)}, bf16[2,128,896]{2,1,0:T(8,128)(2,1)S(1)}, u32[]{:S(2)}, u32[]{:S(2)}) collective-permute-start(bf16[2,128,896]{2,1,0:T(8,128)(2,1)S(1)} %get-tuple-element.29), channel_id=1, source_target_pairs={{0,2},{2,4},{4,6},{6,0},{1,3},{3,5},{5,7},{7,1},{8,10},{10,12},{12... | collective-permute-start | bytes 1376264 | tf_op jit(solution)/shard_map/ppermute | solution.py:71
  50.0 18.8 %collective-permute-start.11 = (bf16[2,128,896]{2,1,0:T(8,128)(2,1)S(1)}, bf16[2,128,896]{2,1,0:T(8,128)(2,1)S(1)}, u32[]{:S(2)}, u32[]{:S(2)}) collective-permute-start(bf16[2,128,896]{2,1,0:T(8,128)(2,1)S(1)} %get-tuple-element.30), channel_id=1, source_target_pairs={{0,4},{2,6},{4,0},{6,2},{1,5},{3,7},{5,1},{7,3},{8,12},{10,14},{12... | collective-permute-start | bytes 1376264 | tf_op jit(solution)/shard_map/ppermute | solution.py:71
  52.6 20.9 %collective-permute-start.12 = (bf16[2,128,896]{2,1,0:T(8,128)(2,1)S(1)}, bf16[2,128,896]{2,1,0:T(8,128)(2,1)S(1)}, u32[]{:S(2)}, u32[]{:S(2)}) collective-permute-start(bf16[2,128,896]{2,1,0:T(8,128)(2,1)S(1)} %get-tuple-element.31), channel_id=1, source_target_pairs={{0,6},{2,0},{4,2},{6,4},{1,7},{3,1},{5,3},{7,5},{8,14},{10,8},{12,... | collective-permute-start | bytes 1376264 | tf_op jit(solution)/shard_map/ppermute | solution.py:71
  62.0 31.5 %copy-start = (bf16[256,896]{1,0:T(8,128)(2,1)S(1)}, bf16[256,896]{1,0:T(8,128)(2,1)}, u32[]{:S(2)}) copy-start(bf16[256,896]{1,0:T(8,128)(2,1)} %gate_ref.1) | copy-start | bytes 1376260
  62.0 31.5 %copy-start.1 = (bf16[256,896]{1,0:T(8,128)(2,1)S(1)}, bf16[256,896]{1,0:T(8,128)(2,1)}, u32[]{:S(2)}) copy-start(bf16[256,896]{1,0:T(8,128)(2,1)} %up_ref.1) | copy-start | bytes 1376260
  62.0 12.4 %collective-permute-start.16 = (bf16[128,896]{1,0:T(8,128)(2,1)S(1)}, bf16[128,896]{1,0:T(8,128)(2,1)S(1)}, u32[]{:S(2)}, u32[]{:S(2)}) collective-permute-start(bf16[128,896]{1,0:T(8,128)(2,1)S(1)} %get-tuple-element.39), channel_id=1, source_target_pairs={{0,2},{2,4},{4,6},{6,0},{1,3},{3,5},{5,7},{7,1},{8,10},{10,12},{12... | collective-permute-start | bytes 688136 | tf_op jit(solution)/shard_map/ppermute | solution.py:71
  63.4 14.9 %collective-permute-start.17 = (bf16[128,896]{1,0:T(8,128)(2,1)S(1)}, bf16[128,896]{1,0:T(8,128)(2,1)S(1)}, u32[]{:S(2)}, u32[]{:S(2)}) collective-permute-start(bf16[128,896]{1,0:T(8,128)(2,1)S(1)} %get-tuple-element.40), channel_id=1, source_target_pairs={{0,4},{2,6},{4,0},{6,2},{1,5},{3,7},{5,1},{7,3},{8,12},{10,14},{12... | collective-permute-start | bytes 688136 | tf_op jit(solution)/shard_map/ppermute | solution.py:71
  66.0 14.9 %collective-permute-start.18 = (bf16[128,896]{1,0:T(8,128)(2,1)S(1)}, bf16[128,896]{1,0:T(8,128)(2,1)S(1)}, u32[]{:S(2)}, u32[]{:S(2)}) collective-permute-start(bf16[128,896]{1,0:T(8,128)(2,1)S(1)} %get-tuple-element.41), channel_id=1, source_target_pairs={{0,6},{2,0},{4,2},{6,4},{1,7},{3,1},{5,3},{7,5},{8,14},{10,8},{12,... | collective-permute-start | bytes 688136 | tf_op jit(solution)/shard_map/ppermute | solution.py:71
  73.7 7.1 %collective-permute-start.13 = (bf16[128,896]{1,0:T(8,128)(2,1)S(1)}, bf16[128,896]{1,0:T(8,128)(2,1)S(1)}, u32[]{:S(2)}, u32[]{:S(2)}) collective-permute-start(bf16[128,896]{1,0:T(8,128)(2,1)S(1)} %get-tuple-element.33), channel_id=1, source_target_pairs={{0,8},{8,0},{1,9},{9,1},{2,10},{10,2},{3,11},{11,3},{4,12},{12,4},... | collective-permute-start | bytes 688136 | tf_op jit(solution)/shard_map/ppermute | solution.py:71
  81.6 12.2 %collective-permute-start.19 = (bf16[128,896]{1,0:T(8,128)(2,1)S(1)}, bf16[128,896]{1,0:T(8,128)(2,1)S(1)}, u32[]{:S(2)}, u32[]{:S(2)}) collective-permute-start(bf16[128,896]{1,0:T(8,128)(2,1)S(1)} %get-tuple-element.42), channel_id=1, source_target_pairs={{0,160},{1,96},{2,224},{3,32},{4,161},{5,97},{6,225},{7,33},{8,0},... | collective-permute-start | bytes 688136 | tf_op jit(solution)/shard_map/ppermute | solution.py:306
  86.7 20.1 %collective-permute-start.20 = (bf16[128,896]{1,0:T(8,128)(2,1)S(1)}, bf16[128,896]{1,0:T(8,128)(2,1)S(1)}, u32[]{:S(2)}, u32[]{:S(2)}) collective-permute-start(bf16[128,896]{1,0:T(8,128)(2,1)S(1)} %get-tuple-element.43), channel_id=1, source_target_pairs={{0,161},{1,97},{2,225},{3,33},{4,160},{5,96},{6,224},{7,32},{8,1},... | collective-permute-start | bytes 688136 | tf_op jit(solution)/shard_map/ppermute | solution.py:306
